TPU v7x, 128 devices: a whole 4x4x4 slice. The times are simulated.
128 devices in a mesh: frames: 4 (over z_lo, core), rows: 32 (over z_hi, y, x).
Axes of the slice: x: 4, y: 4, z: 4 (z_hi: 2, z_lo: 2; z = z_hi * 2 + z_lo), core: 2. Of those that a mesh axis runs over, the one named last changes fastest.
Arguments:
- clip_in: bfloat16 [16, 128, 64, 256], P('frames', 'rows'), may hold values from -6 to 6
- kernel_one: bfloat16 [3, 3, 3, 64, 64], replicated, may hold values from -0.15625 to 0.15625
- bias_one: float32 [64], replicated, may hold values from -3 to 3
- kernel_two: bfloat16 [3, 3, 3, 64, 64], replicated, may hold values from -0.3125 to 0.3125
- cotangent: bfloat16 [16, 128, 64, 256], P('frames', 'rows'), may hold values from -6 to 6
Outputs:
- block_out: bfloat16 [16, 128, 64, 256], P('frames', 'rows')
- grad_input: bfloat16 [16, 128, 64, 256], P('frames', 'rows')
- grad_first: float32 [3, 3, 3, 64, 64], replicated
- grad_second: float32 [3, 3, 3, 64, 64], replicated
- grad_bias: float32 [64], replicated
All inputs are finite; a program needn't handle non-finite values.
Results may differ from a plain program's by a relative error of at most 0.0065.
Values may be sent and summed in bfloat16 or wider, within the bound.
No kernel may reach another device: no remote copies, remote signals or barrier semaphores. Data moves between devices by JAX's collectives and lax.ppermute only.
A program may use at most 64 MiB of HBM per device.

v0:
```python
import math

import jax
import jax.numpy as jnp
from jax import lax
from jax.sharding import PartitionSpec as P


def with_halo(block, sides, width):
    for axis, dim in sides:
        count = lax.axis_size(axis)
        forward = [(i, i + 1) for i in range(count - 1)]
        backward = [(target, source) for source, target in forward]
        low = lax.ppermute(
            lax.slice_in_dim(block, block.shape[dim] - width, None, axis=dim), axis, forward
        )
        high = lax.ppermute(lax.slice_in_dim(block, 0, width, axis=dim), axis, backward)
        block = jnp.concatenate([low, block, high], axis=dim)
    return block


def passed_along(value, axis, by):
    devices = lax.axis_size(axis)
    pairs = [(i, i + by) for i in range(devices) if 0 <= i + by < devices]
    return lax.ppermute(value, axis, pairs)


def extend_rows(field):
    return with_halo(field, (("rows", 1),), 1)


def with_prior(field):
    earlier = passed_along(field[-2:], "frames", 1)
    return jnp.concatenate([earlier, field], axis=0)


def with_later(field):
    following = passed_along(field[:2], "frames", -1)
    return jnp.concatenate([field, following], axis=0)


def spatial_taps(extended, row_count, col_count, flipped):
    padded = jnp.pad(extended, ((0, 0), (0, 0), (0, 0), (1, 1)))
    pieces = []
    for i in range(3):
        for j in range(3):
            row_start = 2 - i if flipped else i
            col_start = 2 - j if flipped else j
            pieces.append(
                padded[:, row_start : row_start + row_count, :, col_start : col_start + col_count]
            )
    return jnp.concatenate(pieces, axis=2)


def forward_conv(extended, kernel, frame_count, row_count, col_count):
    taps = spatial_taps(extended, row_count, col_count, False)
    chan_out = kernel.shape[3]
    running = None
    for t in range(3):
        flat_kernel = jnp.transpose(kernel[t], (2, 0, 1, 3)).reshape((chan_out, -1))
        term = jnp.einsum(
            "ok,frkw->frow",
            flat_kernel,
            taps[t : t + frame_count],
            preferred_element_type=jnp.float32,
        )
        running = term if running is None else running + term
    return running


def adjoint_conv(extended, kernel, frame_count, row_count, col_count):
    taps = spatial_taps(extended, row_count, col_count, True)
    chan_in = kernel.shape[4]
    running = None
    for t in range(3):
        flat_kernel = jnp.transpose(kernel[t], (3, 0, 1, 2)).reshape((chan_in, -1))
        term = jnp.einsum(
            "ck,frkw->frcw",
            flat_kernel,
            taps[2 - t : 2 - t + frame_count],
            preferred_element_type=jnp.float32,
        )
        running = term if running is None else running + term
    return running


def kernel_grad(upstream, extended):
    frame_count, row_count, chan_out, col_count = upstream.shape
    chan_in = extended.shape[2]
    taps = spatial_taps(extended, row_count, col_count, False)
    pieces = []
    for t in range(3):
        flat = jnp.einsum(
            "frow,frkw->ok", upstream, taps[t : t + frame_count], preferred_element_type=jnp.float32
        )
        pieces.append(jnp.transpose(flat.reshape((chan_out, 3, 3, chan_in)), (1, 2, 0, 3)))
    return jnp.stack(pieces, axis=0)


def per_device(clip_in, kernel_one, bias_one, kernel_two, cotangent):
    frame_count, row_count, channels, col_count = clip_in.shape
    input_rows = extend_rows(clip_in)
    cot_rows = None
    input_ext = with_prior(input_rows)
    hidden = (
        forward_conv(input_ext, kernel_one, frame_count, row_count, col_count)
        + bias_one[None, None, :, None]
    )
    active = jax.nn.silu(hidden).astype(jnp.bfloat16)
    active_ext = with_prior(extend_rows(active))
    block_out = (
        clip_in.astype(jnp.float32)
        + forward_conv(active_ext, kernel_two, frame_count, row_count, col_count)
    ).astype(jnp.bfloat16)
    cot_rows = extend_rows(cotangent)
    cot_ext = with_later(cot_rows)
    grad_act = adjoint_conv(cot_ext, kernel_two, frame_count, row_count, col_count)
    sig = jax.nn.sigmoid(hidden)
    grad_pre = (grad_act * sig * (1.0 + hidden * (1.0 - sig))).astype(jnp.bfloat16)
    pre_ext = with_later(extend_rows(grad_pre))
    grad_back = adjoint_conv(pre_ext, kernel_one, frame_count, row_count, col_count)
    grad_input = (cotangent.astype(jnp.float32) + grad_back).astype(jnp.bfloat16)
    term_second = kernel_grad(cotangent, active_ext)
    term_first = kernel_grad(grad_pre, input_ext)
    term_bias = jnp.sum(grad_pre.astype(jnp.float32), axis=(0, 1, 3))
    total_first, total_second, total_bias = lax.psum(
        (term_first, term_second, term_bias), ("frames", "rows")
    )
    cell_total = (
        frame_count * lax.axis_size("frames") * row_count * lax.axis_size("rows") * col_count
    )
    inv_scale = 1.0 / math.sqrt(cell_total)
    return (
        block_out,
        grad_input,
        total_first * inv_scale,
        total_second * inv_scale,
        total_bias * inv_scale,
    )


def solution(mesh):
    in_specs = (P("frames", "rows", None, None), P(), P(), P(), P("frames", "rows", None, None))
    out_specs = (P("frames", "rows", None, None), P("frames", "rows", None, None), P(), P(), P())
    return jax.shard_map(
        per_device, mesh=mesh, in_specs=in_specs, out_specs=out_specs, check_vma=False
    )
```

profile of v0, /device:TPU:1, one launch (start us, length us, event | category | flops | bytes accessed | tf_op | source)
XLA Modules:
  0.0 345.2 jit_solution(11832718589891835297)
XLA Ops:
  7.2 1.7 fusion.59
  10.2 5.2 %collective-permute-start = (bf16[4,1,64,256]{3,2,1,0:T(8,128)(2,1)}, bf16[4,1,64,256]{3,2,1,0:T(8,128)(2,1)}, u32[]{:S(2)}, u32[]{:S(2)}) collective-permute-start(bf16[4,1,64,256]{3,2,1,0:T(8,128)(2,1)} %get-tuple-element.19), channel_id=1, source_target_pairs={{0,1},{1,2},{2,3},{3,4},{4,5},{5,6},{6,7},{7,8},{8,9},{9,10},{10,1... | collective-permute-start | bytes 393224 | tf_op jit(solution)/shard_map/ppermute | solution.py:14
  17.8 4.0 %collective-permute-start.6 = (bf16[4,1,64,256]{3,2,1,0:T(8,128)(2,1)S(1)}, bf16[4,1,64,256]{3,2,1,0:T(8,128)(2,1)S(1)}, u32[]{:S(2)}, u32[]{:S(2)}) collective-permute-start(bf16[4,1,64,256]{3,2,1,0:T(8,128)(2,1)S(1)} %get-tuple-element.15), channel_id=1, source_target_pairs={{0,1},{1,2},{2,3},{3,4},{4,5},{5,6},{6,7},{7,8},{8,9},{9,10},{10,1... | collective-permute-start | bytes 393224 | tf_op jit(solution)/shard_map/ppermute | solution.py:14
  21.8 2.0 fusion.60
  24.9 4.4 %collective-permute-start.8 = (bf16[2,6,64,256]{3,2,1,0:T(8,128)(2,1)S(1)}, bf16[2,6,64,256]{3,2,1,0:T(8,128)(2,1)S(1)}, u32[]{:S(2)}, u32[]{:S(2)}) collective-permute-start(bf16[2,6,64,256]{3,2,1,0:T(8,128)(2,1)S(1)} %slice.318), channel_id=1, source_target_pairs={{32,0},{64,32},{96,64},{33,1},{65,33},{97,65},{34,2},{66,34},{98,6... | collective-permute-start | bytes 1179656 | tf_op jit(solution)/shard_map/ppermute | solution.py:25
  29.3 1.9 fusion.61
  34.4 3.6 %collective-permute-start.2 = (bf16[2,6,64,256]{3,2,1,0:T(8,128)(2,1)S(1)}, bf16[2,6,64,256]{3,2,1,0:T(8,128)(2,1)S(1)}, u32[]{:S(2)}, u32[]{:S(2)}) collective-permute-start(bf16[2,6,64,256]{3,2,1,0:T(8,128)(2,1)S(1)} %slice.306), channel_id=1, source_target_pairs={{0,32},{32,64},{64,96},{1,33},{33,65},{65,97},{2,34},{34,66},{66,9... | collective-permute-start | bytes 1179656 | tf_op jit(solution)/shard_map/ppermute | solution.py:25
  42.4 2.6 collective-permute-done.2
  50.7 1.5 convert_reduce_fusion
  53.6 2.1 fusion.2
  55.7 2.1 fusion.4
  57.8 1.8 collective-permute-start.3
  61.0 4.0 %collective-permute-start.9 = (bf16[4,1,64,256]{3,2,1,0:T(8,128)(2,1)S(1)}, bf16[4,1,64,256]{3,2,1,0:T(8,128)(2,1)S(1)}, u32[]{:S(2)}, u32[]{:S(2)}) collective-permute-start(bf16[4,1,64,256]{3,2,1,0:T(8,128)(2,1)S(1)} %get-tuple-element.12), channel_id=1, source_target_pairs={{0,1},{1,2},{2,3},{3,4},{4,5},{5,6},{6,7},{7,8},{8,9},{9,10},{10,1... | collective-permute-start | bytes 393224 | tf_op jit(solution)/shard_map/ppermute | solution.py:14
  66.3 92.7 %psum.23 = f32[64]{0:T(128)S(1)} all-reduce(f32[64]{0:T(128)S(1)} %get-tuple-element.34), channel_id=1, replica_groups=mesh['frames'=4,'rows'=32] {'frames','rows'}, use_global_device_ids=true, to_apply=%region_3.4 | all-reduce | flops 64 | bytes 512 | tf_op jit(solution)/shard_map/psum | solution.py:126
  159.0 3.9 %collective-permute-start.5 = (bf16[2,6,64,256]{3,2,1,0:T(8,128)(2,1)S(1)}, bf16[2,6,64,256]{3,2,1,0:T(8,128)(2,1)S(1)}, u32[]{:S(2)}, u32[]{:S(2)}) collective-permute-start(bf16[2,6,64,256]{3,2,1,0:T(8,128)(2,1)S(1)} %pad_maximum_fusion.7), channel_id=1, source_target_pairs={{0,32},{32,64},{64,96},{1,33},{33,65},{65,97},{2,34},{34,66},{66,9... | collective-permute-start | bytes 1179656 | tf_op jit(solution)/shard_map/ppermute | solution.py:25
  163.5 2.1 pad_maximum_fusion.3
  166.4 2.1 collective-permute-start.11
  175.9 4.4 %fusion.64 = f32[4,4,256,64]{2,3,1,0:T(8,128)} fusion(bf16[6,4,576,256]{3,2,1,0:T(8,128)(2,1)} %copy-done, bf16[64,576,1,1]{0,1,3,2:T(8,128)(2,1)S(1)} %bitcast.194), kind=kOutput, calls=%fused_computation.143 | convolution fusion | flops 301989888 | bytes 8200192 | tf_op jit(solution)/shard_map/ok,frkw->frow/dot_general | solution.py:61
  182.6 2.9 copy-done.1
  186.6 3.9 %convolution_add_fusion.4 = f32[4,4,256,64]{2,3,1,0:T(8,128)S(1)} fusion(f32[4,4,256,64]{2,3,1,0:T(8,128)} %fusion.64, bf16[6,4,576,256]{3,2,1,0:T(8,128)(2,1)} %copy-done, bf16[64,576,1,1]{0,1,3,2:T(8,128)(2,1)S(1)} %bitcast.192), kind=kOutput, calls=%fused_computation.44 | convolution fusion | flops 302252032 | bytes 9248768 | tf_op jit(solution)/shard_map/ok,frkw->frow/dot_general | solution.py:61
  190.4 4.5 %fusion.19 = bf16[4,4,64,256]{3,2,1,0:T(8,128)(2,1)} fusion(f32[4,4,256,64]{2,3,1,0:T(8,128)S(1)} %convolution_add_fusion.4, bf16[6,4,576,256]{3,2,1,0:T(8,128)(2,1)} %copy-done, bf16[64,576,1,1]{0,1,3,2:T(8,128)(2,1)} %bitcast.193, bf16[4,4,64,256]{3,2,1,0:T(8,128)(2,1)S(1)} %copy-done.4), kind=kOutput, calls=%fused_computation.63 | convolution fusion | flops 303038464 | bytes 9248768 | tf_op jit(solution)/shard_map/ok,frkw->frow/dot_general | solution.py:61
  197.1 1.9 fusion.17
  199.0 135.3 %all-reduce.7.cloned.1.call-done = (f32[3,3,3,64,64]{3,4,2,1,0:T(8,128)}, f32[3,3,3,64,64]{3,4,2,1,0:T(8,128)}) async-done(((f32[3,3,3,64,64]{3,4,2,1,0:T(8,128)}, f32[3,3,3,64,64]{3,4,2,1,0:T(8,128)}), (f32[3,3,3,64,64]{3,4,2,1,0:T(8,128)}, f32[3,3,3,64,64]{3,4,2,1,0:T(8,128)})) %all-reduce.7.cloned.1.call-update) | async-done | bytes 884752 | tf_op jit(solution)/shard_map/psum | solution.py:126
  334.3 1.6 broadcast_multiply_fusion
  (120 shorter events, 38.3 us)
Async XLA Ops:
  7.2 27.2 %copy-start.3 = (bf16[4,4,64,256]{3,2,1,0:T(8,128)(2,1)S(1)}, bf16[4,4,64,256]{3,2,1,0:T(8,128)(2,1)}, u32[]{:S(2)}) copy-start(bf16[4,4,64,256]{3,2,1,0:T(8,128)(2,1)} %param.5) | copy-start | bytes 1572868
  7.2 327.1 %all-reduce.7.cloned.1.call-start = ((), (), s32[]{:S(2)}) async-start(), calls=%async_computation | async-start | bytes 3538944 | tf_op jit(solution)/shard_map/psum | solution.py:126
  9.0 25.4 %collective-permute-start.1 = (bf16[4,1,64,256]{3,2,1,0:T(8,128)(2,1)}, bf16[4,1,64,256]{3,2,1,0:T(8,128)(2,1)S(1)}, u32[]{:S(2)}, u32[]{:S(2)}) collective-permute-start(bf16[4,1,64,256]{3,2,1,0:T(8,128)(2,1)} %get-tuple-element.18), channel_id=1, source_target_pairs={{1,0},{2,1},{3,2},{4,3},{5,4},{6,5},{7,6},{8,7},{9,8},{10,9},{11,1... | collective-permute-start | bytes 393224 | tf_op jit(solution)/shard_map/ppermute | solution.py:17
  10.2 23.2 %collective-permute-start = (bf16[4,1,64,256]{3,2,1,0:T(8,128)(2,1)}, bf16[4,1,64,256]{3,2,1,0:T(8,128)(2,1)}, u32[]{:S(2)}, u32[]{:S(2)}) collective-permute-start(bf16[4,1,64,256]{3,2,1,0:T(8,128)(2,1)} %get-tuple-element.19), channel_id=1, source_target_pairs={{0,1},{1,2},{2,3},{3,4},{4,5},{5,6},{6,7},{7,8},{8,9},{9,10},{10,1... | collective-permute-start | bytes 393224 | tf_op jit(solution)/shard_map/ppermute | solution.py:14
  16.5 8.4 %collective-permute-start.7 = (bf16[4,1,64,256]{3,2,1,0:T(8,128)(2,1)S(1)}, bf16[4,1,64,256]{3,2,1,0:T(8,128)(2,1)S(1)}, u32[]{:S(2)}, u32[]{:S(2)}) collective-permute-start(bf16[4,1,64,256]{3,2,1,0:T(8,128)(2,1)S(1)} %get-tuple-element.14), channel_id=1, source_target_pairs={{1,0},{2,1},{3,2},{4,3},{5,4},{6,5},{7,6},{8,7},{9,8},{10,9},{11,1... | collective-permute-start | bytes 393224 | tf_op jit(solution)/shard_map/ppermute | solution.py:17
  17.8 6.0 %collective-permute-start.6 = (bf16[4,1,64,256]{3,2,1,0:T(8,128)(2,1)S(1)}, bf16[4,1,64,256]{3,2,1,0:T(8,128)(2,1)S(1)}, u32[]{:S(2)}, u32[]{:S(2)}) collective-permute-start(bf16[4,1,64,256]{3,2,1,0:T(8,128)(2,1)S(1)} %get-tuple-element.15), channel_id=1, source_target_pairs={{0,1},{1,2},{2,3},{3,4},{4,5},{5,6},{6,7},{7,8},{8,9},{9,10},{10,1... | collective-permute-start | bytes 393224 | tf_op jit(solution)/shard_map/ppermute | solution.py:14
  24.9 13.1 %collective-permute-start.8 = (bf16[2,6,64,256]{3,2,1,0:T(8,128)(2,1)S(1)}, bf16[2,6,64,256]{3,2,1,0:T(8,128)(2,1)S(1)}, u32[]{:S(2)}, u32[]{:S(2)}) collective-permute-start(bf16[2,6,64,256]{3,2,1,0:T(8,128)(2,1)S(1)} %slice.318), channel_id=1, source_target_pairs={{32,0},{64,32},{96,64},{33,1},{65,33},{97,65},{34,2},{66,34},{98,6... | collective-permute-start | bytes 1179656 | tf_op jit(solution)/shard_map/ppermute | solution.py:25
  34.4 10.5 %collective-permute-start.2 = (bf16[2,6,64,256]{3,2,1,0:T(8,128)(2,1)S(1)}, bf16[2,6,64,256]{3,2,1,0:T(8,128)(2,1)S(1)}, u32[]{:S(2)}, u32[]{:S(2)}) collective-permute-start(bf16[2,6,64,256]{3,2,1,0:T(8,128)(2,1)S(1)} %slice.306), channel_id=1, source_target_pairs={{0,32},{32,64},{64,96},{1,33},{33,65},{65,97},{2,34},{34,66},{66,9... | collective-permute-start | bytes 1179656 | tf_op jit(solution)/shard_map/ppermute | solution.py:25
  46.9 2.5 copy-start.8
  47.0 2.5 copy-start.10
  48.4 2.4 copy-start.9
  57.8 101.2 %collective-permute-start.3 = (bf16[4,1,64,256]{3,2,1,0:T(8,128)(2,1)S(1)}, bf16[4,1,64,256]{3,2,1,0:T(8,128)(2,1)S(1)}, u32[]{:S(2)}, u32[]{:S(2)}) collective-permute-start(bf16[4,1,64,256]{3,2,1,0:T(8,128)(2,1)S(1)} %get-tuple-element.16), channel_id=1, source_target_pairs={{0,1},{1,2},{2,3},{3,4},{4,5},{5,6},{6,7},{7,8},{8,9},{9,10},{10,1... | collective-permute-start | bytes 393224 | tf_op jit(solution)/shard_map/ppermute | solution.py:14
  59.6 99.3 %collective-permute-start.4 = (bf16[4,1,64,256]{3,2,1,0:T(8,128)(2,1)S(1)}, bf16[4,1,64,256]{3,2,1,0:T(8,128)(2,1)S(1)}, u32[]{:S(2)}, u32[]{:S(2)}) collective-permute-start(bf16[4,1,64,256]{3,2,1,0:T(8,128)(2,1)S(1)} %get-tuple-element.17), channel_id=1, source_target_pairs={{1,0},{2,1},{3,2},{4,3},{5,4},{6,5},{7,6},{8,7},{9,8},{10,9},{11,1... | collective-permute-start | bytes 393224 | tf_op jit(solution)/shard_map/ppermute | solution.py:17
  61.0 104.6 %collective-permute-start.9 = (bf16[4,1,64,256]{3,2,1,0:T(8,128)(2,1)S(1)}, bf16[4,1,64,256]{3,2,1,0:T(8,128)(2,1)S(1)}, u32[]{:S(2)}, u32[]{:S(2)}) collective-permute-start(bf16[4,1,64,256]{3,2,1,0:T(8,128)(2,1)S(1)} %get-tuple-element.12), channel_id=1, source_target_pairs={{0,1},{1,2},{2,3},{3,4},{4,5},{5,6},{6,7},{7,8},{8,9},{9,10},{10,1... | collective-permute-start | bytes 393224 | tf_op jit(solution)/shard_map/ppermute | solution.py:14
  65.0 100.6 %collective-permute-start.10 = (bf16[4,1,64,256]{3,2,1,0:T(8,128)(2,1)S(1)}, bf16[4,1,64,256]{3,2,1,0:T(8,128)(2,1)S(1)}, u32[]{:S(2)}, u32[]{:S(2)}) collective-permute-start(bf16[4,1,64,256]{3,2,1,0:T(8,128)(2,1)S(1)} %get-tuple-element.13), channel_id=1, source_target_pairs={{1,0},{2,1},{3,2},{4,3},{5,4},{6,5},{7,6},{8,7},{9,8},{10,9},{11,1... | collective-permute-start | bytes 393224 | tf_op jit(solution)/shard_map/ppermute | solution.py:17
  159.0 9.4 %collective-permute-start.5 = (bf16[2,6,64,256]{3,2,1,0:T(8,128)(2,1)S(1)}, bf16[2,6,64,256]{3,2,1,0:T(8,128)(2,1)S(1)}, u32[]{:S(2)}, u32[]{:S(2)}) collective-permute-start(bf16[2,6,64,256]{3,2,1,0:T(8,128)(2,1)S(1)} %pad_maximum_fusion.7), channel_id=1, source_target_pairs={{0,32},{32,64},{64,96},{1,33},{33,65},{65,97},{2,34},{34,66},{66,9... | collective-permute-start | bytes 1179656 | tf_op jit(solution)/shard_map/ppermute | solution.py:25
  166.4 13.9 %collective-permute-start.11 = (bf16[2,6,64,256]{3,2,1,0:T(8,128)(2,1)}, bf16[2,6,64,256]{3,2,1,0:T(8,128)(2,1)S(1)}, u32[]{:S(2)}, u32[]{:S(2)}) collective-permute-start(bf16[2,6,64,256]{3,2,1,0:T(8,128)(2,1)} %pad_maximum_fusion.5), channel_id=1, source_target_pairs={{32,0},{64,32},{96,64},{33,1},{65,33},{97,65},{34,2},{66,34},{98,6... | collective-permute-start | bytes 1179656 | tf_op jit(solution)/shard_map/ppermute | solution.py:25
  170.9 3.0 copy-start
  182.6 2.9 copy-start.1
  186.5 8.4 %slice-start = ((s8[7077888]{0:T(1024)(128)(4,1)}), s8[2883584]{0:T(1024)(128)(4,1)S(1)}, s32[]{:S(2)}) async-start(s8[7077888]{0:T(1024)(128)(4,1)} %bitcast.187), calls=%async_computation.1 | async-start | bytes 5767168
  186.5 3.9 %copy-start.4 = (bf16[4,4,64,256]{3,2,1,0:T(8,128)(2,1)S(1)}, bf16[4,4,64,256]{3,2,1,0:T(8,128)(2,1)}, u32[]{:S(2)}) copy-start(bf16[4,4,64,256]{3,2,1,0:T(8,128)(2,1)} %param.5) | copy-start | bytes 1572868
  186.5 8.4 %copy-start.7 = (bf16[1,3,3,64,64]{4,3,2,1,0:T(8,128)(2,1)S(1)}, bf16[1,3,3,64,64]{4,3,2,1,0:T(8,128)(2,1)}, u32[]{:S(2)}) copy-start(bf16[1,3,3,64,64]{4,3,2,1,0:T(8,128)(2,1)} %get-tuple-element.25) | copy-start | bytes 221188
  186.6 8.4 %slice-start.1 = ((s8[7077888]{0:T(1024)(128)(4,1)}), s8[4194304]{0:T(1024)(128)(4,1)S(1)}, s32[]{:S(2)}) async-start(s8[7077888]{0:T(1024)(128)(4,1)} %bitcast.187), calls=%async_computation.2 | async-start | bytes 8388608
  190.4 5.6 %copy-start.6 = (bf16[1,3,3,64,64]{4,3,2,1,0:T(8,128)(2,1)S(1)}, bf16[1,3,3,64,64]{4,3,2,1,0:T(8,128)(2,1)}, u32[]{:S(2)}) copy-start(bf16[1,3,3,64,64]{4,3,2,1,0:T(8,128)(2,1)} %get-tuple-element.24) | copy-start | bytes 221188
  (2 other events, 4.1 us)
Sparse Core Ops, SparseCore 0:
  186.7 147.6 all-reduce.6
where the time goes:
time: 346 us; the launch traced here: 345 us
  waiting for transfers between devices  138 us (40%)
  blocking collectives  92.7 us (27%)
  starting transfers between devices  34.2 us (10%)
  matrix products  33.7 us (10%)
  local copies, waits for them, and re-layouts  25 us (7%)
  between operations  14.8 us (4%)
  other arithmetic  6.87 us (2%)
    psum x1, waiting for transfers between devices, per_device(): lax.psum((term_first, term_second, term_bias), ('frames', 'rows'))  135 us
    psum x1, blocking collectives, per_device(): lax.psum((term_first, term_second, term_bias), ('frames', 'rows'))  92.7 us
    dot_general x6, matrix products, forward_conv(): jnp.einsum('ok,frkw->frow', flat_kernel, taps[t:t + frame_count], preferr...  16.1 us
    ppermute x4, starting transfers between devices, with_halo(): lax.ppermute(lax.slice_in_dim(block, block.shape[dim] - width, None, axis...  15 us
    unnamed x58, local copies, waits for them, and re-layouts  14.3 us
    ppermute x4, starting transfers between devices, passed_along(): return lax.ppermute(value, axis, pairs)  13.9 us
    dot_general x6, matrix products, kernel_grad(): jnp.einsum('frow,frkw->ok', upstream, taps[t:t + frame_count], preferred_...  10 us
    dot_general x6, matrix products, adjoint_conv(): jnp.einsum('ck,frkw->frcw', flat_kernel, taps[2 - t:2 - t + frame_count],...  7.64 us
  transfers between devices with their start and end apart: 13, of which 2 were waited for; matrix products, arithmetic and copies ran while one was open for 12% of the time, Pallas kernels for 0%

commit v1 on v0

v1 whole, which is shorter than its diff:
```python
import math

import jax
import jax.numpy as jnp
from jax import lax
from jax.sharding import PartitionSpec as P

AXES = ("frames", "rows")


def pairs_of(count, first):
    pairs = []
    for i in range(first, count - 1, 2):
        pairs += [(i, i + 1), (i + 1, i)]
    return pairs


def swap_neighbours(axis, to_next, to_prior):
    count = lax.axis_size(axis)
    even = lax.axis_index(axis) % 2 == 0
    odd_pairs = lax.ppermute(jnp.where(even, to_prior, to_next), axis, pairs_of(count, 1))
    even_pairs = lax.ppermute(jnp.where(even, to_next, to_prior), axis, pairs_of(count, 0))
    return jnp.where(even, odd_pairs, even_pairs), jnp.where(even, even_pairs, odd_pairs)


def extend(past, future):
    both = jnp.stack([past, future])
    low, high = swap_neighbours("rows", both[:, :, -1:], both[:, :, :1])
    past_rows, future_rows = jnp.concatenate([low, both, high], axis=2)
    earlier, later = swap_neighbours("frames", past_rows[-2:], future_rows[:2])
    return (
        jnp.concatenate([earlier, past_rows], axis=0),
        jnp.concatenate([future_rows, later], axis=0),
    )


def spatial_taps(extended, row_count, col_count, flipped):
    padded = jnp.pad(extended, ((0, 0), (0, 0), (0, 0), (1, 1)))
    pieces = []
    for i in range(3):
        for j in range(3):
            row_start = 2 - i if flipped else i
            col_start = 2 - j if flipped else j
            pieces.append(
                padded[:, row_start : row_start + row_count, :, col_start : col_start + col_count]
            )
    return jnp.concatenate(pieces, axis=2)


def forward_conv(taps, kernel, frame_count):
    running = None
    for t in range(3):
        flat_kernel = jnp.transpose(kernel[t], (2, 0, 1, 3)).reshape((kernel.shape[3], -1))
        term = jnp.einsum(
            "ok,frkw->frow",
            flat_kernel,
            taps[t : t + frame_count],
            preferred_element_type=jnp.float32,
        )
        running = term if running is None else running + term
    return running


def adjoint_conv(taps, kernel, frame_count):
    running = None
    for t in range(3):
        flat_kernel = jnp.transpose(kernel[t], (3, 0, 1, 2)).reshape((kernel.shape[4], -1))
        term = jnp.einsum(
            "ck,frkw->frcw",
            flat_kernel,
            taps[2 - t : 2 - t + frame_count],
            preferred_element_type=jnp.float32,
        )
        running = term if running is None else running + term
    return running


def total_over_devices(value):
    count = lax.axis_size("frames") * lax.axis_size("rows")
    parts = value.astype(jnp.bfloat16).reshape((count, 16, 128))
    mine = lax.all_to_all(parts, AXES, 0, 0, tiled=True)
    mine = jnp.sum(mine.astype(jnp.float32), axis=0).astype(jnp.bfloat16)
    spread = jnp.broadcast_to(mine[None], parts.shape)
    return lax.all_to_all(spread, AXES, 0, 0, tiled=True).reshape(value.shape).astype(jnp.float32)


def per_device(clip_in, kernel_one, bias_one, kernel_two, cotangent):
    frame_count, row_count, channels, col_count = clip_in.shape
    devices = lax.axis_size("frames") * lax.axis_size("rows")
    input_ext, cot_ext = extend(clip_in, cotangent)
    input_taps = spatial_taps(input_ext, row_count, col_count, False)
    cot_taps = spatial_taps(cot_ext, row_count, col_count, True)
    hidden = forward_conv(input_taps, kernel_one, frame_count) + bias_one[None, None, :, None]
    active = jax.nn.silu(hidden).astype(jnp.bfloat16)
    grad_act = adjoint_conv(cot_taps, kernel_two, frame_count)
    sig = jax.nn.sigmoid(hidden)
    grad_pre = (grad_act * sig * (1.0 + hidden * (1.0 - sig))).astype(jnp.bfloat16)

    first, second = [], []
    for t in range(3):
        part = jnp.einsum(
            "frow,frkw->ok",
            grad_pre,
            input_taps[t : t + frame_count],
            preferred_element_type=jnp.float32,
        )
        first.append(jnp.transpose(part.reshape((channels, 9, channels)), (1, 0, 2)))
        part = jnp.einsum(
            "frkw,frcw->kc",
            cot_taps[2 - t : 2 - t + frame_count],
            active,
            preferred_element_type=jnp.float32,
        )
        second.append(part.reshape((9, channels, channels)))
    bias = jnp.sum(grad_pre.astype(jnp.float32), axis=(0, 1, 3))
    terms = jnp.concatenate([jnp.stack(first), jnp.stack(second)], axis=3)
    terms = terms.reshape((-1, 2 * channels))
    tail = jnp.zeros((devices * 16 - terms.shape[0], 2 * channels), jnp.float32)
    tail = tail.at[0, :channels].set(bias)
    total = total_over_devices(jnp.concatenate([terms, tail], axis=0))

    active_ext, pre_ext = extend(active, grad_pre)
    active_taps = spatial_taps(active_ext, row_count, col_count, False)
    pre_taps = spatial_taps(pre_ext, row_count, col_count, True)
    block_out = (
        clip_in.astype(jnp.float32) + forward_conv(active_taps, kernel_two, frame_count)
    ).astype(jnp.bfloat16)
    grad_back = adjoint_conv(pre_taps, kernel_one, frame_count)
    grad_input = (cotangent.astype(jnp.float32) + grad_back).astype(jnp.bfloat16)

    cell_total = (
        frame_count * lax.axis_size("frames") * row_count * lax.axis_size("rows") * col_count
    )
    total = total * (1.0 / math.sqrt(cell_total))
    count = terms.shape[0]
    return (
        block_out,
        grad_input,
        total[:count, :channels].reshape(kernel_one.shape),
        total[:count, channels:].reshape(kernel_two.shape),
        total[count, :channels],
    )


def solution(mesh):
    in_specs = (P("frames", "rows", None, None), P(), P(), P(), P("frames", "rows", None, None))
    out_specs = (P("frames", "rows", None, None), P("frames", "rows", None, None), P(), P(), P())
    return jax.shard_map(
        per_device, mesh=mesh, in_specs=in_specs, out_specs=out_specs, check_vma=False
    )
```

time: 346 us -> 105 us (0.30)
  waiting for transfers between devices: 138 us -> 15.2 us
  blocking collectives: 92.7 us -> 0 us
  between operations: 14.8 us -> 1.44 us
  matrix products: 33.7 us -> 24.1 us
  local copies, waits for them, and re-layouts: 25 us -> 18.2 us
  other arithmetic: 6.87 us -> 11.3 us
    psum x1 -> x0, waiting for transfers between devices: 135 us -> none  [per_device(): lax.psum((term_first, term_second, term_bias), ('frames', 'rows'))]
    psum x1 -> x0, blocking collectives: 92.7 us -> none  [per_device(): lax.psum((term_first, term_second, term_bias), ('frames', 'rows'))]
    all_to_all x0 -> x2, starting transfers between devices: none -> 21.2 us  [the longest x1 17 us: total_over_devices(): mine = lax.all_to_all(parts, AXES, 0, 0, tiled=True)]
    ppermute x12 -> x8, starting transfers between devices: 34.1 us -> 13 us  [the longest x4 10.3 us: swap_neighbours(): lax.ppermute(jnp.where(even, to_prior, to_next), axis, pairs_of(count, 1))]
    dot_general x6, matrix products: 16.1 us -> 7.37 us  [forward_conv(): jnp.einsum('ok,frkw->frow', flat_kernel, taps[t:t + frame_count], preferr...]
    unnamed x58 -> x44, local copies, waits for them, and re-layouts: 14.3 us -> 6.5 us
    ppermute x12 -> x8, waiting for transfers between devices: 2.62 us -> 9.28 us  [the longest x4 6.35 us: swap_neighbours(): lax.ppermute(jnp.where(even, to_prior, to_next), axis, pairs_of(count, 1))]
    select_n x0 -> x10, other arithmetic: none -> 6.22 us  [the longest x3 2.22 us: swap_neighbours(): jnp.where(even, to_prior, to_next)]
  transfers between devices with their start and end apart: 13 -> 10, of which waited for: 2 -> 3; matrix products, arithmetic and copies ran while one was open for 12% -> 24% of each run, Pallas kernels for 0% -> 0%
where the time goes in v1:
time: 105 us; the launch traced here: 104 us
  starting transfers between devices  34.1 us (32%)
  matrix products  24.1 us (23%)
  local copies, waits for them, and re-layouts  18.2 us (17%)
  waiting for transfers between devices  15.2 us (14%)
  other arithmetic  11.3 us (11%)
  between operations  1.44 us (1%)
    all_to_all x1, starting transfers between devices, total_over_devices(): mine = lax.all_to_all(parts, AXES, 0, 0, tiled=True)  17 us
    ppermute x4, starting transfers between devices, swap_neighbours(): lax.ppermute(jnp.where(even, to_prior, to_next), axis, pairs_of(count, 1))  10.3 us
    dot_general x6, matrix products, adjoint_conv(): jnp.einsum('ck,frkw->frcw', flat_kernel, taps[2 - t:2 - t + frame_count],...  7.73 us
    dot_general x6, matrix products, forward_conv(): jnp.einsum('ok,frkw->frow', flat_kernel, taps[t:t + frame_count], preferr...  7.37 us
    unnamed x44, local copies, waits for them, and re-layouts  6.5 us
    ppermute x4, waiting for transfers between devices, swap_neighbours(): lax.ppermute(jnp.where(even, to_prior, to_next), axis, pairs_of(count, 1))  6.35 us
    all_to_all x1, waiting for transfers between devices, total_over_devices(): mine = lax.all_to_all(parts, AXES, 0, 0, tiled=True)  5.93 us
    dot_general x3, matrix products, per_device(): jnp.einsum('frow,frkw->ok', grad_pre, input_taps[t:t + frame_count], pref...  4.52 us
  transfers between devices with their start and end apart: 10, of which 3 were waited for; matrix products, arithmetic and copies ran while one was open for 24% of the time, Pallas kernels for 0%

profile of v1, /device:TPU:1, one launch (start us, length us, event | category | flops | bytes accessed | tf_op | source)
XLA Modules:
  0.0 104.4 jit_solution(9521734044666397465)
XLA Ops:
  0.7 1.2 %broadcast_select_fusion.11 = (bf16[2,4,1,64,256]{4,3,2,1,0:T(8,128)(2,1)S(1)}, bf16[2,4,1,64,256]{4,3,2,1,0:T(8,128)(2,1)S(1)}, bf16[2,4,1,64,256]{4,3,2,1,0:T(8,128)(2,1)S(1)}) fusion(pred[]{:T(512)S(6)} %eq.14, bf16[1,4,4,64,256]{4,3,2,1,0:T(8,128)(2,1)} %bitcast.219, bf16[1,4,4,64,256]{4,3,2,1,0:T(8,128)(2,1)} %bitcast.221), kind=kLoop, calls=%fused_computation.170 | loop fusion | flops 393216 | bytes 1835009 | tf_op jit(solution)/shard_map/jit(_where)/select_n | solution.py:21
  1.9 2.1 %collective-permute-start.1 = (bf16[2,4,1,64,256]{4,3,2,1,0:T(8,128)(2,1)S(1)}, bf16[2,4,1,64,256]{4,3,2,1,0:T(8,128)(2,1)S(1)}, u32[]{:S(2)}, u32[]{:S(2)}) collective-permute-start(bf16[2,4,1,64,256]{4,3,2,1,0:T(8,128)(2,1)S(1)} %broadcast_select_fusion.10), channel_id=1, source_target_pairs={{0,1},{1,0},{2,3},{3,2},{4,5},{5,4},{6,7},{7,6},{8,9},{9,8},{10,11... | collective-permute-start | bytes 786440 | tf_op jit(solution)/shard_map/ppermute | solution.py:22
  4.7 2.0 %fusion.90 = (bf16[1,3,3,64,64]{4,3,2,1,0:T(8,128)(2,1)}, bf16[64,3,3,64]{3,0,2,1:T(8,128)(2,1)S(1)}, bf16[64,3,3,64]{3,0,2,1:T(8,128)(2,1)S(1)}, bf16[64,3,3,64...) fusion(bf16[3,3,3,64,64]{4,3,2,1,0:T(8,128)(2,1)} %param.8), kind=kLoop, calls=%fused_computation.179 | loop fusion | bytes 663552 | tf_op jit(solution)/shard_map/slice | solution.py:53
  6.7 2.9 %collective-permute-done.1 = bf16[2,4,1,64,256]{4,3,2,1,0:T(8,128)(2,1)S(1)} collective-permute-done((bf16[2,4,1,64,256]{4,3,2,1,0:T(8,128)(2,1)S(1)}, bf16[2,4,1,64,256]{4,3,2,1,0:T(8,128)(2,1)S(1)}, u32[]{:S(2)}, u32[]{:S(2)}) %collective-permute-start.1) | collective-permute-done | bytes 262176 | tf_op jit(solution)/shard_map/ppermute | solution.py:22
  10.9 5.3 %collective-permute-start.2 = (bf16[2,6,64,256]{3,2,1,0:T(8,128)(2,1)}, bf16[2,6,64,256]{3,2,1,0:T(8,128)(2,1)S(1)}, u32[]{:S(2)}, u32[]{:S(2)}) collective-permute-start(bf16[2,6,64,256]{3,2,1,0:T(8,128)(2,1)} %get-tuple-element.29), channel_id=1, source_target_pairs={{32,64},{64,32},{33,65},{65,33},{34,66},{66,34},{35,67},{67,35},{3... | collective-permute-start | bytes 1179656 | tf_op jit(solution)/shard_map/ppermute | solution.py:21
  16.3 2.0 %slice_bitcast_fusion.5 = (bf16[64,3,3,64]{3,0,2,1:T(8,128)(2,1)}, bf16[64,3,3,64]{3,0,2,1:T(8,128)(2,1)}, bf16[64,3,3,64]{3,0,2,1:T(8,128)(2,1)S(1)}, bf16[1,3,...) fusion(bf16[3,3,3,64,64]{4,3,2,1,0:T(8,128)(2,1)} %param.10), kind=kLoop, calls=%fused_computation.172 | loop fusion | bytes 663552 | tf_op jit(solution)/shard_map/transpose | solution.py:53
  18.9 6.3 %collective-permute-done.2 = bf16[2,6,64,256]{3,2,1,0:T(8,128)(2,1)S(1)} collective-permute-done((bf16[2,6,64,256]{3,2,1,0:T(8,128)(2,1)}, bf16[2,6,64,256]{3,2,1,0:T(8,128)(2,1)S(1)}, u32[]{:S(2)}, u32[]{:S(2)}) %collective-permute-start.2) | collective-permute-done | bytes 393248 | tf_op jit(solution)/shard_map/ppermute | solution.py:21
  33.1 1.2 %multiply_convert_fusion = (bf16[4,4,64,256]{3,2,1,0:T(8,128)(2,1)S(1)}, f32[4,4,64,256]{3,2,1,0:T(8,128)S(1)}) fusion(f32[64]{0:T(128)S(1)} %copy-done.11, f32[4,4,256,64]{2,3,1,0:T(8,128)S(1)} %convolution_add_fusion.7, bf16[6,4,576,256]{3,2,1,0:T(8,128)(2,1)S(1)} %fusion.69, bf16[64,576,1,1]{0,1,3,2:T(8,128)(2,1)S(1)} %bitcast.244), kind=kOutput, calls=%fused_computation.94 | convolution fusion | flops 303824896 | bytes 9773312 | tf_op jit(solution)/shard_map/ok,frkw->frow/dot_general | solution.py:54
  34.4 1.5 %fusion.27 = bf16[576,64]{0,1:T(8,128)(2,1)S(1)} fusion(bf16[6,4,576,256]{3,2,1,0:T(8,128)(2,1)S(1)} %fusion.75, bf16[4,4,64,256]{3,2,1,0:T(8,128)(2,1)S(1)} %get-tuple-element.53), kind=kOutput, calls=%fused_computation.86 | convolution fusion | flops 302026752 | bytes 7675904 | tf_op jit(solution)/shard_map/frkw,frcw->kc/dot_general | solution.py:108
  35.9 1.5 %fusion.28 = bf16[576,64]{0,1:T(8,128)(2,1)S(1)} fusion(bf16[6,4,576,256]{3,2,1,0:T(8,128)(2,1)S(1)} %fusion.75, bf16[4,4,64,256]{3,2,1,0:T(8,128)(2,1)S(1)} %get-tuple-element.53), kind=kOutput, calls=%fused_computation.87 | convolution fusion | flops 302026752 | bytes 7675904 | tf_op jit(solution)/shard_map/frkw,frcw->kc/dot_general | solution.py:108
  37.4 1.5 %fusion.29 = bf16[576,64]{0,1:T(8,128)(2,1)S(1)} fusion(bf16[6,4,576,256]{3,2,1,0:T(8,128)(2,1)S(1)} %fusion.75, bf16[4,4,64,256]{3,2,1,0:T(8,128)(2,1)S(1)} %get-tuple-element.53), kind=kOutput, calls=%fused_computation.88 | convolution fusion | flops 302026752 | bytes 7675904 | tf_op jit(solution)/shard_map/frkw,frcw->kc/dot_general | solution.py:108
  41.0 1.6 %fusion.91 = (bf16[64]{0:T(256)(128)(2,1)S(1)}, bf16[4,4,64,256]{3,2,1,0:T(8,128)(2,1)S(1)}) fusion(f32[4,4,64,256]{3,2,1,0:T(8,128)S(1)} %get-tuple-element.54, f32[4,4,256,64]{2,3,1,0:T(8,128)S(1)} %convolution_add_fusion.5, bf16[6,4,576,256]{3,2,1,0:T(8,128)(2,1)S(1)} %fusion.75, bf16[64,576,1,1]{0,1,3,2:T(8,128)(2,1)S(1)} %bitcast.245), kind=kOutput, calls=%fused_computation.180 | convolution fusion | flops 304873408 | bytes 9773184 | tf_op jit(solution)/shard_map/ck,frkw->frcw/dot_general | solution.py:68
  42.6 1.5 %fusion.36 = bf16[64,576]{1,0:T(8,128)(2,1)S(1)} fusion(bf16[4,4,64,256]{3,2,1,0:T(8,128)(2,1)S(1)} %get-tuple-element.56, bf16[6,4,576,256]{3,2,1,0:T(8,128)(2,1)S(1)} %fusion.69), kind=kOutput, calls=%fused_computation.91 | convolution fusion | flops 302026752 | bytes 5316608 | tf_op jit(solution)/shard_map/frow,frkw->ok/dot_general | solution.py:101
  44.1 1.5 %fusion.33 = bf16[64,576]{1,0:T(8,128)(2,1)S(1)} fusion(bf16[4,4,64,256]{3,2,1,0:T(8,128)(2,1)S(1)} %get-tuple-element.56, bf16[6,4,576,256]{3,2,1,0:T(8,128)(2,1)S(1)} %fusion.69), kind=kOutput, calls=%fused_computation.90 | convolution fusion | flops 302026752 | bytes 5316608 | tf_op jit(solution)/shard_map/frow,frkw->ok/dot_general | solution.py:101
  45.7 1.5 %fusion.30 = bf16[64,576]{1,0:T(8,128)(2,1)S(1)} fusion(bf16[4,4,64,256]{3,2,1,0:T(8,128)(2,1)S(1)} %get-tuple-element.56, bf16[6,4,576,256]{3,2,1,0:T(8,128)(2,1)S(1)} %fusion.69), kind=kOutput, calls=%fused_computation.89 | convolution fusion | flops 302026752 | bytes 5316608 | tf_op jit(solution)/shard_map/frow,frkw->ok/dot_general | solution.py:101
  51.8 17.0 %all-to-all-start = ((bf16[128,16,128]{2,1,0:T(8,128)(2,1)}), bf16[128,16,128]{2,1,0:T(8,128)(2,1)}, u32[]{:S(2)}, u32[]{:S(2)}) async-start(bf16[128,16,128]{2,1,0:T(8,128)(2,1)} %bitcast.84), calls=%async_computation | async-start | bytes 1048576 | tf_op jit(solution)/shard_map/all_to_all | solution.py:81
  68.9 1.3 %pad_maximum_fusion.5 = bf16[2,4,6,64,256]{4,3,2,1,0:T(8,128)(2,1)S(1)} fusion(bf16[2,4,1,64,256]{4,3,2,1,0:T(8,128)(2,1)S(1)} %get-tuple-element.38, bf16[1,4,4,64,256]{4,3,2,1,0:T(8,128)(2,1)} %bitcast.224, bf16[1,4,4,64,256]{4,3,2,1,0:T(8,128)(2,1)S(1)} %bitcast.216, bf16[2,4,1,64,256]{4,3,2,1,0:T(8,128)(2,1)S(1)} %get-tuple-element.37), kind=kLoop, calls=%fused_computation.47 | loop fusion | flops 2359296 | bytes 3145728 | tf_op jit(solution)/shard_map/concatenate | solution.py:29
  71.1 3.7 %collective-permute-start.6 = (bf16[2,6,64,256]{3,2,1,0:T(8,128)(2,1)}, bf16[2,6,64,256]{3,2,1,0:T(8,128)(2,1)}, u32[]{:S(2)}, u32[]{:S(2)}) collective-permute-start(bf16[2,6,64,256]{3,2,1,0:T(8,128)(2,1)} %get-tuple-element.26), channel_id=1, source_target_pairs={{32,64},{64,32},{33,65},{65,33},{34,66},{66,34},{35,67},{67,35},{3... | collective-permute-start | bytes 1179656 | tf_op jit(solution)/shard_map/ppermute | solution.py:21
  76.2 5.9 %all-to-all-done = bf16[128,16,128]{2,1,0:T(8,128)(2,1)} async-done(((bf16[128,16,128]{2,1,0:T(8,128)(2,1)}), bf16[128,16,128]{2,1,0:T(8,128)(2,1)}, u32[]{:S(2)}, u32[]{:S(2)}) %all-to-all-start) | async-done | bytes 524320 | tf_op jit(solution)/shard_map/all_to_all | solution.py:81
  82.1 1.2 %reduce_sum.22 = bf16[16,128]{1,0:T(8,128)(2,1)S(1)} reduce(bf16[128,16,128]{2,1,0:T(8,128)(2,1)} %all-to-all-done, bf16[]{:T(256)} %constant.65.clone.1), dimensions={0}, to_apply=%region_1.2 | reduce | flops 260096 | bytes 528386 | tf_op jit(solution)/shard_map/reduce_sum | solution.py:82
  84.1 4.1 %all-to-all-start.1 = ((bf16[128,16,128]{2,1,0:T(8,128)(2,1)}), bf16[128,16,128]{2,1,0:T(8,128)(2,1)S(1)}, u32[]{:S(2)}, u32[]{:S(2)}) async-start(bf16[128,16,128]{2,1,0:T(8,128)(2,1)} %broadcast_in_dim.2), calls=%async_computation.1 | async-start | bytes 1048576 | tf_op jit(solution)/shard_map/all_to_all | solution.py:84
  96.3 1.9 %fusion.15 = bf16[4,4,64,256]{3,2,1,0:T(8,128)(2,1)} fusion(f32[4,4,256,64]{2,3,1,0:T(8,128)S(1)} %convolution_add_fusion.1, bf16[6,4,576,256]{3,2,1,0:T(8,128)(2,1)S(1)} %fusion.87, bf16[64,576,1,1]{0,1,3,2:T(8,128)(2,1)S(1)} %bitcast.236, bf16[4,4,64,256]{3,2,1,0:T(8,128)(2,1)S(1)} %copy-done.1), kind=kOutput, calls=%fused_computation.77 | convolution fusion | flops 303038464 | bytes 9248768 | tf_op jit(solution)/shard_map/ck,frkw->frcw/dot_general | solution.py:68
  100.4 1.9 %fusion.16 = bf16[4,4,64,256]{3,2,1,0:T(8,128)(2,1)} fusion(f32[4,4,256,64]{2,3,1,0:T(8,128)S(1)} %convolution_add_fusion.3, bf16[6,4,576,256]{3,2,1,0:T(8,128)(2,1)S(1)} %fusion.81, bf16[64,576,1,1]{0,1,3,2:T(8,128)(2,1)S(1)} %bitcast.230, bf16[4,4,64,256]{3,2,1,0:T(8,128)(2,1)S(1)} %copy-done.3), kind=kOutput, calls=%fused_computation.78 | convolution fusion | flops 303038464 | bytes 9248768 | tf_op jit(solution)/shard_map/ok,frkw->frow/dot_general | solution.py:54
  102.4 1.5 %fusion.89 = (f32[1728,64]{1,0:T(8,128)}, f32[1728,64]{1,0:T(8,128)}) fusion(f32[2048,128]{1,0:T(8,128)S(1)} %bitcast.217), kind=kLoop, calls=%fused_computation.178 | loop fusion | bytes 1769472 | tf_op jit(solution)/shard_map/slice | solution.py:140
  (116 shorter events, 30.6 us)
Async XLA Ops:
  0.6 9.1 %copy-start.2 = (bf16[4,4,64,256]{3,2,1,0:T(8,128)(2,1)S(1)}, bf16[4,4,64,256]{3,2,1,0:T(8,128)(2,1)}, u32[]{:S(2)}) copy-start(bf16[4,4,64,256]{3,2,1,0:T(8,128)(2,1)} %param.7) | copy-start | bytes 1572868
  0.6 9.1 %copy-start = (bf16[4,4,64,256]{3,2,1,0:T(8,128)(2,1)S(1)}, bf16[4,4,64,256]{3,2,1,0:T(8,128)(2,1)}, u32[]{:S(2)}) copy-start(bf16[4,4,64,256]{3,2,1,0:T(8,128)(2,1)} %param.11) | copy-start | bytes 1572868
  1.9 7.7 %collective-permute-start.1 = (bf16[2,4,1,64,256]{4,3,2,1,0:T(8,128)(2,1)S(1)}, bf16[2,4,1,64,256]{4,3,2,1,0:T(8,128)(2,1)S(1)}, u32[]{:S(2)}, u32[]{:S(2)}) collective-permute-start(bf16[2,4,1,64,256]{4,3,2,1,0:T(8,128)(2,1)S(1)} %broadcast_select_fusion.10), channel_id=1, source_target_pairs={{0,1},{1,0},{2,3},{3,2},{4,5},{5,4},{6,7},{7,6},{8,9},{9,8},{10,11... | collective-permute-start | bytes 786440 | tf_op jit(solution)/shard_map/ppermute | solution.py:22
  4.1 5.6 %collective-permute-start = (bf16[2,4,1,64,256]{4,3,2,1,0:T(8,128)(2,1)S(1)}, bf16[2,4,1,64,256]{4,3,2,1,0:T(8,128)(2,1)S(1)}, u32[]{:S(2)}, u32[]{:S(2)}) collective-permute-start(bf16[2,4,1,64,256]{4,3,2,1,0:T(8,128)(2,1)S(1)} %get-tuple-element.20), channel_id=1, source_target_pairs={{1,2},{2,1},{3,4},{4,3},{5,6},{6,5},{7,8},{8,7},{9,10},{10,9},{11,... | collective-permute-start | bytes 786440 | tf_op jit(solution)/shard_map/ppermute | solution.py:21
  10.9 14.4 %collective-permute-start.2 = (bf16[2,6,64,256]{3,2,1,0:T(8,128)(2,1)}, bf16[2,6,64,256]{3,2,1,0:T(8,128)(2,1)S(1)}, u32[]{:S(2)}, u32[]{:S(2)}) collective-permute-start(bf16[2,6,64,256]{3,2,1,0:T(8,128)(2,1)} %get-tuple-element.29), channel_id=1, source_target_pairs={{32,64},{64,32},{33,65},{65,33},{34,66},{66,34},{35,67},{67,35},{3... | collective-permute-start | bytes 1179656 | tf_op jit(solution)/shard_map/ppermute | solution.py:21
  16.2 9.1 %collective-permute-start.3 = (bf16[2,6,64,256]{3,2,1,0:T(8,128)(2,1)}, bf16[2,6,64,256]{3,2,1,0:T(8,128)(2,1)}, u32[]{:S(2)}, u32[]{:S(2)}) collective-permute-start(bf16[2,6,64,256]{3,2,1,0:T(8,128)(2,1)} %get-tuple-element.30), channel_id=1, source_target_pairs={{0,32},{32,0},{64,96},{96,64},{1,33},{33,1},{65,97},{97,65},{2,34}... | collective-permute-start | bytes 1179656 | tf_op jit(solution)/shard_map/ppermute | solution.py:22
  32.0 1.1 %copy-start.11 = (f32[64]{0:T(128)S(1)}, f32[64]{0:T(128)}, u32[]{:S(2)}) copy-start(f32[64]{0:T(128)} %param.9) | copy-start | bytes 772
  42.6 7.8 %copy-start.4 = (bf16[4,4,64,256]{3,2,1,0:T(8,128)(2,1)}, bf16[4,4,64,256]{3,2,1,0:T(8,128)(2,1)S(1)}, u32[]{:S(2)}) copy-start(bf16[4,4,64,256]{3,2,1,0:T(8,128)(2,1)S(1)} %get-tuple-element.56) | copy-start | bytes 1572868
  49.3 19.5 %collective-permute-start.5 = (bf16[2,4,1,64,256]{4,3,2,1,0:T(8,128)(2,1)}, bf16[2,4,1,64,256]{4,3,2,1,0:T(8,128)(2,1)S(1)}, u32[]{:S(2)}, u32[]{:S(2)}) collective-permute-start(bf16[2,4,1,64,256]{4,3,2,1,0:T(8,128)(2,1)} %broadcast_select_fusion.6), channel_id=1, source_target_pairs={{0,1},{1,0},{2,3},{3,2},{4,5},{5,4},{6,7},{7,6},{8,9},{9,8},{10,11... | collective-permute-start | bytes 786440 | tf_op jit(solution)/shard_map/ppermute | solution.py:22
  49.7 19.2 %collective-permute-start.4 = (bf16[2,4,1,64,256]{4,3,2,1,0:T(8,128)(2,1)S(1)}, bf16[2,4,1,64,256]{4,3,2,1,0:T(8,128)(2,1)S(1)}, u32[]{:S(2)}, u32[]{:S(2)}) collective-permute-start(bf16[2,4,1,64,256]{4,3,2,1,0:T(8,128)(2,1)S(1)} %get-tuple-element.17), channel_id=1, source_target_pairs={{1,2},{2,1},{3,4},{4,3},{5,6},{6,5},{7,8},{8,7},{9,10},{10,9},{11,... | collective-permute-start | bytes 786440 | tf_op jit(solution)/shard_map/ppermute | solution.py:21
  51.0 24.1 %copy-start.10 = (bf16[64,3,3,64]{3,0,2,1:T(8,128)(2,1)S(1)}, bf16[64,3,3,64]{3,0,2,1:T(8,128)(2,1)}, u32[]{:S(2)}) copy-start(bf16[64,3,3,64]{3,0,2,1:T(8,128)(2,1)} %get-tuple-element.48) | copy-start | bytes 221188
  51.0 24.2 %copy-start.9 = (bf16[64,3,3,64]{3,0,2,1:T(8,128)(2,1)S(1)}, bf16[64,3,3,64]{3,0,2,1:T(8,128)(2,1)}, u32[]{:S(2)}) copy-start(bf16[64,3,3,64]{3,0,2,1:T(8,128)(2,1)} %get-tuple-element.47) | copy-start | bytes 221188
  51.8 30.3 %all-to-all-start = ((bf16[128,16,128]{2,1,0:T(8,128)(2,1)}), bf16[128,16,128]{2,1,0:T(8,128)(2,1)}, u32[]{:S(2)}, u32[]{:S(2)}) async-start(bf16[128,16,128]{2,1,0:T(8,128)(2,1)} %bitcast.84), calls=%async_computation | async-start | bytes 1048576 | tf_op jit(solution)/shard_map/all_to_all | solution.py:81
  71.1 17.1 %collective-permute-start.6 = (bf16[2,6,64,256]{3,2,1,0:T(8,128)(2,1)}, bf16[2,6,64,256]{3,2,1,0:T(8,128)(2,1)}, u32[]{:S(2)}, u32[]{:S(2)}) collective-permute-start(bf16[2,6,64,256]{3,2,1,0:T(8,128)(2,1)} %get-tuple-element.26), channel_id=1, source_target_pairs={{32,64},{64,32},{33,65},{65,33},{34,66},{66,34},{35,67},{67,35},{3... | collective-permute-start | bytes 1179656 | tf_op jit(solution)/shard_map/ppermute | solution.py:21
  74.8 13.5 %collective-permute-start.7 = (bf16[2,6,64,256]{3,2,1,0:T(8,128)(2,1)}, bf16[2,6,64,256]{3,2,1,0:T(8,128)(2,1)}, u32[]{:S(2)}, u32[]{:S(2)}) collective-permute-start(bf16[2,6,64,256]{3,2,1,0:T(8,128)(2,1)} %get-tuple-element.25), channel_id=1, source_target_pairs={{0,32},{32,0},{64,96},{96,64},{1,33},{33,1},{65,97},{97,65},{2,34}... | collective-permute-start | bytes 1179656 | tf_op jit(solution)/shard_map/ppermute | solution.py:22
  84.1 18.2 %all-to-all-start.1 = ((bf16[128,16,128]{2,1,0:T(8,128)(2,1)}), bf16[128,16,128]{2,1,0:T(8,128)(2,1)S(1)}, u32[]{:S(2)}, u32[]{:S(2)}) async-start(bf16[128,16,128]{2,1,0:T(8,128)(2,1)} %broadcast_in_dim.2), calls=%async_computation.1 | async-start | bytes 1048576 | tf_op jit(solution)/shard_map/all_to_all | solution.py:84
  92.9 1.2 %copy-start.8 = (bf16[1,3,3,64,64]{4,3,2,1,0:T(8,128)(2,1)S(1)}, bf16[1,3,3,64,64]{4,3,2,1,0:T(8,128)(2,1)}, u32[]{:S(2)}) copy-start(bf16[1,3,3,64,64]{4,3,2,1,0:T(8,128)(2,1)} %get-tuple-element.46) | copy-start | bytes 221188
  93.7 1.5 %copy-start.7 = (bf16[1,3,3,64,64]{4,3,2,1,0:T(8,128)(2,1)S(1)}, bf16[1,3,3,64,64]{4,3,2,1,0:T(8,128)(2,1)}, u32[]{:S(2)}) copy-start(bf16[1,3,3,64,64]{4,3,2,1,0:T(8,128)(2,1)} %get-tuple-element.45) | copy-start | bytes 221188
  95.2 1.1 %copy-start.1 = (bf16[4,4,64,256]{3,2,1,0:T(8,128)(2,1)S(1)}, bf16[4,4,64,256]{3,2,1,0:T(8,128)(2,1)}, u32[]{:S(2)}) copy-start(bf16[4,4,64,256]{3,2,1,0:T(8,128)(2,1)} %param.11) | copy-start | bytes 1572868
  95.2 1.1 %copy-start.6 = (bf16[1,3,3,64,64]{4,3,2,1,0:T(8,128)(2,1)S(1)}, bf16[1,3,3,64,64]{4,3,2,1,0:T(8,128)(2,1)}, u32[]{:S(2)}) copy-start(bf16[1,3,3,64,64]{4,3,2,1,0:T(8,128)(2,1)} %get-tuple-element.41) | copy-start | bytes 221188
  99.3 1.1 %copy-start.3 = (bf16[4,4,64,256]{3,2,1,0:T(8,128)(2,1)S(1)}, bf16[4,4,64,256]{3,2,1,0:T(8,128)(2,1)}, u32[]{:S(2)}) copy-start(bf16[4,4,64,256]{3,2,1,0:T(8,128)(2,1)} %param.7) | copy-start | bytes 1572868
  99.3 1.1 %copy-start.5 = (bf16[64,3,3,64]{0,3,2,1:T(8,128)(2,1)S(1)}, bf16[64,3,3,64]{0,3,2,1:T(8,128)(2,1)}, u32[]{:S(2)}) copy-start(bf16[64,3,3,64]{0,3,2,1:T(8,128)(2,1)} %copy.38) | copy-start | bytes 221188

commit v2 on v1

v2 whole, which is shorter than its diff:
```python
import math

import jax
import jax.numpy as jnp
from jax import lax
from jax.experimental import pallas as pl
from jax.experimental.pallas import tpu as pltpu
from jax.sharding import PartitionSpec as P

F32, BF16 = jnp.float32, jnp.bfloat16


def put_taps(dst, g, rr, slab):
    chan, cols = slab.shape
    lane = lax.broadcasted_iota(jnp.int32, slab.shape, 1)
    zero = jnp.zeros_like(slab)
    dst[g, rr, 0:chan, :] = jnp.where(lane == 0, zero, pltpu.roll(slab, 1, 1))
    dst[g, rr, chan : 2 * chan, :] = slab
    dst[g, rr, 2 * chan : 3 * chan, :] = jnp.where(lane == cols - 1, zero, pltpu.roll(slab, cols - 1, 1))


def build(side, past, future, rows_odd, rows_even, main_odd, main_even, rim_odd, rim_even, xp, xf):
    frames, rows = past.shape[0], past.shape[1]
    row_even, frame_even = side[0] == 0, side[1] == 0

    def own(f, carry):
        for k, (src, dst, off) in enumerate(((past, xp, 2), (future, xf, 0))):
            a, b = rows_odd[k, f, 0], rows_even[k, f, 0]
            put_taps(dst, f + off, 0, jnp.where(row_even, a, b))
            for r in range(rows):
                put_taps(dst, f + off, r + 1, src[f, r])
            put_taps(dst, f + off, rows + 1, jnp.where(row_even, b, a))
        return carry

    lax.fori_loop(0, frames, own, 0)

    def edge(f, carry):
        for dst, off, odd_first in ((xp, 0, True), (xf, frames, False)):
            pick = frame_even if odd_first else jnp.logical_not(frame_even)
            for r in range(rows):
                put_taps(dst, f + off, r + 1, jnp.where(pick, main_odd[f, r], main_even[f, r]))
            for s in range(2):
                put_taps(dst, f + off, s * (rows + 1), jnp.where(pick, rim_odd[f, s], rim_even[f, s]))
        return carry

    lax.fori_loop(0, 2, edge, 0)


def convolve(wp, wf, xp, xf, accp, accf):
    frames, rows = xp.shape[0] - 2, xp.shape[1] - 2
    taps, cols = 3 * xp.shape[2], xp.shape[3]
    chan = wp.shape[0] // 3
    accp[...] = jnp.zeros_like(accp)
    accf[...] = jnp.zeros_like(accf)

    def step(g, carry):
        for w, x, acc in ((wp, xp, accp), (wf, xf, accf)):
            for r in range(rows):
                part = jnp.dot(w[...], x[g, r : r + 3].reshape(taps, cols), preferred_element_type=F32)
                for t in range(3):
                    acc[g - t + 2, :, r * cols : (r + 1) * cols] += part[t * chan : (t + 1) * chan]
        return carry

    lax.fori_loop(0, frames + 2, step, 0)


def first_kernel(side, past, future, rows_odd, rows_even, main_odd, main_even, rim_odd, rim_even, wp, wf, bias,
                 active_out, pre_out, grads, xp, xf, accp, accf, upa, upg, d1, d2):
    frames, rows, chan, cols = past.shape
    build(side, past, future, rows_odd, rows_even, main_odd, main_even, rim_odd, rim_even, xp, xf)
    convolve(wp, wf, xp, xf, accp, accf)
    for up in (upa, upg):
        for f in (0, 1, frames + 2, frames + 3):
            up[f] = jnp.zeros(up.shape[1:], up.dtype)

    def point(f, total):
        for r in range(rows):
            span = slice(r * cols, (r + 1) * cols)
            hidden = accp[f + 2, :, span] + bias[...]
            sig = jax.nn.sigmoid(hidden)
            active = (hidden * sig).astype(BF16)
            pre = (accf[f + 2, :, span] * sig * (1.0 + hidden * (1.0 - sig))).astype(BF16)
            active_out[f, r] = active
            pre_out[f, r] = pre
            upa[f + 2, :, span] = active
            upg[f + 2, :, span] = pre
            total = total + pre.astype(F32)
        return total

    total = lax.fori_loop(0, frames, point, jnp.zeros((chan, cols), F32))
    bias_sum = jnp.sum(total, axis=1, keepdims=True)
    d1[...] = jnp.zeros_like(d1)
    d2[...] = jnp.zeros_like(d2)
    nt = (((1,), (1,)), ((), ()))

    def weigh(g, carry):
        pre3 = upg[pl.ds(g, 3)].reshape(3 * chan, rows * cols)
        act3 = upa[pl.ds(g, 3)].reshape(3 * chan, rows * cols)
        xc = jnp.concatenate([xp[g, r : r + 3].reshape(9 * chan, cols) for r in range(rows)], axis=1)
        d1[...] += lax.dot_general(pre3, xc, nt, preferred_element_type=F32)
        xo = jnp.concatenate([xf[g, r : r + 3].reshape(9 * chan, cols) for r in range(rows)], axis=1)
        d2[...] += lax.dot_general(xo, act3, nt, preferred_element_type=F32)
        return carry

    lax.fori_loop(0, frames + 2, weigh, 0)
    per = chan // grads.shape[1]
    for t in range(3):
        for ij in range(9):
            one = d1[(2 - t) * chan : (3 - t) * chan, ij * chan : (ij + 1) * chan]
            two = d2[(8 - ij) * chan : (9 - ij) * chan, t * chan : (t + 1) * chan]
            tap = (t * 9 + ij) * per
            both = jnp.concatenate([one, two], axis=1).astype(grads.dtype)
            grads[tap : tap + per] = both.reshape((per,) + grads.shape[1:])
    used = 27 * per
    grads[used : used + per] = jnp.broadcast_to(bias_sum, (chan, grads.shape[2])).astype(grads.dtype).reshape((per,) + grads.shape[1:])
    if used + per < grads.shape[0]:
        grads[used + per :] = jnp.zeros((grads.shape[0] - used - per,) + grads.shape[1:], grads.dtype)


def second_kernel(side, past, future, rows_odd, rows_even, main_odd, main_even, rim_odd, rim_even, wp, wf,
                  add_past, add_future, out_past, out_future, xp, xf, accp, accf):
    frames, rows, chan, cols = past.shape
    build(side, past, future, rows_odd, rows_even, main_odd, main_even, rim_odd, rim_even, xp, xf)
    convolve(wp, wf, xp, xf, accp, accf)

    def point(f, carry):
        for r in range(rows):
            span = slice(r * cols, (r + 1) * cols)
            out_past[f, r] = (add_past[f, r].astype(F32) + accp[f + 2, :, span]).astype(BF16)
            out_future[f, r] = (add_future[f, r].astype(F32) + accf[f + 2, :, span]).astype(BF16)
        return carry

    lax.fori_loop(0, frames, point, 0)


def specs(n):
    return [pl.BlockSpec(memory_space=pltpu.SMEM)] + [pl.BlockSpec(memory_space=pltpu.VMEM)] * (n - 1)


def shared_scratch(shape):
    frames, rows, chan, cols = shape
    return [pltpu.VMEM((frames + 2, rows + 2, 3 * chan, cols), BF16)] * 2 + [
        pltpu.VMEM((frames + 4, chan, rows * cols), F32)] * 2


def first_call(devices, *args):
    shape = args[1].shape
    frames, rows, chan, cols = shape
    return pl.pallas_call(
        first_kernel,
        out_shape=[jax.ShapeDtypeStruct(shape, BF16)] * 2 + [jax.ShapeDtypeStruct((devices, 16, 2 * chan), BF16)],
        in_specs=specs(len(args)), out_specs=[pl.BlockSpec(memory_space=pltpu.VMEM)] * 3,
        scratch_shapes=shared_scratch(shape) + [pltpu.VMEM((frames + 4, chan, rows * cols), BF16)] * 2
        + [pltpu.VMEM((3 * chan, 9 * chan), F32), pltpu.VMEM((9 * chan, 3 * chan), F32)],
        name="first",
    )(*args)


def second_call(*args):
    shape = args[1].shape
    return pl.pallas_call(
        second_kernel,
        out_shape=[jax.ShapeDtypeStruct(shape, BF16)] * 2,
        in_specs=specs(len(args)), out_specs=[pl.BlockSpec(memory_space=pltpu.VMEM)] * 2,
        scratch_shapes=shared_scratch(shape),
        name="second",
    )(*args)


def flat_forward(kernel):
    chan = kernel.shape[3]
    return jnp.transpose(kernel, (0, 3, 1, 2, 4)).reshape(3 * chan, 9 * chan)


def flat_adjoint(kernel):
    chan = kernel.shape[3]
    return jnp.transpose(kernel[::-1, ::-1, ::-1], (0, 4, 1, 2, 3)).reshape(3 * chan, 9 * chan)


AXES = ("frames", "rows")


def pairs_of(count, first):
    pairs = []
    for i in range(first, count - 1, 2):
        pairs += [(i, i + 1), (i + 1, i)]
    return pairs


def swap_neighbours(axis, even, to_next, to_prior):
    count = lax.axis_size(axis)
    with jax.named_scope("odd"):
        odd_pairs = lax.ppermute(jnp.where(even, to_prior, to_next), axis, pairs_of(count, 1))
    with jax.named_scope("even"):
        even_pairs = lax.ppermute(jnp.where(even, to_next, to_prior), axis, pairs_of(count, 0))
    return odd_pairs, even_pairs


def halo(side, past, future):
    row_even, frame_even = side[0] == 0, side[1] == 0
    both = jnp.stack([past, future])
    with jax.named_scope("rims_of_rows"):
        rows_odd, rows_even = swap_neighbours("rows", row_even, both[:, :, -1:], both[:, :, :1])
    with jax.named_scope("main"):
        main_odd, main_even = swap_neighbours("frames", frame_even, past[-2:], future[:2])
    low = jnp.where(row_even, rows_odd, rows_even)
    high = jnp.where(row_even, rows_even, rows_odd)
    rims = jnp.concatenate([low, high], axis=2)
    with jax.named_scope("rims_of_frames"):
        rim_odd, rim_even = swap_neighbours("frames", frame_even, rims[0, -2:], rims[1, :2])
    return rows_odd, rows_even, main_odd, main_even, rim_odd, rim_even


def total_over_devices(parts):
    with jax.named_scope("gather_terms"):
        mine = lax.all_to_all(parts, AXES, 0, 0, tiled=True)
    mine = jnp.sum(mine.astype(jnp.float32), axis=0).astype(jnp.bfloat16)
    spread = jnp.broadcast_to(mine[None], parts.shape)
    with jax.named_scope("spread_sums"):
        return lax.all_to_all(spread, AXES, 0, 0, tiled=True)


def per_device(clip_in, kernel_one, bias_one, kernel_two, cotangent):
    frame_count, row_count, channels, col_count = clip_in.shape
    devices = lax.axis_size("frames") * lax.axis_size("rows")
    side = jnp.stack([lax.axis_index("rows") % 2, lax.axis_index("frames") % 2]).astype(jnp.int32)
    with jax.named_scope("halo_one"):
        edges = halo(side, clip_in, cotangent)
    active, grad_pre, terms = first_call(
        devices, side, clip_in, cotangent, *edges,
        flat_forward(kernel_one), flat_adjoint(kernel_two), bias_one[:, None],
    )
    total = total_over_devices(terms)
    with jax.named_scope("halo_two"):
        edges = halo(side, active, grad_pre)
    block_out, grad_input = second_call(
        side, active, grad_pre, *edges,
        flat_forward(kernel_two), flat_adjoint(kernel_one), clip_in, cotangent,
    )
    cell_total = (
        frame_count * lax.axis_size("frames") * row_count * lax.axis_size("rows") * col_count
    )
    total = total.reshape((-1, 2 * channels)).astype(jnp.float32) * (1.0 / math.sqrt(cell_total))
    count = 27 * channels
    return (
        block_out,
        grad_input,
        total[:count, :channels].reshape(kernel_one.shape),
        total[:count, channels:].reshape(kernel_two.shape),
        total[count : count + channels, 0],
    )


def solution(mesh):
    in_specs = (P("frames", "rows", None, None), P(), P(), P(), P("frames", "rows", None, None))
    out_specs = (P("frames", "rows", None, None), P("frames", "rows", None, None), P(), P(), P())
    return jax.shard_map(
        per_device, mesh=mesh, in_specs=in_specs, out_specs=out_specs, check_vma=False
    )
```

time: 105 us -> 97.1 us (0.925)
  Pallas kernels: 0 us -> 25.5 us
  matrix products: 24.1 us -> 0 us
  starting transfers between devices: 34.1 us -> 44.5 us
  waiting for transfers between devices: 15.2 us -> 6.18 us
  other arithmetic: 11.3 us -> 5.14 us
  local copies, waits for them, and re-layouts: 18.2 us -> 14.3 us
    pallas_call x0 -> x2, Pallas kernels: none -> 25.5 us  [the longest x1 15.7 us: first_call(): pl.pallas_call(first_kernel, out_shape=[jax.ShapeDtypeStruct(shape, BF16)...]
    dot_general x18 -> x0, matrix products: 24.1 us -> none  [the longest x6 7.73 us: adjoint_conv(): jnp.einsum('ck,frkw->frcw', flat_kernel, taps[2 - t:2 - t + frame_count],...]
    ppermute x4 -> x6, starting transfers between devices: 10.3 us -> 19 us  [swap_neighbours(): lax.ppermute(jnp.where(even, to_prior, to_next), axis, pairs_of(count, 1))]
    ppermute x4 -> x6, starting transfers between devices: 2.65 us -> 8.74 us  [swap_neighbours(): lax.ppermute(jnp.where(even, to_next, to_prior), axis, pairs_of(count, 0))]
    all_to_all x1, starting transfers between devices: 17 us -> 11.4 us  [total_over_devices(): mine = lax.all_to_all(parts, AXES, 0, 0, tiled=True)]
    ppermute x4 -> x6, waiting for transfers between devices: 6.35 us -> 1.7 us  [swap_neighbours(): lax.ppermute(jnp.where(even, to_prior, to_next), axis, pairs_of(count, 1))]
    reshape x0 -> x4, local copies, waits for them, and re-layouts: none -> 4.38 us  [the longest x2 2.19 us: flat_adjoint(): jnp.transpose(kernel[::-1, ::-1, ::-1], (0, 4, 1, 2, 3))]
    concatenate x7 -> x0, other arithmetic: 2.97 us -> none  [the longest x2 1.49 us: extend(): past_rows, future_rows = jnp.concatenate([low, both, high], axis=2)]
  transfers between devices with their start and end apart: 10 -> 14, of which waited for: 3 -> 3; matrix products, arithmetic and copies ran while one was open for 24% -> 13% of each run, Pallas kernels for 0% -> 10%
where the time goes in v2:
time: 97.1 us; the launch traced here: 96.7 us
  starting transfers between devices  44.5 us (46%)
  Pallas kernels  25.5 us (26%)
  local copies, waits for them, and re-layouts  14.3 us (15%)
  waiting for transfers between devices  6.18 us (6%)
  other arithmetic  5.14 us (5%)
  between operations  1 us (1%)
    ppermute x6, starting transfers between devices, swap_neighbours(): lax.ppermute(jnp.where(even, to_prior, to_next), axis, pairs_of(count, 1))  19 us
    pallas_call x1, Pallas kernels, first_call(): pl.pallas_call(first_kernel, out_shape=[jax.ShapeDtypeStruct(shape, BF16)...  15.7 us
    all_to_all x1, starting transfers between devices, total_over_devices(): mine = lax.all_to_all(parts, AXES, 0, 0, tiled=True)  11.4 us
    pallas_call x1, Pallas kernels, second_call(): pl.pallas_call(second_kernel, out_shape=[jax.ShapeDtypeStruct(shape, BF16...  9.86 us
    ppermute x6, starting transfers between devices, swap_neighbours(): lax.ppermute(jnp.where(even, to_next, to_prior), axis, pairs_of(count, 0))  8.74 us
    all_to_all x1, starting transfers between devices, total_over_devices(): return lax.all_to_all(spread, AXES, 0, 0, tiled=True)  5.39 us
    all_to_all x1, waiting for transfers between devices, total_over_devices(): mine = lax.all_to_all(parts, AXES, 0, 0, tiled=True)  3.57 us
    unnamed x34, local copies, waits for them, and re-layouts  3.54 us
  transfers between devices with their start and end apart: 14, of which 3 were waited for; matrix products, arithmetic and copies ran while one was open for 13% of the time, Pallas kernels for 10%

profile of v2, /device:TPU:1, one launch (start us, length us, event | category | flops | bytes accessed | tf_op | source)
XLA Modules:
  0.0 96.7 jit_solution(30045584824185049)
XLA Ops:
  0.7 1.2 %broadcast_select_fusion.10 = (bf16[2,4,1,64,256]{4,3,2,1,0:T(8,128)(2,1)S(1)}, bf16[2,4,1,64,256]{4,3,2,1,0:T(8,128)(2,1)S(1)}, bf16[2,4,1,64,256]{4,3,2,1,0:T(8,128)(2,1)S(1)}) fusion(pred[]{:T(512)S(6)} %eq.11, bf16[1,4,4,64,256]{4,3,2,1,0:T(8,128)(2,1)} %bitcast.27, bf16[1,4,4,64,256]{4,3,2,1,0:T(8,128)(2,1)} %bitcast.26), kind=kLoop, calls=%fused_computation.17 | loop fusion | flops 393216 | bytes 1835009 | tf_op jit(solution)/shard_map/halo_one/rims_of_rows/even/jit(_where)/select_n | solution.py:195
  1.9 0.8 collective-permute-start
  2.7 4.6 %collective-permute-start.1 = (bf16[2,4,1,64,256]{4,3,2,1,0:T(8,128)(2,1)S(1)}, bf16[2,4,1,64,256]{4,3,2,1,0:T(8,128)(2,1)S(1)}, u32[]{:S(2)}, u32[]{:S(2)}) collective-permute-start(bf16[2,4,1,64,256]{4,3,2,1,0:T(8,128)(2,1)S(1)} %get-tuple-element.24), channel_id=1, source_target_pairs={{0,1},{1,0},{2,3},{3,2},{4,5},{5,4},{6,7},{7,6},{8,9},{9,8},{10,11... | collective-permute-start | bytes 786440 | tf_op jit(solution)/shard_map/halo_one/rims_of_rows/even/ppermute | solution.py:195
  7.3 4.7 %collective-permute-start.2 = (bf16[2,4,64,256]{3,2,1,0:T(8,128)(2,1)S(1)}, bf16[2,4,64,256]{3,2,1,0:T(8,128)(2,1)S(1)}, u32[]{:S(2)}, u32[]{:S(2)}) collective-permute-start(bf16[2,4,64,256]{3,2,1,0:T(8,128)(2,1)S(1)} %get-tuple-element.32), channel_id=1, source_target_pairs={{32,64},{64,32},{33,65},{65,33},{34,66},{66,34},{35,67},{67,35},{3... | collective-permute-start | bytes 786440 | tf_op jit(solution)/shard_map/halo_one/main/odd/ppermute | solution.py:193
  12.1 0.9 collective-permute-done.1.rows_even
  13.8 5.1 %collective-permute-start.4 = (bf16[2,2,64,256]{3,2,1,0:T(8,128)(2,1)S(1)}, bf16[2,2,64,256]{3,2,1,0:T(8,128)(2,1)S(1)}, u32[]{:S(2)}, u32[]{:S(2)}) collective-permute-start(bf16[2,2,64,256]{3,2,1,0:T(8,128)(2,1)S(1)} %select_bitcast_fusion.3), channel_id=1, source_target_pairs={{32,64},{64,32},{33,65},{65,33},{34,66},{66,34},{35,67},{67,35},{3... | collective-permute-start | bytes 393224 | tf_op jit(solution)/shard_map/halo_one/rims_of_frames/odd/ppermute | solution.py:193
  19.0 0.9 copy.23
  20.0 1.1 %reshape.42.wf = bf16[192,576]{1,0:T(8,128)(2,1)} reshape(bf16[3,64,3,3,64]{4,3,2,1,0:T(4,128)(2,1)S(1)} %copy.23) | data formatting | bytes 442368 | tf_op jit(solution)/shard_map/reshape | solution.py:177
  21.5 1.1 %reshape.41.wp = bf16[192,576]{1,0:T(8,128)(2,1)} reshape(bf16[3,64,3,3,64]{4,3,2,1,0:T(4,128)(2,1)S(1)} %copy.22) | data formatting | bytes 442368 | tf_op jit(solution)/shard_map/reshape | solution.py:172
  26.1 15.7 %first.1 = (bf16[4,4,64,256]{3,2,1,0:T(8,128)(2,1)}, bf16[4,4,64,256]{3,2,1,0:T(8,128)(2,1)}, bf16[128,16,128]{2,1,0:T(8,128)(2,1)}) custom-call(s32[2]{0:T(128)} %pad_add_fusion.side, bf16[4,4,64,256]{3,2,1,0:T(8,128)(2,1)} %add_past.1, bf16[4,4,64,256]{3,2,1,0:T(8,128)(2,1)} %add_future.1, bf16[2,4,1,64,256]{4,3,2,1,0:T(8,128)(2,1)} %copy-done.6, ...), custom_call_target="tpu_custom_call" | custom-call | tf_op jit(solution)/shard_map/first/pallas_call | solution.py:149
  41.7 11.4 %all-to-all-start = ((bf16[128,16,128]{2,1,0:T(8,128)(2,1)}), bf16[128,16,128]{2,1,0:T(8,128)(2,1)S(1)}, u32[]{:S(2)}, u32[]{:S(2)}) async-start(bf16[128,16,128]{2,1,0:T(8,128)(2,1)} %get-tuple-element.14), calls=%async_computation | async-start | bytes 1048576 | tf_op jit(solution)/shard_map/gather_terms/all_to_all | solution.py:216
  53.2 0.8 broadcast_select_fusion.6
  55.4 3.8 %collective-permute-start.7 = (bf16[2,4,1,64,256]{4,3,2,1,0:T(8,128)(2,1)}, bf16[2,4,1,64,256]{4,3,2,1,0:T(8,128)(2,1)S(1)}, u32[]{:S(2)}, u32[]{:S(2)}) collective-permute-start(bf16[2,4,1,64,256]{4,3,2,1,0:T(8,128)(2,1)} %get-tuple-element.18), channel_id=1, source_target_pairs={{0,1},{1,0},{2,3},{3,2},{4,5},{5,4},{6,7},{7,6},{8,9},{9,8},{10,11... | collective-permute-start | bytes 786440 | tf_op jit(solution)/shard_map/halo_two/rims_of_rows/even/ppermute | solution.py:195
  59.2 4.1 %collective-permute-start.8 = (bf16[2,4,64,256]{3,2,1,0:T(8,128)(2,1)S(1)}, bf16[2,4,64,256]{3,2,1,0:T(8,128)(2,1)S(1)}, u32[]{:S(2)}, u32[]{:S(2)}) collective-permute-start(bf16[2,4,64,256]{3,2,1,0:T(8,128)(2,1)S(1)} %get-tuple-element.30), channel_id=1, source_target_pairs={{32,64},{64,32},{33,65},{65,33},{34,66},{66,34},{35,67},{67,35},{3... | collective-permute-start | bytes 786440 | tf_op jit(solution)/shard_map/halo_two/main/odd/ppermute | solution.py:193
  63.4 3.6 %all-to-all-done = bf16[128,16,128]{2,1,0:T(8,128)(2,1)S(1)} async-done(((bf16[128,16,128]{2,1,0:T(8,128)(2,1)}), bf16[128,16,128]{2,1,0:T(8,128)(2,1)S(1)}, u32[]{:S(2)}, u32[]{:S(2)}) %all-to-all-start) | async-done | bytes 524320 | tf_op jit(solution)/shard_map/gather_terms/all_to_all | solution.py:216
  67.1 0.9 broadcast_in_dim.10
  68.0 5.4 %all-to-all-start.1 = ((bf16[128,16,128]{2,1,0:T(8,128)(2,1)}), bf16[128,16,128]{2,1,0:T(8,128)(2,1)S(1)}, u32[]{:S(2)}, u32[]{:S(2)}) async-start(bf16[128,16,128]{2,1,0:T(8,128)(2,1)} %broadcast_in_dim.10), calls=%async_computation.1 | async-start | bytes 1048576 | tf_op jit(solution)/shard_map/spread_sums/all_to_all | solution.py:220
  75.6 3.7 %collective-permute-start.10 = (bf16[2,2,64,256]{3,2,1,0:T(8,128)(2,1)}, bf16[2,2,64,256]{3,2,1,0:T(8,128)(2,1)}, u32[]{:S(2)}, u32[]{:S(2)}) collective-permute-start(bf16[2,2,64,256]{3,2,1,0:T(8,128)(2,1)} %select_bitcast_fusion.1), channel_id=1, source_target_pairs={{32,64},{64,32},{33,65},{65,33},{34,66},{66,34},{35,67},{67,35},{3... | collective-permute-start | bytes 393224 | tf_op jit(solution)/shard_map/halo_two/rims_of_frames/odd/ppermute | solution.py:193
  79.4 0.9 copy.26
  80.3 1.1 %reshape.44.wf = bf16[192,576]{1,0:T(8,128)(2,1)} reshape(bf16[3,64,3,3,64]{4,3,2,1,0:T(4,128)(2,1)S(1)} %copy.26) | data formatting | bytes 442368 | tf_op jit(solution)/shard_map/reshape | solution.py:177
  81.8 1.1 %reshape.43.wp = bf16[192,576]{1,0:T(8,128)(2,1)} reshape(bf16[3,64,3,3,64]{4,3,2,1,0:T(4,128)(2,1)S(1)} %copy.25) | data formatting | bytes 442368 | tf_op jit(solution)/shard_map/reshape | solution.py:172
  82.9 1.7 %collective-permute-done.10.rim_odd = bf16[2,2,64,256]{3,2,1,0:T(8,128)(2,1)} collective-permute-done((bf16[2,2,64,256]{3,2,1,0:T(8,128)(2,1)}, bf16[2,2,64,256]{3,2,1,0:T(8,128)(2,1)}, u32[]{:S(2)}, u32[]{:S(2)}) %collective-permute-start.10) | collective-permute-done | bytes 131104 | tf_op jit(solution)/shard_map/halo_two/rims_of_frames/odd/ppermute | solution.py:193
  84.6 9.9 %second.1 = (bf16[4,4,64,256]{3,2,1,0:T(8,128)(2,1)}, bf16[4,4,64,256]{3,2,1,0:T(8,128)(2,1)}) custom-call(s32[2]{0:T(128)} %pad_add_fusion.side, bf16[4,4,64,256]{3,2,1,0:T(8,128)(2,1)} %get-tuple-element.10.past, bf16[4,4,64,256]{3,2,1,0:T(8,128)(2,1)} %get-tuple-element.11.future, bf16[2,4,1,64,256]{4,3,2,1,0:T(8,128)(2,1)} %copy-done.8, ...), custom_call_target="tpu_custom_call" | custom-call | tf_op jit(solution)/shard_map/second/pallas_call | solution.py:161
  94.6 1.5 %fusion = (f32[1728,64]{1,0:T(8,128)}, f32[1728,64]{1,0:T(8,128)}) fusion(f32[2048,128]{1,0:T(8,128)S(1)} %bitcast.24), kind=kLoop, calls=%fused_computation.29 | loop fusion | bytes 1769472 | tf_op jit(solution)/shard_map/slice | solution.py:249
  (69 shorter events, 9.9 us)
Async XLA Ops:
  0.6 6.6 %copy-start.1 = (bf16[4,4,64,256]{3,2,1,0:T(8,128)(2,1)S(1)}, bf16[4,4,64,256]{3,2,1,0:T(8,128)(2,1)}, u32[]{:S(2)}) copy-start(bf16[4,4,64,256]{3,2,1,0:T(8,128)(2,1)} %add_future.1) | copy-start | bytes 1572868
  1.9 5.4 %copy-start = (bf16[4,4,64,256]{3,2,1,0:T(8,128)(2,1)S(1)}, bf16[4,4,64,256]{3,2,1,0:T(8,128)(2,1)}, u32[]{:S(2)}) copy-start(bf16[4,4,64,256]{3,2,1,0:T(8,128)(2,1)} %add_past.1) | copy-start | bytes 1572868
  1.9 10.2 %collective-permute-start = (bf16[2,4,1,64,256]{4,3,2,1,0:T(8,128)(2,1)S(1)}, bf16[2,4,1,64,256]{4,3,2,1,0:T(8,128)(2,1)S(1)}, u32[]{:S(2)}, u32[]{:S(2)}) collective-permute-start(bf16[2,4,1,64,256]{4,3,2,1,0:T(8,128)(2,1)S(1)} %broadcast_select_fusion.11), channel_id=1, source_target_pairs={{1,2},{2,1},{3,4},{4,3},{5,6},{6,5},{7,8},{8,7},{9,10},{10,9},{11,... | collective-permute-start | bytes 786440 | tf_op jit(solution)/shard_map/halo_one/rims_of_rows/odd/ppermute | solution.py:193
  2.7 10.3 %collective-permute-start.1 = (bf16[2,4,1,64,256]{4,3,2,1,0:T(8,128)(2,1)S(1)}, bf16[2,4,1,64,256]{4,3,2,1,0:T(8,128)(2,1)S(1)}, u32[]{:S(2)}, u32[]{:S(2)}) collective-permute-start(bf16[2,4,1,64,256]{4,3,2,1,0:T(8,128)(2,1)S(1)} %get-tuple-element.24), channel_id=1, source_target_pairs={{0,1},{1,0},{2,3},{3,2},{4,5},{5,4},{6,7},{7,6},{8,9},{9,8},{10,11... | collective-permute-start | bytes 786440 | tf_op jit(solution)/shard_map/halo_one/rims_of_rows/even/ppermute | solution.py:195
  7.3 17.2 %collective-permute-start.2 = (bf16[2,4,64,256]{3,2,1,0:T(8,128)(2,1)S(1)}, bf16[2,4,64,256]{3,2,1,0:T(8,128)(2,1)S(1)}, u32[]{:S(2)}, u32[]{:S(2)}) collective-permute-start(bf16[2,4,64,256]{3,2,1,0:T(8,128)(2,1)S(1)} %get-tuple-element.32), channel_id=1, source_target_pairs={{32,64},{64,32},{33,65},{65,33},{34,66},{66,34},{35,67},{67,35},{3... | collective-permute-start | bytes 786440 | tf_op jit(solution)/shard_map/halo_one/main/odd/ppermute | solution.py:193
  12.0 12.5 %collective-permute-start.3 = (bf16[2,4,64,256]{3,2,1,0:T(8,128)(2,1)S(1)}, bf16[2,4,64,256]{3,2,1,0:T(8,128)(2,1)S(1)}, u32[]{:S(2)}, u32[]{:S(2)}) collective-permute-start(bf16[2,4,64,256]{3,2,1,0:T(8,128)(2,1)S(1)} %get-tuple-element.31), channel_id=1, source_target_pairs={{0,32},{32,0},{64,96},{96,64},{1,33},{33,1},{65,97},{97,65},{2,34}... | collective-permute-start | bytes 786440 | tf_op jit(solution)/shard_map/halo_one/main/even/ppermute | solution.py:195
  12.1 1.0 copy-start.6
  13.7 5.3 %copy-start.5 = (bf16[3,3,3,64,64]{4,3,2,1,0:T(8,128)(2,1)S(1)}, bf16[3,3,3,64,64]{4,3,2,1,0:T(8,128)(2,1)}, u32[]{:S(2)}) copy-start(bf16[3,3,3,64,64]{4,3,2,1,0:T(8,128)(2,1)} %param.8) | copy-start | bytes 663556
  13.8 10.8 %collective-permute-start.4 = (bf16[2,2,64,256]{3,2,1,0:T(8,128)(2,1)S(1)}, bf16[2,2,64,256]{3,2,1,0:T(8,128)(2,1)S(1)}, u32[]{:S(2)}, u32[]{:S(2)}) collective-permute-start(bf16[2,2,64,256]{3,2,1,0:T(8,128)(2,1)S(1)} %select_bitcast_fusion.3), channel_id=1, source_target_pairs={{32,64},{64,32},{33,65},{65,33},{34,66},{66,34},{35,67},{67,35},{3... | collective-permute-start | bytes 393224 | tf_op jit(solution)/shard_map/halo_one/rims_of_frames/odd/ppermute | solution.py:193
  18.9 5.7 %collective-permute-start.5 = (bf16[2,2,64,256]{3,2,1,0:T(8,128)(2,1)S(1)}, bf16[2,2,64,256]{3,2,1,0:T(8,128)(2,1)S(1)}, u32[]{:S(2)}, u32[]{:S(2)}) collective-permute-start(bf16[2,2,64,256]{3,2,1,0:T(8,128)(2,1)S(1)} %get-tuple-element.21), channel_id=1, source_target_pairs={{0,32},{32,0},{64,96},{96,64},{1,33},{33,1},{65,97},{97,65},{2,34}... | collective-permute-start | bytes 393224 | tf_op jit(solution)/shard_map/halo_one/rims_of_frames/even/ppermute | solution.py:195
  20.0 1.1 %copy-start.4 = (bf16[3,3,3,64,64]{4,3,2,1,0:T(8,128)(2,1)S(1)}, bf16[3,3,3,64,64]{4,3,2,1,0:T(8,128)(2,1)}, u32[]{:S(2)}) copy-start(bf16[3,3,3,64,64]{4,3,2,1,0:T(8,128)(2,1)} %param.6) | copy-start | bytes 663556
  24.6 0.8 copy-start.14
  41.7 11.4 %copy-start.2 = (bf16[4,4,64,256]{3,2,1,0:T(8,128)(2,1)S(1)}, bf16[4,4,64,256]{3,2,1,0:T(8,128)(2,1)}, u32[]{:S(2)}) copy-start(bf16[4,4,64,256]{3,2,1,0:T(8,128)(2,1)} %get-tuple-element.10.past) | copy-start | bytes 1572868
  41.7 11.4 %copy-start.3 = (bf16[4,4,64,256]{3,2,1,0:T(8,128)(2,1)S(1)}, bf16[4,4,64,256]{3,2,1,0:T(8,128)(2,1)}, u32[]{:S(2)}) copy-start(bf16[4,4,64,256]{3,2,1,0:T(8,128)(2,1)} %get-tuple-element.11.future) | copy-start | bytes 1572868
  41.7 25.3 %all-to-all-start = ((bf16[128,16,128]{2,1,0:T(8,128)(2,1)}), bf16[128,16,128]{2,1,0:T(8,128)(2,1)S(1)}, u32[]{:S(2)}, u32[]{:S(2)}) async-start(bf16[128,16,128]{2,1,0:T(8,128)(2,1)} %get-tuple-element.14), calls=%async_computation | async-start | bytes 1048576 | tf_op jit(solution)/shard_map/gather_terms/all_to_all | solution.py:216
  54.7 18.7 %collective-permute-start.6 = (bf16[2,4,1,64,256]{4,3,2,1,0:T(8,128)(2,1)}, bf16[2,4,1,64,256]{4,3,2,1,0:T(8,128)(2,1)S(1)}, u32[]{:S(2)}, u32[]{:S(2)}) collective-permute-start(bf16[2,4,1,64,256]{4,3,2,1,0:T(8,128)(2,1)} %broadcast_select_fusion.7), channel_id=1, source_target_pairs={{1,2},{2,1},{3,4},{4,3},{5,6},{6,5},{7,8},{8,7},{9,10},{10,9},{11,... | collective-permute-start | bytes 786440 | tf_op jit(solution)/shard_map/halo_two/rims_of_rows/odd/ppermute | solution.py:193
  55.4 18.1 %collective-permute-start.7 = (bf16[2,4,1,64,256]{4,3,2,1,0:T(8,128)(2,1)}, bf16[2,4,1,64,256]{4,3,2,1,0:T(8,128)(2,1)S(1)}, u32[]{:S(2)}, u32[]{:S(2)}) collective-permute-start(bf16[2,4,1,64,256]{4,3,2,1,0:T(8,128)(2,1)} %get-tuple-element.18), channel_id=1, source_target_pairs={{0,1},{1,0},{2,3},{3,2},{4,5},{5,4},{6,7},{7,6},{8,9},{9,8},{10,11... | collective-permute-start | bytes 786440 | tf_op jit(solution)/shard_map/halo_two/rims_of_rows/even/ppermute | solution.py:195
  59.2 23.6 %collective-permute-start.8 = (bf16[2,4,64,256]{3,2,1,0:T(8,128)(2,1)S(1)}, bf16[2,4,64,256]{3,2,1,0:T(8,128)(2,1)S(1)}, u32[]{:S(2)}, u32[]{:S(2)}) collective-permute-start(bf16[2,4,64,256]{3,2,1,0:T(8,128)(2,1)S(1)} %get-tuple-element.30), channel_id=1, source_target_pairs={{32,64},{64,32},{33,65},{65,33},{34,66},{66,34},{35,67},{67,35},{3... | collective-permute-start | bytes 786440 | tf_op jit(solution)/shard_map/halo_two/main/odd/ppermute | solution.py:193
  63.3 19.5 %collective-permute-start.9 = (bf16[2,4,64,256]{3,2,1,0:T(8,128)(2,1)S(1)}, bf16[2,4,64,256]{3,2,1,0:T(8,128)(2,1)S(1)}, u32[]{:S(2)}, u32[]{:S(2)}) collective-permute-start(bf16[2,4,64,256]{3,2,1,0:T(8,128)(2,1)S(1)} %get-tuple-element.29), channel_id=1, source_target_pairs={{0,32},{32,0},{64,96},{96,64},{1,33},{33,1},{65,97},{97,65},{2,34}... | collective-permute-start | bytes 786440 | tf_op jit(solution)/shard_map/halo_two/main/even/ppermute | solution.py:195
  68.0 26.5 %all-to-all-start.1 = ((bf16[128,16,128]{2,1,0:T(8,128)(2,1)}), bf16[128,16,128]{2,1,0:T(8,128)(2,1)S(1)}, u32[]{:S(2)}, u32[]{:S(2)}) async-start(bf16[128,16,128]{2,1,0:T(8,128)(2,1)} %broadcast_in_dim.10), calls=%async_computation.1 | async-start | bytes 1048576 | tf_op jit(solution)/shard_map/spread_sums/all_to_all | solution.py:220
  75.6 9.0 %collective-permute-start.10 = (bf16[2,2,64,256]{3,2,1,0:T(8,128)(2,1)}, bf16[2,2,64,256]{3,2,1,0:T(8,128)(2,1)}, u32[]{:S(2)}, u32[]{:S(2)}) collective-permute-start(bf16[2,2,64,256]{3,2,1,0:T(8,128)(2,1)} %select_bitcast_fusion.1), channel_id=1, source_target_pairs={{32,64},{64,32},{33,65},{65,33},{34,66},{66,34},{35,67},{67,35},{3... | collective-permute-start | bytes 393224 | tf_op jit(solution)/shard_map/halo_two/rims_of_frames/odd/ppermute | solution.py:193
  79.2 5.4 %collective-permute-start.11 = (bf16[2,2,64,256]{3,2,1,0:T(8,128)(2,1)}, bf16[2,2,64,256]{3,2,1,0:T(8,128)(2,1)}, u32[]{:S(2)}, u32[]{:S(2)}) collective-permute-start(bf16[2,2,64,256]{3,2,1,0:T(8,128)(2,1)} %get-tuple-element.15), channel_id=1, source_target_pairs={{0,32},{32,0},{64,96},{96,64},{1,33},{33,1},{65,97},{97,65},{2,34}... | collective-permute-start | bytes 393224 | tf_op jit(solution)/shard_map/halo_two/rims_of_frames/even/ppermute | solution.py:195
  82.9 1.7 %copy-start.10 = (bf16[2,4,64,256]{3,2,1,0:T(8,128)(2,1)}, bf16[2,4,64,256]{3,2,1,0:T(8,128)(2,1)S(1)}, u32[]{:S(2)}) copy-start(bf16[2,4,64,256]{3,2,1,0:T(8,128)(2,1)S(1)} %collective-permute-done.8.main_odd) | copy-start | bytes 786436
  82.9 1.7 %copy-start.11 = (bf16[2,4,64,256]{3,2,1,0:T(8,128)(2,1)}, bf16[2,4,64,256]{3,2,1,0:T(8,128)(2,1)S(1)}, u32[]{:S(2)}) copy-start(bf16[2,4,64,256]{3,2,1,0:T(8,128)(2,1)S(1)} %collective-permute-done.9.main_even) | copy-start | bytes 786436
  (7 other events, 5.0 us)

commit v3 on v2

v3 whole, which is shorter than its diff:
```python
import math

import jax
import jax.numpy as jnp
from jax import lax
from jax.experimental import pallas as pl
from jax.experimental.pallas import tpu as pltpu
from jax.sharding import PartitionSpec as P

F32, BF16 = jnp.float32, jnp.bfloat16
NT = (((1,), (1,)), ((), ()))


def shifted(value, by):
    cols = value.shape[1]
    lane = lax.broadcasted_iota(jnp.int32, value.shape, 1)
    outside = lane == (0 if by == 1 else cols - 1)
    return jnp.where(outside, jnp.zeros_like(value), pltpu.roll(value, by % cols, 1))


def convolved(w, taps):
    part = jnp.dot(w[...], taps, preferred_element_type=F32)
    chan = w.shape[0] // 3
    return shifted(part[:chan], 1) + part[chan : 2 * chan] + shifted(part[2 * chan :], -1)


def column_taps(value):
    return jnp.concatenate([shifted(value, -1), value, shifted(value, 1)], axis=0)


def window(x, f, r):
    return x[f : f + 3, r : r + 3].reshape((-1, x.shape[3]))


def rim_window(x, f, r, rims, edge):
    rows = x.shape[1] - 2
    pieces = []
    for g in range(f, f + 3):
        if g not in edge:
            pieces.append(x[g, r : r + 3].reshape((-1, x.shape[3])))
            continue
        corner = rims(g - edge[0], 0 if r == 0 else 1)
        inner = x[g, 1:3] if r == 0 else x[g, rows - 1 : rows + 1]
        inner = inner.reshape((-1, x.shape[3]))
        pieces += [corner, inner] if r == 0 else [inner, corner]
    return jnp.concatenate(pieces, axis=0)


def extend(side, past, future, rows_odd, rows_even, main_odd, main_even, xp, xf):
    frames, rows = past.shape[0], past.shape[1]
    row_even, frame_even = side[0] == 0, side[1] == 0
    for f in range(frames):
        for k, (src, dst, off) in enumerate(((past, xp, 2), (future, xf, 0))):
            odd, even = rows_odd[k, f, 0], rows_even[k, f, 0]
            dst[f + off, 0] = jnp.where(row_even, odd, even)
            dst[f + off, 1 : rows + 1] = src[f]
            dst[f + off, rows + 1] = jnp.where(row_even, even, odd)
    for f in range(2):
        for r in range(rows):
            dst = jnp.where(frame_even, main_odd[f, r], main_even[f, r])
            xp[f, r + 1] = dst
            xf[f + frames, r + 1] = jnp.where(frame_even, main_even[f, r], main_odd[f, r])


def corner_rims(side, rim_odd, rim_even):
    even = side[1] == 0
    past = lambda f, s: jnp.where(even, rim_odd[f, s], rim_even[f, s])
    future = lambda f, s: jnp.where(even, rim_even[f, s], rim_odd[f, s])
    return past, future


def gated(hidden, grad_act):
    sig = jax.nn.sigmoid(hidden)
    return (hidden * sig).astype(BF16), (grad_act * sig * (1.0 + hidden * (1.0 - sig))).astype(BF16)


def weights_kernel(one, two, bias, one_fwd, one_adj, two_fwd, two_adj, bias_out):
    chan = one.shape[1]
    for src, fwd, adj in ((one, one_fwd, one_adj), (two, two_fwd, two_adj)):
        for t in range(3):
            for i in range(3):
                for j in range(3):
                    tap = src[t * 9 + i * 3 + j]
                    left = (t * 3 + i) * chan
                    fwd[j * chan : (j + 1) * chan, left : left + chan] = tap
                    left = (8 - t * 3 - i) * chan
                    flipped = jnp.transpose(tap.astype(F32)).astype(BF16)
                    adj[(2 - j) * chan : (3 - j) * chan, left : left + chan] = flipped
    spread = jnp.broadcast_to(bias[...], (chan, chan))
    lanes = lax.broadcasted_iota(jnp.int32, spread.shape, 1)
    keep = lanes == lax.broadcasted_iota(jnp.int32, spread.shape, 0)
    bias_out[...] = jnp.sum(jnp.where(keep, spread, 0.0), axis=1, keepdims=True)


def first_inner_kernel(side, past, future, rows_odd, rows_even, main_odd, main_even, wp, wf, bias,
                       active_out, pre_out, xp, xf, hid, act, d1, d2, bsum):
    frames, rows, chan, cols = past.shape
    extend(side, past, future, rows_odd, rows_even, main_odd, main_even, xp, xf)
    total = jnp.zeros((chan, cols), F32)
    pres, acts, winp, winf = [], [], [], []
    for f in range(frames):
        for r in range(1, rows - 1):
            winp.append(window(xp, f, r))
            winf.append(window(xf, f, r))
            active, pre = gated(convolved(wp, winp[-1]) + bias[...], convolved(wf, winf[-1]))
            active_out[f, r] = active
            pre_out[f, r] = pre
            acts.append(column_taps(active))
            pres.append(column_taps(pre))
            total = total + pre.astype(F32)
    for k in range(2):
        for s, r in enumerate((0, rows - 1)):
            hid[k, s] = convolved(wp, window(xp, frames - 2 + k, r)) + bias[...]
            act[k, s] = convolved(wf, window(xf, k, r))
    bsum[...] = total
    lanes = lambda parts: jnp.concatenate(parts, axis=1)
    d1[...] = lax.dot_general(lanes(pres), lanes(winp), NT, preferred_element_type=F32)
    d2[...] = lax.dot_general(lanes(winf), lanes(acts), NT, preferred_element_type=F32)


def first_outer_kernel(side, rim_odd, rim_even, xp, xf, hid, act, d1_in, d2_in, bsum, wp, wf, bias, active_in, pre_in,
                       active_out, pre_out, grads, d1, d2):
    frames, rows, chan, cols = active_out.shape
    past_rims, future_rims = corner_rims(side, rim_odd, rim_even)
    total = bsum[...]
    pres, acts, winp, winf = [], [], [], []
    for f in range(frames):
        for s, r in enumerate((0, rows - 1)):
            if f < 2:
                winp.append(rim_window(xp, f, r, past_rims, (0, 1)))
                hidden = convolved(wp, winp[-1]) + bias[...]
                winf.append(window(xf, f, r))
                grad_act = act[f, s]
            else:
                winp.append(window(xp, f, r))
                hidden = hid[f - frames + 2, s]
                winf.append(rim_window(xf, f, r, future_rims, (frames, frames + 1)))
                grad_act = convolved(wf, winf[-1])
            active, pre = gated(hidden, grad_act)
            active_out[f, r] = active
            pre_out[f, r] = pre
            acts.append(column_taps(active))
            pres.append(column_taps(pre))
            total = total + pre.astype(F32)
    for f in range(frames):
        for r in range(1, rows - 1):
            active_out[f, r] = active_in[f, r]
            pre_out[f, r] = pre_in[f, r]
    bias_sum = jnp.sum(total, axis=1, keepdims=True)
    lanes = lambda parts: jnp.concatenate(parts, axis=1)
    d1[...] = d1_in[...] + lax.dot_general(lanes(pres), lanes(winp), NT, preferred_element_type=F32)
    d2[...] = d2_in[...] + lax.dot_general(lanes(winf), lanes(acts), NT, preferred_element_type=F32)
    per = chan // grads.shape[1]
    for t in range(3):
        for i in range(3):
            for j in range(3):
                left, top = (t * 3 + i) * chan, (8 - t * 3 - i) * chan
                one = d1[j * chan : (j + 1) * chan, left : left + chan]
                two = d2[top : top + chan, (2 - j) * chan : (3 - j) * chan]
                tap = (t * 9 + i * 3 + j) * per
                both = jnp.concatenate([one, two], axis=1).astype(grads.dtype)
                grads[tap : tap + per] = both.reshape((per,) + grads.shape[1:])
    used = 27 * per
    bias_rows = jnp.broadcast_to(bias_sum, (chan, grads.shape[2])).astype(grads.dtype)
    grads[used : used + per] = bias_rows.reshape((per,) + grads.shape[1:])
    rest = grads.shape[0] - used - per
    if rest:
        grads[used + per :] = jnp.zeros((rest,) + grads.shape[1:], grads.dtype)


def second_inner_kernel(side, past, future, rows_odd, rows_even, main_odd, main_even, wp, wf, add_past, add_future,
                        out_past, out_future, xp, xf):
    frames, rows, chan, cols = past.shape
    extend(side, past, future, rows_odd, rows_even, main_odd, main_even, xp, xf)
    for f in range(frames):
        for r in range(rows):
            inner = 0 < r < rows - 1
            if f >= 2 or inner:
                out_past[f, r] = (add_past[f, r].astype(F32) + convolved(wp, window(xp, f, r))).astype(BF16)
            if f < frames - 2 or inner:
                out_future[f, r] = (add_future[f, r].astype(F32) + convolved(wf, window(xf, f, r))).astype(BF16)


def second_outer_kernel(side, rim_odd, rim_even, xp, xf, wp, wf, add_past, add_future, past_in, future_in,
                        out_past, out_future):
    frames, rows, chan, cols = out_past.shape
    past_rims, future_rims = corner_rims(side, rim_odd, rim_even)
    for f in range(2):
        for r in (0, rows - 1):
            taps = rim_window(xp, f, r, past_rims, (0, 1))
            out_past[f, r] = (add_past[f, r].astype(F32) + convolved(wp, taps)).astype(BF16)
            g = frames - 2 + f
            taps = rim_window(xf, g, r, future_rims, (frames, frames + 1))
            out_future[g, r] = (add_future[g, r].astype(F32) + convolved(wf, taps)).astype(BF16)
    for f in range(frames):
        for r in range(rows):
            inner = 0 < r < rows - 1
            if f >= 2 or inner:
                out_past[f, r] = past_in[f, r]
            if f < frames - 2 or inner:
                out_future[f, r] = future_in[f, r]


def call(kernel, outs, args, flops, scratch=(), scalars=1):
    vmem = pl.BlockSpec(memory_space=pltpu.VMEM)
    smem = pl.BlockSpec(memory_space=pltpu.SMEM)
    moved = sum(x.size * x.dtype.itemsize for x in list(args) + list(outs))
    return pl.pallas_call(
        kernel,
        out_shape=outs,
        in_specs=[smem] * scalars + [vmem] * (len(args) - scalars),
        out_specs=[vmem] * len(outs),
        scratch_shapes=scratch,
        compiler_params=pltpu.CompilerParams(vmem_limit_bytes=VMEM_LIMIT),
        cost_estimate=pl.CostEstimate(flops=flops, bytes_accessed=moved, transcendentals=0),
        name=kernel.__name__,
    )(*args)


VMEM_LIMIT = 24 * 1024 * 1024


def arrays(*shapes, kind=BF16):
    return [jax.ShapeDtypeStruct(shape, kind) for shape in shapes]


def flat_weights(one, two, bias):
    chan = bias.shape[0]
    taps = (27, chan, chan)
    outs = arrays(*[(3 * chan, 9 * chan)] * 4) + arrays((chan, 1), kind=F32)
    return call(weights_kernel, outs, (one.reshape(taps), two.reshape(taps), bias[None]), 0, scalars=0)


def conv_flops(shape, rows):
    return 2 * 27 * shape[2] * shape[2] * shape[3] * rows


def first_inner(side, past, future, edges, wp, wf, bias):
    shape = past.shape
    frames, rows, chan, cols = shape
    extended = (frames + 2, rows + 2, chan, cols)
    outs = arrays(shape, shape, extended, extended) + arrays(
        (2, 2, chan, cols), (2, 2, chan, cols), (3 * chan, 9 * chan), (9 * chan, 3 * chan), (chan, cols), kind=F32)
    return call(first_inner_kernel, outs, (side, past, future, *edges, wp, wf, bias), conv_flops(shape, 40))


def first_outer(devices, side, rims, inner, wp, wf, bias):
    active, pre, *rest = inner
    frames, rows, chan, cols = active.shape
    outs = arrays(active.shape, pre.shape, (devices, 16, 2 * chan))
    scratch = [pltpu.VMEM((3 * chan, 9 * chan), F32), pltpu.VMEM((9 * chan, 3 * chan), F32)]
    args = (side, *rims, *rest, wp, wf, bias, active, pre)
    return call(first_outer_kernel, outs, args, conv_flops(active.shape, 24), scratch)


def second_inner(side, past, future, edges, wp, wf, add_past, add_future):
    shape = past.shape
    frames, rows, chan, cols = shape
    extended = (frames + 2, rows + 2, chan, cols)
    args = (side, past, future, *edges, wp, wf, add_past, add_future)
    return call(second_inner_kernel, arrays(shape, shape, extended, extended), args, conv_flops(shape, 24))


def second_outer(side, rims, inner, wp, wf, add_past, add_future):
    out_past, out_future, xp, xf = inner
    args = (side, *rims, xp, xf, wp, wf, add_past, add_future, out_past, out_future)
    return call(second_outer_kernel, arrays(out_past.shape, out_past.shape), args, conv_flops(out_past.shape, 8))


AXES = ("frames", "rows")


def pairs_of(count, first):
    pairs = []
    for i in range(first, count - 1, 2):
        pairs += [(i, i + 1), (i + 1, i)]
    return pairs


def swap_neighbours(axis, even, to_next, to_prior):
    count = lax.axis_size(axis)
    with jax.named_scope("odd"):
        odd_pairs = lax.ppermute(jnp.where(even, to_prior, to_next), axis, pairs_of(count, 1))
    with jax.named_scope("even"):
        even_pairs = lax.ppermute(jnp.where(even, to_next, to_prior), axis, pairs_of(count, 0))
    return odd_pairs, even_pairs


def edges_of(side, past, future):
    both = jnp.stack([past, future])
    with jax.named_scope("rims_of_rows"):
        rows = swap_neighbours("rows", side[0] == 0, both[:, :, -1:], both[:, :, :1])
    with jax.named_scope("main"):
        main = swap_neighbours("frames", side[1] == 0, past[-2:], future[:2])
    return (*rows, *main)


def rims_of(side, rows_odd, rows_even):
    row_even = side[0] == 0
    low = jnp.where(row_even, rows_odd, rows_even)
    high = jnp.where(row_even, rows_even, rows_odd)
    rims = jnp.concatenate([low, high], axis=2)
    with jax.named_scope("rims_of_frames"):
        return swap_neighbours("frames", side[1] == 0, rims[0, -2:], rims[1, :2])


def total_over_devices(parts):
    with jax.named_scope("gather_terms"):
        mine = lax.all_to_all(parts, AXES, 0, 0, tiled=True)
    mine = jnp.sum(mine.astype(jnp.float32), axis=0).astype(jnp.bfloat16)
    spread = jnp.broadcast_to(mine[None], parts.shape)
    with jax.named_scope("spread_sums"):
        return lax.all_to_all(spread, AXES, 0, 0, tiled=True)


def per_device(clip_in, kernel_one, bias_one, kernel_two, cotangent):
    frame_count, row_count, channels, col_count = clip_in.shape
    devices = lax.axis_size("frames") * lax.axis_size("rows")
    side = jnp.stack([lax.axis_index("rows") % 2, lax.axis_index("frames") % 2]).astype(jnp.int32)
    with jax.named_scope("halo_one"):
        edges = edges_of(side, clip_in, cotangent)
    one_fwd, one_adj, two_fwd, two_adj, bias = flat_weights(kernel_one, kernel_two, bias_one)
    with jax.named_scope("halo_one"):
        rims = rims_of(side, *edges[:2])
    inner = first_inner(side, clip_in, cotangent, edges, one_fwd, two_adj, bias)
    active, grad_pre, terms = first_outer(devices, side, rims, inner, one_fwd, two_adj, bias)
    total = total_over_devices(terms)
    with jax.named_scope("halo_two"):
        edges = edges_of(side, active, grad_pre)
        rims = rims_of(side, *edges[:2])
    inner = second_inner(side, active, grad_pre, edges, two_fwd, one_adj, clip_in, cotangent)
    block_out, grad_input = second_outer(side, rims, inner, two_fwd, one_adj, clip_in, cotangent)
    cell_total = (
        frame_count * lax.axis_size("frames") * row_count * lax.axis_size("rows") * col_count
    )
    total = total.reshape((-1, 2 * channels)).astype(jnp.float32) * (1.0 / math.sqrt(cell_total))
    count = 27 * channels
    return (
        block_out,
        grad_input,
        total[:count, :channels].reshape(kernel_one.shape),
        total[:count, channels:].reshape(kernel_two.shape),
        total[count : count + channels, 0],
    )


def solution(mesh):
    in_specs = (P("frames", "rows", None, None), P(), P(), P(), P("frames", "rows", None, None))
    out_specs = (P("frames", "rows", None, None), P("frames", "rows", None, None), P(), P(), P())
    return jax.shard_map(
        per_device, mesh=mesh, in_specs=in_specs, out_specs=out_specs, check_vma=False
    )
```

time: 97.1 us -> 83.1 us (0.86)
  local copies, waits for them, and re-layouts: 14.3 us -> 2.98 us
  Pallas kernels: 25.5 us -> 14.3 us
  waiting for transfers between devices: 6.18 us -> 11.6 us
  starting transfers between devices: 44.5 us -> 46.3 us
  other arithmetic: 5.14 us -> 6.55 us
    pallas_call x2 -> x5, Pallas kernels: 25.5 us -> 14.3 us  [call(): pl.pallas_call(kernel, out_shape=outs, in_specs=[smem] * scalars + [vmem]...]
    all_to_all x1, starting transfers between devices: 5.39 us -> 12.1 us  [total_over_devices(): return lax.all_to_all(spread, AXES, 0, 0, tiled=True)]
    ppermute x6, starting transfers between devices: 8.74 us -> 4.06 us  [swap_neighbours(): lax.ppermute(jnp.where(even, to_next, to_prior), axis, pairs_of(count, 0))]
    ppermute x6, waiting for transfers between devices: 0.9 us -> 5.31 us  [swap_neighbours(): lax.ppermute(jnp.where(even, to_next, to_prior), axis, pairs_of(count, 0))]
    reshape x4 -> x0, local copies, waits for them, and re-layouts: 4.38 us -> none  [the longest x2 2.19 us: flat_adjoint(): jnp.transpose(kernel[::-1, ::-1, ::-1], (0, 4, 1, 2, 3))]
    ppermute x6, waiting for transfers between devices: 1.7 us -> 5.3 us  [swap_neighbours(): lax.ppermute(jnp.where(even, to_prior, to_next), axis, pairs_of(count, 1))]
    unnamed x34 -> x10, local copies, waits for them, and re-layouts: 3.54 us -> 0.03 us
    all_to_all x1, waiting for transfers between devices: 3.57 us -> 0.41 us  [total_over_devices(): mine = lax.all_to_all(parts, AXES, 0, 0, tiled=True)]
  transfers between devices with their start and end apart: 14 -> 14, of which waited for: 3 -> 5; matrix products, arithmetic and copies ran while one was open for 13% -> 6% of each run, Pallas kernels for 10% -> 13%
where the time goes in v3:
time: 83.1 us; the launch traced here: 82.6 us
  starting transfers between devices  46.3 us (56%)
  Pallas kernels  14.3 us (17%)
  waiting for transfers between devices  11.6 us (14%)
  other arithmetic  6.55 us (8%)
  local copies, waits for them, and re-layouts  2.98 us (4%)
  between operations  0.96 us (1%)
    ppermute x6, starting transfers between devices, swap_neighbours(): lax.ppermute(jnp.where(even, to_prior, to_next), axis, pairs_of(count, 1))  17.9 us
    pallas_call x5, Pallas kernels, call(): pl.pallas_call(kernel, out_shape=outs, in_specs=[smem] * scalars + [vmem]...  14.3 us
    all_to_all x1, starting transfers between devices, total_over_devices(): mine = lax.all_to_all(parts, AXES, 0, 0, tiled=True)  12.2 us
    all_to_all x1, starting transfers between devices, total_over_devices(): return lax.all_to_all(spread, AXES, 0, 0, tiled=True)  12.1 us
    ppermute x6, waiting for transfers between devices, swap_neighbours(): lax.ppermute(jnp.where(even, to_next, to_prior), axis, pairs_of(count, 0))  5.31 us
    ppermute x6, waiting for transfers between devices, swap_neighbours(): lax.ppermute(jnp.where(even, to_prior, to_next), axis, pairs_of(count, 1))  5.3 us
    ppermute x6, starting transfers between devices, swap_neighbours(): lax.ppermute(jnp.where(even, to_next, to_prior), axis, pairs_of(count, 0))  4.06 us
    select_n x6, other arithmetic, swap_neighbours(): jnp.where(even, to_next, to_prior)  1.96 us
  transfers between devices with their start and end apart: 14, of which 5 were waited for; matrix products, arithmetic and copies ran while one was open for 6% of the time, Pallas kernels for 13%

profile of v3, /device:TPU:1, one launch (start us, length us, event | category | flops | bytes accessed | tf_op | source)
XLA Modules:
  0.0 82.6 jit_solution(17183340707499181219)
XLA Ops:
  0.7 1.2 %broadcast_select_fusion.11 = (bf16[2,4,1,64,256]{4,3,2,1,0:T(8,128)(2,1)S(1)}, bf16[2,4,1,64,256]{4,3,2,1,0:T(8,128)(2,1)S(1)}, bf16[2,4,1,64,256]{4,3,2,1,0:T(8,128)(2,1)S(1)}) fusion(pred[]{:T(512)S(6)} %eq.8, bf16[1,4,4,64,256]{4,3,2,1,0:T(8,128)(2,1)} %bitcast.20, bf16[1,4,4,64,256]{4,3,2,1,0:T(8,128)(2,1)} %bitcast.21), kind=kLoop, calls=%fused_computation.16 | loop fusion | flops 393216 | bytes 1835009 | tf_op jit(solution)/shard_map/halo_one/rims_of_rows/odd/jit(_where)/select_n | solution.py:283
  2.0 2.1 %collective-permute-start.1 = (bf16[2,4,1,64,256]{4,3,2,1,0:T(8,128)(2,1)S(1)}, bf16[2,4,1,64,256]{4,3,2,1,0:T(8,128)(2,1)S(1)}, u32[]{:S(2)}, u32[]{:S(2)}) collective-permute-start(bf16[2,4,1,64,256]{4,3,2,1,0:T(8,128)(2,1)S(1)} %broadcast_select_fusion.10), channel_id=1, source_target_pairs={{0,1},{1,0},{2,3},{3,2},{4,5},{5,4},{6,7},{7,6},{8,9},{9,8},{10,11... | collective-permute-start | bytes 786440 | tf_op jit(solution)/shard_map/halo_one/rims_of_rows/even/ppermute | solution.py:285
  4.8 4.4 %collective-permute-start.4 = (bf16[2,4,64,256]{3,2,1,0:T(8,128)(2,1)S(1)}, bf16[2,4,64,256]{3,2,1,0:T(8,128)(2,1)S(1)}, u32[]{:S(2)}, u32[]{:S(2)}) collective-permute-start(bf16[2,4,64,256]{3,2,1,0:T(8,128)(2,1)S(1)} %get-tuple-element.68), channel_id=1, source_target_pairs={{32,64},{64,32},{33,65},{65,33},{34,66},{66,34},{35,67},{67,35},{3... | collective-permute-start | bytes 786440 | tf_op jit(solution)/shard_map/halo_one/main/odd/ppermute | solution.py:283
  9.4 0.8 weights_kernel.1
  10.4 4.8 %collective-permute-start.2 = (bf16[2,2,64,256]{3,2,1,0:T(8,128)(2,1)S(1)}, bf16[2,2,64,256]{3,2,1,0:T(8,128)(2,1)S(1)}, u32[]{:S(2)}, u32[]{:S(2)}) collective-permute-start(bf16[2,2,64,256]{3,2,1,0:T(8,128)(2,1)S(1)} %select_bitcast_fusion.3), channel_id=1, source_target_pairs={{32,64},{64,32},{33,65},{65,33},{34,66},{66,34},{35,67},{67,35},{3... | collective-permute-start | bytes 393224 | tf_op jit(solution)/shard_map/halo_one/rims_of_frames/odd/ppermute | solution.py:283
  15.3 4.1 %first_inner_kernel.1 = (bf16[4,4,64,256]{3,2,1,0:T(8,128)(2,1)S(1)}, bf16[4,4,64,256]{3,2,1,0:T(8,128)(2,1)S(1)}, bf16[6,6,64,256]{3,2,1,0:T(8,128)(2,1)S(1)}, ...) custom-call(s32[2]{0:T(128)S(1)} %pad_add_fusion.side, ...), custom_call_target="tpu_custom_call" | custom-call | flops 2264924160 | bytes 7422216 | tf_op jit(solution)/shard_map/first_inner_kernel/pallas_call | solution.py:208
  19.4 3.1 %collective-permute-done.2.rim_odd = bf16[2,2,64,256]{3,2,1,0:T(8,128)(2,1)S(1)} collective-permute-done((bf16[2,2,64,256]{3,2,1,0:T(8,128)(2,1)S(1)}, bf16[2,2,64,256]{3,2,1,0:T(8,128)(2,1)S(1)}, u32[]{:S(2)}, u32[]{:S(2)}) %collective-permute-start.2) | collective-permute-done | bytes 131104 | tf_op jit(solution)/shard_map/halo_one/rims_of_frames/odd/ppermute | solution.py:283
  22.5 3.8 %first_outer_kernel.1 = (bf16[4,4,64,256]{3,2,1,0:T(8,128)(2,1)S(1)}, bf16[4,4,64,256]{3,2,1,0:T(8,128)(2,1)S(1)}, bf16[128,16,128]{2,1,0:T(8,128)(2,1)}) custom-call(s32[2]{0:T(128)S(1)} %pad_add_fusion.side, bf16[2,2,64,256]{3,2,1,0:T(8,128)(2,1)S(1)} %collective-permute-done.2.rim_odd, bf16[2,2,64,256]{3,2,1,0:T(8,128)(2,1)S(1)} %collective-permute-done.3.rim_even, ...), custom_call_target="tpu_custom_call" | custom-call | flops 1358954496 | bytes 7160072 | tf_op jit(solution)/shard_map/first_outer_kernel/pallas_call | solution.py:208
  26.3 12.2 %all-to-all-start = ((bf16[128,16,128]{2,1,0:T(8,128)(2,1)}), bf16[128,16,128]{2,1,0:T(8,128)(2,1)}, u32[]{:S(2)}, u32[]{:S(2)}) async-start(bf16[128,16,128]{2,1,0:T(8,128)(2,1)} %get-tuple-element.50), calls=%async_computation | async-start | bytes 1048576 | tf_op jit(solution)/shard_map/gather_terms/all_to_all | solution.py:309
  38.6 1.4 %collective-permute-start.7 = (bf16[2,4,1,64,256]{4,3,2,1,0:T(8,128)(2,1)S(1)}, bf16[2,4,1,64,256]{4,3,2,1,0:T(8,128)(2,1)S(1)}, u32[]{:S(2)}, u32[]{:S(2)}) collective-permute-start(bf16[2,4,1,64,256]{4,3,2,1,0:T(8,128)(2,1)S(1)} %broadcast_select_fusion.6), channel_id=1, source_target_pairs={{0,1},{1,0},{2,3},{3,2},{4,5},{5,4},{6,7},{7,6},{8,9},{9,8},{10,11... | collective-permute-start | bytes 786440 | tf_op jit(solution)/shard_map/halo_two/rims_of_rows/even/ppermute | solution.py:285
  40.7 0.9 %broadcast_select_fusion = (bf16[2,4,64,256]{3,2,1,0:T(8,128)(2,1)}, bf16[2,4,64,256]{3,2,1,0:T(8,128)(2,1)}) fusion(pred[]{:T(512)S(6)} %eq.7, bf16[4,4,64,256]{3,2,1,0:T(8,128)(2,1)S(1)} %get-tuple-element.40.past, bf16[4,4,64,256]{3,2,1,0:T(8,128)(2,1)S(1)} %get-tuple-element.41.future), kind=kLoop, calls=%fused_computation.5 | loop fusion | flops 262144 | bytes 1048577 | tf_op jit(solution)/shard_map/halo_two/main/even/jit(_where)/select_n | solution.py:285
  41.6 3.8 %collective-permute-start.10 = (bf16[2,4,64,256]{3,2,1,0:T(8,128)(2,1)}, bf16[2,4,64,256]{3,2,1,0:T(8,128)(2,1)S(1)}, u32[]{:S(2)}, u32[]{:S(2)}) collective-permute-start(bf16[2,4,64,256]{3,2,1,0:T(8,128)(2,1)} %get-tuple-element.66), channel_id=1, source_target_pairs={{32,64},{64,32},{33,65},{65,33},{34,66},{66,34},{35,67},{67,35},{3... | collective-permute-start | bytes 786440 | tf_op jit(solution)/shard_map/halo_two/main/odd/ppermute | solution.py:283
  45.5 5.3 %collective-permute-done.7.rows_even = bf16[2,4,1,64,256]{4,3,2,1,0:T(8,128)(2,1)S(1)} collective-permute-done((bf16[2,4,1,64,256]{4,3,2,1,0:T(8,128)(2,1)S(1)}, bf16[2,4,1,64,256]{4,3,2,1,0:T(8,128)(2,1)S(1)}, u32[]{:S(2)}, u32[]{:S(2)}) %collective-permute-start.7) | collective-permute-done | bytes 262176 | tf_op jit(solution)/shard_map/halo_two/rims_of_rows/even/ppermute | solution.py:285
  50.8 0.8 %broadcast_select_fusion.5 = (bf16[2,4,1,64,256]{4,3,2,1,0:T(8,128)(2,1)}, bf16[2,4,1,64,256]{4,3,2,1,0:T(8,128)(2,1)}) fusion(bf16[2,4,1,64,256]{4,3,2,1,0:T(8,128)(2,1)S(1)} %collective-permute-done.6.rows_odd, bf16[2,4,1,64,256]{4,3,2,1,0:T(8,128)(2,1)S(1)} %collective-permute-done.7.rows_even, pred[]{:T(512)S(6)} %eq.8), kind=kLoop, calls=%fused_computation.10 | loop fusion | flops 262144 | bytes 1048577 | tf_op jit(solution)/shard_map/halo_two/jit(_where)/select_n | solution.py:300
  52.0 1.2 %reduce_sum.12 = bf16[16,128]{1,0:T(8,128)(2,1)S(1)} reduce(bf16[128,16,128]{2,1,0:T(8,128)(2,1)} %all-to-all-done, bf16[]{:T(256)} %constant.30.clone.1), dimensions={0}, to_apply=%region_0.1 | reduce | flops 260096 | bytes 528386 | tf_op jit(solution)/shard_map/reduce_sum | solution.py:310
  53.2 0.9 %broadcast_in_dim.10 = bf16[128,16,128]{2,1,0:T(8,128)(2,1)} broadcast(bf16[16,128]{1,0:T(8,128)(2,1)S(1)} %reduce_sum.12), dimensions={1,2} | broadcast | bytes 528384 | tf_op jit(solution)/shard_map/broadcast_in_dim | solution.py:311
  54.1 12.1 %all-to-all-start.1 = ((bf16[128,16,128]{2,1,0:T(8,128)(2,1)}), bf16[128,16,128]{2,1,0:T(8,128)(2,1)}, u32[]{:S(2)}, u32[]{:S(2)}) async-start(bf16[128,16,128]{2,1,0:T(8,128)(2,1)} %broadcast_in_dim.10), calls=%async_computation.1 | async-start | bytes 1048576 | tf_op jit(solution)/shard_map/spread_sums/all_to_all | solution.py:313
  66.1 1.0 %select_bitcast_fusion = (bf16[2,2,64,256]{3,2,1,0:T(8,128)(2,1)S(1)}, bf16[1,2,2,64,256]{4,3,2,1,0:T(8,128)(2,1)S(1)}, bf16[1,2,2,64,256]{4,3,2,1,0:T(8,128)(2,1)S(1)}) fusion(pred[]{:T(512)S(6)} %eq.7, bf16[2,4,1,64,256]{4,3,2,1,0:T(8,128)(2,1)} %get-tuple-element.70, bf16[2,4,1,64,256]{4,3,2,1,0:T(8,128)(2,1)} %get-tuple-element.69), kind=kLoop, calls=%fused_computation.21 | loop fusion | flops 196608 | bytes 917505 | tf_op jit(solution)/shard_map/halo_two/rims_of_frames/even/jit(_where)/select_n | solution.py:285
  67.1 3.7 %collective-permute-start.8 = (bf16[2,2,64,256]{3,2,1,0:T(8,128)(2,1)S(1)}, bf16[2,2,64,256]{3,2,1,0:T(8,128)(2,1)S(1)}, u32[]{:S(2)}, u32[]{:S(2)}) collective-permute-start(bf16[2,2,64,256]{3,2,1,0:T(8,128)(2,1)S(1)} %select_bitcast_fusion.1), channel_id=1, source_target_pairs={{32,64},{64,32},{33,65},{65,33},{34,66},{66,34},{35,67},{67,35},{3... | collective-permute-start | bytes 393224 | tf_op jit(solution)/shard_map/halo_two/rims_of_frames/odd/ppermute | solution.py:283
  71.1 3.1 %second_inner_kernel.1 = (bf16[4,4,64,256]{3,2,1,0:T(8,128)(2,1)S(1)}, bf16[4,4,64,256]{3,2,1,0:T(8,128)(2,1)S(1)}, bf16[6,6,64,256]{3,2,1,0:T(8,128)(2,1)S(1)}, bf16[6,6,64,256]{3,2,1,0:T(8,128)(2,1)S(1)}) custom-call(s32[2]{0:T(128)S(1)} %pad_add_fusion.side, bf16[4,4,64,256]{3,2,1,0:T(8,128)(2,1)S(1)} %get-tuple-element.40.past, ...), custom_call_target="tpu_custom_call" | custom-call | flops 1358954496 | bytes 6995976 | tf_op jit(solution)/shard_map/second_inner_kernel/pallas_call | solution.py:208
  74.2 2.2 %collective-permute-done.8.rim_odd = bf16[2,2,64,256]{3,2,1,0:T(8,128)(2,1)S(1)} collective-permute-done((bf16[2,2,64,256]{3,2,1,0:T(8,128)(2,1)S(1)}, bf16[2,2,64,256]{3,2,1,0:T(8,128)(2,1)S(1)}, u32[]{:S(2)}, u32[]{:S(2)}) %collective-permute-start.8) | collective-permute-done | bytes 131104 | tf_op jit(solution)/shard_map/halo_two/rims_of_frames/odd/ppermute | solution.py:283
  76.4 2.4 %second_outer_kernel.1 = (bf16[4,4,64,256]{3,2,1,0:T(8,128)(2,1)}, bf16[4,4,64,256]{3,2,1,0:T(8,128)(2,1)}) custom-call(s32[2]{0:T(128)S(1)} %pad_add_fusion.side, bf16[2,2,64,256]{3,2,1,0:T(8,128)(2,1)S(1)} %collective-permute-done.8.rim_odd, bf16[2,2,64,256]{3,2,1,0:T(8,128)(2,1)S(1)} %collective-permute-done.9.rim_even, ...), custom_call_target="tpu_custom_call" | custom-call | flops 452984832 | bytes 6209544 | tf_op jit(solution)/shard_map/second_outer_kernel/pallas_call | solution.py:208
  79.4 1.1 %convert_multiply_fusion = f32[128,16,128]{2,1,0:T(8,128)S(1)} fusion(bf16[128,16,128]{2,1,0:T(8,128)(2,1)} %all-to-all-done.1), kind=kLoop, calls=%fused_computation | loop fusion | flops 524288 | bytes 1572864 | tf_op jit(solution)/shard_map/mul | solution.py:336
  80.5 1.5 %fusion = (f32[1728,64]{1,0:T(8,128)}, f32[1728,64]{1,0:T(8,128)}) fusion(f32[2048,128]{1,0:T(8,128)S(1)} %bitcast.27), kind=kLoop, calls=%fused_computation.27 | loop fusion | bytes 1769472 | tf_op jit(solution)/shard_map/slice | solution.py:342
  (37 shorter events, 3.8 us)
Async XLA Ops:
  0.6 4.1 %copy-start = (bf16[4,4,64,256]{3,2,1,0:T(8,128)(2,1)S(1)}, bf16[4,4,64,256]{3,2,1,0:T(8,128)(2,1)}, u32[]{:S(2)}) copy-start(bf16[4,4,64,256]{3,2,1,0:T(8,128)(2,1)} %add_future.3) | copy-start | bytes 1572868
  0.7 4.1 %copy-start.1 = (bf16[4,4,64,256]{3,2,1,0:T(8,128)(2,1)S(1)}, bf16[4,4,64,256]{3,2,1,0:T(8,128)(2,1)}, u32[]{:S(2)}) copy-start(bf16[4,4,64,256]{3,2,1,0:T(8,128)(2,1)} %add_past.3) | copy-start | bytes 1572868
  1.9 7.4 %copy-start.2 = (bf16[3,3,3,64,64]{4,3,2,1,0:T(8,128)(2,1)S(1)}, bf16[3,3,3,64,64]{4,3,2,1,0:T(8,128)(2,1)}, u32[]{:S(2)}) copy-start(bf16[3,3,3,64,64]{4,3,2,1,0:T(8,128)(2,1)} %param.6) | copy-start | bytes 663556
  1.9 7.4 %copy-start.3 = (bf16[3,3,3,64,64]{4,3,2,1,0:T(8,128)(2,1)S(1)}, bf16[3,3,3,64,64]{4,3,2,1,0:T(8,128)(2,1)}, u32[]{:S(2)}) copy-start(bf16[3,3,3,64,64]{4,3,2,1,0:T(8,128)(2,1)} %param.8) | copy-start | bytes 663556
  1.9 7.4 %copy-start.4 = (f32[64]{0:T(128)S(1)}, f32[64]{0:T(128)}, u32[]{:S(2)}) copy-start(f32[64]{0:T(128)} %param.7) | copy-start | bytes 772
  2.0 8.3 %collective-permute-start.1 = (bf16[2,4,1,64,256]{4,3,2,1,0:T(8,128)(2,1)S(1)}, bf16[2,4,1,64,256]{4,3,2,1,0:T(8,128)(2,1)S(1)}, u32[]{:S(2)}, u32[]{:S(2)}) collective-permute-start(bf16[2,4,1,64,256]{4,3,2,1,0:T(8,128)(2,1)S(1)} %broadcast_select_fusion.10), channel_id=1, source_target_pairs={{0,1},{1,0},{2,3},{3,2},{4,5},{5,4},{6,7},{7,6},{8,9},{9,8},{10,11... | collective-permute-start | bytes 786440 | tf_op jit(solution)/shard_map/halo_one/rims_of_rows/even/ppermute | solution.py:285
  4.1 6.2 %collective-permute-start = (bf16[2,4,1,64,256]{4,3,2,1,0:T(8,128)(2,1)S(1)}, bf16[2,4,1,64,256]{4,3,2,1,0:T(8,128)(2,1)S(1)}, u32[]{:S(2)}, u32[]{:S(2)}) collective-permute-start(bf16[2,4,1,64,256]{4,3,2,1,0:T(8,128)(2,1)S(1)} %get-tuple-element.60), channel_id=1, source_target_pairs={{1,2},{2,1},{3,4},{4,3},{5,6},{6,5},{7,8},{8,7},{9,10},{10,9},{11,... | collective-permute-start | bytes 786440 | tf_op jit(solution)/shard_map/halo_one/rims_of_rows/odd/ppermute | solution.py:283
  4.8 10.4 %collective-permute-start.4 = (bf16[2,4,64,256]{3,2,1,0:T(8,128)(2,1)S(1)}, bf16[2,4,64,256]{3,2,1,0:T(8,128)(2,1)S(1)}, u32[]{:S(2)}, u32[]{:S(2)}) collective-permute-start(bf16[2,4,64,256]{3,2,1,0:T(8,128)(2,1)S(1)} %get-tuple-element.68), channel_id=1, source_target_pairs={{32,64},{64,32},{33,65},{65,33},{34,66},{66,34},{35,67},{67,35},{3... | collective-permute-start | bytes 786440 | tf_op jit(solution)/shard_map/halo_one/main/odd/ppermute | solution.py:283
  9.2 6.0 %collective-permute-start.5 = (bf16[2,4,64,256]{3,2,1,0:T(8,128)(2,1)S(1)}, bf16[2,4,64,256]{3,2,1,0:T(8,128)(2,1)S(1)}, u32[]{:S(2)}, u32[]{:S(2)}) collective-permute-start(bf16[2,4,64,256]{3,2,1,0:T(8,128)(2,1)S(1)} %get-tuple-element.67), channel_id=1, source_target_pairs={{0,32},{32,0},{64,96},{96,64},{1,33},{33,1},{65,97},{97,65},{2,34}... | collective-permute-start | bytes 786440 | tf_op jit(solution)/shard_map/halo_one/main/even/ppermute | solution.py:285
  10.4 12.1 %collective-permute-start.2 = (bf16[2,2,64,256]{3,2,1,0:T(8,128)(2,1)S(1)}, bf16[2,2,64,256]{3,2,1,0:T(8,128)(2,1)S(1)}, u32[]{:S(2)}, u32[]{:S(2)}) collective-permute-start(bf16[2,2,64,256]{3,2,1,0:T(8,128)(2,1)S(1)} %select_bitcast_fusion.3), channel_id=1, source_target_pairs={{32,64},{64,32},{33,65},{65,33},{34,66},{66,34},{35,67},{67,35},{3... | collective-permute-start | bytes 393224 | tf_op jit(solution)/shard_map/halo_one/rims_of_frames/odd/ppermute | solution.py:283
  15.2 7.4 %collective-permute-start.3 = (bf16[2,2,64,256]{3,2,1,0:T(8,128)(2,1)S(1)}, bf16[2,2,64,256]{3,2,1,0:T(8,128)(2,1)S(1)}, u32[]{:S(2)}, u32[]{:S(2)}) collective-permute-start(bf16[2,2,64,256]{3,2,1,0:T(8,128)(2,1)S(1)} %get-tuple-element.57), channel_id=1, source_target_pairs={{0,32},{32,0},{64,96},{96,64},{1,33},{33,1},{65,97},{97,65},{2,34}... | collective-permute-start | bytes 393224 | tf_op jit(solution)/shard_map/halo_one/rims_of_frames/even/ppermute | solution.py:285
  26.3 25.7 %all-to-all-start = ((bf16[128,16,128]{2,1,0:T(8,128)(2,1)}), bf16[128,16,128]{2,1,0:T(8,128)(2,1)}, u32[]{:S(2)}, u32[]{:S(2)}) async-start(bf16[128,16,128]{2,1,0:T(8,128)(2,1)} %get-tuple-element.50), calls=%async_computation | async-start | bytes 1048576 | tf_op jit(solution)/shard_map/gather_terms/all_to_all | solution.py:309
  38.6 12.1 %collective-permute-start.7 = (bf16[2,4,1,64,256]{4,3,2,1,0:T(8,128)(2,1)S(1)}, bf16[2,4,1,64,256]{4,3,2,1,0:T(8,128)(2,1)S(1)}, u32[]{:S(2)}, u32[]{:S(2)}) collective-permute-start(bf16[2,4,1,64,256]{4,3,2,1,0:T(8,128)(2,1)S(1)} %broadcast_select_fusion.6), channel_id=1, source_target_pairs={{0,1},{1,0},{2,3},{3,2},{4,5},{5,4},{6,7},{7,6},{8,9},{9,8},{10,11... | collective-permute-start | bytes 786440 | tf_op jit(solution)/shard_map/halo_two/rims_of_rows/even/ppermute | solution.py:285
  40.1 10.7 %collective-permute-start.6 = (bf16[2,4,1,64,256]{4,3,2,1,0:T(8,128)(2,1)S(1)}, bf16[2,4,1,64,256]{4,3,2,1,0:T(8,128)(2,1)S(1)}, u32[]{:S(2)}, u32[]{:S(2)}) collective-permute-start(bf16[2,4,1,64,256]{4,3,2,1,0:T(8,128)(2,1)S(1)} %get-tuple-element.54), channel_id=1, source_target_pairs={{1,2},{2,1},{3,4},{4,3},{5,6},{6,5},{7,8},{8,7},{9,10},{10,9},{11,... | collective-permute-start | bytes 786440 | tf_op jit(solution)/shard_map/halo_two/rims_of_rows/odd/ppermute | solution.py:283
  41.6 29.5 %collective-permute-start.10 = (bf16[2,4,64,256]{3,2,1,0:T(8,128)(2,1)}, bf16[2,4,64,256]{3,2,1,0:T(8,128)(2,1)S(1)}, u32[]{:S(2)}, u32[]{:S(2)}) collective-permute-start(bf16[2,4,64,256]{3,2,1,0:T(8,128)(2,1)} %get-tuple-element.66), channel_id=1, source_target_pairs={{32,64},{64,32},{33,65},{65,33},{34,66},{66,34},{35,67},{67,35},{3... | collective-permute-start | bytes 786440 | tf_op jit(solution)/shard_map/halo_two/main/odd/ppermute | solution.py:283
  45.4 25.7 %collective-permute-start.11 = (bf16[2,4,64,256]{3,2,1,0:T(8,128)(2,1)}, bf16[2,4,64,256]{3,2,1,0:T(8,128)(2,1)}, u32[]{:S(2)}, u32[]{:S(2)}) collective-permute-start(bf16[2,4,64,256]{3,2,1,0:T(8,128)(2,1)} %get-tuple-element.65), channel_id=1, source_target_pairs={{0,32},{32,0},{64,96},{96,64},{1,33},{33,1},{65,97},{97,65},{2,34}... | collective-permute-start | bytes 786440 | tf_op jit(solution)/shard_map/halo_two/main/even/ppermute | solution.py:285
  54.1 25.3 %all-to-all-start.1 = ((bf16[128,16,128]{2,1,0:T(8,128)(2,1)}), bf16[128,16,128]{2,1,0:T(8,128)(2,1)}, u32[]{:S(2)}, u32[]{:S(2)}) async-start(bf16[128,16,128]{2,1,0:T(8,128)(2,1)} %broadcast_in_dim.10), calls=%async_computation.1 | async-start | bytes 1048576 | tf_op jit(solution)/shard_map/spread_sums/all_to_all | solution.py:313
  67.1 9.3 %collective-permute-start.8 = (bf16[2,2,64,256]{3,2,1,0:T(8,128)(2,1)S(1)}, bf16[2,2,64,256]{3,2,1,0:T(8,128)(2,1)S(1)}, u32[]{:S(2)}, u32[]{:S(2)}) collective-permute-start(bf16[2,2,64,256]{3,2,1,0:T(8,128)(2,1)S(1)} %select_bitcast_fusion.1), channel_id=1, source_target_pairs={{32,64},{64,32},{33,65},{65,33},{34,66},{66,34},{35,67},{67,35},{3... | collective-permute-start | bytes 393224 | tf_op jit(solution)/shard_map/halo_two/rims_of_frames/odd/ppermute | solution.py:283
  70.8 5.6 %collective-permute-start.9 = (bf16[2,2,64,256]{3,2,1,0:T(8,128)(2,1)S(1)}, bf16[2,2,64,256]{3,2,1,0:T(8,128)(2,1)S(1)}, u32[]{:S(2)}, u32[]{:S(2)}) collective-permute-start(bf16[2,2,64,256]{3,2,1,0:T(8,128)(2,1)S(1)} %get-tuple-element.51), channel_id=1, source_target_pairs={{0,32},{32,0},{64,96},{96,64},{1,33},{33,1},{65,97},{97,65},{2,34}... | collective-permute-start | bytes 393224 | tf_op jit(solution)/shard_map/halo_two/rims_of_frames/even/ppermute | solution.py:285

commit v4 on v3

--- a/solution.py
+++ b/solution.py
@@ -1,3 +1,4 @@
+import functools
 import math
 
 import jax
@@ -51,7 +52,7 @@
     row_even, frame_even = side[0] == 0, side[1] == 0
     for f in range(frames):
         for k, (src, dst, off) in enumerate(((past, xp, 2), (future, xf, 0))):
-            odd, even = rows_odd[k, f, 0], rows_even[k, f, 0]
+            odd, even = rows_odd[k, f], rows_even[k, f]
             dst[f + off, 0] = jnp.where(row_even, odd, even)
             dst[f + off, 1 : rows + 1] = src[f]
             dst[f + off, rows + 1] = jnp.where(row_even, even, odd)
@@ -72,6 +73,47 @@
 def gated(hidden, grad_act):
     sig = jax.nn.sigmoid(hidden)
     return (hidden * sig).astype(BF16), (grad_act * sig * (1.0 + hidden * (1.0 - sig))).astype(BF16)
+
+
+def rows_kernel(side, past, future, odd, even, sems):
+    rows = past.shape[1]
+    over_odd = side[0] * (rows - 1)
+    copies = []
+    for k, src in enumerate((past, future)):
+        for s, (dst, r) in enumerate(((odd, over_odd), (even, rows - 1 - over_odd))):
+            copies.append(pltpu.make_async_copy(src.at[:, r], dst.at[k], sems.at[k, s]))
+    for copy in copies:
+        copy.start()
+    for copy in copies:
+        copy.wait()
+
+
+def rims_kernel(side, rows_odd, rows_even, odd, even):
+    row_even, frame_even = side[0] == 0, side[1] == 0
+    last = rows_odd.shape[1] - 2
+    for f in range(2):
+        for s in range(2):
+            one, two = (rows_odd, rows_even) if s == 0 else (rows_even, rows_odd)
+            past = jnp.where(row_even, one[0, f + last], two[0, f + last])
+            future = jnp.where(row_even, one[1, f], two[1, f])
+            odd[f, s] = jnp.where(frame_even, future, past)
+            even[f, s] = jnp.where(frame_even, past, future)
+
+
+def frames_kernel(side, past, future, rows_odd, rows_even, odd, even):
+    row_even, frame_even = side[0] == 0, side[1] == 0
+    frames, rows = past.shape[0], past.shape[1]
+    for f in range(2):
+        g = f + frames - 2
+        for r in range(rows + 2):
+            if 0 < r <= rows:
+                one, two = past[g, r - 1], future[f, r - 1]
+            else:
+                a, b = (rows_odd, rows_even) if r == 0 else (rows_even, rows_odd)
+                one = jnp.where(row_even, a[0, g], b[0, g])
+                two = jnp.where(row_even, a[1, f], b[1, f])
+            odd[f, r] = jnp.where(frame_even, two, one)
+            even[f, r] = jnp.where(frame_even, one, two)
 
 
 def weights_kernel(one, two, bias, one_fwd, one_adj, two_fwd, two_adj, bias_out):
@@ -119,12 +161,14 @@
 
 
 def first_outer_kernel(side, rim_odd, rim_even, xp, xf, hid, act, d1_in, d2_in, bsum, wp, wf, bias, active_in, pre_in,
-                       active_out, pre_out, grads, d1, d2):
+                       active_out, pre_out, rows_odd, rows_even, grads, d1, d2):
     frames, rows, chan, cols = active_out.shape
+    row_even = side[0] == 0
     past_rims, future_rims = corner_rims(side, rim_odd, rim_even)
     total = bsum[...]
     pres, acts, winp, winf = [], [], [], []
     for f in range(frames):
+        ends_active, ends_pre = [], []
         for s, r in enumerate((0, rows - 1)):
             if f < 2:
                 winp.append(rim_window(xp, f, r, past_rims, (0, 1)))
@@ -139,10 +183,14 @@
             active, pre = gated(hidden, grad_act)
             active_out[f, r] = active
             pre_out[f, r] = pre
+            ends_active.append(active)
+            ends_pre.append(pre)
             acts.append(column_taps(active))
             pres.append(column_taps(pre))
             total = total + pre.astype(F32)
-    for f in range(frames):
+        for k, ends in enumerate((ends_active, ends_pre)):
+            rows_odd[k, f] = jnp.where(row_even, ends[0], ends[1])
+            rows_even[k, f] = jnp.where(row_even, ends[1], ends[0])
         for r in range(1, rows - 1):
             active_out[f, r] = active_in[f, r]
             pre_out[f, r] = pre_in[f, r]
@@ -168,52 +216,87 @@
         grads[used + per :] = jnp.zeros((rest,) + grads.shape[1:], grads.dtype)
 
 
-def second_inner_kernel(side, past, future, rows_odd, rows_even, main_odd, main_even, wp, wf, add_past, add_future,
+def extend_rows(side, past, future, rows_odd, rows_even, xp, xf):
+    frames, rows = past.shape[0], past.shape[1]
+    row_even = side[0] == 0
+    for f in range(frames):
+        for k, (src, dst) in enumerate(((past, xp), (future, xf))):
+            odd, even = rows_odd[k, f], rows_even[k, f]
+            dst[f, 0] = jnp.where(row_even, odd, even)
+            dst[f, 1 : rows + 1] = src[f]
+            dst[f, rows + 1] = jnp.where(row_even, even, odd)
+
+
+def second_inner_kernel(side, past, future, rows_odd, rows_even, wp, wf, add_past, add_future,
                         out_past, out_future, xp, xf):
     frames, rows, chan, cols = past.shape
-    extend(side, past, future, rows_odd, rows_even, main_odd, main_even, xp, xf)
-    for f in range(frames):
+    extend_rows(side, past, future, rows_odd, rows_even, xp, xf)
+    for f in range(frames - 2):
         for r in range(rows):
-            inner = 0 < r < rows - 1
-            if f >= 2 or inner:
-                out_past[f, r] = (add_past[f, r].astype(F32) + convolved(wp, window(xp, f, r))).astype(BF16)
-            if f < frames - 2 or inner:
-                out_future[f, r] = (add_future[f, r].astype(F32) + convolved(wf, window(xf, f, r))).astype(BF16)
-
-
-def second_outer_kernel(side, rim_odd, rim_even, xp, xf, wp, wf, add_past, add_future, past_in, future_in,
-                        out_past, out_future):
+            g = f + 2
+            out_past[g, r] = (add_past[g, r].astype(F32) + convolved(wp, window(xp, f, r))).astype(BF16)
+            out_future[f, r] = (add_future[f, r].astype(F32) + convolved(wf, window(xf, f, r))).astype(BF16)
+
+
+def second_outer_kernel(side, odd, even, xp, xf, wp, wf, add_past, add_future, past_in, future_in,
+                        out_past, out_future, edge_past, edge_future):
     frames, rows, chan, cols = out_past.shape
-    past_rims, future_rims = corner_rims(side, rim_odd, rim_even)
+    frame_even = side[1] == 0
     for f in range(2):
-        for r in (0, rows - 1):
-            taps = rim_window(xp, f, r, past_rims, (0, 1))
+        for r in range(rows + 2):
+            edge_past[f, r] = jnp.where(frame_even, odd[f, r], even[f, r])
+            edge_future[f, r] = jnp.where(frame_even, even[f, r], odd[f, r])
+    slab = lambda x, f, r: x[f, r : r + 3].reshape((3 * chan, cols))
+    for f in range(2):
+        for r in range(rows):
+            pieces = [slab(edge_past, g, r) if g < 2 else slab(xp, g - 2, r) for g in range(f, f + 3)]
+            taps = jnp.concatenate(pieces, axis=0)
             out_past[f, r] = (add_past[f, r].astype(F32) + convolved(wp, taps)).astype(BF16)
-            g = frames - 2 + f
-            taps = rim_window(xf, g, r, future_rims, (frames, frames + 1))
-            out_future[g, r] = (add_future[g, r].astype(F32) + convolved(wf, taps)).astype(BF16)
-    for f in range(frames):
-        for r in range(rows):
-            inner = 0 < r < rows - 1
-            if f >= 2 or inner:
-                out_past[f, r] = past_in[f, r]
-            if f < frames - 2 or inner:
-                out_future[f, r] = future_in[f, r]
-
-
-def call(kernel, outs, args, flops, scratch=(), scalars=1):
+            k = frames - 2 + f
+            pieces = [slab(xf, g, r) if g < frames else slab(edge_future, g - frames, r) for g in range(k, k + 3)]
+            taps = jnp.concatenate(pieces, axis=0)
+            out_future[k, r] = (add_future[k, r].astype(F32) + convolved(wf, taps)).astype(BF16)
+    for f in range(frames - 2):
+        out_past[f + 2] = past_in[f + 2]
+        out_future[f] = future_in[f]
+
+
+def sum_kernel(parts, out, *, scale):
+    total = parts[0].astype(F32)
+    for k in range(1, parts.shape[0]):
+        total = total + parts[k].astype(F32)
+    out[...] = jnp.broadcast_to((total * scale).astype(out.dtype)[None], out.shape)
+
+
+def unpack_kernel(parts, one, two, bias):
+    taps, chan = one.shape[0], one.shape[1]
+    per = chan // parts.shape[1]
+    for k in range(taps):
+        both = parts[k * per : (k + 1) * per].astype(F32).reshape((chan, 2 * chan))
+        one[k] = both[:, :chan]
+        two[k] = both[:, chan:]
+    column = parts[taps * per : (taps + 1) * per].astype(F32).reshape((chan, 2 * chan))[:, :chan]
+    keep = lax.broadcasted_iota(jnp.int32, column.shape, 0) == lax.broadcasted_iota(jnp.int32, column.shape, 1)
+    bias[...] = jnp.sum(jnp.where(keep, column, 0.0), axis=0, keepdims=True)
+
+
+def sides():
+    return lax.axis_index("rows") % 2, lax.axis_index("frames") % 2
+
+
+def call(kernel, outs, args, flops, scratch=(), sided=True, whole=0, name=None):
     vmem = pl.BlockSpec(memory_space=pltpu.VMEM)
-    smem = pl.BlockSpec(memory_space=pltpu.SMEM)
     moved = sum(x.size * x.dtype.itemsize for x in list(args) + list(outs))
+    body = (lambda *refs: kernel(sides(), *refs)) if sided else kernel
     return pl.pallas_call(
-        kernel,
+        body,
         out_shape=outs,
-        in_specs=[smem] * scalars + [vmem] * (len(args) - scalars),
+        in_specs=[pl.BlockSpec(memory_space=pltpu.HBM)] * whole + [vmem] * (len(args) - whole),
         out_specs=[vmem] * len(outs),
         scratch_shapes=scratch,
-        compiler_params=pltpu.CompilerParams(vmem_limit_bytes=VMEM_LIMIT),
+        compiler_params=pltpu.CompilerParams(vmem_limit_bytes=None if whole else VMEM_LIMIT),
         cost_estimate=pl.CostEstimate(flops=flops, bytes_accessed=moved, transcendentals=0),
-        name=kernel.__name__,
+        name=name or kernel.__name__,
     )(*args)
 
 
@@ -228,43 +311,73 @@
     chan = bias.shape[0]
     taps = (27, chan, chan)
     outs = arrays(*[(3 * chan, 9 * chan)] * 4) + arrays((chan, 1), kind=F32)
-    return call(weights_kernel, outs, (one.reshape(taps), two.reshape(taps), bias[None]), 0, scalars=0)
+    return call(weights_kernel, outs, (one.reshape(taps), two.reshape(taps), bias[None]), 0, sided=False)
 
 
 def conv_flops(shape, rows):
     return 2 * 27 * shape[2] * shape[2] * shape[3] * rows
 
 
-def first_inner(side, past, future, edges, wp, wf, bias):
+def first_inner(past, future, edges, wp, wf, bias):
     shape = past.shape
     frames, rows, chan, cols = shape
     extended = (frames + 2, rows + 2, chan, cols)
     outs = arrays(shape, shape, extended, extended) + arrays(
         (2, 2, chan, cols), (2, 2, chan, cols), (3 * chan, 9 * chan), (9 * chan, 3 * chan), (chan, cols), kind=F32)
-    return call(first_inner_kernel, outs, (side, past, future, *edges, wp, wf, bias), conv_flops(shape, 40))
-
-
-def first_outer(devices, side, rims, inner, wp, wf, bias):
+    return call(first_inner_kernel, outs, (past, future, *edges, wp, wf, bias), conv_flops(shape, 40))
+
+
+def first_outer(devices, rims, inner, wp, wf, bias):
     active, pre, *rest = inner
     frames, rows, chan, cols = active.shape
-    outs = arrays(active.shape, pre.shape, (devices, 16, 2 * chan))
+    ends = (2, frames, chan, cols)
+    outs = arrays(active.shape, pre.shape, ends, ends, (devices, 16, 2 * chan))
     scratch = [pltpu.VMEM((3 * chan, 9 * chan), F32), pltpu.VMEM((9 * chan, 3 * chan), F32)]
-    args = (side, *rims, *rest, wp, wf, bias, active, pre)
+    args = (*rims, *rest, wp, wf, bias, active, pre)
     return call(first_outer_kernel, outs, args, conv_flops(active.shape, 24), scratch)
 
 
-def second_inner(side, past, future, edges, wp, wf, add_past, add_future):
+def second_inner(past, future, edges, wp, wf, add_past, add_future):
     shape = past.shape
     frames, rows, chan, cols = shape
-    extended = (frames + 2, rows + 2, chan, cols)
-    args = (side, past, future, *edges, wp, wf, add_past, add_future)
-    return call(second_inner_kernel, arrays(shape, shape, extended, extended), args, conv_flops(shape, 24))
-
-
-def second_outer(side, rims, inner, wp, wf, add_past, add_future):
+    extended = (frames, rows + 2, chan, cols)
+    args = (past, future, *edges, wp, wf, add_past, add_future)
+    return call(second_inner_kernel, arrays(shape, shape, extended, extended), args, conv_flops(shape, 16))
+
+
+def second_outer(edges, inner, wp, wf, add_past, add_future):
     out_past, out_future, xp, xf = inner
-    args = (side, *rims, xp, xf, wp, wf, add_past, add_future, out_past, out_future)
-    return call(second_outer_kernel, arrays(out_past.shape, out_past.shape), args, conv_flops(out_past.shape, 8))
+    frames, rows, chan, cols = out_past.shape
+    args = (*edges, xp, xf, wp, wf, add_past, add_future, out_past, out_future)
+    scratch = [pltpu.VMEM((2, rows + 2, chan, cols), BF16)] * 2
+    return call(second_outer_kernel, arrays(out_past.shape, out_past.shape), args, conv_flops(out_past.shape, 16), scratch)
+
+
+def rows_to_send(past, future):
+    frames, rows, chan, cols = past.shape
+    ends = (2, frames, chan, cols)
+    scratch = [pltpu.SemaphoreType.DMA((2, 2))]
+    return call(rows_kernel, arrays(ends, ends), (past, future), 0, scratch, whole=2)
+
+
+def rims_to_send(rows_odd, rows_even):
+    rims = (2, 2) + rows_odd.shape[2:]
+    return call(rims_kernel, arrays(rims, rims), (rows_odd, rows_even), 0)
+
+
+def frames_to_send(past, future, rows_odd, rows_even):
+    edge = (2, past.shape[1] + 2) + past.shape[2:]
+    return call(frames_kernel, arrays(edge, edge), (past, future, rows_odd, rows_even), 0)
+
+
+def summed(parts, scale):
+    kernel = functools.partial(sum_kernel, scale=scale)
+    return call(kernel, arrays(parts.shape), (parts,), 0, sided=False, name="sum_kernel")[0]
+
+
+def unpacked(parts, chan):
+    outs = arrays((27, chan, chan), (27, chan, chan), (1, chan), kind=F32)
+    return call(unpack_kernel, outs, (parts,), 0, sided=False)
 
 
 AXES = ("frames", "rows")
@@ -277,70 +390,52 @@
     return pairs
 
 
-def swap_neighbours(axis, even, to_next, to_prior):
+def swap(axis, odd, even):
     count = lax.axis_size(axis)
+    with jax.named_scope("even"):
+        even = lax.ppermute(even, axis, pairs_of(count, 0))
     with jax.named_scope("odd"):
-        odd_pairs = lax.ppermute(jnp.where(even, to_prior, to_next), axis, pairs_of(count, 1))
-    with jax.named_scope("even"):
-        even_pairs = lax.ppermute(jnp.where(even, to_next, to_prior), axis, pairs_of(count, 0))
-    return odd_pairs, even_pairs
-
-
-def edges_of(side, past, future):
-    both = jnp.stack([past, future])
-    with jax.named_scope("rims_of_rows"):
-        rows = swap_neighbours("rows", side[0] == 0, both[:, :, -1:], both[:, :, :1])
-    with jax.named_scope("main"):
-        main = swap_neighbours("frames", side[1] == 0, past[-2:], future[:2])
-    return (*rows, *main)
-
-
-def rims_of(side, rows_odd, rows_even):
-    row_even = side[0] == 0
-    low = jnp.where(row_even, rows_odd, rows_even)
-    high = jnp.where(row_even, rows_even, rows_odd)
-    rims = jnp.concatenate([low, high], axis=2)
-    with jax.named_scope("rims_of_frames"):
-        return swap_neighbours("frames", side[1] == 0, rims[0, -2:], rims[1, :2])
-
-
-def total_over_devices(parts):
-    with jax.named_scope("gather_terms"):
-        mine = lax.all_to_all(parts, AXES, 0, 0, tiled=True)
-    mine = jnp.sum(mine.astype(jnp.float32), axis=0).astype(jnp.bfloat16)
-    spread = jnp.broadcast_to(mine[None], parts.shape)
-    with jax.named_scope("spread_sums"):
-        return lax.all_to_all(spread, AXES, 0, 0, tiled=True)
+        return lax.ppermute(odd, axis, pairs_of(count, 1)), even
 
 
 def per_device(clip_in, kernel_one, bias_one, kernel_two, cotangent):
     frame_count, row_count, channels, col_count = clip_in.shape
     devices = lax.axis_size("frames") * lax.axis_size("rows")
-    side = jnp.stack([lax.axis_index("rows") % 2, lax.axis_index("frames") % 2]).astype(jnp.int32)
-    with jax.named_scope("halo_one"):
-        edges = edges_of(side, clip_in, cotangent)
-    one_fwd, one_adj, two_fwd, two_adj, bias = flat_weights(kernel_one, kernel_two, bias_one)
-    with jax.named_scope("halo_one"):
-        rims = rims_of(side, *edges[:2])
-    inner = first_inner(side, clip_in, cotangent, edges, one_fwd, two_adj, bias)
-    active, grad_pre, terms = first_outer(devices, side, rims, inner, one_fwd, two_adj, bias)
-    total = total_over_devices(terms)
-    with jax.named_scope("halo_two"):
-        edges = edges_of(side, active, grad_pre)
-        rims = rims_of(side, *edges[:2])
-    inner = second_inner(side, active, grad_pre, edges, two_fwd, one_adj, clip_in, cotangent)
-    block_out, grad_input = second_outer(side, rims, inner, two_fwd, one_adj, clip_in, cotangent)
     cell_total = (
         frame_count * lax.axis_size("frames") * row_count * lax.axis_size("rows") * col_count
     )
-    total = total.reshape((-1, 2 * channels)).astype(jnp.float32) * (1.0 / math.sqrt(cell_total))
-    count = 27 * channels
+    frame_even = sides()[1] == 0
+    with jax.named_scope("rows_one"):
+        rows = swap("rows", *rows_to_send(clip_in, cotangent))
+    past, future = clip_in[-2:], cotangent[:2]
+    with jax.named_scope("frames_one"):
+        main = swap("frames", jnp.where(frame_even, future, past), jnp.where(frame_even, past, future))
+    with jax.named_scope("rims_one"):
+        rims = swap("frames", *rims_to_send(*rows))
+    one_fwd, one_adj, two_fwd, two_adj, bias = flat_weights(kernel_one, kernel_two, bias_one)
+    inner = first_inner(clip_in, cotangent, (*rows, *main), one_fwd, two_adj, bias)
+    active, grad_pre, *ends, terms = first_outer(devices, rims, inner, one_fwd, two_adj, bias)
+
+    with jax.named_scope("gather_terms"):
+        terms = lax.all_to_all(terms, AXES, 0, 0, tiled=True)
+    spread = summed(terms, 1.0 / math.sqrt(cell_total))
+    with jax.named_scope("spread_sums"):
+        total = lax.all_to_all(spread, AXES, 0, 0, tiled=True)
+
+    with jax.named_scope("rows_two"):
+        rows = swap("rows", *ends)
+    *rows, _ = lax.optimization_barrier((*rows, spread))
+    with jax.named_scope("frames_two"):
+        edges = swap("frames", *frames_to_send(active, grad_pre, *rows))
+    inner = second_inner(active, grad_pre, rows, two_fwd, one_adj, clip_in, cotangent)
+    block_out, grad_input = second_outer(edges, inner, two_fwd, one_adj, clip_in, cotangent)
+    first, second, bias = unpacked(total, channels)
     return (
         block_out,
         grad_input,
-        total[:count, :channels].reshape(kernel_one.shape),
-        total[:count, channels:].reshape(kernel_two.shape),
-        total[count : count + channels, 0],
+        first.reshape(kernel_one.shape),
+        second.reshape(kernel_two.shape),
+        bias.reshape(bias_one.shape),
     )
 
 

time: 83.1 us -> 74.7 us (0.90)
  starting transfers between devices: 46.3 us -> 35.5 us
  waiting for transfers between devices: 11.6 us -> 21.1 us
  other arithmetic: 6.55 us -> 0.04 us
  local copies, waits for them, and re-layouts: 2.98 us -> 0.73 us
  Pallas kernels: 14.3 us -> 16 us
    all_to_all x2, starting transfers between devices: 24.3 us -> 12 us  [the longest x1 7.73 us: per_device(): terms = lax.all_to_all(terms, AXES, 0, 0, tiled=True)]
    all_to_all x2, waiting for transfers between devices: 0.96 us -> 9.3 us  [the longest x1 9.3 us: per_device(): terms = lax.all_to_all(terms, AXES, 0, 0, tiled=True)]
    select_n x12 -> x1, other arithmetic: 4.16 us -> 0.04 us  [per_device(): jnp.where(frame_even, past, future)]
    slice x2 -> x0, local copies, waits for them, and re-layouts: 2.09 us -> none  [the longest x1 1.47 us: per_device(): total[:count, channels:].reshape(kernel_two.shape)]
    pallas_call x5 -> x10, Pallas kernels: 14.3 us -> 16 us  [call(): pl.pallas_call(body, out_shape=outs, in_specs=[pl.BlockSpec(memory_space=...]
    ppermute x12 -> x10, starting transfers between devices: 22 us -> 23.5 us  [the longest x5 13.4 us: swap(): return (lax.ppermute(odd, axis, pairs_of(count, 1)), even)]
    ppermute x12 -> x10, waiting for transfers between devices: 10.6 us -> 11.8 us  [the longest x5 11.5 us: swap(): return (lax.ppermute(odd, axis, pairs_of(count, 1)), even)]
    reduce_sum x1 -> x0, other arithmetic: 1.18 us -> none  [total_over_devices(): mine = jnp.sum(mine.astype(jnp.float32), axis=0).astype(jnp.bfloat16)]
  transfers between devices with their start and end apart: 14 -> 12, of which waited for: 5 -> 4; matrix products, arithmetic and copies ran while one was open for 6% -> 0% of each run, Pallas kernels for 13% -> 13%
where the time goes in v4:
time: 74.7 us; the launch traced here: 74.4 us
  starting transfers between devices  35.5 us (48%)
  waiting for transfers between devices  21.1 us (28%)
  Pallas kernels  16 us (21%)
  between operations  0.89 us (1%)
    pallas_call x10, Pallas kernels, call(): pl.pallas_call(body, out_shape=outs, in_specs=[pl.BlockSpec(memory_space=...  16 us
    ppermute x5, starting transfers between devices, swap(): return (lax.ppermute(odd, axis, pairs_of(count, 1)), even)  13.4 us
    ppermute x5, waiting for transfers between devices, swap(): return (lax.ppermute(odd, axis, pairs_of(count, 1)), even)  11.5 us
    ppermute x5, starting transfers between devices, swap(): even = lax.ppermute(even, axis, pairs_of(count, 0))  10.1 us
    all_to_all x1, waiting for transfers between devices, per_device(): terms = lax.all_to_all(terms, AXES, 0, 0, tiled=True)  9.3 us
    all_to_all x1, starting transfers between devices, per_device(): terms = lax.all_to_all(terms, AXES, 0, 0, tiled=True)  7.73 us
    all_to_all x1, starting transfers between devices, per_device(): total = lax.all_to_all(spread, AXES, 0, 0, tiled=True)  4.3 us
  transfers between devices with their start and end apart: 12, of which 4 were waited for; matrix products, arithmetic and copies ran while one was open for 0% of the time, Pallas kernels for 13%

profile of v4, /device:TPU:1, one launch (start us, length us, event | category | flops | bytes accessed | tf_op | source)
XLA Modules:
  0.0 74.4 jit_solution(1002207260234096458)
XLA Ops:
  0.7 2.1 %rows_kernel.1 = (bf16[2,4,64,256]{3,2,1,0:T(8,128)(2,1)}, bf16[2,4,64,256]{3,2,1,0:T(8,128)(2,1)}) custom-call(bf16[4,4,64,256]{3,2,1,0:T(8,128)(2,1)} %refs_6_.3, bf16[4,4,64,256]{3,2,1,0:T(8,128)(2,1)} %refs_7_.3), custom_call_target="tpu_custom_call" | custom-call | bytes 1572864 | tf_op jit(solution)/shard_map/rows_one/rows_kernel/pallas_call | solution.py:291
  2.7 0.7 collective-permute-start
  3.4 4.5 %collective-permute-start.1 = (bf16[2,4,64,256]{3,2,1,0:T(8,128)(2,1)}, bf16[2,4,64,256]{3,2,1,0:T(8,128)(2,1)S(1)}, u32[]{:S(2)}, u32[]{:S(2)}) collective-permute-start(bf16[2,4,64,256]{3,2,1,0:T(8,128)(2,1)} %get-tuple-element.42), channel_id=1, source_target_pairs={{0,1},{1,0},{2,3},{3,2},{4,5},{5,4},{6,7},{7,6},{8,9},{9,8},{10,11... | collective-permute-start | bytes 786440 | tf_op jit(solution)/shard_map/rows_one/even/ppermute | solution.py:396
  8.0 1.3 %collective-permute-start.5 = (bf16[2,4,64,256]{3,2,1,0:T(8,128)(2,1)S(1)}, bf16[2,4,64,256]{3,2,1,0:T(8,128)(2,1)S(1)}, u32[]{:S(2)}, u32[]{:S(2)}) collective-permute-start(bf16[2,4,64,256]{3,2,1,0:T(8,128)(2,1)S(1)} %get-tuple-element.77), channel_id=1, source_target_pairs={{0,32},{32,0},{64,96},{96,64},{1,33},{33,1},{65,97},{97,65},{2,34}... | collective-permute-start | bytes 786440 | tf_op jit(solution)/shard_map/frames_one/even/ppermute | solution.py:396
  9.3 3.4 %collective-permute-start.4 = (bf16[2,4,64,256]{3,2,1,0:T(8,128)(2,1)S(1)}, bf16[2,4,64,256]{3,2,1,0:T(8,128)(2,1)S(1)}, u32[]{:S(2)}, u32[]{:S(2)}) collective-permute-start(bf16[2,4,64,256]{3,2,1,0:T(8,128)(2,1)S(1)} %get-tuple-element.78), channel_id=1, source_target_pairs={{32,64},{64,32},{33,65},{65,33},{34,66},{66,34},{35,67},{67,35},{3... | collective-permute-start | bytes 786440 | tf_op jit(solution)/shard_map/frames_one/odd/ppermute | solution.py:398
  12.8 0.8 %weights_kernel.1 = (bf16[192,576]{1,0:T(8,128)(2,1)S(1)}, bf16[192,576]{1,0:T(8,128)(2,1)S(1)}, bf16[192,576]{1,0:T(8,128)(2,1)S(1)}, bf16[192,576]{1,0:T(8,128)(2,1)S(1)}, f32[64,1]{1,0:T(8,128)S(1)}) custom-call(bf16[27,64,64]{2,1,0:T(8,128)(2,1)S(1)} %bitcast.6, bf16[27,64,64]{2,1,0:T(8,128)(2,1)S(1)} %bitcast.7, f32[1,64]{1,0:T(1,128)S(1)} %bitcast.8), custom_call_target="tpu_custom_call" | custom-call | bytes 1327616 | tf_op jit(solution)/shard_map/weights_kernel/pallas_call | solution.py:291
  13.6 0.3 collective-permute-done.1.refs_1_.refs_3_
  14.0 5.0 %collective-permute-start.2 = (bf16[2,2,64,256]{3,2,1,0:T(8,128)(2,1)S(1)}, bf16[2,2,64,256]{3,2,1,0:T(8,128)(2,1)S(1)}, u32[]{:S(2)}, u32[]{:S(2)}) collective-permute-start(bf16[2,2,64,256]{3,2,1,0:T(8,128)(2,1)S(1)} %get-tuple-element.43), channel_id=1, source_target_pairs={{32,64},{64,32},{33,65},{65,33},{34,66},{66,34},{35,67},{67,35},{3... | collective-permute-start | bytes 393224 | tf_op jit(solution)/shard_map/rims_one/odd/ppermute | solution.py:398
  19.0 3.6 %collective-permute-done.4.refs_4_ = bf16[2,4,64,256]{3,2,1,0:T(8,128)(2,1)S(1)} collective-permute-done((bf16[2,4,64,256]{3,2,1,0:T(8,128)(2,1)S(1)}, bf16[2,4,64,256]{3,2,1,0:T(8,128)(2,1)S(1)}, u32[]{:S(2)}, u32[]{:S(2)}) %collective-permute-start.4) | collective-permute-done | bytes 262176 | tf_op jit(solution)/shard_map/frames_one/odd/ppermute | solution.py:398
  22.6 3.6 %first_inner_kernel.1 = (bf16[4,4,64,256]{3,2,1,0:T(8,128)(2,1)S(1)}, bf16[4,4,64,256]{3,2,1,0:T(8,128)(2,1)S(1)}, bf16[6,6,64,256]{3,2,1,0:T(8,128)(2,1)S(1)}, ...) custom-call(bf16[4,4,64,256]{3,2,1,0:T(8,128)(2,1)S(1)} %copy-done, ...), custom_call_target="tpu_custom_call" | custom-call | flops 2264924160 | bytes 7422208 | tf_op jit(solution)/shard_map/first_inner_kernel/pallas_call | solution.py:291
  26.3 3.3 %first_outer_kernel.1 = (bf16[4,4,64,256]{3,2,1,0:T(8,128)(2,1)S(1)}, bf16[4,4,64,256]{3,2,1,0:T(8,128)(2,1)S(1)}, bf16[2,4,64,256]{3,2,1,0:T(8,128)(2,1)}, bf16...) custom-call(bf16[2,2,64,256]{3,2,1,0:T(8,128)(2,1)S(1)} %collective-permute-done.2.refs_0_, ...), custom_call_target="tpu_custom_call" | custom-call | flops 1358954496 | bytes 7684352 | tf_op jit(solution)/shard_map/first_outer_kernel/pallas_call | solution.py:291
  29.5 0.7 copy-done.7
  30.2 7.7 %all-to-all-start = ((bf16[128,16,128]{2,1,0:T(8,128)(2,1)}), bf16[128,16,128]{2,1,0:T(8,128)(2,1)S(1)}, u32[]{:S(2)}, u32[]{:S(2)}) async-start(bf16[128,16,128]{2,1,0:T(8,128)(2,1)} %get-tuple-element.61), calls=%async_computation | async-start | bytes 1048576 | tf_op jit(solution)/shard_map/gather_terms/all_to_all | solution.py:420
  37.9 0.7 collective-permute-start.6
  38.6 3.8 %collective-permute-start.7 = (bf16[2,4,64,256]{3,2,1,0:T(8,128)(2,1)}, bf16[2,4,64,256]{3,2,1,0:T(8,128)(2,1)S(1)}, u32[]{:S(2)}, u32[]{:S(2)}) collective-permute-start(bf16[2,4,64,256]{3,2,1,0:T(8,128)(2,1)} %copy-done.7), channel_id=1, source_target_pairs={{0,1},{1,0},{2,3},{3,2},{4,5},{5,4},{6,7},{7,6},{8,9},{9,8},{10,11... | collective-permute-start | bytes 786440 | tf_op jit(solution)/shard_map/rows_two/even/ppermute | solution.py:396
  42.5 9.3 %all-to-all-done.parts = bf16[128,16,128]{2,1,0:T(8,128)(2,1)S(1)} async-done(((bf16[128,16,128]{2,1,0:T(8,128)(2,1)}), bf16[128,16,128]{2,1,0:T(8,128)(2,1)S(1)}, u32[]{:S(2)}, u32[]{:S(2)}) %all-to-all-start) | async-done | bytes 524320 | tf_op jit(solution)/shard_map/gather_terms/all_to_all | solution.py:420
  51.8 1.0 %sum_kernel.1 = bf16[128,16,128]{2,1,0:T(8,128)(2,1)} custom-call(bf16[128,16,128]{2,1,0:T(8,128)(2,1)S(1)} %all-to-all-done.parts), custom_call_target="tpu_custom_call" | custom-call | bytes 1048576 | tf_op jit(solution)/shard_map/sum_kernel/pallas_call | solution.py:291
  52.7 4.3 %all-to-all-start.1 = ((bf16[128,16,128]{2,1,0:T(8,128)(2,1)}), bf16[128,16,128]{2,1,0:T(8,128)(2,1)S(1)}, u32[]{:S(2)}, u32[]{:S(2)}) async-start(bf16[128,16,128]{2,1,0:T(8,128)(2,1)} %sum_kernel.1), calls=%async_computation.1 | async-start | bytes 1048576 | tf_op jit(solution)/shard_map/spread_sums/all_to_all | solution.py:423
  57.2 3.7 %collective-permute-start.8 = (bf16[2,6,64,256]{3,2,1,0:T(8,128)(2,1)S(1)}, bf16[2,6,64,256]{3,2,1,0:T(8,128)(2,1)S(1)}, u32[]{:S(2)}, u32[]{:S(2)}) collective-permute-start(bf16[2,6,64,256]{3,2,1,0:T(8,128)(2,1)S(1)} %get-tuple-element.64), channel_id=1, source_target_pairs={{32,64},{64,32},{33,65},{65,33},{34,66},{66,34},{35,67},{67,35},{3... | collective-permute-start | bytes 1179656 | tf_op jit(solution)/shard_map/frames_two/odd/ppermute | solution.py:398
  60.8 0.3 collective-permute-start.9
  61.1 1.5 %second_inner_kernel.1 = (bf16[4,4,64,256]{3,2,1,0:T(8,128)(2,1)S(1)}, bf16[4,4,64,256]{3,2,1,0:T(8,128)(2,1)S(1)}, bf16[4,6,64,256]{3,2,1,0:T(8,128)(2,1)S(1)}, bf16[4,6,64,256]{3,2,1,0:T(8,128)(2,1)S(1)}) custom-call(bf16[4,4,64,256]{3,2,1,0:T(8,128)(2,1)S(1)} %get-tuple-element.57.refs_0_, bf16[4,4,64,256]{3,2,1,0:T(8,128)(2,1)S(1)} %get-tuple-element.58.refs_1_, ...), custom_call_target="tpu_custom_call" | custom-call | flops 905969664 | bytes 5685248 | tf_op jit(solution)/shard_map/second_inner_kernel/pallas_call | solution.py:291
  62.6 7.9 %collective-permute-done.8.refs_0_ = bf16[2,6,64,256]{3,2,1,0:T(8,128)(2,1)S(1)} collective-permute-done((bf16[2,6,64,256]{3,2,1,0:T(8,128)(2,1)S(1)}, bf16[2,6,64,256]{3,2,1,0:T(8,128)(2,1)S(1)}, u32[]{:S(2)}, u32[]{:S(2)}) %collective-permute-start.8) | collective-permute-done | bytes 393248 | tf_op jit(solution)/shard_map/frames_two/odd/ppermute | solution.py:398
  70.6 2.4 %second_outer_kernel.1 = (bf16[4,4,64,256]{3,2,1,0:T(8,128)(2,1)}, bf16[4,4,64,256]{3,2,1,0:T(8,128)(2,1)}) custom-call(bf16[2,6,64,256]{3,2,1,0:T(8,128)(2,1)S(1)} %collective-permute-done.8.refs_0_, bf16[2,6,64,256]{3,2,1,0:T(8,128)(2,1)S(1)} %collective-permute-done.9.refs_1_, bf16[4,6,64,256]{3,2,1,0:T(8,128)(2,1)S(1)} %get-tuple-element.68.refs_2_, ...), custom_call_target="tpu_custom_call" | custom-call | flops 905969664 | bytes 5947392 | tf_op jit(solution)/shard_map/second_outer_kernel/pallas_call | solution.py:291
  73.0 1.3 %unpack_kernel.1 = (f32[27,64,64]{2,1,0:T(8,128)}, f32[27,64,64]{2,1,0:T(8,128)}, f32[1,64]{1,0:T(1,128)}) custom-call(bf16[128,16,128]{2,1,0:T(8,128)(2,1)S(1)} %all-to-all-done.1.parts), custom_call_target="tpu_custom_call" | custom-call | bytes 1409280 | tf_op jit(solution)/shard_map/unpack_kernel/pallas_call | solution.py:291
  (27 shorter events, 0.3 us)
Async XLA Ops:
  0.6 7.4 %copy-start.1 = (bf16[4,4,64,256]{3,2,1,0:T(8,128)(2,1)S(1)}, bf16[4,4,64,256]{3,2,1,0:T(8,128)(2,1)}, u32[]{:S(2)}) copy-start(bf16[4,4,64,256]{3,2,1,0:T(8,128)(2,1)} %refs_7_.3) | copy-start | bytes 1572868
  0.6 7.3 %copy-start = (bf16[4,4,64,256]{3,2,1,0:T(8,128)(2,1)S(1)}, bf16[4,4,64,256]{3,2,1,0:T(8,128)(2,1)}, u32[]{:S(2)}) copy-start(bf16[4,4,64,256]{3,2,1,0:T(8,128)(2,1)} %refs_6_.3) | copy-start | bytes 1572868
  0.7 12.1 %copy-start.3 = (bf16[3,3,3,64,64]{4,3,2,1,0:T(8,128)(2,1)S(1)}, bf16[3,3,3,64,64]{4,3,2,1,0:T(8,128)(2,1)}, u32[]{:S(2)}) copy-start(bf16[3,3,3,64,64]{4,3,2,1,0:T(8,128)(2,1)} %param.8) | copy-start | bytes 663556
  0.7 12.1 %copy-start.6 = (f32[64]{0:T(128)S(1)}, f32[64]{0:T(128)}, u32[]{:S(2)}) copy-start(f32[64]{0:T(128)} %param.7) | copy-start | bytes 772
  0.7 12.1 %copy-start.2 = (bf16[3,3,3,64,64]{4,3,2,1,0:T(8,128)(2,1)S(1)}, bf16[3,3,3,64,64]{4,3,2,1,0:T(8,128)(2,1)}, u32[]{:S(2)}) copy-start(bf16[3,3,3,64,64]{4,3,2,1,0:T(8,128)(2,1)} %param.6) | copy-start | bytes 663556
  2.7 10.9 %collective-permute-start = (bf16[2,4,64,256]{3,2,1,0:T(8,128)(2,1)}, bf16[2,4,64,256]{3,2,1,0:T(8,128)(2,1)S(1)}, u32[]{:S(2)}, u32[]{:S(2)}) collective-permute-start(bf16[2,4,64,256]{3,2,1,0:T(8,128)(2,1)} %get-tuple-element.41), channel_id=1, source_target_pairs={{1,2},{2,1},{3,4},{4,3},{5,6},{6,5},{7,8},{8,7},{9,10},{10,9},{11,... | collective-permute-start | bytes 786440 | tf_op jit(solution)/shard_map/rows_one/odd/ppermute | solution.py:398
  3.4 10.5 %collective-permute-start.1 = (bf16[2,4,64,256]{3,2,1,0:T(8,128)(2,1)}, bf16[2,4,64,256]{3,2,1,0:T(8,128)(2,1)S(1)}, u32[]{:S(2)}, u32[]{:S(2)}) collective-permute-start(bf16[2,4,64,256]{3,2,1,0:T(8,128)(2,1)} %get-tuple-element.42), channel_id=1, source_target_pairs={{0,1},{1,0},{2,3},{3,2},{4,5},{5,4},{6,7},{7,6},{8,9},{9,8},{10,11... | collective-permute-start | bytes 786440 | tf_op jit(solution)/shard_map/rows_one/even/ppermute | solution.py:396
  8.0 11.0 %collective-permute-start.5 = (bf16[2,4,64,256]{3,2,1,0:T(8,128)(2,1)S(1)}, bf16[2,4,64,256]{3,2,1,0:T(8,128)(2,1)S(1)}, u32[]{:S(2)}, u32[]{:S(2)}) collective-permute-start(bf16[2,4,64,256]{3,2,1,0:T(8,128)(2,1)S(1)} %get-tuple-element.77), channel_id=1, source_target_pairs={{0,32},{32,0},{64,96},{96,64},{1,33},{33,1},{65,97},{97,65},{2,34}... | collective-permute-start | bytes 786440 | tf_op jit(solution)/shard_map/frames_one/even/ppermute | solution.py:396
  9.3 13.3 %collective-permute-start.4 = (bf16[2,4,64,256]{3,2,1,0:T(8,128)(2,1)S(1)}, bf16[2,4,64,256]{3,2,1,0:T(8,128)(2,1)S(1)}, u32[]{:S(2)}, u32[]{:S(2)}) collective-permute-start(bf16[2,4,64,256]{3,2,1,0:T(8,128)(2,1)S(1)} %get-tuple-element.78), channel_id=1, source_target_pairs={{32,64},{64,32},{33,65},{65,33},{34,66},{66,34},{35,67},{67,35},{3... | collective-permute-start | bytes 786440 | tf_op jit(solution)/shard_map/frames_one/odd/ppermute | solution.py:398
  13.6 12.6 %copy-start.4 = (bf16[192,576]{1,0:T(8,128)(2,1)}, bf16[192,576]{1,0:T(8,128)(2,1)S(1)}, u32[]{:S(2)}) copy-start(bf16[192,576]{1,0:T(8,128)(2,1)S(1)} %get-tuple-element.66.refs_4_) | copy-start | bytes 663556
  14.0 12.3 %collective-permute-start.2 = (bf16[2,2,64,256]{3,2,1,0:T(8,128)(2,1)S(1)}, bf16[2,2,64,256]{3,2,1,0:T(8,128)(2,1)S(1)}, u32[]{:S(2)}, u32[]{:S(2)}) collective-permute-start(bf16[2,2,64,256]{3,2,1,0:T(8,128)(2,1)S(1)} %get-tuple-element.43), channel_id=1, source_target_pairs={{32,64},{64,32},{33,65},{65,33},{34,66},{66,34},{35,67},{67,35},{3... | collective-permute-start | bytes 393224 | tf_op jit(solution)/shard_map/rims_one/odd/ppermute | solution.py:398
  18.9 7.3 %collective-permute-start.3 = (bf16[2,2,64,256]{3,2,1,0:T(8,128)(2,1)S(1)}, bf16[2,2,64,256]{3,2,1,0:T(8,128)(2,1)S(1)}, u32[]{:S(2)}, u32[]{:S(2)}) collective-permute-start(bf16[2,2,64,256]{3,2,1,0:T(8,128)(2,1)S(1)} %get-tuple-element.44), channel_id=1, source_target_pairs={{0,32},{32,0},{64,96},{96,64},{1,33},{33,1},{65,97},{97,65},{2,34}... | collective-permute-start | bytes 393224 | tf_op jit(solution)/shard_map/rims_one/even/ppermute | solution.py:396
  29.5 0.7 copy-start.7
  30.2 21.6 %all-to-all-start = ((bf16[128,16,128]{2,1,0:T(8,128)(2,1)}), bf16[128,16,128]{2,1,0:T(8,128)(2,1)S(1)}, u32[]{:S(2)}, u32[]{:S(2)}) async-start(bf16[128,16,128]{2,1,0:T(8,128)(2,1)} %get-tuple-element.61), calls=%async_computation | async-start | bytes 1048576 | tf_op jit(solution)/shard_map/gather_terms/all_to_all | solution.py:420
  37.9 19.1 %collective-permute-start.6 = (bf16[2,4,64,256]{3,2,1,0:T(8,128)(2,1)}, bf16[2,4,64,256]{3,2,1,0:T(8,128)(2,1)S(1)}, u32[]{:S(2)}, u32[]{:S(2)}) collective-permute-start(bf16[2,4,64,256]{3,2,1,0:T(8,128)(2,1)} %get-tuple-element.59), channel_id=1, source_target_pairs={{1,2},{2,1},{3,4},{4,3},{5,6},{6,5},{7,8},{8,7},{9,10},{10,9},{11,... | collective-permute-start | bytes 786440 | tf_op jit(solution)/shard_map/rows_two/odd/ppermute | solution.py:398
  38.6 18.4 %collective-permute-start.7 = (bf16[2,4,64,256]{3,2,1,0:T(8,128)(2,1)}, bf16[2,4,64,256]{3,2,1,0:T(8,128)(2,1)S(1)}, u32[]{:S(2)}, u32[]{:S(2)}) collective-permute-start(bf16[2,4,64,256]{3,2,1,0:T(8,128)(2,1)} %copy-done.7), channel_id=1, source_target_pairs={{0,1},{1,0},{2,3},{3,2},{4,5},{5,4},{6,7},{7,6},{8,9},{9,8},{10,11... | collective-permute-start | bytes 786440 | tf_op jit(solution)/shard_map/rows_two/even/ppermute | solution.py:396
  52.7 20.3 %all-to-all-start.1 = ((bf16[128,16,128]{2,1,0:T(8,128)(2,1)}), bf16[128,16,128]{2,1,0:T(8,128)(2,1)S(1)}, u32[]{:S(2)}, u32[]{:S(2)}) async-start(bf16[128,16,128]{2,1,0:T(8,128)(2,1)} %sum_kernel.1), calls=%async_computation.1 | async-start | bytes 1048576 | tf_op jit(solution)/shard_map/spread_sums/all_to_all | solution.py:423
  57.1 4.1 %copy-start.5 = (bf16[192,576]{1,0:T(8,128)(2,1)S(1)}, bf16[192,576]{1,0:T(8,128)(2,1)}, u32[]{:S(2)}) copy-start(bf16[192,576]{1,0:T(8,128)(2,1)} %copy-done.4) | copy-start | bytes 663556
  57.2 13.4 %collective-permute-start.8 = (bf16[2,6,64,256]{3,2,1,0:T(8,128)(2,1)S(1)}, bf16[2,6,64,256]{3,2,1,0:T(8,128)(2,1)S(1)}, u32[]{:S(2)}, u32[]{:S(2)}) collective-permute-start(bf16[2,6,64,256]{3,2,1,0:T(8,128)(2,1)S(1)} %get-tuple-element.64), channel_id=1, source_target_pairs={{32,64},{64,32},{33,65},{65,33},{34,66},{66,34},{35,67},{67,35},{3... | collective-permute-start | bytes 1179656 | tf_op jit(solution)/shard_map/frames_two/odd/ppermute | solution.py:398
  60.8 9.7 %collective-permute-start.9 = (bf16[2,6,64,256]{3,2,1,0:T(8,128)(2,1)S(1)}, bf16[2,6,64,256]{3,2,1,0:T(8,128)(2,1)S(1)}, u32[]{:S(2)}, u32[]{:S(2)}) collective-permute-start(bf16[2,6,64,256]{3,2,1,0:T(8,128)(2,1)S(1)} %get-tuple-element.65), channel_id=1, source_target_pairs={{0,32},{32,0},{64,96},{96,64},{1,33},{33,1},{65,97},{97,65},{2,34}... | collective-permute-start | bytes 1179656 | tf_op jit(solution)/shard_map/frames_two/even/ppermute | solution.py:396

commit v5 on v3

v5 whole, which is shorter than its diff:
```python
import functools
import math

import jax
import jax.numpy as jnp
from jax import lax
from jax.experimental import pallas as pl
from jax.experimental.pallas import tpu as pltpu
from jax.sharding import PartitionSpec as P

F32, BF16 = jnp.float32, jnp.bfloat16
NT = (((1,), (1,)), ((), ()))


def shifted(value, by):
    cols = value.shape[1]
    lane = lax.broadcasted_iota(jnp.int32, value.shape, 1)
    outside = lane == (0 if by == 1 else cols - 1)
    return jnp.where(outside, jnp.zeros_like(value), pltpu.roll(value, by % cols, 1))


def convolved(w, taps):
    part = jnp.dot(w[...], taps, preferred_element_type=F32)
    chan = w.shape[0] // 3
    return shifted(part[:chan], 1) + part[chan : 2 * chan] + shifted(part[2 * chan :], -1)


def column_taps(value):
    return jnp.concatenate([shifted(value, -1), value, shifted(value, 1)], axis=0)


def picker(even, odd_ref, even_ref, swapped):
    one, two = (even_ref, odd_ref) if swapped else (odd_ref, even_ref)
    return lambda *at: jnp.where(even, one[at], two[at])


def field(own, before, after, corner):
    frames, rows, _, cols = own.shape

    def rows_of(g, low, high):
        first = 0 if before is None else before.shape[0]
        if g < first:
            return before[g, low:high]
        if g < first + frames:
            return own[g - first, low:high]
        return after[g - first - frames, low:high]

    def taps(f, r):
        pieces = []
        for g in range(f, f + 3):
            if r == 0:
                pieces.append(corner(g, 0))
            pieces.append(rows_of(g, max(r - 1, 0), min(r + 2, rows)).reshape((-1, cols)))
            if r == rows - 1:
                pieces.append(corner(g, 1))
        return jnp.concatenate(pieces, axis=0)

    return taps


def corners(side, frames, rows_odd, rows_even, rim_odd=None, rim_even=None):
    low = picker(side[0] == 0, rows_odd, rows_even, False)
    high = picker(side[0] == 0, rows_odd, rows_even, True)
    past_rim = picker(side[1] == 0, rim_odd, rim_even, False)
    future_rim = picker(side[1] == 0, rim_odd, rim_even, True)
    past = lambda g, s: past_rim(g, s) if g < 2 else (low, high)[s](0, g - 2)
    future = lambda g, s: future_rim(g - frames, s) if g >= frames else (low, high)[s](1, g)
    return past, future


def pick_main(side, main_odd, main_even, before, after):
    even = side[1] == 0
    past = picker(even, main_odd, main_even, False)
    future = picker(even, main_odd, main_even, True)
    for f in range(before.shape[0]):
        for r in range(before.shape[1]):
            before[f, r] = past(f, r)
            after[f, r] = future(f, r)


def gated(hidden, grad_act):
    sig = jax.nn.sigmoid(hidden)
    return (hidden * sig).astype(BF16), (grad_act * sig * (1.0 + hidden * (1.0 - sig))).astype(BF16)


def pack_kernel(side, past, future, rows_odd, rows_even, main_odd, main_even, sems):
    frames, rows = past.shape[0], past.shape[1]
    over_odd = side[0] * (rows - 1)

    def run(first, second):
        copies = [
            pltpu.make_async_copy(first, main_odd, sems.at[4]),
            pltpu.make_async_copy(second, main_even, sems.at[5]),
        ]
        for k, src in enumerate((past, future)):
            copies.append(pltpu.make_async_copy(src.at[:, over_odd], rows_odd.at[k], sems.at[2 * k]))
            over_even = rows - 1 - over_odd
            copies.append(pltpu.make_async_copy(src.at[:, over_even], rows_even.at[k], sems.at[2 * k + 1]))
        for copy in copies:
            copy.start()
        for copy in copies:
            copy.wait()

    last, first = past.at[frames - 2 : frames], future.at[0:2]
    pl.when(side[1] == 0)(lambda: run(first, last))
    pl.when(side[1] != 0)(lambda: run(last, first))


def repack_kernel(side, past, future, rows_odd, rows_even, main_odd, main_even):
    frames, rows = past.shape[0], past.shape[1]
    row_even, frame_even = side[0] == 0, side[1] == 0
    for f in range(frames):
        for k, src in enumerate((past, future)):
            low, high = src[f, 0], src[f, rows - 1]
            rows_odd[k, f] = jnp.where(row_even, low, high)
            rows_even[k, f] = jnp.where(row_even, high, low)
    for f in range(2):
        for r in range(rows):
            last, first = past[f + frames - 2, r], future[f, r]
            main_odd[f, r] = jnp.where(frame_even, first, last)
            main_even[f, r] = jnp.where(frame_even, last, first)


def rims_kernel(side, rows_odd, rows_even, odd, even):
    row_even, frame_even = side[0] == 0, side[1] == 0
    last = rows_odd.shape[1] - 2
    for f in range(2):
        for s in range(2):
            one, two = (rows_odd, rows_even) if s == 0 else (rows_even, rows_odd)
            past = jnp.where(row_even, one[0, f + last], two[0, f + last])
            future = jnp.where(row_even, one[1, f], two[1, f])
            odd[f, s] = jnp.where(frame_even, future, past)
            even[f, s] = jnp.where(frame_even, past, future)


def weights_kernel(one, two, bias, one_fwd, one_adj, two_fwd, two_adj, bias_out):
    chan = one.shape[1]
    for src, fwd, adj in ((one, one_fwd, one_adj), (two, two_fwd, two_adj)):
        for t in range(3):
            for i in range(3):
                for j in range(3):
                    tap = src[t * 9 + i * 3 + j]
                    left = (t * 3 + i) * chan
                    fwd[j * chan : (j + 1) * chan, left : left + chan] = tap
                    left = (8 - t * 3 - i) * chan
                    flipped = jnp.transpose(tap.astype(F32)).astype(BF16)
                    adj[(2 - j) * chan : (3 - j) * chan, left : left + chan] = flipped
    spread = jnp.broadcast_to(bias[...], (chan, chan))
    lanes = lax.broadcasted_iota(jnp.int32, spread.shape, 1)
    keep = lanes == lax.broadcasted_iota(jnp.int32, spread.shape, 0)
    bias_out[...] = jnp.sum(jnp.where(keep, spread, 0.0), axis=1, keepdims=True)


def first_inner_kernel(side, past, future, main_odd, main_even, wp, wf, bias,
                       active_out, pre_out, before, after, d1, d2, bsum):
    frames, rows, chan, cols = past.shape
    pick_main(side, main_odd, main_even, before, after)
    past_taps = field(past, before, None, None)
    future_taps = field(future, None, after, None)
    total = jnp.zeros((chan, cols), F32)
    pres, acts, winp, winf = [], [], [], []
    for f in range(frames):
        for r in range(1, rows - 1):
            winp.append(past_taps(f, r))
            winf.append(future_taps(f, r))
            active, pre = gated(convolved(wp, winp[-1]) + bias[...], convolved(wf, winf[-1]))
            active_out[f, r] = active
            pre_out[f, r] = pre
            acts.append(column_taps(active))
            pres.append(column_taps(pre))
            total = total + pre.astype(F32)
    bsum[...] = total
    lanes = lambda parts: jnp.concatenate(parts, axis=1)
    d1[...] = lax.dot_general(lanes(pres), lanes(winp), NT, preferred_element_type=F32)
    d2[...] = lax.dot_general(lanes(winf), lanes(acts), NT, preferred_element_type=F32)


def first_middle_kernel(side, past, future, rows_odd, rows_even, wp, wf, bias, hid, act):
    frames, rows, _, _ = past.shape
    past_corner, future_corner = corners(side, frames, rows_odd, rows_even)
    past_taps = field(past, past.at[0:2], None, past_corner)
    future_taps = field(future, None, future, future_corner)
    for k in range(2):
        for s, r in enumerate((0, rows - 1)):
            hid[k, s] = convolved(wp, past_taps(frames - 2 + k, r)) + bias[...]
            act[k, s] = convolved(wf, future_taps(k, r))


def first_outer_kernel(side, rim_odd, rim_even, rows_in_odd, rows_in_even, past, future, before, after, hid, act,
                       d1_in, d2_in, bsum, wp, wf, bias, active_in, pre_in,
                       active_out, pre_out, grads, d1, d2):
    frames, rows, chan, _ = active_out.shape
    past_corner, future_corner = corners(side, frames, rows_in_odd, rows_in_even, rim_odd, rim_even)
    past_taps = field(past, before, None, past_corner)
    future_taps = field(future, None, after, future_corner)
    total = bsum[...]
    pres, acts, winp, winf = [], [], [], []
    for f in range(frames):
        for s, r in enumerate((0, rows - 1)):
            winp.append(past_taps(f, r))
            winf.append(future_taps(f, r))
            hidden = convolved(wp, winp[-1]) + bias[...] if f < 2 else hid[f - frames + 2, s]
            grad_act = act[f, s] if f < 2 else convolved(wf, winf[-1])
            active, pre = gated(hidden, grad_act)
            active_out[f, r] = active
            pre_out[f, r] = pre
            acts.append(column_taps(active))
            pres.append(column_taps(pre))
            total = total + pre.astype(F32)
        for r in range(1, rows - 1):
            active_out[f, r] = active_in[f, r]
            pre_out[f, r] = pre_in[f, r]
    bias_sum = jnp.sum(total, axis=1, keepdims=True)
    lanes = lambda parts: jnp.concatenate(parts, axis=1)
    d1[...] = d1_in[...] + lax.dot_general(lanes(pres), lanes(winp), NT, preferred_element_type=F32)
    d2[...] = d2_in[...] + lax.dot_general(lanes(winf), lanes(acts), NT, preferred_element_type=F32)
    per = chan // grads.shape[1]
    for t in range(3):
        for i in range(3):
            for j in range(3):
                left, top = (t * 3 + i) * chan, (8 - t * 3 - i) * chan
                one = d1[j * chan : (j + 1) * chan, left : left + chan]
                two = d2[top : top + chan, (2 - j) * chan : (3 - j) * chan]
                tap = (t * 9 + i * 3 + j) * per
                both = jnp.concatenate([one, two], axis=1).astype(grads.dtype)
                grads[tap : tap + per] = both.reshape((per,) + grads.shape[1:])
    used = 27 * per
    bias_rows = jnp.broadcast_to(bias_sum, (chan, grads.shape[2])).astype(grads.dtype)
    grads[used : used + per] = bias_rows.reshape((per,) + grads.shape[1:])
    rest = grads.shape[0] - used - per
    if rest:
        grads[used + per :] = jnp.zeros((rest,) + grads.shape[1:], grads.dtype)


def second_inner_kernel(side, past, future, rows_odd, rows_even, main_odd, main_even, wp, wf, add_past, add_future,
                        out_past, out_future, before, after):
    frames, rows, _, _ = past.shape
    pick_main(side, main_odd, main_even, before, after)
    past_corner, future_corner = corners(side, frames, rows_odd, rows_even)
    past_taps = field(past, before, None, past_corner)
    future_taps = field(future, None, after, future_corner)
    for f in range(frames):
        for r in range(rows):
            inner = 0 < r < rows - 1
            if f >= 2 or inner:
                out_past[f, r] = (add_past[f, r].astype(F32) + convolved(wp, past_taps(f, r))).astype(BF16)
            if f < frames - 2 or inner:
                out_future[f, r] = (add_future[f, r].astype(F32) + convolved(wf, future_taps(f, r))).astype(BF16)


def second_outer_kernel(side, rim_odd, rim_even, past, future, rows_odd, rows_even, before, after, wp, wf,
                        add_past, add_future, past_in, future_in, out_past, out_future):
    frames, rows, _, _ = out_past.shape
    past_corner, future_corner = corners(side, frames, rows_odd, rows_even, rim_odd, rim_even)
    past_taps = field(past, before, None, past_corner)
    future_taps = field(future, None, after, future_corner)
    for f in range(2):
        for r in (0, rows - 1):
            g = frames - 2 + f
            out_past[f, r] = (add_past[f, r].astype(F32) + convolved(wp, past_taps(f, r))).astype(BF16)
            out_future[g, r] = (add_future[g, r].astype(F32) + convolved(wf, future_taps(g, r))).astype(BF16)
    for f in range(frames):
        for r in range(rows):
            inner = 0 < r < rows - 1
            if f >= 2 or inner:
                out_past[f, r] = past_in[f, r]
            if f < frames - 2 or inner:
                out_future[f, r] = future_in[f, r]


def sum_kernel(parts, out, *, scale):
    total = parts[0].astype(F32)
    for k in range(1, parts.shape[0]):
        total = total + parts[k].astype(F32)
    out[...] = jnp.broadcast_to((total * scale).astype(out.dtype)[None], out.shape)


def unpack_kernel(parts, one, two, bias):
    taps, chan = one.shape[0], one.shape[1]
    per = chan // parts.shape[1]
    for k in range(taps):
        both = parts[k * per : (k + 1) * per].astype(F32).reshape((chan, 2 * chan))
        one[k] = both[:, :chan]
        two[k] = both[:, chan:]
    column = parts[taps * per : (taps + 1) * per].astype(F32).reshape((chan, 2 * chan))[:, :chan]
    keep = lax.broadcasted_iota(jnp.int32, column.shape, 0) == lax.broadcasted_iota(jnp.int32, column.shape, 1)
    bias[...] = jnp.sum(jnp.where(keep, column, 0.0), axis=0, keepdims=True)


def sides():
    return lax.axis_index("rows") % 2, lax.axis_index("frames") % 2


def call(kernel, outs, args, flops, scratch=(), sided=True, whole=0):
    vmem = pl.BlockSpec(memory_space=pltpu.VMEM)
    moved = sum(x.size * x.dtype.itemsize for x in list(args) + list(outs))
    body = (lambda *refs: kernel(sides(), *refs)) if sided else kernel
    return pl.pallas_call(
        body,
        out_shape=outs,
        in_specs=[pl.BlockSpec(memory_space=pltpu.HBM)] * whole + [vmem] * (len(args) - whole),
        out_specs=[vmem] * len(outs),
        scratch_shapes=scratch,
        compiler_params=pltpu.CompilerParams(vmem_limit_bytes=None if whole else VMEM_LIMIT),
        cost_estimate=pl.CostEstimate(flops=flops, bytes_accessed=moved, transcendentals=0),
    )(*args)


VMEM_LIMIT = 24 * 1024 * 1024


def arrays(*shapes, kind=BF16):
    return [jax.ShapeDtypeStruct(shape, kind) for shape in shapes]


def flat_weights(one, two, bias):
    chan = bias.shape[0]
    taps = (27, chan, chan)
    outs = arrays(*[(3 * chan, 9 * chan)] * 4) + arrays((chan, 1), kind=F32)
    return call(weights_kernel, outs, (one.reshape(taps), two.reshape(taps), bias[None]), 0, sided=False)


def conv_flops(shape, rows):
    return 2 * 27 * shape[2] * shape[2] * shape[3] * rows


def frame_pair(shape):
    return (2,) + shape[1:]


def first_inner(past, future, main, wp, wf, bias):
    shape = past.shape
    chan, cols = shape[2:]
    outs = arrays(shape, shape, frame_pair(shape), frame_pair(shape)) + arrays(
        (3 * chan, 9 * chan), (9 * chan, 3 * chan), (chan, cols), kind=F32)
    return call(first_inner_kernel, outs, (past, future, *main, wp, wf, bias), conv_flops(shape, 32))


def first_middle(past, future, rows, wp, wf, bias):
    part = (2, 2) + past.shape[2:]
    return call(first_middle_kernel, arrays(part, part, kind=F32), (past, future, *rows, wp, wf, bias),
                conv_flops(past.shape, 8))


def first_outer(devices, past, future, rows, rims, inner, middle, wp, wf, bias):
    active, pre, before, after, *sums = inner
    _, _, chan, _ = active.shape
    outs = arrays(active.shape, pre.shape, (devices, 16, 2 * chan))
    scratch = [pltpu.VMEM((3 * chan, 9 * chan), F32), pltpu.VMEM((9 * chan, 3 * chan), F32)]
    args = (*rims, *rows, past, future, before, after, *middle, *sums, wp, wf, bias, active, pre)
    return call(first_outer_kernel, outs, args, conv_flops(active.shape, 24), scratch)


def second_inner(past, future, rows, main, wp, wf, add_past, add_future):
    shape = past.shape
    outs = arrays(shape, shape, frame_pair(shape), frame_pair(shape))
    args = (past, future, *rows, *main, wp, wf, add_past, add_future)
    return call(second_inner_kernel, outs, args, conv_flops(shape, 24))


def second_outer(past, future, rows, rims, inner, wp, wf, add_past, add_future):
    out_past, out_future, before, after = inner
    args = (*rims, past, future, *rows, before, after, wp, wf, add_past, add_future, out_past, out_future)
    return call(second_outer_kernel, arrays(out_past.shape, out_past.shape), args, conv_flops(out_past.shape, 8))


def pack(past, future):
    frames, _, chan, cols = past.shape
    ends = (2, frames, chan, cols)
    scratch = [pltpu.SemaphoreType.DMA((6,))]
    outs = arrays(ends, ends, frame_pair(past.shape), frame_pair(past.shape))
    return call(pack_kernel, outs, (past, future), 0, scratch, whole=2)


def repack(past, future):
    frames, _, chan, cols = past.shape
    ends = (2, frames, chan, cols)
    outs = arrays(ends, ends, frame_pair(past.shape), frame_pair(past.shape))
    return call(repack_kernel, outs, (past, future), 0)


def rims_to_send(rows_odd, rows_even):
    rims = (2, 2) + rows_odd.shape[2:]
    return call(rims_kernel, arrays(rims, rims), (rows_odd, rows_even), 0)


def summed(parts, scale):
    kernel = functools.partial(sum_kernel, scale=scale)
    return call(kernel, arrays(parts.shape), (parts,), 0, sided=False)[0]


def unpacked(parts, chan):
    outs = arrays((27, chan, chan), (27, chan, chan), (1, chan), kind=F32)
    return call(unpack_kernel, outs, (parts,), 0, sided=False)


AXES = ("frames", "rows")


def pairs_of(count, first):
    pairs = []
    for i in range(first, count - 1, 2):
        pairs += [(i, i + 1), (i + 1, i)]
    return pairs


def swap(axis, odd, even):
    count = lax.axis_size(axis)
    even = lax.ppermute(even, axis, pairs_of(count, 0))
    return lax.ppermute(odd, axis, pairs_of(count, 1)), even


def per_device(clip_in, kernel_one, bias_one, kernel_two, cotangent):
    frame_count, row_count, channels, col_count = clip_in.shape
    devices = lax.axis_size("frames") * lax.axis_size("rows")
    cell_total = (
        frame_count * lax.axis_size("frames") * row_count * lax.axis_size("rows") * col_count
    )
    rows_odd, rows_even, main_odd, main_even = pack(clip_in, cotangent)
    main = swap("frames", main_odd, main_even)
    rows = swap("rows", rows_odd, rows_even)
    one_fwd, one_adj, two_fwd, two_adj, bias = flat_weights(kernel_one, kernel_two, bias_one)
    inner = first_inner(clip_in, cotangent, main, one_fwd, two_adj, bias)
    *rows, _ = lax.optimization_barrier((*rows, inner[-1]))
    rims = swap("frames", *rims_to_send(*rows))
    middle = first_middle(clip_in, cotangent, rows, one_fwd, two_adj, bias)
    active, grad_pre, terms = first_outer(
        devices, clip_in, cotangent, rows, rims, inner, middle, one_fwd, two_adj, bias
    )

    terms = lax.all_to_all(terms, AXES, 0, 0, tiled=True)
    spread = summed(terms, 1.0 / math.sqrt(cell_total))
    total = lax.all_to_all(spread, AXES, 0, 0, tiled=True)

    rows_odd, rows_even, main_odd, main_even = repack(active, grad_pre)
    rows = swap("rows", rows_odd, rows_even)
    main = swap("frames", main_odd, main_even)
    *rows, _ = lax.optimization_barrier((*rows, spread))
    rims = swap("frames", *rims_to_send(*rows))
    inner = second_inner(active, grad_pre, rows, main, two_fwd, one_adj, clip_in, cotangent)
    block_out, grad_input = second_outer(
        active, grad_pre, rows, rims, inner, two_fwd, one_adj, clip_in, cotangent
    )
    first, second, bias = unpacked(total, channels)
    return (
        block_out,
        grad_input,
        first.reshape(kernel_one.shape),
        second.reshape(kernel_two.shape),
        bias.reshape(bias_one.shape),
    )


def solution(mesh):
    in_specs = (P("frames", "rows", None, None), P(), P(), P(), P("frames", "rows", None, None))
    out_specs = (P("frames", "rows", None, None), P("frames", "rows", None, None), P(), P(), P())
    return jax.shard_map(per_device, mesh=mesh, in_specs=in_specs, out_specs=out_specs, check_vma=False)
```

time: 83.1 us -> 83.3 us (level)
  blocking collectives: 0 us -> 25 us
  starting transfers between devices: 46.3 us -> 30 us
  other arithmetic: 6.55 us -> 0 us
  waiting for transfers between devices: 11.6 us -> 9.62 us
  local copies, waits for them, and re-layouts: 2.98 us -> 1.03 us
  Pallas kernels: 14.3 us -> 15.7 us
    all_to_all x0 -> x1, blocking collectives: none -> 25 us  [per_device(): terms = lax.all_to_all(terms, AXES, 0, 0, tiled=True)]
    all_to_all x2 -> x1, starting transfers between devices: 24.3 us -> 4.14 us  [per_device(): total = lax.all_to_all(spread, AXES, 0, 0, tiled=True)]
    select_n x12 -> x0, other arithmetic: 4.16 us -> none  [the longest x6 1.96 us: swap_neighbours(): jnp.where(even, to_next, to_prior)]
    ppermute x12, starting transfers between devices: 22 us -> 25.9 us  [the longest x6 17.8 us: swap(): return (lax.ppermute(odd, axis, pairs_of(count, 1)), even)]
    slice x2 -> x0, local copies, waits for them, and re-layouts: 2.09 us -> none  [the longest x1 1.47 us: per_device(): total[:count, channels:].reshape(kernel_two.shape)]
    pallas_call x5 -> x12, Pallas kernels: 14.3 us -> 15.7 us  [call(): pl.pallas_call(body, out_shape=outs, in_specs=[pl.BlockSpec(memory_space=...]
    reduce_sum x1 -> x0, other arithmetic: 1.18 us -> none  [total_over_devices(): mine = jnp.sum(mine.astype(jnp.float32), axis=0).astype(jnp.bfloat16)]
    mul x1 -> x0, other arithmetic: 1.14 us -> none  [per_device(): total.reshape((-1, 2 * channels)).astype(jnp.float32)]
  transfers between devices with their start and end apart: 14 -> 13, of which waited for: 5 -> 4; matrix products, arithmetic and copies ran while one was open for 6% -> 0% of each run, Pallas kernels for 13% -> 11%
where the time goes in v5:
time: 83.3 us; the launch traced here: 82.3 us
  starting transfers between devices  30 us (36%)
  blocking collectives  25 us (30%)
  Pallas kernels  15.7 us (19%)
  waiting for transfers between devices  9.62 us (12%)
  local copies, waits for them, and re-layouts  1.03 us (1%)
  between operations  0.86 us (1%)
    all_to_all x1, blocking collectives, per_device(): terms = lax.all_to_all(terms, AXES, 0, 0, tiled=True)  25 us
    ppermute x6, starting transfers between devices, swap(): return (lax.ppermute(odd, axis, pairs_of(count, 1)), even)  17.8 us
    pallas_call x12, Pallas kernels, call(): pl.pallas_call(body, out_shape=outs, in_specs=[pl.BlockSpec(memory_space=...  15.7 us
    ppermute x6, starting transfers between devices, swap(): even = lax.ppermute(even, axis, pairs_of(count, 0))  8.1 us
    ppermute x6, waiting for transfers between devices, swap(): even = lax.ppermute(even, axis, pairs_of(count, 0))  5.2 us
    ppermute x6, waiting for transfers between devices, swap(): return (lax.ppermute(odd, axis, pairs_of(count, 1)), even)  4.41 us
    all_to_all x1, starting transfers between devices, per_device(): total = lax.all_to_all(spread, AXES, 0, 0, tiled=True)  4.14 us
  transfers between devices with their start and end apart: 13, of which 4 were waited for; matrix products, arithmetic and copies ran while one was open for 0% of the time, Pallas kernels for 11%

profile of v5, /device:TPU:1, one launch (start us, length us, event | category | flops | bytes accessed | tf_op | source)
XLA Modules:
  0.0 82.3 jit_solution(9571700808809223317)
XLA Ops:
  0.7 2.3 %shard_map.92 = (bf16[2,4,64,256]{3,2,1,0:T(8,128)(2,1)}, bf16[2,4,64,256]{3,2,1,0:T(8,128)(2,1)}, bf16[2,4,64,256]{3,2,1,0:T(8,128)(2,1)}, bf16[2,4,64,256]{3,2,1,0:T(8,128)(2,1)}) custom-call(bf16[4,4,64,256]{3,2,1,0:T(8,128)(2,1)} %refs_10_.1, bf16[4,4,64,256]{3,2,1,0:T(8,128)(2,1)} %refs_11_.1), custom_call_target="tpu_custom_call" | custom-call | bytes 2097152 | tf_op jit(solution)/shard_map/pallas_call | solution.py:298
  3.0 5.0 %collective-permute-start.2 = (bf16[2,4,64,256]{3,2,1,0:T(8,128)(2,1)}, bf16[2,4,64,256]{3,2,1,0:T(8,128)(2,1)S(1)}, u32[]{:S(2)}, u32[]{:S(2)}) collective-permute-start(bf16[2,4,64,256]{3,2,1,0:T(8,128)(2,1)} %get-tuple-element.49), channel_id=1, source_target_pairs={{32,64},{64,32},{33,65},{65,33},{34,66},{66,34},{35,67},{67,35},{3... | collective-permute-start | bytes 786440 | tf_op jit(solution)/shard_map/ppermute | solution.py:410
  8.1 0.7 collective-permute-start
  8.8 3.7 %collective-permute-start.1 = (bf16[2,4,64,256]{3,2,1,0:T(8,128)(2,1)}, bf16[2,4,64,256]{3,2,1,0:T(8,128)(2,1)S(1)}, u32[]{:S(2)}, u32[]{:S(2)}) collective-permute-start(bf16[2,4,64,256]{3,2,1,0:T(8,128)(2,1)} %get-tuple-element.48), channel_id=1, source_target_pairs={{0,1},{1,0},{2,3},{3,2},{4,5},{5,4},{6,7},{7,6},{8,9},{9,8},{10,11... | collective-permute-start | bytes 786440 | tf_op jit(solution)/shard_map/ppermute | solution.py:409
  12.5 1.0 %copy-done.3 = bf16[3,3,3,64,64]{4,3,2,1,0:T(8,128)(2,1)S(1)} copy-done((bf16[3,3,3,64,64]{4,3,2,1,0:T(8,128)(2,1)S(1)}, bf16[3,3,3,64,64]{4,3,2,1,0:T(8,128)(2,1)}, u32[]{:S(2)}) %copy-start.3) | copy-done | bytes 221208
  13.6 0.8 shard_map.93
  14.4 2.9 %shard_map.94 = (bf16[4,4,64,256]{3,2,1,0:T(8,128)(2,1)S(1)}, bf16[4,4,64,256]{3,2,1,0:T(8,128)(2,1)S(1)}, bf16[2,4,64,256]{3,2,1,0:T(8,128)(2,1)S(1)}, bf16[2,4...) custom-call(bf16[4,4,64,256]{3,2,1,0:T(8,128)(2,1)S(1)} %copy-done, ...), custom_call_target="tpu_custom_call" | custom-call | flops 1811939328 | bytes 4538624 | tf_op jit(solution)/shard_map/pallas_call | solution.py:298
  17.3 1.4 %collective-permute-done.1.refs_1_.refs_3_ = bf16[2,4,64,256]{3,2,1,0:T(8,128)(2,1)S(1)} collective-permute-done((bf16[2,4,64,256]{3,2,1,0:T(8,128)(2,1)}, bf16[2,4,64,256]{3,2,1,0:T(8,128)(2,1)S(1)}, u32[]{:S(2)}, u32[]{:S(2)}) %collective-permute-start.1) | collective-permute-done | bytes 262176 | tf_op jit(solution)/shard_map/ppermute | solution.py:409
  18.7 3.2 %collective-permute-start.4 = (bf16[2,2,64,256]{3,2,1,0:T(8,128)(2,1)S(1)}, bf16[2,2,64,256]{3,2,1,0:T(8,128)(2,1)S(1)}, u32[]{:S(2)}, u32[]{:S(2)}) collective-permute-start(bf16[2,2,64,256]{3,2,1,0:T(8,128)(2,1)S(1)} %get-tuple-element.57), channel_id=1, source_target_pairs={{32,64},{64,32},{33,65},{65,33},{34,66},{66,34},{35,67},{67,35},{3... | collective-permute-start | bytes 393224 | tf_op jit(solution)/shard_map/ppermute | solution.py:410
  22.0 0.9 %shard_map.96 = (f32[2,2,64,256]{3,2,1,0:T(8,128)S(1)}, f32[2,2,64,256]{3,2,1,0:T(8,128)S(1)}) custom-call(bf16[4,4,64,256]{3,2,1,0:T(8,128)(2,1)S(1)} %copy-done, bf16[4,4,64,256]{3,2,1,0:T(8,128)(2,1)S(1)} %copy-done.1, bf16[2,4,64,256]{3,2,1,0:T(8,128)(2,1)S(1)} %collective-permute-done.refs_0_.refs_2_, ...), custom_call_target="tpu_custom_call" | custom-call | flops 452984832 | bytes 2539776 | tf_op jit(solution)/shard_map/pallas_call | solution.py:298
  23.0 2.3 %collective-permute-done.4.refs_0_ = bf16[2,2,64,256]{3,2,1,0:T(8,128)(2,1)S(1)} collective-permute-done((bf16[2,2,64,256]{3,2,1,0:T(8,128)(2,1)S(1)}, bf16[2,2,64,256]{3,2,1,0:T(8,128)(2,1)S(1)}, u32[]{:S(2)}, u32[]{:S(2)}) %collective-permute-start.4) | collective-permute-done | bytes 131104 | tf_op jit(solution)/shard_map/ppermute | solution.py:410
  25.3 2.5 %shard_map.97 = (bf16[4,4,64,256]{3,2,1,0:T(8,128)(2,1)S(1)}, bf16[4,4,64,256]{3,2,1,0:T(8,128)(2,1)S(1)}, bf16[128,16,128]{2,1,0:T(8,128)(2,1)S(1)}) custom-call(bf16[2,2,64,256]{3,2,1,0:T(8,128)(2,1)S(1)} %collective-permute-done.4.refs_0_, bf16[2,2,64,256]{3,2,1,0:T(8,128)(2,1)S(1)} %collective-permute-done.5.refs_1_, ...), custom_call_target="tpu_custom_call" | custom-call | flops 1358954496 | bytes 6897920 | tf_op jit(solution)/shard_map/pallas_call | solution.py:298
  27.8 25.0 %all_to_all.10.parts = bf16[128,16,128]{2,1,0:T(8,128)(2,1)S(1)} all-to-all(bf16[128,16,128]{2,1,0:T(8,128)(2,1)S(1)} %get-tuple-element.71), channel_id=1, replica_groups=mesh['frames'=4,'rows'=32] {'frames','rows'}, dimensions={0} | all-to-all | bytes 1048576 | tf_op jit(solution)/shard_map/all_to_all | solution.py:431
  52.7 1.0 %shard_map.99 = bf16[128,16,128]{2,1,0:T(8,128)(2,1)} custom-call(bf16[128,16,128]{2,1,0:T(8,128)(2,1)S(1)} %all_to_all.10.parts), custom_call_target="tpu_custom_call" | custom-call | bytes 1048576 | tf_op jit(solution)/shard_map/pallas_call | solution.py:298
  53.7 4.1 %all-to-all-start.1 = ((bf16[128,16,128]{2,1,0:T(8,128)(2,1)}), bf16[128,16,128]{2,1,0:T(8,128)(2,1)S(1)}, u32[]{:S(2)}, u32[]{:S(2)}) async-start(bf16[128,16,128]{2,1,0:T(8,128)(2,1)} %shard_map.99), calls=%async_computation.1 | async-start | bytes 1048576 | tf_op jit(solution)/shard_map/all_to_all | solution.py:433
  57.9 0.7 collective-permute-start.6
  58.6 3.8 %collective-permute-start.7 = (bf16[2,4,64,256]{3,2,1,0:T(8,128)(2,1)S(1)}, bf16[2,4,64,256]{3,2,1,0:T(8,128)(2,1)S(1)}, u32[]{:S(2)}, u32[]{:S(2)}) collective-permute-start(bf16[2,4,64,256]{3,2,1,0:T(8,128)(2,1)S(1)} %get-tuple-element.70), channel_id=1, source_target_pairs={{0,1},{1,0},{2,3},{3,2},{4,5},{5,4},{6,7},{7,6},{8,9},{9,8},{10,11... | collective-permute-start | bytes 786440 | tf_op jit(solution)/shard_map/ppermute | solution.py:409
  62.5 4.1 %collective-permute-start.10 = (bf16[2,4,64,256]{3,2,1,0:T(8,128)(2,1)S(1)}, bf16[2,4,64,256]{3,2,1,0:T(8,128)(2,1)S(1)}, u32[]{:S(2)}, u32[]{:S(2)}) collective-permute-start(bf16[2,4,64,256]{3,2,1,0:T(8,128)(2,1)S(1)} %get-tuple-element.76), channel_id=1, source_target_pairs={{32,64},{64,32},{33,65},{65,33},{34,66},{66,34},{35,67},{67,35},{3... | collective-permute-start | bytes 786440 | tf_op jit(solution)/shard_map/ppermute | solution.py:410
  66.7 3.8 %collective-permute-done.7.refs_1_.refs_3_.refs_5_ = bf16[2,4,64,256]{3,2,1,0:T(8,128)(2,1)S(1)} collective-permute-done((bf16[2,4,64,256]{3,2,1,0:T(8,128)(2,1)S(1)}, bf16[2,4,64,256]{3,2,1,0:T(8,128)(2,1)S(1)}, u32[]{:S(2)}, u32[]{:S(2)}) %collective-permute-start.7) | collective-permute-done | bytes 262176 | tf_op jit(solution)/shard_map/ppermute | solution.py:409
  70.5 4.1 %collective-permute-start.8 = (bf16[2,2,64,256]{3,2,1,0:T(8,128)(2,1)S(1)}, bf16[2,2,64,256]{3,2,1,0:T(8,128)(2,1)S(1)}, u32[]{:S(2)}, u32[]{:S(2)}) collective-permute-start(bf16[2,2,64,256]{3,2,1,0:T(8,128)(2,1)S(1)} %get-tuple-element.74), channel_id=1, source_target_pairs={{32,64},{64,32},{33,65},{65,33},{34,66},{66,34},{35,67},{67,35},{3... | collective-permute-start | bytes 393224 | tf_op jit(solution)/shard_map/ppermute | solution.py:410
  74.9 2.1 %collective-permute-done.10.refs_4_ = bf16[2,4,64,256]{3,2,1,0:T(8,128)(2,1)S(1)} collective-permute-done((bf16[2,4,64,256]{3,2,1,0:T(8,128)(2,1)S(1)}, bf16[2,4,64,256]{3,2,1,0:T(8,128)(2,1)S(1)}, u32[]{:S(2)}, u32[]{:S(2)}) %collective-permute-start.10) | collective-permute-done | bytes 262176 | tf_op jit(solution)/shard_map/ppermute | solution.py:410
  77.0 2.1 %shard_map.101 = (bf16[4,4,64,256]{3,2,1,0:T(8,128)(2,1)S(1)}, bf16[4,4,64,256]{3,2,1,0:T(8,128)(2,1)S(1)}, bf16[2,4,64,256]{3,2,1,0:T(8,128)(2,1)S(1)}, bf16[2,4,64,256]{3,2,1,0:T(8,128)(2,1)S(1)}) custom-call(bf16[4,4,64,256]{3,2,1,0:T(8,128)(2,1)S(1)} %get-tuple-element.67.refs_0_.refs_2_, bf16[4,4,64,256]{3,2,1,0:T(8,128)(2,1)S(1)} %get-tuple-element.68.refs_1_.refs_3_, ...), custom_call_target="tpu_custom_call" | custom-call | flops 1358954496 | bytes 5160960 | tf_op jit(solution)/shard_map/pallas_call | solution.py:298
  79.1 1.9 %shard_map.102 = (bf16[4,4,64,256]{3,2,1,0:T(8,128)(2,1)}, bf16[4,4,64,256]{3,2,1,0:T(8,128)(2,1)}) custom-call(bf16[2,2,64,256]{3,2,1,0:T(8,128)(2,1)S(1)} %collective-permute-done.8.refs_0_, bf16[2,2,64,256]{3,2,1,0:T(8,128)(2,1)S(1)} %collective-permute-done.9.refs_1_, bf16[4,4,64,256]{3,2,1,0:T(8,128)(2,1)S(1)} %get-tuple-element.67.refs_0_.refs_2_, ...), custom_call_target="tpu_custom_call" | custom-call | flops 452984832 | bytes 5947392 | tf_op jit(solution)/shard_map/pallas_call | solution.py:298
  81.0 1.3 %shard_map.103 = (f32[27,64,64]{2,1,0:T(8,128)}, f32[27,64,64]{2,1,0:T(8,128)}, f32[1,64]{1,0:T(1,128)}) custom-call(bf16[128,16,128]{2,1,0:T(8,128)(2,1)S(1)} %all-to-all-done.1.parts), custom_call_target="tpu_custom_call" | custom-call | bytes 1409280 | tf_op jit(solution)/shard_map/pallas_call | solution.py:298
  (25 shorter events, 0.7 us)
Async XLA Ops:
  0.6 11.9 %copy-start.2 = (bf16[3,3,3,64,64]{4,3,2,1,0:T(8,128)(2,1)S(1)}, bf16[3,3,3,64,64]{4,3,2,1,0:T(8,128)(2,1)}, u32[]{:S(2)}) copy-start(bf16[3,3,3,64,64]{4,3,2,1,0:T(8,128)(2,1)} %param.6) | copy-start | bytes 663556
  0.6 11.9 %copy-start.4 = (f32[64]{0:T(128)S(1)}, f32[64]{0:T(128)}, u32[]{:S(2)}) copy-start(f32[64]{0:T(128)} %param.7) | copy-start | bytes 772
  0.7 13.7 %copy-start.1 = (bf16[4,4,64,256]{3,2,1,0:T(8,128)(2,1)S(1)}, bf16[4,4,64,256]{3,2,1,0:T(8,128)(2,1)}, u32[]{:S(2)}) copy-start(bf16[4,4,64,256]{3,2,1,0:T(8,128)(2,1)} %refs_11_.1) | copy-start | bytes 1572868
  3.0 11.4 %copy-start = (bf16[4,4,64,256]{3,2,1,0:T(8,128)(2,1)S(1)}, bf16[4,4,64,256]{3,2,1,0:T(8,128)(2,1)}, u32[]{:S(2)}) copy-start(bf16[4,4,64,256]{3,2,1,0:T(8,128)(2,1)} %refs_10_.1) | copy-start | bytes 1572868
  3.0 11.4 %collective-permute-start.2 = (bf16[2,4,64,256]{3,2,1,0:T(8,128)(2,1)}, bf16[2,4,64,256]{3,2,1,0:T(8,128)(2,1)S(1)}, u32[]{:S(2)}, u32[]{:S(2)}) collective-permute-start(bf16[2,4,64,256]{3,2,1,0:T(8,128)(2,1)} %get-tuple-element.49), channel_id=1, source_target_pairs={{32,64},{64,32},{33,65},{65,33},{34,66},{66,34},{35,67},{67,35},{3... | collective-permute-start | bytes 786440 | tf_op jit(solution)/shard_map/ppermute | solution.py:410
  8.0 6.3 %collective-permute-start.3 = (bf16[2,4,64,256]{3,2,1,0:T(8,128)(2,1)}, bf16[2,4,64,256]{3,2,1,0:T(8,128)(2,1)S(1)}, u32[]{:S(2)}, u32[]{:S(2)}) collective-permute-start(bf16[2,4,64,256]{3,2,1,0:T(8,128)(2,1)} %get-tuple-element.50), channel_id=1, source_target_pairs={{0,32},{32,0},{64,96},{96,64},{1,33},{33,1},{65,97},{97,65},{2,34}... | collective-permute-start | bytes 786440 | tf_op jit(solution)/shard_map/ppermute | solution.py:409
  8.1 9.1 %collective-permute-start = (bf16[2,4,64,256]{3,2,1,0:T(8,128)(2,1)}, bf16[2,4,64,256]{3,2,1,0:T(8,128)(2,1)S(1)}, u32[]{:S(2)}, u32[]{:S(2)}) collective-permute-start(bf16[2,4,64,256]{3,2,1,0:T(8,128)(2,1)} %get-tuple-element.47), channel_id=1, source_target_pairs={{1,2},{2,1},{3,4},{4,3},{5,6},{6,5},{7,8},{8,7},{9,10},{10,9},{11,... | collective-permute-start | bytes 786440 | tf_op jit(solution)/shard_map/ppermute | solution.py:410
  8.8 9.9 %collective-permute-start.1 = (bf16[2,4,64,256]{3,2,1,0:T(8,128)(2,1)}, bf16[2,4,64,256]{3,2,1,0:T(8,128)(2,1)S(1)}, u32[]{:S(2)}, u32[]{:S(2)}) collective-permute-start(bf16[2,4,64,256]{3,2,1,0:T(8,128)(2,1)} %get-tuple-element.48), channel_id=1, source_target_pairs={{0,1},{1,0},{2,3},{3,2},{4,5},{5,4},{6,7},{7,6},{8,9},{9,8},{10,11... | collective-permute-start | bytes 786440 | tf_op jit(solution)/shard_map/ppermute | solution.py:409
  12.5 1.0 %copy-start.3 = (bf16[3,3,3,64,64]{4,3,2,1,0:T(8,128)(2,1)S(1)}, bf16[3,3,3,64,64]{4,3,2,1,0:T(8,128)(2,1)}, u32[]{:S(2)}) copy-start(bf16[3,3,3,64,64]{4,3,2,1,0:T(8,128)(2,1)} %param.8) | copy-start | bytes 663556
  18.7 6.6 %collective-permute-start.4 = (bf16[2,2,64,256]{3,2,1,0:T(8,128)(2,1)S(1)}, bf16[2,2,64,256]{3,2,1,0:T(8,128)(2,1)S(1)}, u32[]{:S(2)}, u32[]{:S(2)}) collective-permute-start(bf16[2,2,64,256]{3,2,1,0:T(8,128)(2,1)S(1)} %get-tuple-element.57), channel_id=1, source_target_pairs={{32,64},{64,32},{33,65},{65,33},{34,66},{66,34},{35,67},{67,35},{3... | collective-permute-start | bytes 393224 | tf_op jit(solution)/shard_map/ppermute | solution.py:410
  21.9 3.3 %collective-permute-start.5 = (bf16[2,2,64,256]{3,2,1,0:T(8,128)(2,1)S(1)}, bf16[2,2,64,256]{3,2,1,0:T(8,128)(2,1)S(1)}, u32[]{:S(2)}, u32[]{:S(2)}) collective-permute-start(bf16[2,2,64,256]{3,2,1,0:T(8,128)(2,1)S(1)} %get-tuple-element.58), channel_id=1, source_target_pairs={{0,32},{32,0},{64,96},{96,64},{1,33},{33,1},{65,97},{97,65},{2,34}... | collective-permute-start | bytes 393224 | tf_op jit(solution)/shard_map/ppermute | solution.py:409
  53.7 27.3 %all-to-all-start.1 = ((bf16[128,16,128]{2,1,0:T(8,128)(2,1)}), bf16[128,16,128]{2,1,0:T(8,128)(2,1)S(1)}, u32[]{:S(2)}, u32[]{:S(2)}) async-start(bf16[128,16,128]{2,1,0:T(8,128)(2,1)} %shard_map.99), calls=%async_computation.1 | async-start | bytes 1048576 | tf_op jit(solution)/shard_map/all_to_all | solution.py:433
  57.9 8.7 %collective-permute-start.6 = (bf16[2,4,64,256]{3,2,1,0:T(8,128)(2,1)S(1)}, bf16[2,4,64,256]{3,2,1,0:T(8,128)(2,1)S(1)}, u32[]{:S(2)}, u32[]{:S(2)}) collective-permute-start(bf16[2,4,64,256]{3,2,1,0:T(8,128)(2,1)S(1)} %get-tuple-element.69), channel_id=1, source_target_pairs={{1,2},{2,1},{3,4},{4,3},{5,6},{6,5},{7,8},{8,7},{9,10},{10,9},{11,... | collective-permute-start | bytes 786440 | tf_op jit(solution)/shard_map/ppermute | solution.py:410
  58.6 11.8 %collective-permute-start.7 = (bf16[2,4,64,256]{3,2,1,0:T(8,128)(2,1)S(1)}, bf16[2,4,64,256]{3,2,1,0:T(8,128)(2,1)S(1)}, u32[]{:S(2)}, u32[]{:S(2)}) collective-permute-start(bf16[2,4,64,256]{3,2,1,0:T(8,128)(2,1)S(1)} %get-tuple-element.70), channel_id=1, source_target_pairs={{0,1},{1,0},{2,3},{3,2},{4,5},{5,4},{6,7},{7,6},{8,9},{9,8},{10,11... | collective-permute-start | bytes 786440 | tf_op jit(solution)/shard_map/ppermute | solution.py:409
  62.5 14.5 %collective-permute-start.10 = (bf16[2,4,64,256]{3,2,1,0:T(8,128)(2,1)S(1)}, bf16[2,4,64,256]{3,2,1,0:T(8,128)(2,1)S(1)}, u32[]{:S(2)}, u32[]{:S(2)}) collective-permute-start(bf16[2,4,64,256]{3,2,1,0:T(8,128)(2,1)S(1)} %get-tuple-element.76), channel_id=1, source_target_pairs={{32,64},{64,32},{33,65},{65,33},{34,66},{66,34},{35,67},{67,35},{3... | collective-permute-start | bytes 786440 | tf_op jit(solution)/shard_map/ppermute | solution.py:410
  66.6 10.4 %collective-permute-start.11 = (bf16[2,4,64,256]{3,2,1,0:T(8,128)(2,1)S(1)}, bf16[2,4,64,256]{3,2,1,0:T(8,128)(2,1)S(1)}, u32[]{:S(2)}, u32[]{:S(2)}) collective-permute-start(bf16[2,4,64,256]{3,2,1,0:T(8,128)(2,1)S(1)} %get-tuple-element.77), channel_id=1, source_target_pairs={{0,32},{32,0},{64,96},{96,64},{1,33},{33,1},{65,97},{97,65},{2,34}... | collective-permute-start | bytes 786440 | tf_op jit(solution)/shard_map/ppermute | solution.py:409
  70.5 8.6 %collective-permute-start.8 = (bf16[2,2,64,256]{3,2,1,0:T(8,128)(2,1)S(1)}, bf16[2,2,64,256]{3,2,1,0:T(8,128)(2,1)S(1)}, u32[]{:S(2)}, u32[]{:S(2)}) collective-permute-start(bf16[2,2,64,256]{3,2,1,0:T(8,128)(2,1)S(1)} %get-tuple-element.74), channel_id=1, source_target_pairs={{32,64},{64,32},{33,65},{65,33},{34,66},{66,34},{35,67},{67,35},{3... | collective-permute-start | bytes 393224 | tf_op jit(solution)/shard_map/ppermute | solution.py:410
  74.6 4.5 %collective-permute-start.9 = (bf16[2,2,64,256]{3,2,1,0:T(8,128)(2,1)S(1)}, bf16[2,2,64,256]{3,2,1,0:T(8,128)(2,1)S(1)}, u32[]{:S(2)}, u32[]{:S(2)}) collective-permute-start(bf16[2,2,64,256]{3,2,1,0:T(8,128)(2,1)S(1)} %get-tuple-element.75), channel_id=1, source_target_pairs={{0,32},{32,0},{64,96},{96,64},{1,33},{33,1},{65,97},{97,65},{2,34}... | collective-permute-start | bytes 393224 | tf_op jit(solution)/shard_map/ppermute | solution.py:409

commit v6 on v5

--- a/solution.py
+++ b/solution.py
@@ -29,9 +29,13 @@
     return jnp.concatenate([shifted(value, -1), value, shifted(value, 1)], axis=0)
 
 
+def slab_of(ref, *at):
+    return ref[at + (0,) * (len(ref.shape) - 2 - len(at))]
+
+
 def picker(even, odd_ref, even_ref, swapped):
     one, two = (even_ref, odd_ref) if swapped else (odd_ref, even_ref)
-    return lambda *at: jnp.where(even, one[at], two[at])
+    return lambda *at: jnp.where(even, slab_of(one, *at), slab_of(two, *at))
 
 
 def field(own, before, after, corner):
@@ -81,29 +85,6 @@
 def gated(hidden, grad_act):
     sig = jax.nn.sigmoid(hidden)
     return (hidden * sig).astype(BF16), (grad_act * sig * (1.0 + hidden * (1.0 - sig))).astype(BF16)
-
-
-def pack_kernel(side, past, future, rows_odd, rows_even, main_odd, main_even, sems):
-    frames, rows = past.shape[0], past.shape[1]
-    over_odd = side[0] * (rows - 1)
-
-    def run(first, second):
-        copies = [
-            pltpu.make_async_copy(first, main_odd, sems.at[4]),
-            pltpu.make_async_copy(second, main_even, sems.at[5]),
-        ]
-        for k, src in enumerate((past, future)):
-            copies.append(pltpu.make_async_copy(src.at[:, over_odd], rows_odd.at[k], sems.at[2 * k]))
-            over_even = rows - 1 - over_odd
-            copies.append(pltpu.make_async_copy(src.at[:, over_even], rows_even.at[k], sems.at[2 * k + 1]))
-        for copy in copies:
-            copy.start()
-        for copy in copies:
-            copy.wait()
-
-    last, first = past.at[frames - 2 : frames], future.at[0:2]
-    pl.when(side[1] == 0)(lambda: run(first, last))
-    pl.when(side[1] != 0)(lambda: run(last, first))
 
 
 def repack_kernel(side, past, future, rows_odd, rows_even, main_odd, main_even):
@@ -122,18 +103,18 @@
 
 
 def rims_kernel(side, rows_odd, rows_even, odd, even):
-    row_even, frame_even = side[0] == 0, side[1] == 0
+    frame_even = side[1] == 0
     last = rows_odd.shape[1] - 2
+    low = picker(side[0] == 0, rows_odd, rows_even, False)
+    high = picker(side[0] == 0, rows_odd, rows_even, True)
     for f in range(2):
-        for s in range(2):
-            one, two = (rows_odd, rows_even) if s == 0 else (rows_even, rows_odd)
-            past = jnp.where(row_even, one[0, f + last], two[0, f + last])
-            future = jnp.where(row_even, one[1, f], two[1, f])
+        for s, rim in enumerate((low, high)):
+            past, future = rim(0, f + last), rim(1, f)
             odd[f, s] = jnp.where(frame_even, future, past)
             even[f, s] = jnp.where(frame_even, past, future)
 
 
-def weights_kernel(one, two, bias, one_fwd, one_adj, two_fwd, two_adj, bias_out):
+def weights_kernel(one, two, one_fwd, one_adj, two_fwd, two_adj):
     chan = one.shape[1]
     for src, fwd, adj in ((one, one_fwd, one_adj), (two, two_fwd, two_adj)):
         for t in range(3):
@@ -145,10 +126,13 @@
                     left = (8 - t * 3 - i) * chan
                     flipped = jnp.transpose(tap.astype(F32)).astype(BF16)
                     adj[(2 - j) * chan : (3 - j) * chan, left : left + chan] = flipped
-    spread = jnp.broadcast_to(bias[...], (chan, chan))
-    lanes = lax.broadcasted_iota(jnp.int32, spread.shape, 1)
-    keep = lanes == lax.broadcasted_iota(jnp.int32, spread.shape, 0)
-    bias_out[...] = jnp.sum(jnp.where(keep, spread, 0.0), axis=1, keepdims=True)
+
+
+def column(row):
+    n = row.shape[1]
+    spread = jnp.broadcast_to(row, (n, n))
+    keep = lax.broadcasted_iota(jnp.int32, (n, n), 0) == lax.broadcasted_iota(jnp.int32, (n, n), 1)
+    return jnp.sum(jnp.where(keep, spread, 0.0), axis=1, keepdims=True)
 
 
 def first_inner_kernel(side, past, future, main_odd, main_even, wp, wf, bias,
@@ -157,13 +141,14 @@
     pick_main(side, main_odd, main_even, before, after)
     past_taps = field(past, before, None, None)
     future_taps = field(future, None, after, None)
+    shift = column(bias[...])
     total = jnp.zeros((chan, cols), F32)
     pres, acts, winp, winf = [], [], [], []
     for f in range(frames):
         for r in range(1, rows - 1):
             winp.append(past_taps(f, r))
             winf.append(future_taps(f, r))
-            active, pre = gated(convolved(wp, winp[-1]) + bias[...], convolved(wf, winf[-1]))
+            active, pre = gated(convolved(wp, winp[-1]) + shift, convolved(wf, winf[-1]))
             active_out[f, r] = active
             pre_out[f, r] = pre
             acts.append(column_taps(active))
@@ -180,9 +165,10 @@
     past_corner, future_corner = corners(side, frames, rows_odd, rows_even)
     past_taps = field(past, past.at[0:2], None, past_corner)
     future_taps = field(future, None, future, future_corner)
+    shift = column(bias[...])
     for k in range(2):
         for s, r in enumerate((0, rows - 1)):
-            hid[k, s] = convolved(wp, past_taps(frames - 2 + k, r)) + bias[...]
+            hid[k, s] = convolved(wp, past_taps(frames - 2 + k, r)) + shift
             act[k, s] = convolved(wf, future_taps(k, r))
 
 
@@ -193,13 +179,14 @@
     past_corner, future_corner = corners(side, frames, rows_in_odd, rows_in_even, rim_odd, rim_even)
     past_taps = field(past, before, None, past_corner)
     future_taps = field(future, None, after, future_corner)
+    shift = column(bias[...])
     total = bsum[...]
     pres, acts, winp, winf = [], [], [], []
     for f in range(frames):
         for s, r in enumerate((0, rows - 1)):
             winp.append(past_taps(f, r))
             winf.append(future_taps(f, r))
-            hidden = convolved(wp, winp[-1]) + bias[...] if f < 2 else hid[f - frames + 2, s]
+            hidden = convolved(wp, winp[-1]) + shift if f < 2 else hid[f - frames + 2, s]
             grad_act = act[f, s] if f < 2 else convolved(wf, winf[-1])
             active, pre = gated(hidden, grad_act)
             active_out[f, r] = active
@@ -269,10 +256,13 @@
 
 
 def sum_kernel(parts, out, *, scale):
-    total = parts[0].astype(F32)
-    for k in range(1, parts.shape[0]):
-        total = total + parts[k].astype(F32)
-    out[...] = jnp.broadcast_to((total * scale).astype(out.dtype)[None], out.shape)
+    lanes = 8
+    sums = [parts[k].astype(F32) for k in range(lanes)]
+    for k in range(lanes, parts.shape[0]):
+        sums[k % lanes] = sums[k % lanes] + parts[k].astype(F32)
+    while len(sums) > 1:
+        sums = [a + b for a, b in zip(sums[::2], sums[1::2])]
+    out[...] = jnp.broadcast_to((sums[0] * scale).astype(out.dtype)[None], out.shape)
 
 
 def unpack_kernel(parts, one, two, bias):
@@ -291,17 +281,17 @@
     return lax.axis_index("rows") % 2, lax.axis_index("frames") % 2
 
 
-def call(kernel, outs, args, flops, scratch=(), sided=True, whole=0):
+def call(kernel, outs, args, flops, scratch=(), sided=True):
     vmem = pl.BlockSpec(memory_space=pltpu.VMEM)
     moved = sum(x.size * x.dtype.itemsize for x in list(args) + list(outs))
     body = (lambda *refs: kernel(sides(), *refs)) if sided else kernel
     return pl.pallas_call(
         body,
         out_shape=outs,
-        in_specs=[pl.BlockSpec(memory_space=pltpu.HBM)] * whole + [vmem] * (len(args) - whole),
+        in_specs=[vmem] * len(args),
         out_specs=[vmem] * len(outs),
         scratch_shapes=scratch,
-        compiler_params=pltpu.CompilerParams(vmem_limit_bytes=None if whole else VMEM_LIMIT),
+        compiler_params=pltpu.CompilerParams(vmem_limit_bytes=VMEM_LIMIT),
         cost_estimate=pl.CostEstimate(flops=flops, bytes_accessed=moved, transcendentals=0),
     )(*args)
 
@@ -313,11 +303,11 @@
     return [jax.ShapeDtypeStruct(shape, kind) for shape in shapes]
 
 
-def flat_weights(one, two, bias):
-    chan = bias.shape[0]
+def flat_weights(one, two):
+    chan = one.shape[3]
     taps = (27, chan, chan)
-    outs = arrays(*[(3 * chan, 9 * chan)] * 4) + arrays((chan, 1), kind=F32)
-    return call(weights_kernel, outs, (one.reshape(taps), two.reshape(taps), bias[None]), 0, sided=False)
+    outs = arrays(*[(3 * chan, 9 * chan)] * 4)
+    return call(weights_kernel, outs, (one.reshape(taps), two.reshape(taps)), 0, sided=False)
 
 
 def conv_flops(shape, rows):
@@ -364,14 +354,6 @@
     return call(second_outer_kernel, arrays(out_past.shape, out_past.shape), args, conv_flops(out_past.shape, 8))
 
 
-def pack(past, future):
-    frames, _, chan, cols = past.shape
-    ends = (2, frames, chan, cols)
-    scratch = [pltpu.SemaphoreType.DMA((6,))]
-    outs = arrays(ends, ends, frame_pair(past.shape), frame_pair(past.shape))
-    return call(pack_kernel, outs, (past, future), 0, scratch, whole=2)
-
-
 def repack(past, future):
     frames, _, chan, cols = past.shape
     ends = (2, frames, chan, cols)
@@ -380,7 +362,7 @@
 
 
 def rims_to_send(rows_odd, rows_even):
-    rims = (2, 2) + rows_odd.shape[2:]
+    rims = (2, 2) + rows_odd.shape[-2:]
     return call(rims_kernel, arrays(rims, rims), (rows_odd, rows_even), 0)
 
 
@@ -416,10 +398,16 @@
     cell_total = (
         frame_count * lax.axis_size("frames") * row_count * lax.axis_size("rows") * col_count
     )
-    rows_odd, rows_even, main_odd, main_even = pack(clip_in, cotangent)
-    main = swap("frames", main_odd, main_even)
-    rows = swap("rows", rows_odd, rows_even)
-    one_fwd, one_adj, two_fwd, two_adj, bias = flat_weights(kernel_one, kernel_two, bias_one)
+    row_even, frame_even = (side == 0 for side in sides())
+    both = jnp.stack([clip_in, cotangent])
+    first_row, last_row = both[:, :, :1], both[:, :, -1:]
+    rows = swap(
+        "rows", jnp.where(row_even, first_row, last_row), jnp.where(row_even, last_row, first_row)
+    )
+    past, future = clip_in[-2:], cotangent[:2]
+    main = swap("frames", jnp.where(frame_even, future, past), jnp.where(frame_even, past, future))
+    one_fwd, one_adj, two_fwd, two_adj = flat_weights(kernel_one, kernel_two)
+    bias = bias_one[None]
     inner = first_inner(clip_in, cotangent, main, one_fwd, two_adj, bias)
     *rows, _ = lax.optimization_barrier((*rows, inner[-1]))
     rims = swap("frames", *rims_to_send(*rows))

time: 83.3 us -> 80.9 us (0.971)
  Pallas kernels: 15.7 us -> 13.6 us
  waiting for transfers between devices: 9.62 us -> 8.14 us
  other arithmetic: 0 us -> 1.24 us
    pallas_call x12 -> x11, Pallas kernels: 15.7 us -> 13.6 us  [call(): pl.pallas_call(body, out_shape=outs, in_specs=[vmem] * len(args), out_spe...]
    ppermute x6, waiting for transfers between devices: 5.2 us -> 3.79 us  [swap(): even = lax.ppermute(even, axis, pairs_of(count, 0))]
    ppermute x6, starting transfers between devices: 8.1 us -> 9.48 us  [swap(): even = lax.ppermute(even, axis, pairs_of(count, 0))]
    select_n x0 -> x3, other arithmetic: none -> 1.24 us  [the longest x1 1.15 us: per_device(): jnp.where(frame_even, past, future)]
    ppermute x6, starting transfers between devices: 17.8 us -> 16.6 us  [swap(): return (lax.ppermute(odd, axis, pairs_of(count, 1)), even)]
  transfers between devices with their start and end apart: 13 -> 13, of which waited for: 4 -> 3; matrix products, arithmetic and copies ran while one was open for 0% -> 0% of each run, Pallas kernels for 11% -> 11%
where the time goes in v6:
time: 80.9 us; the launch traced here: 79.9 us
  starting transfers between devices  30.2 us (37%)
  blocking collectives  25.1 us (31%)
  Pallas kernels  13.6 us (17%)
  waiting for transfers between devices  8.14 us (10%)
  other arithmetic  1.24 us (2%)
  between operations  0.93 us (1%)
    all_to_all x1, blocking collectives, per_device(): terms = lax.all_to_all(terms, AXES, 0, 0, tiled=True)  25.1 us
    ppermute x6, starting transfers between devices, swap(): return (lax.ppermute(odd, axis, pairs_of(count, 1)), even)  16.6 us
    pallas_call x11, Pallas kernels, call(): pl.pallas_call(body, out_shape=outs, in_specs=[vmem] * len(args), out_spe...  13.6 us
    ppermute x6, starting transfers between devices, swap(): even = lax.ppermute(even, axis, pairs_of(count, 0))  9.48 us
    ppermute x6, waiting for transfers between devices, swap(): return (lax.ppermute(odd, axis, pairs_of(count, 1)), even)  4.34 us
    all_to_all x1, starting transfers between devices, per_device(): total = lax.all_to_all(spread, AXES, 0, 0, tiled=True)  4.14 us
    ppermute x6, waiting for transfers between devices, swap(): even = lax.ppermute(even, axis, pairs_of(count, 0))  3.79 us
  transfers between devices with their start and end apart: 13, of which 3 were waited for; matrix products, arithmetic and copies ran while one was open for 0% of the time, Pallas kernels for 11%

profile of v6, /device:TPU:1, one launch (start us, length us, event | category | flops | bytes accessed | tf_op | source)
XLA Modules:
  0.0 79.9 jit_solution(3749183115122657105)
XLA Ops:
  0.7 1.2 %broadcast_select_fusion = (bf16[2,4,64,256]{3,2,1,0:T(8,128)(2,1)S(1)}, bf16[2,4,64,256]{3,2,1,0:T(8,128)(2,1)S(1)}) fusion(pred[]{:T(512)S(6)} %eq.10, bf16[4,4,64,256]{3,2,1,0:T(8,128)(2,1)} %refs_10_.1, bf16[4,4,64,256]{3,2,1,0:T(8,128)(2,1)} %refs_11_.1), kind=kLoop, calls=%fused_computation.2 | loop fusion | flops 262144 | bytes 1048577 | tf_op jit(solution)/shard_map/jit(_where)/select_n | solution.py:408
  1.8 1.5 %collective-permute-start.3 = (bf16[2,4,64,256]{3,2,1,0:T(8,128)(2,1)S(1)}, bf16[2,4,64,256]{3,2,1,0:T(8,128)(2,1)S(1)}, u32[]{:S(2)}, u32[]{:S(2)}) collective-permute-start(bf16[2,4,64,256]{3,2,1,0:T(8,128)(2,1)S(1)} %get-tuple-element.82), channel_id=1, source_target_pairs={{0,32},{32,0},{64,96},{96,64},{1,33},{33,1},{65,97},{97,65},{2,34}... | collective-permute-start | bytes 786440 | tf_op jit(solution)/shard_map/ppermute | solution.py:391
  3.3 3.6 %collective-permute-start.2 = (bf16[2,4,64,256]{3,2,1,0:T(8,128)(2,1)S(1)}, bf16[2,4,64,256]{3,2,1,0:T(8,128)(2,1)S(1)}, u32[]{:S(2)}, u32[]{:S(2)}) collective-permute-start(bf16[2,4,64,256]{3,2,1,0:T(8,128)(2,1)S(1)} %get-tuple-element.83), channel_id=1, source_target_pairs={{32,64},{64,32},{33,65},{65,33},{34,66},{66,34},{35,67},{67,35},{3... | collective-permute-start | bytes 786440 | tf_op jit(solution)/shard_map/ppermute | solution.py:392
  7.0 0.8 %collective-permute-start = (bf16[2,4,1,64,256]{4,3,2,1,0:T(8,128)(2,1)S(1)}, bf16[2,4,1,64,256]{4,3,2,1,0:T(8,128)(2,1)S(1)}, u32[]{:S(2)}, u32[]{:S(2)}) collective-permute-start(bf16[2,4,1,64,256]{4,3,2,1,0:T(8,128)(2,1)S(1)} %broadcast_select_fusion.3), channel_id=1, source_target_pairs={{1,2},{2,1},{3,4},{4,3},{5,6},{6,5},{7,8},{8,7},{9,10},{10,9},{11,... | collective-permute-start | bytes 786440 | tf_op jit(solution)/shard_map/ppermute | solution.py:392
  7.8 3.7 %collective-permute-start.1 = (bf16[2,4,1,64,256]{4,3,2,1,0:T(8,128)(2,1)S(1)}, bf16[2,4,1,64,256]{4,3,2,1,0:T(8,128)(2,1)S(1)}, u32[]{:S(2)}, u32[]{:S(2)}) collective-permute-start(bf16[2,4,1,64,256]{4,3,2,1,0:T(8,128)(2,1)S(1)} %get-tuple-element.79), channel_id=1, source_target_pairs={{0,1},{1,0},{2,3},{3,2},{4,5},{5,4},{6,7},{7,6},{8,9},{9,8},{10,11... | collective-permute-start | bytes 786440 | tf_op jit(solution)/shard_map/ppermute | solution.py:391
  11.6 0.9 %shard_map.92 = (bf16[192,576]{1,0:T(8,128)(2,1)S(1)}, bf16[192,576]{1,0:T(8,128)(2,1)S(1)}, bf16[192,576]{1,0:T(8,128)(2,1)S(1)}, bf16[192,576]{1,0:T(8,128)(2,1)S(1)}) custom-call(bf16[27,64,64]{2,1,0:T(8,128)(2,1)S(1)} %bitcast.10, bf16[27,64,64]{2,1,0:T(8,128)(2,1)S(1)} %bitcast.11), custom_call_target="tpu_custom_call" | custom-call | bytes 1327104 | tf_op jit(solution)/shard_map/pallas_call | solution.py:288
  12.5 0.6 copy-done.4
  13.1 2.9 %shard_map.93 = (bf16[4,4,64,256]{3,2,1,0:T(8,128)(2,1)S(1)}, bf16[4,4,64,256]{3,2,1,0:T(8,128)(2,1)S(1)}, bf16[2,4,64,256]{3,2,1,0:T(8,128)(2,1)S(1)}, bf16[2,4...) custom-call(bf16[4,4,64,256]{3,2,1,0:T(8,128)(2,1)S(1)} %copy-done.1, ...), custom_call_target="tpu_custom_call" | custom-call | flops 1811939328 | bytes 4538624 | tf_op jit(solution)/shard_map/pallas_call | solution.py:288
  16.1 3.4 %collective-permute-start.4 = (bf16[2,2,64,256]{3,2,1,0:T(8,128)(2,1)S(1)}, bf16[2,2,64,256]{3,2,1,0:T(8,128)(2,1)S(1)}, u32[]{:S(2)}, u32[]{:S(2)}) collective-permute-start(bf16[2,2,64,256]{3,2,1,0:T(8,128)(2,1)S(1)} %get-tuple-element.47), channel_id=1, source_target_pairs={{32,64},{64,32},{33,65},{65,33},{34,66},{66,34},{35,67},{67,35},{3... | collective-permute-start | bytes 393224 | tf_op jit(solution)/shard_map/ppermute | solution.py:392
  19.6 0.9 %shard_map.95 = (f32[2,2,64,256]{3,2,1,0:T(8,128)S(1)}, f32[2,2,64,256]{3,2,1,0:T(8,128)S(1)}) custom-call(bf16[4,4,64,256]{3,2,1,0:T(8,128)(2,1)S(1)} %copy-done.1, bf16[4,4,64,256]{3,2,1,0:T(8,128)(2,1)S(1)} %copy-done, bf16[2,4,1,64,256]{4,3,2,1,0:T(8,128)(2,1)S(1)} %collective-permute-done.refs_0_.refs_2_, ...), custom_call_target="tpu_custom_call" | custom-call | flops 452984832 | bytes 2539776 | tf_op jit(solution)/shard_map/pallas_call | solution.py:288
  20.5 2.2 %collective-permute-done.4.refs_0_ = bf16[2,2,64,256]{3,2,1,0:T(8,128)(2,1)S(1)} collective-permute-done((bf16[2,2,64,256]{3,2,1,0:T(8,128)(2,1)S(1)}, bf16[2,2,64,256]{3,2,1,0:T(8,128)(2,1)S(1)}, u32[]{:S(2)}, u32[]{:S(2)}) %collective-permute-start.4) | collective-permute-done | bytes 131104 | tf_op jit(solution)/shard_map/ppermute | solution.py:392
  22.8 2.5 %shard_map.96 = (bf16[4,4,64,256]{3,2,1,0:T(8,128)(2,1)S(1)}, bf16[4,4,64,256]{3,2,1,0:T(8,128)(2,1)S(1)}, bf16[128,16,128]{2,1,0:T(8,128)(2,1)S(1)}) custom-call(bf16[2,2,64,256]{3,2,1,0:T(8,128)(2,1)S(1)} %collective-permute-done.4.refs_0_, bf16[2,2,64,256]{3,2,1,0:T(8,128)(2,1)S(1)} %collective-permute-done.5.refs_1_, ...), custom_call_target="tpu_custom_call" | custom-call | flops 1358954496 | bytes 6897920 | tf_op jit(solution)/shard_map/pallas_call | solution.py:288
  25.3 25.1 %all_to_all.10.parts = bf16[128,16,128]{2,1,0:T(8,128)(2,1)S(1)} all-to-all(bf16[128,16,128]{2,1,0:T(8,128)(2,1)S(1)} %get-tuple-element.61), channel_id=1, replica_groups=mesh['frames'=4,'rows'=32] {'frames','rows'}, dimensions={0} | all-to-all | bytes 1048576 | tf_op jit(solution)/shard_map/all_to_all | solution.py:419
  50.4 0.9 %shard_map.98 = bf16[128,16,128]{2,1,0:T(8,128)(2,1)} custom-call(bf16[128,16,128]{2,1,0:T(8,128)(2,1)S(1)} %all_to_all.10.parts), custom_call_target="tpu_custom_call" | custom-call | bytes 1048576 | tf_op jit(solution)/shard_map/pallas_call | solution.py:288
  51.3 4.1 %all-to-all-start.1 = ((bf16[128,16,128]{2,1,0:T(8,128)(2,1)}), bf16[128,16,128]{2,1,0:T(8,128)(2,1)S(1)}, u32[]{:S(2)}, u32[]{:S(2)}) async-start(bf16[128,16,128]{2,1,0:T(8,128)(2,1)} %shard_map.98), calls=%async_computation.1 | async-start | bytes 1048576 | tf_op jit(solution)/shard_map/all_to_all | solution.py:421
  55.5 0.7 collective-permute-start.6
  56.2 3.8 %collective-permute-start.7 = (bf16[2,4,64,256]{3,2,1,0:T(8,128)(2,1)S(1)}, bf16[2,4,64,256]{3,2,1,0:T(8,128)(2,1)S(1)}, u32[]{:S(2)}, u32[]{:S(2)}) collective-permute-start(bf16[2,4,64,256]{3,2,1,0:T(8,128)(2,1)S(1)} %get-tuple-element.60), channel_id=1, source_target_pairs={{0,1},{1,0},{2,3},{3,2},{4,5},{5,4},{6,7},{7,6},{8,9},{9,8},{10,11... | collective-permute-start | bytes 786440 | tf_op jit(solution)/shard_map/ppermute | solution.py:391
  60.1 4.1 %collective-permute-start.10 = (bf16[2,4,64,256]{3,2,1,0:T(8,128)(2,1)S(1)}, bf16[2,4,64,256]{3,2,1,0:T(8,128)(2,1)S(1)}, u32[]{:S(2)}, u32[]{:S(2)}) collective-permute-start(bf16[2,4,64,256]{3,2,1,0:T(8,128)(2,1)S(1)} %get-tuple-element.66), channel_id=1, source_target_pairs={{32,64},{64,32},{33,65},{65,33},{34,66},{66,34},{35,67},{67,35},{3... | collective-permute-start | bytes 786440 | tf_op jit(solution)/shard_map/ppermute | solution.py:392
  64.2 3.8 %collective-permute-done.7.refs_1_.refs_3_.refs_5_ = bf16[2,4,64,256]{3,2,1,0:T(8,128)(2,1)S(1)} collective-permute-done((bf16[2,4,64,256]{3,2,1,0:T(8,128)(2,1)S(1)}, bf16[2,4,64,256]{3,2,1,0:T(8,128)(2,1)S(1)}, u32[]{:S(2)}, u32[]{:S(2)}) %collective-permute-start.7) | collective-permute-done | bytes 262176 | tf_op jit(solution)/shard_map/ppermute | solution.py:391
  68.0 4.1 %collective-permute-start.8 = (bf16[2,2,64,256]{3,2,1,0:T(8,128)(2,1)S(1)}, bf16[2,2,64,256]{3,2,1,0:T(8,128)(2,1)S(1)}, u32[]{:S(2)}, u32[]{:S(2)}) collective-permute-start(bf16[2,2,64,256]{3,2,1,0:T(8,128)(2,1)S(1)} %get-tuple-element.64), channel_id=1, source_target_pairs={{32,64},{64,32},{33,65},{65,33},{34,66},{66,34},{35,67},{67,35},{3... | collective-permute-start | bytes 393224 | tf_op jit(solution)/shard_map/ppermute | solution.py:392
  72.4 2.1 %collective-permute-done.10.refs_4_ = bf16[2,4,64,256]{3,2,1,0:T(8,128)(2,1)S(1)} collective-permute-done((bf16[2,4,64,256]{3,2,1,0:T(8,128)(2,1)S(1)}, bf16[2,4,64,256]{3,2,1,0:T(8,128)(2,1)S(1)}, u32[]{:S(2)}, u32[]{:S(2)}) %collective-permute-start.10) | collective-permute-done | bytes 262176 | tf_op jit(solution)/shard_map/ppermute | solution.py:392
  74.5 2.1 %shard_map.100 = (bf16[4,4,64,256]{3,2,1,0:T(8,128)(2,1)S(1)}, bf16[4,4,64,256]{3,2,1,0:T(8,128)(2,1)S(1)}, bf16[2,4,64,256]{3,2,1,0:T(8,128)(2,1)S(1)}, bf16[2,4,64,256]{3,2,1,0:T(8,128)(2,1)S(1)}) custom-call(bf16[4,4,64,256]{3,2,1,0:T(8,128)(2,1)S(1)} %get-tuple-element.57.refs_0_.refs_2_, bf16[4,4,64,256]{3,2,1,0:T(8,128)(2,1)S(1)} %get-tuple-element.58.refs_1_.refs_3_, ...), custom_call_target="tpu_custom_call" | custom-call | flops 1358954496 | bytes 5160960 | tf_op jit(solution)/shard_map/pallas_call | solution.py:288
  76.7 1.9 %shard_map.101 = (bf16[4,4,64,256]{3,2,1,0:T(8,128)(2,1)}, bf16[4,4,64,256]{3,2,1,0:T(8,128)(2,1)}) custom-call(bf16[2,2,64,256]{3,2,1,0:T(8,128)(2,1)S(1)} %collective-permute-done.8.refs_0_, bf16[2,2,64,256]{3,2,1,0:T(8,128)(2,1)S(1)} %collective-permute-done.9.refs_1_, bf16[4,4,64,256]{3,2,1,0:T(8,128)(2,1)S(1)} %get-tuple-element.57.refs_0_.refs_2_, ...), custom_call_target="tpu_custom_call" | custom-call | flops 452984832 | bytes 5947392 | tf_op jit(solution)/shard_map/pallas_call | solution.py:288
  78.5 1.3 %shard_map.102 = (f32[27,64,64]{2,1,0:T(8,128)}, f32[27,64,64]{2,1,0:T(8,128)}, f32[1,64]{1,0:T(1,128)}) custom-call(bf16[128,16,128]{2,1,0:T(8,128)(2,1)S(1)} %all-to-all-done.1.parts), custom_call_target="tpu_custom_call" | custom-call | bytes 1409280 | tf_op jit(solution)/shard_map/pallas_call | solution.py:288
  (27 shorter events, 0.7 us)
Async XLA Ops:
  0.6 6.2 %copy-start = (bf16[4,4,64,256]{3,2,1,0:T(8,128)(2,1)S(1)}, bf16[4,4,64,256]{3,2,1,0:T(8,128)(2,1)}, u32[]{:S(2)}) copy-start(bf16[4,4,64,256]{3,2,1,0:T(8,128)(2,1)} %refs_11_.1) | copy-start | bytes 1572868
  0.7 6.2 %copy-start.1 = (bf16[4,4,64,256]{3,2,1,0:T(8,128)(2,1)S(1)}, bf16[4,4,64,256]{3,2,1,0:T(8,128)(2,1)}, u32[]{:S(2)}) copy-start(bf16[4,4,64,256]{3,2,1,0:T(8,128)(2,1)} %refs_10_.1) | copy-start | bytes 1572868
  1.8 10.6 %collective-permute-start.3 = (bf16[2,4,64,256]{3,2,1,0:T(8,128)(2,1)S(1)}, bf16[2,4,64,256]{3,2,1,0:T(8,128)(2,1)S(1)}, u32[]{:S(2)}, u32[]{:S(2)}) collective-permute-start(bf16[2,4,64,256]{3,2,1,0:T(8,128)(2,1)S(1)} %get-tuple-element.82), channel_id=1, source_target_pairs={{0,32},{32,0},{64,96},{96,64},{1,33},{33,1},{65,97},{97,65},{2,34}... | collective-permute-start | bytes 786440 | tf_op jit(solution)/shard_map/ppermute | solution.py:391
  3.3 9.2 %collective-permute-start.2 = (bf16[2,4,64,256]{3,2,1,0:T(8,128)(2,1)S(1)}, bf16[2,4,64,256]{3,2,1,0:T(8,128)(2,1)S(1)}, u32[]{:S(2)}, u32[]{:S(2)}) collective-permute-start(bf16[2,4,64,256]{3,2,1,0:T(8,128)(2,1)S(1)} %get-tuple-element.83), channel_id=1, source_target_pairs={{32,64},{64,32},{33,65},{65,33},{34,66},{66,34},{35,67},{67,35},{3... | collective-permute-start | bytes 786440 | tf_op jit(solution)/shard_map/ppermute | solution.py:392
  6.9 4.7 %copy-start.3 = (bf16[3,3,3,64,64]{4,3,2,1,0:T(8,128)(2,1)S(1)}, bf16[3,3,3,64,64]{4,3,2,1,0:T(8,128)(2,1)}, u32[]{:S(2)}) copy-start(bf16[3,3,3,64,64]{4,3,2,1,0:T(8,128)(2,1)} %param.8) | copy-start | bytes 663556
  7.0 4.6 %copy-start.2 = (bf16[3,3,3,64,64]{4,3,2,1,0:T(8,128)(2,1)S(1)}, bf16[3,3,3,64,64]{4,3,2,1,0:T(8,128)(2,1)}, u32[]{:S(2)}) copy-start(bf16[3,3,3,64,64]{4,3,2,1,0:T(8,128)(2,1)} %param.6) | copy-start | bytes 663556
  7.0 9.0 %collective-permute-start = (bf16[2,4,1,64,256]{4,3,2,1,0:T(8,128)(2,1)S(1)}, bf16[2,4,1,64,256]{4,3,2,1,0:T(8,128)(2,1)S(1)}, u32[]{:S(2)}, u32[]{:S(2)}) collective-permute-start(bf16[2,4,1,64,256]{4,3,2,1,0:T(8,128)(2,1)S(1)} %broadcast_select_fusion.3), channel_id=1, source_target_pairs={{1,2},{2,1},{3,4},{4,3},{5,6},{6,5},{7,8},{8,7},{9,10},{10,9},{11,... | collective-permute-start | bytes 786440 | tf_op jit(solution)/shard_map/ppermute | solution.py:392
  7.8 8.2 %collective-permute-start.1 = (bf16[2,4,1,64,256]{4,3,2,1,0:T(8,128)(2,1)S(1)}, bf16[2,4,1,64,256]{4,3,2,1,0:T(8,128)(2,1)S(1)}, u32[]{:S(2)}, u32[]{:S(2)}) collective-permute-start(bf16[2,4,1,64,256]{4,3,2,1,0:T(8,128)(2,1)S(1)} %get-tuple-element.79), channel_id=1, source_target_pairs={{0,1},{1,0},{2,3},{3,2},{4,5},{5,4},{6,7},{7,6},{8,9},{9,8},{10,11... | collective-permute-start | bytes 786440 | tf_op jit(solution)/shard_map/ppermute | solution.py:391
  12.5 0.7 copy-start.4
  16.1 6.7 %collective-permute-start.4 = (bf16[2,2,64,256]{3,2,1,0:T(8,128)(2,1)S(1)}, bf16[2,2,64,256]{3,2,1,0:T(8,128)(2,1)S(1)}, u32[]{:S(2)}, u32[]{:S(2)}) collective-permute-start(bf16[2,2,64,256]{3,2,1,0:T(8,128)(2,1)S(1)} %get-tuple-element.47), channel_id=1, source_target_pairs={{32,64},{64,32},{33,65},{65,33},{34,66},{66,34},{35,67},{67,35},{3... | collective-permute-start | bytes 393224 | tf_op jit(solution)/shard_map/ppermute | solution.py:392
  19.5 3.3 %collective-permute-start.5 = (bf16[2,2,64,256]{3,2,1,0:T(8,128)(2,1)S(1)}, bf16[2,2,64,256]{3,2,1,0:T(8,128)(2,1)S(1)}, u32[]{:S(2)}, u32[]{:S(2)}) collective-permute-start(bf16[2,2,64,256]{3,2,1,0:T(8,128)(2,1)S(1)} %get-tuple-element.48), channel_id=1, source_target_pairs={{0,32},{32,0},{64,96},{96,64},{1,33},{33,1},{65,97},{97,65},{2,34}... | collective-permute-start | bytes 393224 | tf_op jit(solution)/shard_map/ppermute | solution.py:391
  51.3 27.3 %all-to-all-start.1 = ((bf16[128,16,128]{2,1,0:T(8,128)(2,1)}), bf16[128,16,128]{2,1,0:T(8,128)(2,1)S(1)}, u32[]{:S(2)}, u32[]{:S(2)}) async-start(bf16[128,16,128]{2,1,0:T(8,128)(2,1)} %shard_map.98), calls=%async_computation.1 | async-start | bytes 1048576 | tf_op jit(solution)/shard_map/all_to_all | solution.py:421
  55.5 8.7 %collective-permute-start.6 = (bf16[2,4,64,256]{3,2,1,0:T(8,128)(2,1)S(1)}, bf16[2,4,64,256]{3,2,1,0:T(8,128)(2,1)S(1)}, u32[]{:S(2)}, u32[]{:S(2)}) collective-permute-start(bf16[2,4,64,256]{3,2,1,0:T(8,128)(2,1)S(1)} %get-tuple-element.59), channel_id=1, source_target_pairs={{1,2},{2,1},{3,4},{4,3},{5,6},{6,5},{7,8},{8,7},{9,10},{10,9},{11,... | collective-permute-start | bytes 786440 | tf_op jit(solution)/shard_map/ppermute | solution.py:392
  56.2 11.8 %collective-permute-start.7 = (bf16[2,4,64,256]{3,2,1,0:T(8,128)(2,1)S(1)}, bf16[2,4,64,256]{3,2,1,0:T(8,128)(2,1)S(1)}, u32[]{:S(2)}, u32[]{:S(2)}) collective-permute-start(bf16[2,4,64,256]{3,2,1,0:T(8,128)(2,1)S(1)} %get-tuple-element.60), channel_id=1, source_target_pairs={{0,1},{1,0},{2,3},{3,2},{4,5},{5,4},{6,7},{7,6},{8,9},{9,8},{10,11... | collective-permute-start | bytes 786440 | tf_op jit(solution)/shard_map/ppermute | solution.py:391
  60.1 14.5 %collective-permute-start.10 = (bf16[2,4,64,256]{3,2,1,0:T(8,128)(2,1)S(1)}, bf16[2,4,64,256]{3,2,1,0:T(8,128)(2,1)S(1)}, u32[]{:S(2)}, u32[]{:S(2)}) collective-permute-start(bf16[2,4,64,256]{3,2,1,0:T(8,128)(2,1)S(1)} %get-tuple-element.66), channel_id=1, source_target_pairs={{32,64},{64,32},{33,65},{65,33},{34,66},{66,34},{35,67},{67,35},{3... | collective-permute-start | bytes 786440 | tf_op jit(solution)/shard_map/ppermute | solution.py:392
  64.1 10.4 %collective-permute-start.11 = (bf16[2,4,64,256]{3,2,1,0:T(8,128)(2,1)S(1)}, bf16[2,4,64,256]{3,2,1,0:T(8,128)(2,1)S(1)}, u32[]{:S(2)}, u32[]{:S(2)}) collective-permute-start(bf16[2,4,64,256]{3,2,1,0:T(8,128)(2,1)S(1)} %get-tuple-element.67), channel_id=1, source_target_pairs={{0,32},{32,0},{64,96},{96,64},{1,33},{33,1},{65,97},{97,65},{2,34}... | collective-permute-start | bytes 786440 | tf_op jit(solution)/shard_map/ppermute | solution.py:391
  68.0 8.6 %collective-permute-start.8 = (bf16[2,2,64,256]{3,2,1,0:T(8,128)(2,1)S(1)}, bf16[2,2,64,256]{3,2,1,0:T(8,128)(2,1)S(1)}, u32[]{:S(2)}, u32[]{:S(2)}) collective-permute-start(bf16[2,2,64,256]{3,2,1,0:T(8,128)(2,1)S(1)} %get-tuple-element.64), channel_id=1, source_target_pairs={{32,64},{64,32},{33,65},{65,33},{34,66},{66,34},{35,67},{67,35},{3... | collective-permute-start | bytes 393224 | tf_op jit(solution)/shard_map/ppermute | solution.py:392
  72.2 4.5 %collective-permute-start.9 = (bf16[2,2,64,256]{3,2,1,0:T(8,128)(2,1)S(1)}, bf16[2,2,64,256]{3,2,1,0:T(8,128)(2,1)S(1)}, u32[]{:S(2)}, u32[]{:S(2)}) collective-permute-start(bf16[2,2,64,256]{3,2,1,0:T(8,128)(2,1)S(1)} %get-tuple-element.65), channel_id=1, source_target_pairs={{0,32},{32,0},{64,96},{96,64},{1,33},{33,1},{65,97},{97,65},{2,34}... | collective-permute-start | bytes 393224 | tf_op jit(solution)/shard_map/ppermute | solution.py:391

commit v7 on v6

--- a/solution.py
+++ b/solution.py
@@ -114,7 +114,8 @@
             even[f, s] = jnp.where(frame_even, past, future)
 
 
-def weights_kernel(one, two, one_fwd, one_adj, two_fwd, two_adj):
+def weights_kernel(one, two, bias, one_fwd, one_adj, two_fwd, two_adj, bias_out):
+    bias_out[...] = column(bias[...])
     chan = one.shape[1]
     for src, fwd, adj in ((one, one_fwd, one_adj), (two, two_fwd, two_adj)):
         for t in range(3):
@@ -135,13 +136,14 @@
     return jnp.sum(jnp.where(keep, spread, 0.0), axis=1, keepdims=True)
 
 
-def first_inner_kernel(side, past, future, main_odd, main_even, wp, wf, bias,
-                       active_out, pre_out, before, after, d1, d2, bsum):
+def first_inner_kernel(side, past, future, rows_odd, rows_even, main_odd, main_even, wp, wf, bias,
+                       active_out, pre_out, before, after, hid, act, d1, d2, bsum):
     frames, rows, chan, cols = past.shape
     pick_main(side, main_odd, main_even, before, after)
-    past_taps = field(past, before, None, None)
-    future_taps = field(future, None, after, None)
-    shift = column(bias[...])
+    past_corner, future_corner = corners(side, frames, rows_odd, rows_even)
+    past_taps = field(past, before, None, past_corner)
+    future_taps = field(future, None, after, future_corner)
+    shift = bias[...]
     total = jnp.zeros((chan, cols), F32)
     pres, acts, winp, winf = [], [], [], []
     for f in range(frames):
@@ -154,22 +156,14 @@
             acts.append(column_taps(active))
             pres.append(column_taps(pre))
             total = total + pre.astype(F32)
+    for k in range(2):
+        for s, r in enumerate((0, rows - 1)):
+            hid[k, s] = convolved(wp, past_taps(frames - 2 + k, r)) + shift
+            act[k, s] = convolved(wf, future_taps(k, r))
     bsum[...] = total
     lanes = lambda parts: jnp.concatenate(parts, axis=1)
     d1[...] = lax.dot_general(lanes(pres), lanes(winp), NT, preferred_element_type=F32)
     d2[...] = lax.dot_general(lanes(winf), lanes(acts), NT, preferred_element_type=F32)
-
-
-def first_middle_kernel(side, past, future, rows_odd, rows_even, wp, wf, bias, hid, act):
-    frames, rows, _, _ = past.shape
-    past_corner, future_corner = corners(side, frames, rows_odd, rows_even)
-    past_taps = field(past, past.at[0:2], None, past_corner)
-    future_taps = field(future, None, future, future_corner)
-    shift = column(bias[...])
-    for k in range(2):
-        for s, r in enumerate((0, rows - 1)):
-            hid[k, s] = convolved(wp, past_taps(frames - 2 + k, r)) + shift
-            act[k, s] = convolved(wf, future_taps(k, r))
 
 
 def first_outer_kernel(side, rim_odd, rim_even, rows_in_odd, rows_in_even, past, future, before, after, hid, act,
@@ -179,7 +173,7 @@
     past_corner, future_corner = corners(side, frames, rows_in_odd, rows_in_even, rim_odd, rim_even)
     past_taps = field(past, before, None, past_corner)
     future_taps = field(future, None, after, future_corner)
-    shift = column(bias[...])
+    shift = bias[...]
     total = bsum[...]
     pres, acts, winp, winf = [], [], [], []
     for f in range(frames):
@@ -303,11 +297,11 @@
     return [jax.ShapeDtypeStruct(shape, kind) for shape in shapes]
 
 
-def flat_weights(one, two):
+def flat_weights(one, two, bias):
     chan = one.shape[3]
     taps = (27, chan, chan)
-    outs = arrays(*[(3 * chan, 9 * chan)] * 4)
-    return call(weights_kernel, outs, (one.reshape(taps), two.reshape(taps)), 0, sided=False)
+    outs = arrays(*[(3 * chan, 9 * chan)] * 4) + arrays((chan, 1), kind=F32)
+    return call(weights_kernel, outs, (one.reshape(taps), two.reshape(taps), bias[None]), 0, sided=False)
 
 
 def conv_flops(shape, rows):
@@ -318,26 +312,21 @@
     return (2,) + shape[1:]
 
 
-def first_inner(past, future, main, wp, wf, bias):
+def first_inner(past, future, rows, main, wp, wf, bias):
     shape = past.shape
     chan, cols = shape[2:]
+    part = (2, 2, chan, cols)
     outs = arrays(shape, shape, frame_pair(shape), frame_pair(shape)) + arrays(
-        (3 * chan, 9 * chan), (9 * chan, 3 * chan), (chan, cols), kind=F32)
-    return call(first_inner_kernel, outs, (past, future, *main, wp, wf, bias), conv_flops(shape, 32))
-
-
-def first_middle(past, future, rows, wp, wf, bias):
-    part = (2, 2) + past.shape[2:]
-    return call(first_middle_kernel, arrays(part, part, kind=F32), (past, future, *rows, wp, wf, bias),
-                conv_flops(past.shape, 8))
-
-
-def first_outer(devices, past, future, rows, rims, inner, middle, wp, wf, bias):
+        part, part, (3 * chan, 9 * chan), (9 * chan, 3 * chan), (chan, cols), kind=F32)
+    return call(first_inner_kernel, outs, (past, future, *rows, *main, wp, wf, bias), conv_flops(shape, 40))
+
+
+def first_outer(devices, past, future, rows, rims, inner, wp, wf, bias):
     active, pre, before, after, *sums = inner
     _, _, chan, _ = active.shape
     outs = arrays(active.shape, pre.shape, (devices, 16, 2 * chan))
     scratch = [pltpu.VMEM((3 * chan, 9 * chan), F32), pltpu.VMEM((9 * chan, 3 * chan), F32)]
-    args = (*rims, *rows, past, future, before, after, *middle, *sums, wp, wf, bias, active, pre)
+    args = (*rims, *rows, past, future, before, after, *sums, wp, wf, bias, active, pre)
     return call(first_outer_kernel, outs, args, conv_flops(active.shape, 24), scratch)
 
 
@@ -406,14 +395,11 @@
     )
     past, future = clip_in[-2:], cotangent[:2]
     main = swap("frames", jnp.where(frame_even, future, past), jnp.where(frame_even, past, future))
-    one_fwd, one_adj, two_fwd, two_adj = flat_weights(kernel_one, kernel_two)
-    bias = bias_one[None]
-    inner = first_inner(clip_in, cotangent, main, one_fwd, two_adj, bias)
-    *rows, _ = lax.optimization_barrier((*rows, inner[-1]))
+    one_fwd, one_adj, two_fwd, two_adj, bias = flat_weights(kernel_one, kernel_two, bias_one)
     rims = swap("frames", *rims_to_send(*rows))
-    middle = first_middle(clip_in, cotangent, rows, one_fwd, two_adj, bias)
+    inner = first_inner(clip_in, cotangent, rows, main, one_fwd, two_adj, bias)
     active, grad_pre, terms = first_outer(
-        devices, clip_in, cotangent, rows, rims, inner, middle, one_fwd, two_adj, bias
+        devices, clip_in, cotangent, rows, rims, inner, one_fwd, two_adj, bias
     )
 
     terms = lax.all_to_all(terms, AXES, 0, 0, tiled=True)

time: 80.9 us -> 79.4 us (0.981)
  blocking collectives: 25.1 us -> 21 us
  waiting for transfers between devices: 8.14 us -> 9.75 us
  starting transfers between devices: 30.2 us -> 31.7 us
    all_to_all x1, blocking collectives: 25.1 us -> 21 us  [per_device(): terms = lax.all_to_all(terms, AXES, 0, 0, tiled=True)]
    ppermute x6, waiting for transfers between devices: 4.34 us -> 5.95 us  [swap(): return (lax.ppermute(odd, axis, pairs_of(count, 1)), even)]
    select_n x1, other arithmetic: 0.06 us -> 1.21 us  [per_device(): jnp.where(row_even, last_row, first_row)]
    select_n x1, other arithmetic: 1.15 us -> 0.04 us  [per_device(): jnp.where(frame_even, past, future)]
    pallas_call x11 -> x10, Pallas kernels: 13.6 us -> 13.1 us  [call(): pl.pallas_call(body, out_shape=outs, in_specs=[vmem] * len(args), out_spe...]
where the time goes in v7:
time: 79.4 us; the launch traced here: 78.4 us
  starting transfers between devices  31.7 us (40%)
  blocking collectives  21 us (26%)
  Pallas kernels  13.1 us (16%)
  waiting for transfers between devices  9.75 us (12%)
  other arithmetic  1.28 us (2%)
  between operations  0.9 us (1%)
    all_to_all x1, blocking collectives, per_device(): terms = lax.all_to_all(terms, AXES, 0, 0, tiled=True)  21 us
    ppermute x6, starting transfers between devices, swap(): return (lax.ppermute(odd, axis, pairs_of(count, 1)), even)  17.4 us
    pallas_call x10, Pallas kernels, call(): pl.pallas_call(body, out_shape=outs, in_specs=[vmem] * len(args), out_spe...  13.1 us
    ppermute x6, starting transfers between devices, swap(): even = lax.ppermute(even, axis, pairs_of(count, 0))  10.1 us
    ppermute x6, waiting for transfers between devices, swap(): return (lax.ppermute(odd, axis, pairs_of(count, 1)), even)  5.95 us
    all_to_all x1, starting transfers between devices, per_device(): total = lax.all_to_all(spread, AXES, 0, 0, tiled=True)  4.14 us
    ppermute x6, waiting for transfers between devices, swap(): even = lax.ppermute(even, axis, pairs_of(count, 0))  3.79 us
  transfers between devices with their start and end apart: 13, of which 3 were waited for; matrix products, arithmetic and copies ran while one was open for 0% of the time, Pallas kernels for 11%

profile of v7, /device:TPU:1, one launch (start us, length us, event | category | flops | bytes accessed | tf_op | source)
XLA Modules:
  0.0 78.4 jit_solution(8557778868288149071)
XLA Ops:
  0.7 1.2 %broadcast_select_fusion.2 = (bf16[2,4,1,64,256]{4,3,2,1,0:T(8,128)(2,1)S(1)}, bf16[2,4,1,64,256]{4,3,2,1,0:T(8,128)(2,1)S(1)}, bf16[2,4,1,64,256]{4,3,2,1,0:T(8,128)(2,1)S(1)}) fusion(pred[]{:T(512)S(6)} %eq.9, bf16[1,4,4,64,256]{4,3,2,1,0:T(8,128)(2,1)} %bitcast.8, bf16[1,4,4,64,256]{4,3,2,1,0:T(8,128)(2,1)} %bitcast.9), kind=kLoop, calls=%fused_computation.4 | loop fusion | flops 393216 | bytes 1835009 | tf_op jit(solution)/shard_map/jit(_where)/select_n | solution.py:394
  1.9 0.8 %collective-permute-start = (bf16[2,4,1,64,256]{4,3,2,1,0:T(8,128)(2,1)S(1)}, bf16[2,4,1,64,256]{4,3,2,1,0:T(8,128)(2,1)S(1)}, u32[]{:S(2)}, u32[]{:S(2)}) collective-permute-start(bf16[2,4,1,64,256]{4,3,2,1,0:T(8,128)(2,1)S(1)} %broadcast_select_fusion.3), channel_id=1, source_target_pairs={{1,2},{2,1},{3,4},{4,3},{5,6},{6,5},{7,8},{8,7},{9,10},{10,9},{11,... | collective-permute-start | bytes 786440 | tf_op jit(solution)/shard_map/ppermute | solution.py:381
  2.7 4.6 %collective-permute-start.1 = (bf16[2,4,1,64,256]{4,3,2,1,0:T(8,128)(2,1)S(1)}, bf16[2,4,1,64,256]{4,3,2,1,0:T(8,128)(2,1)S(1)}, u32[]{:S(2)}, u32[]{:S(2)}) collective-permute-start(bf16[2,4,1,64,256]{4,3,2,1,0:T(8,128)(2,1)S(1)} %get-tuple-element.77), channel_id=1, source_target_pairs={{0,1},{1,0},{2,3},{3,2},{4,5},{5,4},{6,7},{7,6},{8,9},{9,8},{10,11... | collective-permute-start | bytes 786440 | tf_op jit(solution)/shard_map/ppermute | solution.py:380
  7.3 1.3 %collective-permute-start.5 = (bf16[2,4,64,256]{3,2,1,0:T(8,128)(2,1)S(1)}, bf16[2,4,64,256]{3,2,1,0:T(8,128)(2,1)S(1)}, u32[]{:S(2)}, u32[]{:S(2)}) collective-permute-start(bf16[2,4,64,256]{3,2,1,0:T(8,128)(2,1)S(1)} %get-tuple-element.80), channel_id=1, source_target_pairs={{0,32},{32,0},{64,96},{96,64},{1,33},{33,1},{65,97},{97,65},{2,34}... | collective-permute-start | bytes 786440 | tf_op jit(solution)/shard_map/ppermute | solution.py:380
  8.7 3.6 %collective-permute-start.4 = (bf16[2,4,64,256]{3,2,1,0:T(8,128)(2,1)S(1)}, bf16[2,4,64,256]{3,2,1,0:T(8,128)(2,1)S(1)}, u32[]{:S(2)}, u32[]{:S(2)}) collective-permute-start(bf16[2,4,64,256]{3,2,1,0:T(8,128)(2,1)S(1)} %get-tuple-element.81), channel_id=1, source_target_pairs={{32,64},{64,32},{33,65},{65,33},{34,66},{66,34},{35,67},{67,35},{3... | collective-permute-start | bytes 786440 | tf_op jit(solution)/shard_map/ppermute | solution.py:381
  12.3 0.6 copy-done.4
  12.9 0.9 %shard_map.93 = (bf16[192,576]{1,0:T(8,128)(2,1)S(1)}, bf16[192,576]{1,0:T(8,128)(2,1)S(1)}, bf16[192,576]{1,0:T(8,128)(2,1)S(1)}, bf16[192,576]{1,0:T(8,128)(2,1)S(1)}, f32[64,1]{1,0:T(8,128)S(1)}) custom-call(bf16[27,64,64]{2,1,0:T(8,128)(2,1)S(1)} %bitcast.10, bf16[27,64,64]{2,1,0:T(8,128)(2,1)S(1)} %bitcast.11, f32[1,64]{1,0:T(1,128)S(1)} %bitcast.12), custom_call_target="tpu_custom_call" | custom-call | bytes 1327616 | tf_op jit(solution)/shard_map/pallas_call | solution.py:282
  13.8 4.2 %collective-permute-start.2 = (bf16[2,2,64,256]{3,2,1,0:T(8,128)(2,1)S(1)}, bf16[2,2,64,256]{3,2,1,0:T(8,128)(2,1)S(1)}, u32[]{:S(2)}, u32[]{:S(2)}) collective-permute-start(bf16[2,2,64,256]{3,2,1,0:T(8,128)(2,1)S(1)} %get-tuple-element.41), channel_id=1, source_target_pairs={{32,64},{64,32},{33,65},{65,33},{34,66},{66,34},{35,67},{67,35},{3... | collective-permute-start | bytes 393224 | tf_op jit(solution)/shard_map/ppermute | solution.py:381
  18.1 3.8 %collective-permute-done.4.refs_4_ = bf16[2,4,64,256]{3,2,1,0:T(8,128)(2,1)S(1)} collective-permute-done((bf16[2,4,64,256]{3,2,1,0:T(8,128)(2,1)S(1)}, bf16[2,4,64,256]{3,2,1,0:T(8,128)(2,1)S(1)}, u32[]{:S(2)}, u32[]{:S(2)}) %collective-permute-start.4) | collective-permute-done | bytes 262176 | tf_op jit(solution)/shard_map/ppermute | solution.py:381
  22.0 3.4 %shard_map.94 = (bf16[4,4,64,256]{3,2,1,0:T(8,128)(2,1)S(1)}, bf16[4,4,64,256]{3,2,1,0:T(8,128)(2,1)S(1)}, bf16[2,4,64,256]{3,2,1,0:T(8,128)(2,1)S(1)}, bf16[2,4...) custom-call(bf16[4,4,64,256]{3,2,1,0:T(8,128)(2,1)S(1)} %copy-done.1, ...), custom_call_target="tpu_custom_call" | custom-call | flops 2264924160 | bytes 5587200 | tf_op jit(solution)/shard_map/pallas_call | solution.py:282
  25.4 2.5 %shard_map.95 = (bf16[4,4,64,256]{3,2,1,0:T(8,128)(2,1)S(1)}, bf16[4,4,64,256]{3,2,1,0:T(8,128)(2,1)S(1)}, bf16[128,16,128]{2,1,0:T(8,128)(2,1)S(1)}) custom-call(bf16[2,2,64,256]{3,2,1,0:T(8,128)(2,1)S(1)} %collective-permute-done.2.refs_0_, bf16[2,2,64,256]{3,2,1,0:T(8,128)(2,1)S(1)} %collective-permute-done.3.refs_1_, ...), custom_call_target="tpu_custom_call" | custom-call | flops 1358954496 | bytes 6897920 | tf_op jit(solution)/shard_map/pallas_call | solution.py:282
  27.9 21.0 %all_to_all.10.parts = bf16[128,16,128]{2,1,0:T(8,128)(2,1)S(1)} all-to-all(bf16[128,16,128]{2,1,0:T(8,128)(2,1)S(1)} %get-tuple-element.59), channel_id=1, replica_groups=mesh['frames'=4,'rows'=32] {'frames','rows'}, dimensions={0} | all-to-all | bytes 1048576 | tf_op jit(solution)/shard_map/all_to_all | solution.py:405
  48.9 0.9 %shard_map.97 = bf16[128,16,128]{2,1,0:T(8,128)(2,1)} custom-call(bf16[128,16,128]{2,1,0:T(8,128)(2,1)S(1)} %all_to_all.10.parts), custom_call_target="tpu_custom_call" | custom-call | bytes 1048576 | tf_op jit(solution)/shard_map/pallas_call | solution.py:282
  49.8 4.1 %all-to-all-start.1 = ((bf16[128,16,128]{2,1,0:T(8,128)(2,1)}), bf16[128,16,128]{2,1,0:T(8,128)(2,1)S(1)}, u32[]{:S(2)}, u32[]{:S(2)}) async-start(bf16[128,16,128]{2,1,0:T(8,128)(2,1)} %shard_map.97), calls=%async_computation.1 | async-start | bytes 1048576 | tf_op jit(solution)/shard_map/all_to_all | solution.py:407
  54.0 0.7 collective-permute-start.6
  54.7 3.8 %collective-permute-start.7 = (bf16[2,4,64,256]{3,2,1,0:T(8,128)(2,1)S(1)}, bf16[2,4,64,256]{3,2,1,0:T(8,128)(2,1)S(1)}, u32[]{:S(2)}, u32[]{:S(2)}) collective-permute-start(bf16[2,4,64,256]{3,2,1,0:T(8,128)(2,1)S(1)} %get-tuple-element.58), channel_id=1, source_target_pairs={{0,1},{1,0},{2,3},{3,2},{4,5},{5,4},{6,7},{7,6},{8,9},{9,8},{10,11... | collective-permute-start | bytes 786440 | tf_op jit(solution)/shard_map/ppermute | solution.py:380
  58.6 4.1 %collective-permute-start.10 = (bf16[2,4,64,256]{3,2,1,0:T(8,128)(2,1)S(1)}, bf16[2,4,64,256]{3,2,1,0:T(8,128)(2,1)S(1)}, u32[]{:S(2)}, u32[]{:S(2)}) collective-permute-start(bf16[2,4,64,256]{3,2,1,0:T(8,128)(2,1)S(1)} %get-tuple-element.64), channel_id=1, source_target_pairs={{32,64},{64,32},{33,65},{65,33},{34,66},{66,34},{35,67},{67,35},{3... | collective-permute-start | bytes 786440 | tf_op jit(solution)/shard_map/ppermute | solution.py:381
  62.8 3.8 %collective-permute-done.7.refs_1_.refs_3_.refs_5_ = bf16[2,4,64,256]{3,2,1,0:T(8,128)(2,1)S(1)} collective-permute-done((bf16[2,4,64,256]{3,2,1,0:T(8,128)(2,1)S(1)}, bf16[2,4,64,256]{3,2,1,0:T(8,128)(2,1)S(1)}, u32[]{:S(2)}, u32[]{:S(2)}) %collective-permute-start.7) | collective-permute-done | bytes 262176 | tf_op jit(solution)/shard_map/ppermute | solution.py:380
  66.6 4.1 %collective-permute-start.8 = (bf16[2,2,64,256]{3,2,1,0:T(8,128)(2,1)S(1)}, bf16[2,2,64,256]{3,2,1,0:T(8,128)(2,1)S(1)}, u32[]{:S(2)}, u32[]{:S(2)}) collective-permute-start(bf16[2,2,64,256]{3,2,1,0:T(8,128)(2,1)S(1)} %get-tuple-element.62), channel_id=1, source_target_pairs={{32,64},{64,32},{33,65},{65,33},{34,66},{66,34},{35,67},{67,35},{3... | collective-permute-start | bytes 393224 | tf_op jit(solution)/shard_map/ppermute | solution.py:381
  70.7 0.3 collective-permute-start.9
  70.9 2.1 %collective-permute-done.10.refs_4_ = bf16[2,4,64,256]{3,2,1,0:T(8,128)(2,1)S(1)} collective-permute-done((bf16[2,4,64,256]{3,2,1,0:T(8,128)(2,1)S(1)}, bf16[2,4,64,256]{3,2,1,0:T(8,128)(2,1)S(1)}, u32[]{:S(2)}, u32[]{:S(2)}) %collective-permute-start.10) | collective-permute-done | bytes 262176 | tf_op jit(solution)/shard_map/ppermute | solution.py:381
  73.1 2.1 %shard_map.99 = (bf16[4,4,64,256]{3,2,1,0:T(8,128)(2,1)S(1)}, bf16[4,4,64,256]{3,2,1,0:T(8,128)(2,1)S(1)}, bf16[2,4,64,256]{3,2,1,0:T(8,128)(2,1)S(1)}, bf16[2,4,64,256]{3,2,1,0:T(8,128)(2,1)S(1)}) custom-call(bf16[4,4,64,256]{3,2,1,0:T(8,128)(2,1)S(1)} %get-tuple-element.55.refs_0_.refs_2_, bf16[4,4,64,256]{3,2,1,0:T(8,128)(2,1)S(1)} %get-tuple-element.56.refs_1_.refs_3_, ...), custom_call_target="tpu_custom_call" | custom-call | flops 1358954496 | bytes 5160960 | tf_op jit(solution)/shard_map/pallas_call | solution.py:282
  75.2 1.9 %shard_map.100 = (bf16[4,4,64,256]{3,2,1,0:T(8,128)(2,1)}, bf16[4,4,64,256]{3,2,1,0:T(8,128)(2,1)}) custom-call(bf16[2,2,64,256]{3,2,1,0:T(8,128)(2,1)S(1)} %collective-permute-done.8.refs_0_, bf16[2,2,64,256]{3,2,1,0:T(8,128)(2,1)S(1)} %collective-permute-done.9.refs_1_, bf16[4,4,64,256]{3,2,1,0:T(8,128)(2,1)S(1)} %get-tuple-element.55.refs_0_.refs_2_, ...), custom_call_target="tpu_custom_call" | custom-call | flops 452984832 | bytes 5947392 | tf_op jit(solution)/shard_map/pallas_call | solution.py:282
  77.1 1.3 %shard_map.101 = (f32[27,64,64]{2,1,0:T(8,128)}, f32[27,64,64]{2,1,0:T(8,128)}, f32[1,64]{1,0:T(1,128)}) custom-call(bf16[128,16,128]{2,1,0:T(8,128)(2,1)S(1)} %all-to-all-done.1.parts), custom_call_target="tpu_custom_call" | custom-call | bytes 1409280 | tf_op jit(solution)/shard_map/pallas_call | solution.py:282
  (26 shorter events, 0.4 us)
Async XLA Ops:
  0.6 6.6 %copy-start.1 = (bf16[4,4,64,256]{3,2,1,0:T(8,128)(2,1)S(1)}, bf16[4,4,64,256]{3,2,1,0:T(8,128)(2,1)}, u32[]{:S(2)}) copy-start(bf16[4,4,64,256]{3,2,1,0:T(8,128)(2,1)} %refs_10_.1) | copy-start | bytes 1572868
  1.9 5.4 %copy-start = (bf16[4,4,64,256]{3,2,1,0:T(8,128)(2,1)S(1)}, bf16[4,4,64,256]{3,2,1,0:T(8,128)(2,1)}, u32[]{:S(2)}) copy-start(bf16[4,4,64,256]{3,2,1,0:T(8,128)(2,1)} %refs_11_.1) | copy-start | bytes 1572868
  1.9 11.9 %collective-permute-start = (bf16[2,4,1,64,256]{4,3,2,1,0:T(8,128)(2,1)S(1)}, bf16[2,4,1,64,256]{4,3,2,1,0:T(8,128)(2,1)S(1)}, u32[]{:S(2)}, u32[]{:S(2)}) collective-permute-start(bf16[2,4,1,64,256]{4,3,2,1,0:T(8,128)(2,1)S(1)} %broadcast_select_fusion.3), channel_id=1, source_target_pairs={{1,2},{2,1},{3,4},{4,3},{5,6},{6,5},{7,8},{8,7},{9,10},{10,9},{11,... | collective-permute-start | bytes 786440 | tf_op jit(solution)/shard_map/ppermute | solution.py:381
  2.7 11.1 %collective-permute-start.1 = (bf16[2,4,1,64,256]{4,3,2,1,0:T(8,128)(2,1)S(1)}, bf16[2,4,1,64,256]{4,3,2,1,0:T(8,128)(2,1)S(1)}, u32[]{:S(2)}, u32[]{:S(2)}) collective-permute-start(bf16[2,4,1,64,256]{4,3,2,1,0:T(8,128)(2,1)S(1)} %get-tuple-element.77), channel_id=1, source_target_pairs={{0,1},{1,0},{2,3},{3,2},{4,5},{5,4},{6,7},{7,6},{8,9},{9,8},{10,11... | collective-permute-start | bytes 786440 | tf_op jit(solution)/shard_map/ppermute | solution.py:380
  7.3 5.0 %copy-start.2 = (bf16[3,3,3,64,64]{4,3,2,1,0:T(8,128)(2,1)S(1)}, bf16[3,3,3,64,64]{4,3,2,1,0:T(8,128)(2,1)}, u32[]{:S(2)}) copy-start(bf16[3,3,3,64,64]{4,3,2,1,0:T(8,128)(2,1)} %param.6) | copy-start | bytes 663556
  7.3 5.0 %copy-start.3 = (bf16[3,3,3,64,64]{4,3,2,1,0:T(8,128)(2,1)S(1)}, bf16[3,3,3,64,64]{4,3,2,1,0:T(8,128)(2,1)}, u32[]{:S(2)}) copy-start(bf16[3,3,3,64,64]{4,3,2,1,0:T(8,128)(2,1)} %param.8) | copy-start | bytes 663556
  7.3 10.8 %collective-permute-start.5 = (bf16[2,4,64,256]{3,2,1,0:T(8,128)(2,1)S(1)}, bf16[2,4,64,256]{3,2,1,0:T(8,128)(2,1)S(1)}, u32[]{:S(2)}, u32[]{:S(2)}) collective-permute-start(bf16[2,4,64,256]{3,2,1,0:T(8,128)(2,1)S(1)} %get-tuple-element.80), channel_id=1, source_target_pairs={{0,32},{32,0},{64,96},{96,64},{1,33},{33,1},{65,97},{97,65},{2,34}... | collective-permute-start | bytes 786440 | tf_op jit(solution)/shard_map/ppermute | solution.py:380
  8.7 13.3 %collective-permute-start.4 = (bf16[2,4,64,256]{3,2,1,0:T(8,128)(2,1)S(1)}, bf16[2,4,64,256]{3,2,1,0:T(8,128)(2,1)S(1)}, u32[]{:S(2)}, u32[]{:S(2)}) collective-permute-start(bf16[2,4,64,256]{3,2,1,0:T(8,128)(2,1)S(1)} %get-tuple-element.81), channel_id=1, source_target_pairs={{32,64},{64,32},{33,65},{65,33},{34,66},{66,34},{35,67},{67,35},{3... | collective-permute-start | bytes 786440 | tf_op jit(solution)/shard_map/ppermute | solution.py:381
  12.2 0.7 copy-start.4
  13.8 11.6 %collective-permute-start.2 = (bf16[2,2,64,256]{3,2,1,0:T(8,128)(2,1)S(1)}, bf16[2,2,64,256]{3,2,1,0:T(8,128)(2,1)S(1)}, u32[]{:S(2)}, u32[]{:S(2)}) collective-permute-start(bf16[2,2,64,256]{3,2,1,0:T(8,128)(2,1)S(1)} %get-tuple-element.41), channel_id=1, source_target_pairs={{32,64},{64,32},{33,65},{65,33},{34,66},{66,34},{35,67},{67,35},{3... | collective-permute-start | bytes 393224 | tf_op jit(solution)/shard_map/ppermute | solution.py:381
  18.0 7.4 %collective-permute-start.3 = (bf16[2,2,64,256]{3,2,1,0:T(8,128)(2,1)S(1)}, bf16[2,2,64,256]{3,2,1,0:T(8,128)(2,1)S(1)}, u32[]{:S(2)}, u32[]{:S(2)}) collective-permute-start(bf16[2,2,64,256]{3,2,1,0:T(8,128)(2,1)S(1)} %get-tuple-element.42), channel_id=1, source_target_pairs={{0,32},{32,0},{64,96},{96,64},{1,33},{33,1},{65,97},{97,65},{2,34}... | collective-permute-start | bytes 393224 | tf_op jit(solution)/shard_map/ppermute | solution.py:380
  49.8 27.3 %all-to-all-start.1 = ((bf16[128,16,128]{2,1,0:T(8,128)(2,1)}), bf16[128,16,128]{2,1,0:T(8,128)(2,1)S(1)}, u32[]{:S(2)}, u32[]{:S(2)}) async-start(bf16[128,16,128]{2,1,0:T(8,128)(2,1)} %shard_map.97), calls=%async_computation.1 | async-start | bytes 1048576 | tf_op jit(solution)/shard_map/all_to_all | solution.py:407
  54.0 8.7 %collective-permute-start.6 = (bf16[2,4,64,256]{3,2,1,0:T(8,128)(2,1)S(1)}, bf16[2,4,64,256]{3,2,1,0:T(8,128)(2,1)S(1)}, u32[]{:S(2)}, u32[]{:S(2)}) collective-permute-start(bf16[2,4,64,256]{3,2,1,0:T(8,128)(2,1)S(1)} %get-tuple-element.57), channel_id=1, source_target_pairs={{1,2},{2,1},{3,4},{4,3},{5,6},{6,5},{7,8},{8,7},{9,10},{10,9},{11,... | collective-permute-start | bytes 786440 | tf_op jit(solution)/shard_map/ppermute | solution.py:381
  54.7 11.8 %collective-permute-start.7 = (bf16[2,4,64,256]{3,2,1,0:T(8,128)(2,1)S(1)}, bf16[2,4,64,256]{3,2,1,0:T(8,128)(2,1)S(1)}, u32[]{:S(2)}, u32[]{:S(2)}) collective-permute-start(bf16[2,4,64,256]{3,2,1,0:T(8,128)(2,1)S(1)} %get-tuple-element.58), channel_id=1, source_target_pairs={{0,1},{1,0},{2,3},{3,2},{4,5},{5,4},{6,7},{7,6},{8,9},{9,8},{10,11... | collective-permute-start | bytes 786440 | tf_op jit(solution)/shard_map/ppermute | solution.py:380
  58.6 14.5 %collective-permute-start.10 = (bf16[2,4,64,256]{3,2,1,0:T(8,128)(2,1)S(1)}, bf16[2,4,64,256]{3,2,1,0:T(8,128)(2,1)S(1)}, u32[]{:S(2)}, u32[]{:S(2)}) collective-permute-start(bf16[2,4,64,256]{3,2,1,0:T(8,128)(2,1)S(1)} %get-tuple-element.64), channel_id=1, source_target_pairs={{32,64},{64,32},{33,65},{65,33},{34,66},{66,34},{35,67},{67,35},{3... | collective-permute-start | bytes 786440 | tf_op jit(solution)/shard_map/ppermute | solution.py:381
  62.7 10.4 %collective-permute-start.11 = (bf16[2,4,64,256]{3,2,1,0:T(8,128)(2,1)S(1)}, bf16[2,4,64,256]{3,2,1,0:T(8,128)(2,1)S(1)}, u32[]{:S(2)}, u32[]{:S(2)}) collective-permute-start(bf16[2,4,64,256]{3,2,1,0:T(8,128)(2,1)S(1)} %get-tuple-element.65), channel_id=1, source_target_pairs={{0,32},{32,0},{64,96},{96,64},{1,33},{33,1},{65,97},{97,65},{2,34}... | collective-permute-start | bytes 786440 | tf_op jit(solution)/shard_map/ppermute | solution.py:380
  66.6 8.6 %collective-permute-start.8 = (bf16[2,2,64,256]{3,2,1,0:T(8,128)(2,1)S(1)}, bf16[2,2,64,256]{3,2,1,0:T(8,128)(2,1)S(1)}, u32[]{:S(2)}, u32[]{:S(2)}) collective-permute-start(bf16[2,2,64,256]{3,2,1,0:T(8,128)(2,1)S(1)} %get-tuple-element.62), channel_id=1, source_target_pairs={{32,64},{64,32},{33,65},{65,33},{34,66},{66,34},{35,67},{67,35},{3... | collective-permute-start | bytes 393224 | tf_op jit(solution)/shard_map/ppermute | solution.py:381
  70.7 4.5 %collective-permute-start.9 = (bf16[2,2,64,256]{3,2,1,0:T(8,128)(2,1)S(1)}, bf16[2,2,64,256]{3,2,1,0:T(8,128)(2,1)S(1)}, u32[]{:S(2)}, u32[]{:S(2)}) collective-permute-start(bf16[2,2,64,256]{3,2,1,0:T(8,128)(2,1)S(1)} %get-tuple-element.63), channel_id=1, source_target_pairs={{0,32},{32,0},{64,96},{96,64},{1,33},{33,1},{65,97},{97,65},{2,34}... | collective-permute-start | bytes 393224 | tf_op jit(solution)/shard_map/ppermute | solution.py:380

commit v8 on v7

--- a/solution.py
+++ b/solution.py
@@ -38,23 +38,39 @@
     return lambda *at: jnp.where(even, slab_of(one, *at), slab_of(two, *at))
 
 
-def field(own, before, after, corner):
-    frames, rows, _, cols = own.shape
+def whole(ref):
+    return lambda f, low, high: [ref[f, low:high].reshape((-1, ref.shape[3]))]
+
+
+def parted(side, k, inner, rows_odd, rows_even):
+    count = inner.shape[1] + 2
+    first = picker(side[0] == 0, rows_odd, rows_even, False)
+    last = picker(side[0] == 0, rows_odd, rows_even, True)
+
+    def rows(f, low, high):
+        pieces = [first(k, f)] if low == 0 else []
+        pieces.append(inner[f, max(low, 1) - 1 : min(high, count - 1) - 1].reshape((-1, inner.shape[3])))
+        return pieces + [last(k, f)] if high == count else pieces
+
+    return rows
+
+
+def field(own, frames, rows, before, after, corner):
+    first = 0 if before is None else before.shape[0]
 
     def rows_of(g, low, high):
-        first = 0 if before is None else before.shape[0]
         if g < first:
-            return before[g, low:high]
+            return whole(before)(g, low, high)
         if g < first + frames:
-            return own[g - first, low:high]
-        return after[g - first - frames, low:high]
+            return own(g - first, low, high)
+        return whole(after)(g - first - frames, low, high)
 
     def taps(f, r):
         pieces = []
         for g in range(f, f + 3):
             if r == 0:
                 pieces.append(corner(g, 0))
-            pieces.append(rows_of(g, max(r - 1, 0), min(r + 2, rows)).reshape((-1, cols)))
+            pieces += rows_of(g, max(r - 1, 0), min(r + 2, rows))
             if r == rows - 1:
                 pieces.append(corner(g, 1))
         return jnp.concatenate(pieces, axis=0)
@@ -87,19 +103,16 @@
     return (hidden * sig).astype(BF16), (grad_act * sig * (1.0 + hidden * (1.0 - sig))).astype(BF16)
 
 
-def repack_kernel(side, past, future, rows_odd, rows_even, main_odd, main_even):
-    frames, rows = past.shape[0], past.shape[1]
-    row_even, frame_even = side[0] == 0, side[1] == 0
-    for f in range(frames):
-        for k, src in enumerate((past, future)):
-            low, high = src[f, 0], src[f, rows - 1]
-            rows_odd[k, f] = jnp.where(row_even, low, high)
-            rows_even[k, f] = jnp.where(row_even, high, low)
+def frames_kernel(side, active, pre, rows_odd, rows_even, main_odd, main_even):
+    frame_even = side[1] == 0
+    frames, rows = active.shape[0], active.shape[1] + 2
+    past = parted(side, 0, active, rows_odd, rows_even)
+    future = parted(side, 1, pre, rows_odd, rows_even)
     for f in range(2):
-        for r in range(rows):
-            last, first = past[f + frames - 2, r], future[f, r]
-            main_odd[f, r] = jnp.where(frame_even, first, last)
-            main_even[f, r] = jnp.where(frame_even, last, first)
+        last = jnp.concatenate(past(f + frames - 2, 0, rows), axis=0)
+        first = jnp.concatenate(future(f, 0, rows), axis=0)
+        main_odd[f] = jnp.where(frame_even, first, last).reshape(main_odd.shape[1:])
+        main_even[f] = jnp.where(frame_even, last, first).reshape(main_even.shape[1:])
 
 
 def rims_kernel(side, rows_odd, rows_even, odd, even):
@@ -141,8 +154,8 @@
     frames, rows, chan, cols = past.shape
     pick_main(side, main_odd, main_even, before, after)
     past_corner, future_corner = corners(side, frames, rows_odd, rows_even)
-    past_taps = field(past, before, None, past_corner)
-    future_taps = field(future, None, after, future_corner)
+    past_taps = field(whole(past), frames, rows, before, None, past_corner)
+    future_taps = field(whole(future), frames, rows, None, after, future_corner)
     shift = bias[...]
     total = jnp.zeros((chan, cols), F32)
     pres, acts, winp, winf = [], [], [], []
@@ -151,8 +164,8 @@
             winp.append(past_taps(f, r))
             winf.append(future_taps(f, r))
             active, pre = gated(convolved(wp, winp[-1]) + shift, convolved(wf, winf[-1]))
-            active_out[f, r] = active
-            pre_out[f, r] = pre
+            active_out[f, r - 1] = active
+            pre_out[f, r - 1] = pre
             acts.append(column_taps(active))
             pres.append(column_taps(pre))
             total = total + pre.astype(F32)
@@ -167,30 +180,30 @@
 
 
 def first_outer_kernel(side, rim_odd, rim_even, rows_in_odd, rows_in_even, past, future, before, after, hid, act,
-                       d1_in, d2_in, bsum, wp, wf, bias, active_in, pre_in,
-                       active_out, pre_out, grads, d1, d2):
-    frames, rows, chan, _ = active_out.shape
+                       d1_in, d2_in, bsum, wp, wf, bias, rows_odd, rows_even, grads, d1, d2):
+    frames, rows, chan, _ = past.shape
+    row_even = side[0] == 0
     past_corner, future_corner = corners(side, frames, rows_in_odd, rows_in_even, rim_odd, rim_even)
-    past_taps = field(past, before, None, past_corner)
-    future_taps = field(future, None, after, future_corner)
+    past_taps = field(whole(past), frames, rows, before, None, past_corner)
+    future_taps = field(whole(future), frames, rows, None, after, future_corner)
     shift = bias[...]
     total = bsum[...]
     pres, acts, winp, winf = [], [], [], []
     for f in range(frames):
+        ends = []
         for s, r in enumerate((0, rows - 1)):
             winp.append(past_taps(f, r))
             winf.append(future_taps(f, r))
             hidden = convolved(wp, winp[-1]) + shift if f < 2 else hid[f - frames + 2, s]
             grad_act = act[f, s] if f < 2 else convolved(wf, winf[-1])
             active, pre = gated(hidden, grad_act)
-            active_out[f, r] = active
-            pre_out[f, r] = pre
+            ends.append((active, pre))
             acts.append(column_taps(active))
             pres.append(column_taps(pre))
             total = total + pre.astype(F32)
-        for r in range(1, rows - 1):
-            active_out[f, r] = active_in[f, r]
-            pre_out[f, r] = pre_in[f, r]
+        for k, (first, last) in enumerate(zip(*ends)):
+            rows_odd[k, f] = jnp.where(row_even, first, last)
+            rows_even[k, f] = jnp.where(row_even, last, first)
     bias_sum = jnp.sum(total, axis=1, keepdims=True)
     lanes = lambda parts: jnp.concatenate(parts, axis=1)
     d1[...] = d1_in[...] + lax.dot_general(lanes(pres), lanes(winp), NT, preferred_element_type=F32)
@@ -213,13 +226,19 @@
         grads[used + per :] = jnp.zeros((rest,) + grads.shape[1:], grads.dtype)
 
 
-def second_inner_kernel(side, past, future, rows_odd, rows_even, main_odd, main_even, wp, wf, add_past, add_future,
-                        out_past, out_future, before, after):
-    frames, rows, _, _ = past.shape
+def second_fields(side, active, pre, sent, rows, before, after, rims=(None, None)):
+    frames, count = active.shape[0], active.shape[1] + 2
+    past_corner, future_corner = corners(side, frames, *rows, *rims)
+    past = field(parted(side, 0, active, *sent), frames, count, before, None, past_corner)
+    return past, field(parted(side, 1, pre, *sent), frames, count, None, after, future_corner)
+
+
+def second_inner_kernel(side, active, pre, sent_odd, sent_even, rows_odd, rows_even, main_odd, main_even, wp, wf,
+                        add_past, add_future, out_past, out_future, before, after):
+    frames, rows, _, _ = out_past.shape
     pick_main(side, main_odd, main_even, before, after)
-    past_corner, future_corner = corners(side, frames, rows_odd, rows_even)
-    past_taps = field(past, before, None, past_corner)
-    future_taps = field(future, None, after, future_corner)
+    past_taps, future_taps = second_fields(
+        side, active, pre, (sent_odd, sent_even), (rows_odd, rows_even), before, after)
     for f in range(frames):
         for r in range(rows):
             inner = 0 < r < rows - 1
@@ -229,12 +248,11 @@
                 out_future[f, r] = (add_future[f, r].astype(F32) + convolved(wf, future_taps(f, r))).astype(BF16)
 
 
-def second_outer_kernel(side, rim_odd, rim_even, past, future, rows_odd, rows_even, before, after, wp, wf,
-                        add_past, add_future, past_in, future_in, out_past, out_future):
+def second_outer_kernel(side, rim_odd, rim_even, active, pre, sent_odd, sent_even, rows_odd, rows_even, before, after,
+                        wp, wf, add_past, add_future, past_in, future_in, out_past, out_future):
     frames, rows, _, _ = out_past.shape
-    past_corner, future_corner = corners(side, frames, rows_odd, rows_even, rim_odd, rim_even)
-    past_taps = field(past, before, None, past_corner)
-    future_taps = field(future, None, after, future_corner)
+    past_taps, future_taps = second_fields(
+        side, active, pre, (sent_odd, sent_even), (rows_odd, rows_even), before, after, (rim_odd, rim_even))
     for f in range(2):
         for r in (0, rows - 1):
             g = frames - 2 + f
@@ -313,41 +331,39 @@
 
 
 def first_inner(past, future, rows, main, wp, wf, bias):
-    shape = past.shape
-    chan, cols = shape[2:]
-    part = (2, 2, chan, cols)
-    outs = arrays(shape, shape, frame_pair(shape), frame_pair(shape)) + arrays(
+    frames, count, chan, cols = shape = past.shape
+    part, inner = (2, 2, chan, cols), (frames, count - 2, chan, cols)
+    outs = arrays(inner, inner, frame_pair(shape), frame_pair(shape)) + arrays(
         part, part, (3 * chan, 9 * chan), (9 * chan, 3 * chan), (chan, cols), kind=F32)
     return call(first_inner_kernel, outs, (past, future, *rows, *main, wp, wf, bias), conv_flops(shape, 40))
 
 
-def first_outer(devices, past, future, rows, rims, inner, wp, wf, bias):
-    active, pre, before, after, *sums = inner
-    _, _, chan, _ = active.shape
-    outs = arrays(active.shape, pre.shape, (devices, 16, 2 * chan))
-    scratch = [pltpu.VMEM((3 * chan, 9 * chan), F32), pltpu.VMEM((9 * chan, 3 * chan), F32)]
-    args = (*rims, *rows, past, future, before, after, *sums, wp, wf, bias, active, pre)
-    return call(first_outer_kernel, outs, args, conv_flops(active.shape, 24), scratch)
-
-
-def second_inner(past, future, rows, main, wp, wf, add_past, add_future):
-    shape = past.shape
-    outs = arrays(shape, shape, frame_pair(shape), frame_pair(shape))
-    args = (past, future, *rows, *main, wp, wf, add_past, add_future)
-    return call(second_inner_kernel, outs, args, conv_flops(shape, 24))
-
-
-def second_outer(past, future, rows, rims, inner, wp, wf, add_past, add_future):
-    out_past, out_future, before, after = inner
-    args = (*rims, past, future, *rows, before, after, wp, wf, add_past, add_future, out_past, out_future)
-    return call(second_outer_kernel, arrays(out_past.shape, out_past.shape), args, conv_flops(out_past.shape, 8))
-
-
-def repack(past, future):
+def first_outer(devices, past, future, rows, rims, partial, wp, wf, bias):
     frames, _, chan, cols = past.shape
     ends = (2, frames, chan, cols)
-    outs = arrays(ends, ends, frame_pair(past.shape), frame_pair(past.shape))
-    return call(repack_kernel, outs, (past, future), 0)
+    outs = arrays(ends, ends, (devices, 16, 2 * chan))
+    scratch = [pltpu.VMEM((3 * chan, 9 * chan), F32), pltpu.VMEM((9 * chan, 3 * chan), F32)]
+    args = (*rims, *rows, past, future, *partial, wp, wf, bias)
+    return call(first_outer_kernel, outs, args, conv_flops(past.shape, 24), scratch)
+
+
+def second_inner(active, pre, sent, rows, main, wp, wf, add_past, add_future):
+    shape = add_past.shape
+    outs = arrays(shape, shape, frame_pair(shape), frame_pair(shape))
+    args = (active, pre, *sent, *rows, *main, wp, wf, add_past, add_future)
+    return call(second_inner_kernel, outs, args, conv_flops(shape, 24))
+
+
+def second_outer(active, pre, sent, rows, rims, inner, wp, wf, add_past, add_future):
+    out_past, out_future, before, after = inner
+    args = (*rims, active, pre, *sent, *rows, before, after, wp, wf, add_past, add_future, out_past, out_future)
+    return call(second_outer_kernel, arrays(out_past.shape, out_past.shape), args, conv_flops(out_past.shape, 8))
+
+
+def frames_to_send(active, pre, rows_odd, rows_even):
+    _, inner, chan, cols = active.shape
+    pair = (2, inner + 2, chan, cols)
+    return call(frames_kernel, arrays(pair, pair), (active, pre, rows_odd, rows_even), 0)
 
 
 def rims_to_send(rows_odd, rows_even):
@@ -397,23 +413,20 @@
     main = swap("frames", jnp.where(frame_even, future, past), jnp.where(frame_even, past, future))
     one_fwd, one_adj, two_fwd, two_adj, bias = flat_weights(kernel_one, kernel_two, bias_one)
     rims = swap("frames", *rims_to_send(*rows))
-    inner = first_inner(clip_in, cotangent, rows, main, one_fwd, two_adj, bias)
-    active, grad_pre, terms = first_outer(
-        devices, clip_in, cotangent, rows, rims, inner, one_fwd, two_adj, bias
-    )
+    active, grad_pre, *partial = first_inner(clip_in, cotangent, rows, main, one_fwd, two_adj, bias)
+    *sent, terms = first_outer(devices, clip_in, cotangent, rows, rims, partial, one_fwd, two_adj, bias)
 
     terms = lax.all_to_all(terms, AXES, 0, 0, tiled=True)
     spread = summed(terms, 1.0 / math.sqrt(cell_total))
     total = lax.all_to_all(spread, AXES, 0, 0, tiled=True)
 
-    rows_odd, rows_even, main_odd, main_even = repack(active, grad_pre)
-    rows = swap("rows", rows_odd, rows_even)
-    main = swap("frames", main_odd, main_even)
+    rows = swap("rows", *sent)
+    main = swap("frames", *frames_to_send(active, grad_pre, *sent))
     *rows, _ = lax.optimization_barrier((*rows, spread))
     rims = swap("frames", *rims_to_send(*rows))
-    inner = second_inner(active, grad_pre, rows, main, two_fwd, one_adj, clip_in, cotangent)
+    inner = second_inner(active, grad_pre, sent, rows, main, two_fwd, one_adj, clip_in, cotangent)
     block_out, grad_input = second_outer(
-        active, grad_pre, rows, rims, inner, two_fwd, one_adj, clip_in, cotangent
+        active, grad_pre, sent, rows, rims, inner, two_fwd, one_adj, clip_in, cotangent
     )
     first, second, bias = unpacked(total, channels)
     return (

time: 79.4 us -> 79.4 us (level)
  no operation moved by 1% of the time
where the time goes in v8:
time: 79.4 us; the launch traced here: 78.4 us
  starting transfers between devices  31.1 us (39%)
  blocking collectives  20.9 us (26%)
  Pallas kernels  13.3 us (17%)
  waiting for transfers between devices  9.73 us (12%)
  other arithmetic  1.28 us (2%)
  local copies, waits for them, and re-layouts  1.27 us (2%)
  between operations  0.92 us (1%)
    all_to_all x1, blocking collectives, per_device(): terms = lax.all_to_all(terms, AXES, 0, 0, tiled=True)  20.9 us
    ppermute x6, starting transfers between devices, swap(): return (lax.ppermute(odd, axis, pairs_of(count, 1)), even)  16.8 us
    pallas_call x10, Pallas kernels, call(): pl.pallas_call(body, out_shape=outs, in_specs=[vmem] * len(args), out_spe...  13.3 us
    ppermute x6, starting transfers between devices, swap(): even = lax.ppermute(even, axis, pairs_of(count, 0))  10.1 us
    ppermute x6, waiting for transfers between devices, swap(): return (lax.ppermute(odd, axis, pairs_of(count, 1)), even)  5.94 us
    all_to_all x1, starting transfers between devices, per_device(): total = lax.all_to_all(spread, AXES, 0, 0, tiled=True)  4.14 us
    ppermute x6, waiting for transfers between devices, swap(): even = lax.ppermute(even, axis, pairs_of(count, 0))  3.79 us
  transfers between devices with their start and end apart: 13, of which 3 were waited for; matrix products, arithmetic and copies ran while one was open for 0% of the time, Pallas kernels for 11%

profile of v8, /device:TPU:1, one launch (start us, length us, event | category | flops | bytes accessed | tf_op | source)
XLA Modules:
  0.0 78.4 jit_solution(10522435253019666185)
XLA Ops:
  0.7 1.2 %broadcast_select_fusion.2 = (bf16[2,4,1,64,256]{4,3,2,1,0:T(8,128)(2,1)S(1)}, bf16[2,4,1,64,256]{4,3,2,1,0:T(8,128)(2,1)S(1)}, bf16[2,4,1,64,256]{4,3,2,1,0:T(8,128)(2,1)S(1)}) fusion(pred[]{:T(512)S(6)} %eq.9, bf16[1,4,4,64,256]{4,3,2,1,0:T(8,128)(2,1)} %bitcast.8, bf16[1,4,4,64,256]{4,3,2,1,0:T(8,128)(2,1)} %bitcast.9), kind=kLoop, calls=%fused_computation.4 | loop fusion | flops 393216 | bytes 1835009 | tf_op jit(solution)/shard_map/jit(_where)/select_n | solution.py:410
  1.9 0.8 %collective-permute-start = (bf16[2,4,1,64,256]{4,3,2,1,0:T(8,128)(2,1)S(1)}, bf16[2,4,1,64,256]{4,3,2,1,0:T(8,128)(2,1)S(1)}, u32[]{:S(2)}, u32[]{:S(2)}) collective-permute-start(bf16[2,4,1,64,256]{4,3,2,1,0:T(8,128)(2,1)S(1)} %broadcast_select_fusion.3), channel_id=1, source_target_pairs={{1,2},{2,1},{3,4},{4,3},{5,6},{6,5},{7,8},{8,7},{9,10},{10,9},{11,... | collective-permute-start | bytes 786440 | tf_op jit(solution)/shard_map/ppermute | solution.py:397
  2.7 4.6 %collective-permute-start.1 = (bf16[2,4,1,64,256]{4,3,2,1,0:T(8,128)(2,1)S(1)}, bf16[2,4,1,64,256]{4,3,2,1,0:T(8,128)(2,1)S(1)}, u32[]{:S(2)}, u32[]{:S(2)}) collective-permute-start(bf16[2,4,1,64,256]{4,3,2,1,0:T(8,128)(2,1)S(1)} %get-tuple-element.73), channel_id=1, source_target_pairs={{0,1},{1,0},{2,3},{3,2},{4,5},{5,4},{6,7},{7,6},{8,9},{9,8},{10,11... | collective-permute-start | bytes 786440 | tf_op jit(solution)/shard_map/ppermute | solution.py:396
  7.3 1.3 %collective-permute-start.5 = (bf16[2,4,64,256]{3,2,1,0:T(8,128)(2,1)S(1)}, bf16[2,4,64,256]{3,2,1,0:T(8,128)(2,1)S(1)}, u32[]{:S(2)}, u32[]{:S(2)}) collective-permute-start(bf16[2,4,64,256]{3,2,1,0:T(8,128)(2,1)S(1)} %get-tuple-element.76), channel_id=1, source_target_pairs={{0,32},{32,0},{64,96},{96,64},{1,33},{33,1},{65,97},{97,65},{2,34}... | collective-permute-start | bytes 786440 | tf_op jit(solution)/shard_map/ppermute | solution.py:396
  8.7 3.6 %collective-permute-start.4 = (bf16[2,4,64,256]{3,2,1,0:T(8,128)(2,1)S(1)}, bf16[2,4,64,256]{3,2,1,0:T(8,128)(2,1)S(1)}, u32[]{:S(2)}, u32[]{:S(2)}) collective-permute-start(bf16[2,4,64,256]{3,2,1,0:T(8,128)(2,1)S(1)} %get-tuple-element.77), channel_id=1, source_target_pairs={{32,64},{64,32},{33,65},{65,33},{34,66},{66,34},{35,67},{67,35},{3... | collective-permute-start | bytes 786440 | tf_op jit(solution)/shard_map/ppermute | solution.py:397
  12.3 0.6 copy-done.6
  12.9 0.9 %shard_map.93 = (bf16[192,576]{1,0:T(8,128)(2,1)S(1)}, bf16[192,576]{1,0:T(8,128)(2,1)S(1)}, bf16[192,576]{1,0:T(8,128)(2,1)S(1)}, bf16[192,576]{1,0:T(8,128)(2,1)S(1)}, f32[64,1]{1,0:T(8,128)S(1)}) custom-call(bf16[27,64,64]{2,1,0:T(8,128)(2,1)S(1)} %bitcast.10, bf16[27,64,64]{2,1,0:T(8,128)(2,1)S(1)} %bitcast.11, f32[1,64]{1,0:T(1,128)S(1)} %bitcast.12), custom_call_target="tpu_custom_call" | custom-call | bytes 1327616 | tf_op jit(solution)/shard_map/pallas_call | solution.py:300
  13.9 0.6 copy-done.4
  14.5 3.6 %collective-permute-start.2 = (bf16[2,2,64,256]{3,2,1,0:T(8,128)(2,1)S(1)}, bf16[2,2,64,256]{3,2,1,0:T(8,128)(2,1)S(1)}, u32[]{:S(2)}, u32[]{:S(2)}) collective-permute-start(bf16[2,2,64,256]{3,2,1,0:T(8,128)(2,1)S(1)} %get-tuple-element.39), channel_id=1, source_target_pairs={{32,64},{64,32},{33,65},{65,33},{34,66},{66,34},{35,67},{67,35},{3... | collective-permute-start | bytes 393224 | tf_op jit(solution)/shard_map/ppermute | solution.py:397
  18.1 3.8 %collective-permute-done.4.refs_4_ = bf16[2,4,64,256]{3,2,1,0:T(8,128)(2,1)S(1)} collective-permute-done((bf16[2,4,64,256]{3,2,1,0:T(8,128)(2,1)S(1)}, bf16[2,4,64,256]{3,2,1,0:T(8,128)(2,1)S(1)}, u32[]{:S(2)}, u32[]{:S(2)}) %collective-permute-start.4) | collective-permute-done | bytes 262176 | tf_op jit(solution)/shard_map/ppermute | solution.py:397
  22.0 3.6 %shard_map.94 = (bf16[4,2,64,256]{3,2,1,0:T(8,128)(2,1)S(1)}, bf16[4,2,64,256]{3,2,1,0:T(8,128)(2,1)S(1)}, bf16[2,4,64,256]{3,2,1,0:T(8,128)(2,1)S(1)}, bf16[2,4...) custom-call(bf16[4,4,64,256]{3,2,1,0:T(8,128)(2,1)S(1)} %copy-done.1, ...), custom_call_target="tpu_custom_call" | custom-call | flops 2264924160 | bytes 5062912 | tf_op jit(solution)/shard_map/pallas_call | solution.py:300
  25.6 2.5 %shard_map.95 = (bf16[2,4,64,256]{3,2,1,0:T(8,128)(2,1)S(1)}, bf16[2,4,64,256]{3,2,1,0:T(8,128)(2,1)S(1)}, bf16[128,16,128]{2,1,0:T(8,128)(2,1)S(1)}) custom-call(bf16[2,2,64,256]{3,2,1,0:T(8,128)(2,1)S(1)} %collective-permute-done.2.refs_0_, bf16[2,2,64,256]{3,2,1,0:T(8,128)(2,1)S(1)} %collective-permute-done.3.refs_1_, ...), custom_call_target="tpu_custom_call" | custom-call | flops 1358954496 | bytes 5325056 | tf_op jit(solution)/shard_map/pallas_call | solution.py:300
  28.0 20.9 %all_to_all.10.parts = bf16[128,16,128]{2,1,0:T(8,128)(2,1)S(1)} all-to-all(bf16[128,16,128]{2,1,0:T(8,128)(2,1)S(1)} %get-tuple-element.53), channel_id=1, replica_groups=mesh['frames'=4,'rows'=32] {'frames','rows'}, dimensions={0} | all-to-all | bytes 1048576 | tf_op jit(solution)/shard_map/all_to_all | solution.py:419
  48.9 0.9 %shard_map.96 = bf16[128,16,128]{2,1,0:T(8,128)(2,1)} custom-call(bf16[128,16,128]{2,1,0:T(8,128)(2,1)S(1)} %all_to_all.10.parts), custom_call_target="tpu_custom_call" | custom-call | bytes 1048576 | tf_op jit(solution)/shard_map/pallas_call | solution.py:300
  49.8 4.1 %all-to-all-start.1 = ((bf16[128,16,128]{2,1,0:T(8,128)(2,1)}), bf16[128,16,128]{2,1,0:T(8,128)(2,1)S(1)}, u32[]{:S(2)}, u32[]{:S(2)}) async-start(bf16[128,16,128]{2,1,0:T(8,128)(2,1)} %shard_map.96), calls=%async_computation.1 | async-start | bytes 1048576 | tf_op jit(solution)/shard_map/all_to_all | solution.py:421
  54.0 0.7 collective-permute-start.6
  54.7 3.8 %collective-permute-start.7 = (bf16[2,4,64,256]{3,2,1,0:T(8,128)(2,1)S(1)}, bf16[2,4,64,256]{3,2,1,0:T(8,128)(2,1)S(1)}, u32[]{:S(2)}, u32[]{:S(2)}) collective-permute-start(bf16[2,4,64,256]{3,2,1,0:T(8,128)(2,1)S(1)} %get-tuple-element.52.refs_3_.refs_5_), channel_id=1, source_target_pairs={{0,1},{1,0},{2,3},{3,2},{4,5},{5,4},{6,7},{7,6},{8,9},{9,8},{10,11... | collective-permute-start | bytes 786440 | tf_op jit(solution)/shard_map/ppermute | solution.py:396
  58.6 4.1 %collective-permute-start.10 = (bf16[2,4,64,256]{3,2,1,0:T(8,128)(2,1)S(1)}, bf16[2,4,64,256]{3,2,1,0:T(8,128)(2,1)S(1)}, u32[]{:S(2)}, u32[]{:S(2)}) collective-permute-start(bf16[2,4,64,256]{3,2,1,0:T(8,128)(2,1)S(1)} %get-tuple-element.60), channel_id=1, source_target_pairs={{32,64},{64,32},{33,65},{65,33},{34,66},{66,34},{35,67},{67,35},{3... | collective-permute-start | bytes 786440 | tf_op jit(solution)/shard_map/ppermute | solution.py:397
  62.8 3.8 %collective-permute-done.7.refs_1_.refs_5_.refs_7_ = bf16[2,4,64,256]{3,2,1,0:T(8,128)(2,1)S(1)} collective-permute-done((bf16[2,4,64,256]{3,2,1,0:T(8,128)(2,1)S(1)}, bf16[2,4,64,256]{3,2,1,0:T(8,128)(2,1)S(1)}, u32[]{:S(2)}, u32[]{:S(2)}) %collective-permute-start.7) | collective-permute-done | bytes 262176 | tf_op jit(solution)/shard_map/ppermute | solution.py:396
  66.6 4.1 %collective-permute-start.8 = (bf16[2,2,64,256]{3,2,1,0:T(8,128)(2,1)S(1)}, bf16[2,2,64,256]{3,2,1,0:T(8,128)(2,1)S(1)}, u32[]{:S(2)}, u32[]{:S(2)}) collective-permute-start(bf16[2,2,64,256]{3,2,1,0:T(8,128)(2,1)S(1)} %get-tuple-element.56), channel_id=1, source_target_pairs={{32,64},{64,32},{33,65},{65,33},{34,66},{66,34},{35,67},{67,35},{3... | collective-permute-start | bytes 393224 | tf_op jit(solution)/shard_map/ppermute | solution.py:397
  71.0 2.1 %collective-permute-done.10.refs_6_ = bf16[2,4,64,256]{3,2,1,0:T(8,128)(2,1)S(1)} collective-permute-done((bf16[2,4,64,256]{3,2,1,0:T(8,128)(2,1)S(1)}, bf16[2,4,64,256]{3,2,1,0:T(8,128)(2,1)S(1)}, u32[]{:S(2)}, u32[]{:S(2)}) %collective-permute-start.10) | collective-permute-done | bytes 262176 | tf_op jit(solution)/shard_map/ppermute | solution.py:397
  73.1 2.1 %shard_map.99 = (bf16[4,4,64,256]{3,2,1,0:T(8,128)(2,1)S(1)}, bf16[4,4,64,256]{3,2,1,0:T(8,128)(2,1)S(1)}, bf16[2,4,64,256]{3,2,1,0:T(8,128)(2,1)S(1)}, bf16[2,4,64,256]{3,2,1,0:T(8,128)(2,1)S(1)}) custom-call(bf16[4,2,64,256]{3,2,1,0:T(8,128)(2,1)S(1)} %get-tuple-element.58.refs_0_.refs_2_, bf16[4,2,64,256]{3,2,1,0:T(8,128)(2,1)S(1)} %get-tuple-element.59.refs_1_.refs_3_, ...), custom_call_target="tpu_custom_call" | custom-call | flops 1358954496 | bytes 5160960 | tf_op jit(solution)/shard_map/pallas_call | solution.py:300
  75.2 1.9 %shard_map.100 = (bf16[4,4,64,256]{3,2,1,0:T(8,128)(2,1)}, bf16[4,4,64,256]{3,2,1,0:T(8,128)(2,1)}) custom-call(bf16[2,2,64,256]{3,2,1,0:T(8,128)(2,1)S(1)} %collective-permute-done.8.refs_0_, bf16[2,2,64,256]{3,2,1,0:T(8,128)(2,1)S(1)} %collective-permute-done.9.refs_1_, bf16[4,2,64,256]{3,2,1,0:T(8,128)(2,1)S(1)} %get-tuple-element.58.refs_0_.refs_2_, ...), custom_call_target="tpu_custom_call" | custom-call | flops 452984832 | bytes 5947392 | tf_op jit(solution)/shard_map/pallas_call | solution.py:300
  77.1 1.3 %shard_map.101 = (f32[27,64,64]{2,1,0:T(8,128)}, f32[27,64,64]{2,1,0:T(8,128)}, f32[1,64]{1,0:T(1,128)}) custom-call(bf16[128,16,128]{2,1,0:T(8,128)(2,1)S(1)} %all-to-all-done.1.parts), custom_call_target="tpu_custom_call" | custom-call | bytes 1409280 | tf_op jit(solution)/shard_map/pallas_call | solution.py:300
  (30 shorter events, 0.7 us)
Async XLA Ops:
  0.6 6.6 %copy-start.1 = (bf16[4,4,64,256]{3,2,1,0:T(8,128)(2,1)S(1)}, bf16[4,4,64,256]{3,2,1,0:T(8,128)(2,1)}, u32[]{:S(2)}) copy-start(bf16[4,4,64,256]{3,2,1,0:T(8,128)(2,1)} %refs_12_.1) | copy-start | bytes 1572868
  1.9 5.4 %copy-start = (bf16[4,4,64,256]{3,2,1,0:T(8,128)(2,1)S(1)}, bf16[4,4,64,256]{3,2,1,0:T(8,128)(2,1)}, u32[]{:S(2)}) copy-start(bf16[4,4,64,256]{3,2,1,0:T(8,128)(2,1)} %refs_13_.1) | copy-start | bytes 1572868
  1.9 11.9 %collective-permute-start = (bf16[2,4,1,64,256]{4,3,2,1,0:T(8,128)(2,1)S(1)}, bf16[2,4,1,64,256]{4,3,2,1,0:T(8,128)(2,1)S(1)}, u32[]{:S(2)}, u32[]{:S(2)}) collective-permute-start(bf16[2,4,1,64,256]{4,3,2,1,0:T(8,128)(2,1)S(1)} %broadcast_select_fusion.3), channel_id=1, source_target_pairs={{1,2},{2,1},{3,4},{4,3},{5,6},{6,5},{7,8},{8,7},{9,10},{10,9},{11,... | collective-permute-start | bytes 786440 | tf_op jit(solution)/shard_map/ppermute | solution.py:397
  2.7 11.1 %collective-permute-start.1 = (bf16[2,4,1,64,256]{4,3,2,1,0:T(8,128)(2,1)S(1)}, bf16[2,4,1,64,256]{4,3,2,1,0:T(8,128)(2,1)S(1)}, u32[]{:S(2)}, u32[]{:S(2)}) collective-permute-start(bf16[2,4,1,64,256]{4,3,2,1,0:T(8,128)(2,1)S(1)} %get-tuple-element.73), channel_id=1, source_target_pairs={{0,1},{1,0},{2,3},{3,2},{4,5},{5,4},{6,7},{7,6},{8,9},{9,8},{10,11... | collective-permute-start | bytes 786440 | tf_op jit(solution)/shard_map/ppermute | solution.py:396
  7.3 5.0 %copy-start.2 = (bf16[3,3,3,64,64]{4,3,2,1,0:T(8,128)(2,1)S(1)}, bf16[3,3,3,64,64]{4,3,2,1,0:T(8,128)(2,1)}, u32[]{:S(2)}) copy-start(bf16[3,3,3,64,64]{4,3,2,1,0:T(8,128)(2,1)} %param.6) | copy-start | bytes 663556
  7.3 5.0 %copy-start.3 = (bf16[3,3,3,64,64]{4,3,2,1,0:T(8,128)(2,1)S(1)}, bf16[3,3,3,64,64]{4,3,2,1,0:T(8,128)(2,1)}, u32[]{:S(2)}) copy-start(bf16[3,3,3,64,64]{4,3,2,1,0:T(8,128)(2,1)} %param.8) | copy-start | bytes 663556
  7.3 10.8 %collective-permute-start.5 = (bf16[2,4,64,256]{3,2,1,0:T(8,128)(2,1)S(1)}, bf16[2,4,64,256]{3,2,1,0:T(8,128)(2,1)S(1)}, u32[]{:S(2)}, u32[]{:S(2)}) collective-permute-start(bf16[2,4,64,256]{3,2,1,0:T(8,128)(2,1)S(1)} %get-tuple-element.76), channel_id=1, source_target_pairs={{0,32},{32,0},{64,96},{96,64},{1,33},{33,1},{65,97},{97,65},{2,34}... | collective-permute-start | bytes 786440 | tf_op jit(solution)/shard_map/ppermute | solution.py:396
  8.7 13.3 %collective-permute-start.4 = (bf16[2,4,64,256]{3,2,1,0:T(8,128)(2,1)S(1)}, bf16[2,4,64,256]{3,2,1,0:T(8,128)(2,1)S(1)}, u32[]{:S(2)}, u32[]{:S(2)}) collective-permute-start(bf16[2,4,64,256]{3,2,1,0:T(8,128)(2,1)S(1)} %get-tuple-element.77), channel_id=1, source_target_pairs={{32,64},{64,32},{33,65},{65,33},{34,66},{66,34},{35,67},{67,35},{3... | collective-permute-start | bytes 786440 | tf_op jit(solution)/shard_map/ppermute | solution.py:397
  12.2 0.7 copy-start.6
  13.8 0.7 copy-start.4
  14.5 11.1 %collective-permute-start.2 = (bf16[2,2,64,256]{3,2,1,0:T(8,128)(2,1)S(1)}, bf16[2,2,64,256]{3,2,1,0:T(8,128)(2,1)S(1)}, u32[]{:S(2)}, u32[]{:S(2)}) collective-permute-start(bf16[2,2,64,256]{3,2,1,0:T(8,128)(2,1)S(1)} %get-tuple-element.39), channel_id=1, source_target_pairs={{32,64},{64,32},{33,65},{65,33},{34,66},{66,34},{35,67},{67,35},{3... | collective-permute-start | bytes 393224 | tf_op jit(solution)/shard_map/ppermute | solution.py:397
  18.0 7.5 %collective-permute-start.3 = (bf16[2,2,64,256]{3,2,1,0:T(8,128)(2,1)S(1)}, bf16[2,2,64,256]{3,2,1,0:T(8,128)(2,1)S(1)}, u32[]{:S(2)}, u32[]{:S(2)}) collective-permute-start(bf16[2,2,64,256]{3,2,1,0:T(8,128)(2,1)S(1)} %get-tuple-element.40), channel_id=1, source_target_pairs={{0,32},{32,0},{64,96},{96,64},{1,33},{33,1},{65,97},{97,65},{2,34}... | collective-permute-start | bytes 393224 | tf_op jit(solution)/shard_map/ppermute | solution.py:396
  49.8 27.3 %all-to-all-start.1 = ((bf16[128,16,128]{2,1,0:T(8,128)(2,1)}), bf16[128,16,128]{2,1,0:T(8,128)(2,1)S(1)}, u32[]{:S(2)}, u32[]{:S(2)}) async-start(bf16[128,16,128]{2,1,0:T(8,128)(2,1)} %shard_map.96), calls=%async_computation.1 | async-start | bytes 1048576 | tf_op jit(solution)/shard_map/all_to_all | solution.py:421
  54.0 8.8 %collective-permute-start.6 = (bf16[2,4,64,256]{3,2,1,0:T(8,128)(2,1)S(1)}, bf16[2,4,64,256]{3,2,1,0:T(8,128)(2,1)S(1)}, u32[]{:S(2)}, u32[]{:S(2)}) collective-permute-start(bf16[2,4,64,256]{3,2,1,0:T(8,128)(2,1)S(1)} %get-tuple-element.51.refs_2_.refs_4_), channel_id=1, source_target_pairs={{1,2},{2,1},{3,4},{4,3},{5,6},{6,5},{7,8},{8,7},{9,10},{10,9},{11,... | collective-permute-start | bytes 786440 | tf_op jit(solution)/shard_map/ppermute | solution.py:397
  54.7 11.9 %collective-permute-start.7 = (bf16[2,4,64,256]{3,2,1,0:T(8,128)(2,1)S(1)}, bf16[2,4,64,256]{3,2,1,0:T(8,128)(2,1)S(1)}, u32[]{:S(2)}, u32[]{:S(2)}) collective-permute-start(bf16[2,4,64,256]{3,2,1,0:T(8,128)(2,1)S(1)} %get-tuple-element.52.refs_3_.refs_5_), channel_id=1, source_target_pairs={{0,1},{1,0},{2,3},{3,2},{4,5},{5,4},{6,7},{7,6},{8,9},{9,8},{10,11... | collective-permute-start | bytes 786440 | tf_op jit(solution)/shard_map/ppermute | solution.py:396
  58.6 14.5 %collective-permute-start.10 = (bf16[2,4,64,256]{3,2,1,0:T(8,128)(2,1)S(1)}, bf16[2,4,64,256]{3,2,1,0:T(8,128)(2,1)S(1)}, u32[]{:S(2)}, u32[]{:S(2)}) collective-permute-start(bf16[2,4,64,256]{3,2,1,0:T(8,128)(2,1)S(1)} %get-tuple-element.60), channel_id=1, source_target_pairs={{32,64},{64,32},{33,65},{65,33},{34,66},{66,34},{35,67},{67,35},{3... | collective-permute-start | bytes 786440 | tf_op jit(solution)/shard_map/ppermute | solution.py:397
  62.7 10.4 %copy-start.5 = (bf16[192,576]{1,0:T(8,128)(2,1)S(1)}, bf16[192,576]{1,0:T(8,128)(2,1)}, u32[]{:S(2)}) copy-start(bf16[192,576]{1,0:T(8,128)(2,1)} %copy-done.4) | copy-start | bytes 663556
  62.7 10.4 %collective-permute-start.11 = (bf16[2,4,64,256]{3,2,1,0:T(8,128)(2,1)S(1)}, bf16[2,4,64,256]{3,2,1,0:T(8,128)(2,1)S(1)}, u32[]{:S(2)}, u32[]{:S(2)}) collective-permute-start(bf16[2,4,64,256]{3,2,1,0:T(8,128)(2,1)S(1)} %get-tuple-element.61), channel_id=1, source_target_pairs={{0,32},{32,0},{64,96},{96,64},{1,33},{33,1},{65,97},{97,65},{2,34}... | collective-permute-start | bytes 786440 | tf_op jit(solution)/shard_map/ppermute | solution.py:396
  66.6 8.6 %collective-permute-start.8 = (bf16[2,2,64,256]{3,2,1,0:T(8,128)(2,1)S(1)}, bf16[2,2,64,256]{3,2,1,0:T(8,128)(2,1)S(1)}, u32[]{:S(2)}, u32[]{:S(2)}) collective-permute-start(bf16[2,2,64,256]{3,2,1,0:T(8,128)(2,1)S(1)} %get-tuple-element.56), channel_id=1, source_target_pairs={{32,64},{64,32},{33,65},{65,33},{34,66},{66,34},{35,67},{67,35},{3... | collective-permute-start | bytes 393224 | tf_op jit(solution)/shard_map/ppermute | solution.py:397
  70.7 4.5 %collective-permute-start.9 = (bf16[2,2,64,256]{3,2,1,0:T(8,128)(2,1)S(1)}, bf16[2,2,64,256]{3,2,1,0:T(8,128)(2,1)S(1)}, u32[]{:S(2)}, u32[]{:S(2)}) collective-permute-start(bf16[2,2,64,256]{3,2,1,0:T(8,128)(2,1)S(1)} %get-tuple-element.57), channel_id=1, source_target_pairs={{0,32},{32,0},{64,96},{96,64},{1,33},{33,1},{65,97},{97,65},{2,34}... | collective-permute-start | bytes 393224 | tf_op jit(solution)/shard_map/ppermute | solution.py:396

commit v9 on v8

--- a/solution.py
+++ b/solution.py
@@ -149,7 +149,17 @@
     return jnp.sum(jnp.where(keep, spread, 0.0), axis=1, keepdims=True)
 
 
-def first_inner_kernel(side, past, future, rows_odd, rows_even, main_odd, main_even, wp, wf, bias,
+def first_local_kernel(past, future, wp, wf, bias, hid, act):
+    frames, rows, _, _ = past.shape
+    past_taps = field(whole(past), frames, rows, None, None, None)
+    future_taps = field(whole(future), frames, rows, None, None, None)
+    for k in range(2):
+        for r in range(1, rows - 1):
+            hid[k, r - 1] = convolved(wp, past_taps(k + frames - 4, r)) + bias[...]
+            act[k, r - 1] = convolved(wf, future_taps(k, r))
+
+
+def first_inner_kernel(side, past, future, rows_odd, rows_even, main_odd, main_even, local_hid, local_act, wp, wf, bias,
                        active_out, pre_out, before, after, hid, act, d1, d2, bsum):
     frames, rows, chan, cols = past.shape
     pick_main(side, main_odd, main_even, before, after)
@@ -163,7 +173,9 @@
         for r in range(1, rows - 1):
             winp.append(past_taps(f, r))
             winf.append(future_taps(f, r))
-            active, pre = gated(convolved(wp, winp[-1]) + shift, convolved(wf, winf[-1]))
+            hidden = convolved(wp, winp[-1]) + shift if f < 2 else local_hid[f - frames + 2, r - 1]
+            grad_act = local_act[f, r - 1] if f < 2 else convolved(wf, winf[-1])
+            active, pre = gated(hidden, grad_act)
             active_out[f, r - 1] = active
             pre_out[f, r - 1] = pre
             acts.append(column_taps(active))
@@ -277,23 +289,32 @@
     out[...] = jnp.broadcast_to((sums[0] * scale).astype(out.dtype)[None], out.shape)
 
 
-def unpack_kernel(parts, one, two, bias):
+def unpack_kernel(parts, one_out, two_out, bias, one, two, sems):
     taps, chan = one.shape[0], one.shape[1]
     per = chan // parts.shape[1]
-    for k in range(taps):
-        both = parts[k * per : (k + 1) * per].astype(F32).reshape((chan, 2 * chan))
-        one[k] = both[:, :chan]
-        two[k] = both[:, chan:]
+    third = taps // 3
+    copies = []
+    for t in range(3):
+        group = pl.ds(t * third, third)
+        for k in range(t * third, (t + 1) * third):
+            both = parts[k * per : (k + 1) * per].astype(F32).reshape((chan, 2 * chan))
+            one[k] = both[:, :chan]
+            two[k] = both[:, chan:]
+        for s, (src, dst) in enumerate(((one, one_out), (two, two_out))):
+            copies.append(pltpu.make_async_copy(src.at[group], dst.at[group], sems.at[t, s]))
+            copies[-1].start()
     column = parts[taps * per : (taps + 1) * per].astype(F32).reshape((chan, 2 * chan))[:, :chan]
     keep = lax.broadcasted_iota(jnp.int32, column.shape, 0) == lax.broadcasted_iota(jnp.int32, column.shape, 1)
     bias[...] = jnp.sum(jnp.where(keep, column, 0.0), axis=0, keepdims=True)
+    for copy in copies:
+        copy.wait()
 
 
 def sides():
     return lax.axis_index("rows") % 2, lax.axis_index("frames") % 2
 
 
-def call(kernel, outs, args, flops, scratch=(), sided=True):
+def call(kernel, outs, args, flops, scratch=(), sided=True, copied=0):
     vmem = pl.BlockSpec(memory_space=pltpu.VMEM)
     moved = sum(x.size * x.dtype.itemsize for x in list(args) + list(outs))
     body = (lambda *refs: kernel(sides(), *refs)) if sided else kernel
@@ -301,7 +322,7 @@
         body,
         out_shape=outs,
         in_specs=[vmem] * len(args),
-        out_specs=[vmem] * len(outs),
+        out_specs=[pl.BlockSpec(memory_space=pl.ANY)] * copied + [vmem] * (len(outs) - copied),
         scratch_shapes=scratch,
         compiler_params=pltpu.CompilerParams(vmem_limit_bytes=VMEM_LIMIT),
         cost_estimate=pl.CostEstimate(flops=flops, bytes_accessed=moved, transcendentals=0),
@@ -330,12 +351,19 @@
     return (2,) + shape[1:]
 
 
-def first_inner(past, future, rows, main, wp, wf, bias):
+def first_local(past, future, wp, wf, bias):
+    _, count, chan, cols = past.shape
+    part = (2, count - 2, chan, cols)
+    args = (past, future, wp, wf, bias)
+    return call(first_local_kernel, arrays(part, part, kind=F32), args, conv_flops(past.shape, 8), sided=False)
+
+
+def first_inner(past, future, rows, main, local, wp, wf, bias):
     frames, count, chan, cols = shape = past.shape
     part, inner = (2, 2, chan, cols), (frames, count - 2, chan, cols)
     outs = arrays(inner, inner, frame_pair(shape), frame_pair(shape)) + arrays(
         part, part, (3 * chan, 9 * chan), (9 * chan, 3 * chan), (chan, cols), kind=F32)
-    return call(first_inner_kernel, outs, (past, future, *rows, *main, wp, wf, bias), conv_flops(shape, 40))
+    return call(first_inner_kernel, outs, (past, future, *rows, *main, *local, wp, wf, bias), conv_flops(shape, 32))
 
 
 def first_outer(devices, past, future, rows, rims, partial, wp, wf, bias):
@@ -378,7 +406,8 @@
 
 def unpacked(parts, chan):
     outs = arrays((27, chan, chan), (27, chan, chan), (1, chan), kind=F32)
-    return call(unpack_kernel, outs, (parts,), 0, sided=False)
+    scratch = [pltpu.VMEM((27, chan, chan), F32)] * 2 + [pltpu.SemaphoreType.DMA((3, 2))]
+    return call(unpack_kernel, outs, (parts,), 0, scratch, sided=False, copied=2)
 
 
 AXES = ("frames", "rows")
@@ -412,8 +441,10 @@
     past, future = clip_in[-2:], cotangent[:2]
     main = swap("frames", jnp.where(frame_even, future, past), jnp.where(frame_even, past, future))
     one_fwd, one_adj, two_fwd, two_adj, bias = flat_weights(kernel_one, kernel_two, bias_one)
+    local = first_local(clip_in, cotangent, one_fwd, two_adj, bias)
+    *rows, _ = lax.optimization_barrier((*rows, local[0]))
     rims = swap("frames", *rims_to_send(*rows))
-    active, grad_pre, *partial = first_inner(clip_in, cotangent, rows, main, one_fwd, two_adj, bias)
+    active, grad_pre, *partial = first_inner(clip_in, cotangent, rows, main, local, one_fwd, two_adj, bias)
     *sent, terms = first_outer(devices, clip_in, cotangent, rows, rims, partial, one_fwd, two_adj, bias)
 
     terms = lax.all_to_all(terms, AXES, 0, 0, tiled=True)

time: 79.4 us -> 80 us (level)
    pallas_call x10 -> x11, Pallas kernels: 13.3 us -> 13.9 us  [call(): pl.pallas_call(body, out_shape=outs, in_specs=[vmem] * len(args), out_spe...]
where the time goes in v9:
time: 80 us; the launch traced here: 79 us
  starting transfers between devices  30.8 us (38%)
  blocking collectives  21.5 us (27%)
  Pallas kernels  13.9 us (17%)
  waiting for transfers between devices  9.74 us (12%)
  other arithmetic  1.28 us (2%)
  between operations  1.09 us (1%)
    all_to_all x1, blocking collectives, per_device(): terms = lax.all_to_all(terms, AXES, 0, 0, tiled=True)  21.5 us
    ppermute x6, starting transfers between devices, swap(): return (lax.ppermute(odd, axis, pairs_of(count, 1)), even)  16.5 us
    pallas_call x11, Pallas kernels, call(): pl.pallas_call(body, out_shape=outs, in_specs=[vmem] * len(args), out_spe...  13.9 us
    ppermute x6, starting transfers between devices, swap(): even = lax.ppermute(even, axis, pairs_of(count, 0))  10.1 us
    ppermute x6, waiting for transfers between devices, swap(): return (lax.ppermute(odd, axis, pairs_of(count, 1)), even)  5.95 us
    all_to_all x1, starting transfers between devices, per_device(): total = lax.all_to_all(spread, AXES, 0, 0, tiled=True)  4.14 us
    ppermute x6, waiting for transfers between devices, swap(): even = lax.ppermute(even, axis, pairs_of(count, 0))  3.79 us
  transfers between devices with their start and end apart: 13, of which 3 were waited for; matrix products, arithmetic and copies ran while one was open for 0% of the time, Pallas kernels for 11%

profile of v9, /device:TPU:1, one launch (start us, length us, event | category | flops | bytes accessed | tf_op | source)
XLA Modules:
  0.0 79.0 jit_solution(13662393908645347888)
XLA Ops:
  0.7 1.2 %broadcast_select_fusion.2 = (bf16[2,4,1,64,256]{4,3,2,1,0:T(8,128)(2,1)S(1)}, bf16[2,4,1,64,256]{4,3,2,1,0:T(8,128)(2,1)S(1)}, bf16[2,4,1,64,256]{4,3,2,1,0:T(8,128)(2,1)S(1)}) fusion(pred[]{:T(512)S(6)} %eq.9, bf16[1,4,4,64,256]{4,3,2,1,0:T(8,128)(2,1)} %bitcast.8, bf16[1,4,4,64,256]{4,3,2,1,0:T(8,128)(2,1)} %bitcast.9), kind=kLoop, calls=%fused_computation.4 | loop fusion | flops 393216 | bytes 1835009 | tf_op jit(solution)/shard_map/jit(_where)/select_n | solution.py:439
  1.9 0.8 %collective-permute-start = (bf16[2,4,1,64,256]{4,3,2,1,0:T(8,128)(2,1)S(1)}, bf16[2,4,1,64,256]{4,3,2,1,0:T(8,128)(2,1)S(1)}, u32[]{:S(2)}, u32[]{:S(2)}) collective-permute-start(bf16[2,4,1,64,256]{4,3,2,1,0:T(8,128)(2,1)S(1)} %broadcast_select_fusion.3), channel_id=1, source_target_pairs={{1,2},{2,1},{3,4},{4,3},{5,6},{6,5},{7,8},{8,7},{9,10},{10,9},{11,... | collective-permute-start | bytes 786440 | tf_op jit(solution)/shard_map/ppermute | solution.py:426
  2.7 4.6 %collective-permute-start.1 = (bf16[2,4,1,64,256]{4,3,2,1,0:T(8,128)(2,1)S(1)}, bf16[2,4,1,64,256]{4,3,2,1,0:T(8,128)(2,1)S(1)}, u32[]{:S(2)}, u32[]{:S(2)}) collective-permute-start(bf16[2,4,1,64,256]{4,3,2,1,0:T(8,128)(2,1)S(1)} %get-tuple-element.81), channel_id=1, source_target_pairs={{0,1},{1,0},{2,3},{3,2},{4,5},{5,4},{6,7},{7,6},{8,9},{9,8},{10,11... | collective-permute-start | bytes 786440 | tf_op jit(solution)/shard_map/ppermute | solution.py:425
  7.3 1.3 %collective-permute-start.5 = (bf16[2,4,64,256]{3,2,1,0:T(8,128)(2,1)S(1)}, bf16[2,4,64,256]{3,2,1,0:T(8,128)(2,1)S(1)}, u32[]{:S(2)}, u32[]{:S(2)}) collective-permute-start(bf16[2,4,64,256]{3,2,1,0:T(8,128)(2,1)S(1)} %get-tuple-element.84), channel_id=1, source_target_pairs={{0,32},{32,0},{64,96},{96,64},{1,33},{33,1},{65,97},{97,65},{2,34}... | collective-permute-start | bytes 786440 | tf_op jit(solution)/shard_map/ppermute | solution.py:425
  8.7 3.6 %collective-permute-start.4 = (bf16[2,4,64,256]{3,2,1,0:T(8,128)(2,1)S(1)}, bf16[2,4,64,256]{3,2,1,0:T(8,128)(2,1)S(1)}, u32[]{:S(2)}, u32[]{:S(2)}) collective-permute-start(bf16[2,4,64,256]{3,2,1,0:T(8,128)(2,1)S(1)} %get-tuple-element.85), channel_id=1, source_target_pairs={{32,64},{64,32},{33,65},{65,33},{34,66},{66,34},{35,67},{67,35},{3... | collective-permute-start | bytes 786440 | tf_op jit(solution)/shard_map/ppermute | solution.py:426
  12.3 0.6 copy-done.6
  12.9 0.9 %shard_map.92 = (bf16[192,576]{1,0:T(8,128)(2,1)S(1)}, bf16[192,576]{1,0:T(8,128)(2,1)S(1)}, bf16[192,576]{1,0:T(8,128)(2,1)S(1)}, bf16[192,576]{1,0:T(8,128)(2,1)S(1)}, f32[64,1]{1,0:T(8,128)S(1)}) custom-call(bf16[27,64,64]{2,1,0:T(8,128)(2,1)S(1)} %bitcast.10, bf16[27,64,64]{2,1,0:T(8,128)(2,1)S(1)} %bitcast.11, f32[1,64]{1,0:T(1,128)S(1)} %bitcast.12), custom_call_target="tpu_custom_call" | custom-call | bytes 1327616 | tf_op jit(solution)/shard_map/pallas_call | solution.py:321
  13.8 0.9 %shard_map.93 = (f32[2,2,64,256]{3,2,1,0:T(8,128)S(1)}, f32[2,2,64,256]{3,2,1,0:T(8,128)S(1)}) custom-call(bf16[4,4,64,256]{3,2,1,0:T(8,128)(2,1)S(1)} %copy-done.1, bf16[4,4,64,256]{3,2,1,0:T(8,128)(2,1)S(1)} %copy-done, bf16[192,576]{1,0:T(8,128)(2,1)S(1)} %get-tuple-element.43.wp.refs_8_.refs_13_, ...), custom_call_target="tpu_custom_call" | custom-call | flops 452984832 | bytes 2015488 | tf_op jit(solution)/shard_map/pallas_call | solution.py:321
  14.7 3.3 %collective-permute-start.2 = (bf16[2,2,64,256]{3,2,1,0:T(8,128)(2,1)S(1)}, bf16[2,2,64,256]{3,2,1,0:T(8,128)(2,1)S(1)}, u32[]{:S(2)}, u32[]{:S(2)}) collective-permute-start(bf16[2,2,64,256]{3,2,1,0:T(8,128)(2,1)S(1)} %get-tuple-element.49), channel_id=1, source_target_pairs={{32,64},{64,32},{33,65},{65,33},{34,66},{66,34},{35,67},{67,35},{3... | collective-permute-start | bytes 393224 | tf_op jit(solution)/shard_map/ppermute | solution.py:426
  18.1 3.8 %collective-permute-done.4.refs_4_ = bf16[2,4,64,256]{3,2,1,0:T(8,128)(2,1)S(1)} collective-permute-done((bf16[2,4,64,256]{3,2,1,0:T(8,128)(2,1)S(1)}, bf16[2,4,64,256]{3,2,1,0:T(8,128)(2,1)S(1)}, u32[]{:S(2)}, u32[]{:S(2)}) %collective-permute-start.4) | collective-permute-done | bytes 262176 | tf_op jit(solution)/shard_map/ppermute | solution.py:426
  22.0 2.9 %shard_map.95 = (bf16[4,2,64,256]{3,2,1,0:T(8,128)(2,1)S(1)}, bf16[4,2,64,256]{3,2,1,0:T(8,128)(2,1)S(1)}, bf16[2,4,64,256]{3,2,1,0:T(8,128)(2,1)S(1)}, bf16[2,4...) custom-call(bf16[4,4,64,256]{3,2,1,0:T(8,128)(2,1)S(1)} %copy-done.1, ...), custom_call_target="tpu_custom_call" | custom-call | flops 1811939328 | bytes 5587200 | tf_op jit(solution)/shard_map/pallas_call | solution.py:321
  24.9 2.4 %shard_map.96 = (bf16[2,4,64,256]{3,2,1,0:T(8,128)(2,1)S(1)}, bf16[2,4,64,256]{3,2,1,0:T(8,128)(2,1)S(1)}, bf16[128,16,128]{2,1,0:T(8,128)(2,1)S(1)}) custom-call(bf16[2,2,64,256]{3,2,1,0:T(8,128)(2,1)S(1)} %collective-permute-done.2.refs_0_, bf16[2,2,64,256]{3,2,1,0:T(8,128)(2,1)S(1)} %collective-permute-done.3.refs_1_, ...), custom_call_target="tpu_custom_call" | custom-call | flops 1358954496 | bytes 5325056 | tf_op jit(solution)/shard_map/pallas_call | solution.py:321
  27.4 21.5 %all_to_all.10.parts = bf16[128,16,128]{2,1,0:T(8,128)(2,1)S(1)} all-to-all(bf16[128,16,128]{2,1,0:T(8,128)(2,1)S(1)} %get-tuple-element.61), channel_id=1, replica_groups=mesh['frames'=4,'rows'=32] {'frames','rows'}, dimensions={0} | all-to-all | bytes 1048576 | tf_op jit(solution)/shard_map/all_to_all | solution.py:450
  48.9 0.9 %shard_map.97 = bf16[128,16,128]{2,1,0:T(8,128)(2,1)} custom-call(bf16[128,16,128]{2,1,0:T(8,128)(2,1)S(1)} %all_to_all.10.parts), custom_call_target="tpu_custom_call" | custom-call | bytes 1048576 | tf_op jit(solution)/shard_map/pallas_call | solution.py:321
  49.8 4.1 %all-to-all-start.1 = ((bf16[128,16,128]{2,1,0:T(8,128)(2,1)}), bf16[128,16,128]{2,1,0:T(8,128)(2,1)S(1)}, u32[]{:S(2)}, u32[]{:S(2)}) async-start(bf16[128,16,128]{2,1,0:T(8,128)(2,1)} %shard_map.97), calls=%async_computation.1 | async-start | bytes 1048576 | tf_op jit(solution)/shard_map/all_to_all | solution.py:452
  53.9 0.7 collective-permute-start.6
  54.6 3.8 %collective-permute-start.7 = (bf16[2,4,64,256]{3,2,1,0:T(8,128)(2,1)S(1)}, bf16[2,4,64,256]{3,2,1,0:T(8,128)(2,1)S(1)}, u32[]{:S(2)}, u32[]{:S(2)}) collective-permute-start(bf16[2,4,64,256]{3,2,1,0:T(8,128)(2,1)S(1)} %get-tuple-element.60.refs_3_.refs_5_), channel_id=1, source_target_pairs={{0,1},{1,0},{2,3},{3,2},{4,5},{5,4},{6,7},{7,6},{8,9},{9,8},{10,11... | collective-permute-start | bytes 786440 | tf_op jit(solution)/shard_map/ppermute | solution.py:425
  58.5 4.1 %collective-permute-start.10 = (bf16[2,4,64,256]{3,2,1,0:T(8,128)(2,1)S(1)}, bf16[2,4,64,256]{3,2,1,0:T(8,128)(2,1)S(1)}, u32[]{:S(2)}, u32[]{:S(2)}) collective-permute-start(bf16[2,4,64,256]{3,2,1,0:T(8,128)(2,1)S(1)} %get-tuple-element.68), channel_id=1, source_target_pairs={{32,64},{64,32},{33,65},{65,33},{34,66},{66,34},{35,67},{67,35},{3... | collective-permute-start | bytes 786440 | tf_op jit(solution)/shard_map/ppermute | solution.py:426
  62.7 3.8 %collective-permute-done.7.refs_1_.refs_5_.refs_7_ = bf16[2,4,64,256]{3,2,1,0:T(8,128)(2,1)S(1)} collective-permute-done((bf16[2,4,64,256]{3,2,1,0:T(8,128)(2,1)S(1)}, bf16[2,4,64,256]{3,2,1,0:T(8,128)(2,1)S(1)}, u32[]{:S(2)}, u32[]{:S(2)}) %collective-permute-start.7) | collective-permute-done | bytes 262176 | tf_op jit(solution)/shard_map/ppermute | solution.py:425
  66.6 4.1 %collective-permute-start.8 = (bf16[2,2,64,256]{3,2,1,0:T(8,128)(2,1)S(1)}, bf16[2,2,64,256]{3,2,1,0:T(8,128)(2,1)S(1)}, u32[]{:S(2)}, u32[]{:S(2)}) collective-permute-start(bf16[2,2,64,256]{3,2,1,0:T(8,128)(2,1)S(1)} %get-tuple-element.64), channel_id=1, source_target_pairs={{32,64},{64,32},{33,65},{65,33},{34,66},{66,34},{35,67},{67,35},{3... | collective-permute-start | bytes 393224 | tf_op jit(solution)/shard_map/ppermute | solution.py:426
  70.9 2.1 %collective-permute-done.10.refs_6_ = bf16[2,4,64,256]{3,2,1,0:T(8,128)(2,1)S(1)} collective-permute-done((bf16[2,4,64,256]{3,2,1,0:T(8,128)(2,1)S(1)}, bf16[2,4,64,256]{3,2,1,0:T(8,128)(2,1)S(1)}, u32[]{:S(2)}, u32[]{:S(2)}) %collective-permute-start.10) | collective-permute-done | bytes 262176 | tf_op jit(solution)/shard_map/ppermute | solution.py:426
  73.0 2.1 %shard_map.100 = (bf16[4,4,64,256]{3,2,1,0:T(8,128)(2,1)S(1)}, bf16[4,4,64,256]{3,2,1,0:T(8,128)(2,1)S(1)}, bf16[2,4,64,256]{3,2,1,0:T(8,128)(2,1)S(1)}, bf16[2,4,64,256]{3,2,1,0:T(8,128)(2,1)S(1)}) custom-call(bf16[4,2,64,256]{3,2,1,0:T(8,128)(2,1)S(1)} %get-tuple-element.66.refs_0_.refs_2_, bf16[4,2,64,256]{3,2,1,0:T(8,128)(2,1)S(1)} %get-tuple-element.67.refs_1_.refs_3_, ...), custom_call_target="tpu_custom_call" | custom-call | flops 1358954496 | bytes 5160960 | tf_op jit(solution)/shard_map/pallas_call | solution.py:321
  75.2 1.9 %shard_map.101 = (bf16[4,4,64,256]{3,2,1,0:T(8,128)(2,1)}, bf16[4,4,64,256]{3,2,1,0:T(8,128)(2,1)}) custom-call(bf16[2,2,64,256]{3,2,1,0:T(8,128)(2,1)S(1)} %collective-permute-done.8.refs_0_, bf16[2,2,64,256]{3,2,1,0:T(8,128)(2,1)S(1)} %collective-permute-done.9.refs_1_, bf16[4,2,64,256]{3,2,1,0:T(8,128)(2,1)S(1)} %get-tuple-element.66.refs_0_.refs_2_, ...), custom_call_target="tpu_custom_call" | custom-call | flops 452984832 | bytes 5947392 | tf_op jit(solution)/shard_map/pallas_call | solution.py:321
  77.0 1.8 %shard_map.102 = (f32[27,64,64]{2,1,0:T(8,128)}, f32[27,64,64]{2,1,0:T(8,128)}, f32[1,64]{1,0:T(1,128)}) custom-call(bf16[128,16,128]{2,1,0:T(8,128)(2,1)S(1)} %all-to-all-done.1.parts), custom_call_target="tpu_custom_call" | custom-call | bytes 1409280 | tf_op jit(solution)/shard_map/pallas_call | solution.py:321
  (31 shorter events, 0.7 us)
Async XLA Ops:
  0.6 6.6 %copy-start.1 = (bf16[4,4,64,256]{3,2,1,0:T(8,128)(2,1)S(1)}, bf16[4,4,64,256]{3,2,1,0:T(8,128)(2,1)}, u32[]{:S(2)}) copy-start(bf16[4,4,64,256]{3,2,1,0:T(8,128)(2,1)} %refs_12_.1) | copy-start | bytes 1572868
  1.9 5.4 %copy-start = (bf16[4,4,64,256]{3,2,1,0:T(8,128)(2,1)S(1)}, bf16[4,4,64,256]{3,2,1,0:T(8,128)(2,1)}, u32[]{:S(2)}) copy-start(bf16[4,4,64,256]{3,2,1,0:T(8,128)(2,1)} %refs_13_.1) | copy-start | bytes 1572868
  1.9 12.8 %collective-permute-start = (bf16[2,4,1,64,256]{4,3,2,1,0:T(8,128)(2,1)S(1)}, bf16[2,4,1,64,256]{4,3,2,1,0:T(8,128)(2,1)S(1)}, u32[]{:S(2)}, u32[]{:S(2)}) collective-permute-start(bf16[2,4,1,64,256]{4,3,2,1,0:T(8,128)(2,1)S(1)} %broadcast_select_fusion.3), channel_id=1, source_target_pairs={{1,2},{2,1},{3,4},{4,3},{5,6},{6,5},{7,8},{8,7},{9,10},{10,9},{11,... | collective-permute-start | bytes 786440 | tf_op jit(solution)/shard_map/ppermute | solution.py:426
  2.7 12.0 %collective-permute-start.1 = (bf16[2,4,1,64,256]{4,3,2,1,0:T(8,128)(2,1)S(1)}, bf16[2,4,1,64,256]{4,3,2,1,0:T(8,128)(2,1)S(1)}, u32[]{:S(2)}, u32[]{:S(2)}) collective-permute-start(bf16[2,4,1,64,256]{4,3,2,1,0:T(8,128)(2,1)S(1)} %get-tuple-element.81), channel_id=1, source_target_pairs={{0,1},{1,0},{2,3},{3,2},{4,5},{5,4},{6,7},{7,6},{8,9},{9,8},{10,11... | collective-permute-start | bytes 786440 | tf_op jit(solution)/shard_map/ppermute | solution.py:425
  7.3 5.0 %copy-start.2 = (bf16[3,3,3,64,64]{4,3,2,1,0:T(8,128)(2,1)S(1)}, bf16[3,3,3,64,64]{4,3,2,1,0:T(8,128)(2,1)}, u32[]{:S(2)}) copy-start(bf16[3,3,3,64,64]{4,3,2,1,0:T(8,128)(2,1)} %param.6) | copy-start | bytes 663556
  7.3 5.0 %copy-start.3 = (bf16[3,3,3,64,64]{4,3,2,1,0:T(8,128)(2,1)S(1)}, bf16[3,3,3,64,64]{4,3,2,1,0:T(8,128)(2,1)}, u32[]{:S(2)}) copy-start(bf16[3,3,3,64,64]{4,3,2,1,0:T(8,128)(2,1)} %param.8) | copy-start | bytes 663556
  7.3 10.8 %collective-permute-start.5 = (bf16[2,4,64,256]{3,2,1,0:T(8,128)(2,1)S(1)}, bf16[2,4,64,256]{3,2,1,0:T(8,128)(2,1)S(1)}, u32[]{:S(2)}, u32[]{:S(2)}) collective-permute-start(bf16[2,4,64,256]{3,2,1,0:T(8,128)(2,1)S(1)} %get-tuple-element.84), channel_id=1, source_target_pairs={{0,32},{32,0},{64,96},{96,64},{1,33},{33,1},{65,97},{97,65},{2,34}... | collective-permute-start | bytes 786440 | tf_op jit(solution)/shard_map/ppermute | solution.py:425
  8.7 13.3 %collective-permute-start.4 = (bf16[2,4,64,256]{3,2,1,0:T(8,128)(2,1)S(1)}, bf16[2,4,64,256]{3,2,1,0:T(8,128)(2,1)S(1)}, u32[]{:S(2)}, u32[]{:S(2)}) collective-permute-start(bf16[2,4,64,256]{3,2,1,0:T(8,128)(2,1)S(1)} %get-tuple-element.85), channel_id=1, source_target_pairs={{32,64},{64,32},{33,65},{65,33},{34,66},{66,34},{35,67},{67,35},{3... | collective-permute-start | bytes 786440 | tf_op jit(solution)/shard_map/ppermute | solution.py:426
  12.2 0.7 copy-start.6
  13.8 0.9 %copy-start.4 = (bf16[192,576]{1,0:T(8,128)(2,1)}, bf16[192,576]{1,0:T(8,128)(2,1)S(1)}, u32[]{:S(2)}) copy-start(bf16[192,576]{1,0:T(8,128)(2,1)S(1)} %get-tuple-element.70.refs_8_.refs_10_) | copy-start | bytes 663556
  14.7 10.2 %collective-permute-start.2 = (bf16[2,2,64,256]{3,2,1,0:T(8,128)(2,1)S(1)}, bf16[2,2,64,256]{3,2,1,0:T(8,128)(2,1)S(1)}, u32[]{:S(2)}, u32[]{:S(2)}) collective-permute-start(bf16[2,2,64,256]{3,2,1,0:T(8,128)(2,1)S(1)} %get-tuple-element.49), channel_id=1, source_target_pairs={{32,64},{64,32},{33,65},{65,33},{34,66},{66,34},{35,67},{67,35},{3... | collective-permute-start | bytes 393224 | tf_op jit(solution)/shard_map/ppermute | solution.py:426
  18.0 6.9 %collective-permute-start.3 = (bf16[2,2,64,256]{3,2,1,0:T(8,128)(2,1)S(1)}, bf16[2,2,64,256]{3,2,1,0:T(8,128)(2,1)S(1)}, u32[]{:S(2)}, u32[]{:S(2)}) collective-permute-start(bf16[2,2,64,256]{3,2,1,0:T(8,128)(2,1)S(1)} %get-tuple-element.50), channel_id=1, source_target_pairs={{0,32},{32,0},{64,96},{96,64},{1,33},{33,1},{65,97},{97,65},{2,34}... | collective-permute-start | bytes 393224 | tf_op jit(solution)/shard_map/ppermute | solution.py:425
  49.8 27.3 %all-to-all-start.1 = ((bf16[128,16,128]{2,1,0:T(8,128)(2,1)}), bf16[128,16,128]{2,1,0:T(8,128)(2,1)S(1)}, u32[]{:S(2)}, u32[]{:S(2)}) async-start(bf16[128,16,128]{2,1,0:T(8,128)(2,1)} %shard_map.97), calls=%async_computation.1 | async-start | bytes 1048576 | tf_op jit(solution)/shard_map/all_to_all | solution.py:452
  53.9 8.8 %collective-permute-start.6 = (bf16[2,4,64,256]{3,2,1,0:T(8,128)(2,1)S(1)}, bf16[2,4,64,256]{3,2,1,0:T(8,128)(2,1)S(1)}, u32[]{:S(2)}, u32[]{:S(2)}) collective-permute-start(bf16[2,4,64,256]{3,2,1,0:T(8,128)(2,1)S(1)} %get-tuple-element.59.refs_2_.refs_4_), channel_id=1, source_target_pairs={{1,2},{2,1},{3,4},{4,3},{5,6},{6,5},{7,8},{8,7},{9,10},{10,9},{11,... | collective-permute-start | bytes 786440 | tf_op jit(solution)/shard_map/ppermute | solution.py:426
  54.6 11.9 %collective-permute-start.7 = (bf16[2,4,64,256]{3,2,1,0:T(8,128)(2,1)S(1)}, bf16[2,4,64,256]{3,2,1,0:T(8,128)(2,1)S(1)}, u32[]{:S(2)}, u32[]{:S(2)}) collective-permute-start(bf16[2,4,64,256]{3,2,1,0:T(8,128)(2,1)S(1)} %get-tuple-element.60.refs_3_.refs_5_), channel_id=1, source_target_pairs={{0,1},{1,0},{2,3},{3,2},{4,5},{5,4},{6,7},{7,6},{8,9},{9,8},{10,11... | collective-permute-start | bytes 786440 | tf_op jit(solution)/shard_map/ppermute | solution.py:425
  58.5 14.5 %collective-permute-start.10 = (bf16[2,4,64,256]{3,2,1,0:T(8,128)(2,1)S(1)}, bf16[2,4,64,256]{3,2,1,0:T(8,128)(2,1)S(1)}, u32[]{:S(2)}, u32[]{:S(2)}) collective-permute-start(bf16[2,4,64,256]{3,2,1,0:T(8,128)(2,1)S(1)} %get-tuple-element.68), channel_id=1, source_target_pairs={{32,64},{64,32},{33,65},{65,33},{34,66},{66,34},{35,67},{67,35},{3... | collective-permute-start | bytes 786440 | tf_op jit(solution)/shard_map/ppermute | solution.py:426
  62.6 10.4 %copy-start.5 = (bf16[192,576]{1,0:T(8,128)(2,1)S(1)}, bf16[192,576]{1,0:T(8,128)(2,1)}, u32[]{:S(2)}) copy-start(bf16[192,576]{1,0:T(8,128)(2,1)} %copy-done.4) | copy-start | bytes 663556
  62.6 10.4 %collective-permute-start.11 = (bf16[2,4,64,256]{3,2,1,0:T(8,128)(2,1)S(1)}, bf16[2,4,64,256]{3,2,1,0:T(8,128)(2,1)S(1)}, u32[]{:S(2)}, u32[]{:S(2)}) collective-permute-start(bf16[2,4,64,256]{3,2,1,0:T(8,128)(2,1)S(1)} %get-tuple-element.69), channel_id=1, source_target_pairs={{0,32},{32,0},{64,96},{96,64},{1,33},{33,1},{65,97},{97,65},{2,34}... | collective-permute-start | bytes 786440 | tf_op jit(solution)/shard_map/ppermute | solution.py:425
  66.6 8.6 %collective-permute-start.8 = (bf16[2,2,64,256]{3,2,1,0:T(8,128)(2,1)S(1)}, bf16[2,2,64,256]{3,2,1,0:T(8,128)(2,1)S(1)}, u32[]{:S(2)}, u32[]{:S(2)}) collective-permute-start(bf16[2,2,64,256]{3,2,1,0:T(8,128)(2,1)S(1)} %get-tuple-element.64), channel_id=1, source_target_pairs={{32,64},{64,32},{33,65},{65,33},{34,66},{66,34},{35,67},{67,35},{3... | collective-permute-start | bytes 393224 | tf_op jit(solution)/shard_map/ppermute | solution.py:426
  70.7 4.5 %collective-permute-start.9 = (bf16[2,2,64,256]{3,2,1,0:T(8,128)(2,1)S(1)}, bf16[2,2,64,256]{3,2,1,0:T(8,128)(2,1)S(1)}, u32[]{:S(2)}, u32[]{:S(2)}) collective-permute-start(bf16[2,2,64,256]{3,2,1,0:T(8,128)(2,1)S(1)} %get-tuple-element.65), channel_id=1, source_target_pairs={{0,32},{32,0},{64,96},{96,64},{1,33},{33,1},{65,97},{97,65},{2,34}... | collective-permute-start | bytes 393224 | tf_op jit(solution)/shard_map/ppermute | solution.py:425

commit v10 on v9

--- a/solution.py
+++ b/solution.py
@@ -289,32 +289,23 @@
     out[...] = jnp.broadcast_to((sums[0] * scale).astype(out.dtype)[None], out.shape)
 
 
-def unpack_kernel(parts, one_out, two_out, bias, one, two, sems):
+def unpack_kernel(parts, one, two, bias):
     taps, chan = one.shape[0], one.shape[1]
     per = chan // parts.shape[1]
-    third = taps // 3
-    copies = []
-    for t in range(3):
-        group = pl.ds(t * third, third)
-        for k in range(t * third, (t + 1) * third):
-            both = parts[k * per : (k + 1) * per].astype(F32).reshape((chan, 2 * chan))
-            one[k] = both[:, :chan]
-            two[k] = both[:, chan:]
-        for s, (src, dst) in enumerate(((one, one_out), (two, two_out))):
-            copies.append(pltpu.make_async_copy(src.at[group], dst.at[group], sems.at[t, s]))
-            copies[-1].start()
+    for k in range(taps):
+        both = parts[k * per : (k + 1) * per].astype(F32).reshape((chan, 2 * chan))
+        one[k] = both[:, :chan]
+        two[k] = both[:, chan:]
     column = parts[taps * per : (taps + 1) * per].astype(F32).reshape((chan, 2 * chan))[:, :chan]
     keep = lax.broadcasted_iota(jnp.int32, column.shape, 0) == lax.broadcasted_iota(jnp.int32, column.shape, 1)
     bias[...] = jnp.sum(jnp.where(keep, column, 0.0), axis=0, keepdims=True)
-    for copy in copies:
-        copy.wait()
 
 
 def sides():
     return lax.axis_index("rows") % 2, lax.axis_index("frames") % 2
 
 
-def call(kernel, outs, args, flops, scratch=(), sided=True, copied=0):
+def call(kernel, outs, args, flops, scratch=(), sided=True):
     vmem = pl.BlockSpec(memory_space=pltpu.VMEM)
     moved = sum(x.size * x.dtype.itemsize for x in list(args) + list(outs))
     body = (lambda *refs: kernel(sides(), *refs)) if sided else kernel
@@ -322,7 +313,7 @@
         body,
         out_shape=outs,
         in_specs=[vmem] * len(args),
-        out_specs=[pl.BlockSpec(memory_space=pl.ANY)] * copied + [vmem] * (len(outs) - copied),
+        out_specs=[vmem] * len(outs),
         scratch_shapes=scratch,
         compiler_params=pltpu.CompilerParams(vmem_limit_bytes=VMEM_LIMIT),
         cost_estimate=pl.CostEstimate(flops=flops, bytes_accessed=moved, transcendentals=0),
@@ -406,8 +397,7 @@
 
 def unpacked(parts, chan):
     outs = arrays((27, chan, chan), (27, chan, chan), (1, chan), kind=F32)
-    scratch = [pltpu.VMEM((27, chan, chan), F32)] * 2 + [pltpu.SemaphoreType.DMA((3, 2))]
-    return call(unpack_kernel, outs, (parts,), 0, scratch, sided=False, copied=2)
+    return call(unpack_kernel, outs, (parts,), 0, sided=False)
 
 
 AXES = ("frames", "rows")
@@ -432,12 +422,14 @@
     cell_total = (
         frame_count * lax.axis_size("frames") * row_count * lax.axis_size("rows") * col_count
     )
-    row_even, frame_even = (side == 0 for side in sides())
-    both = jnp.stack([clip_in, cotangent])
-    first_row, last_row = both[:, :, :1], both[:, :, -1:]
-    rows = swap(
-        "rows", jnp.where(row_even, first_row, last_row), jnp.where(row_even, last_row, first_row)
-    )
+    row_side, frame_side = sides()
+    frame_even = frame_side == 0
+    over_odd = row_side * (row_count - 1)
+
+    def row_of_both(r):
+        return jnp.stack([lax.dynamic_slice_in_dim(x, r, 1, axis=1) for x in (clip_in, cotangent)])
+
+    rows = swap("rows", row_of_both(over_odd), row_of_both(row_count - 1 - over_odd))
     past, future = clip_in[-2:], cotangent[:2]
     main = swap("frames", jnp.where(frame_even, future, past), jnp.where(frame_even, past, future))
     one_fwd, one_adj, two_fwd, two_adj, bias = flat_weights(kernel_one, kernel_two, bias_one)

time: 80 us -> 79.3 us (level)
  other arithmetic: 1.28 us -> 0.1 us
  local copies, waits for them, and re-layouts: 0.66 us -> 1.81 us
    select_n x2 -> x0, other arithmetic: 1.24 us -> none  [the longest x1 1.21 us: per_device(): jnp.where(row_even, last_row, first_row)]
    another operation x0 -> x1, local copies, waits for them, and re-layouts: none -> 1.14 us  [row_of_both(): jnp.stack([lax.dynamic_slice_in_dim(x, r, 1, axis=1) for x in (clip_in, c...]
where the time goes in v10:
time: 79.3 us; the launch traced here: 78.3 us
  starting transfers between devices  30.8 us (39%)
  blocking collectives  21.5 us (27%)
  Pallas kernels  13.4 us (17%)
  waiting for transfers between devices  9.74 us (12%)
  local copies, waits for them, and re-layouts  1.81 us (2%)
  between operations  0.95 us (1%)
    all_to_all x1, blocking collectives, per_device(): terms = lax.all_to_all(terms, AXES, 0, 0, tiled=True)  21.5 us
    ppermute x6, starting transfers between devices, swap(): return (lax.ppermute(odd, axis, pairs_of(count, 1)), even)  16.5 us
    pallas_call x11, Pallas kernels, call(): pl.pallas_call(body, out_shape=outs, in_specs=[vmem] * len(args), out_spe...  13.4 us
    ppermute x6, starting transfers between devices, swap(): even = lax.ppermute(even, axis, pairs_of(count, 0))  10.1 us
    ppermute x6, waiting for transfers between devices, swap(): return (lax.ppermute(odd, axis, pairs_of(count, 1)), even)  5.95 us
    all_to_all x1, starting transfers between devices, per_device(): total = lax.all_to_all(spread, AXES, 0, 0, tiled=True)  4.14 us
    ppermute x6, waiting for transfers between devices, swap(): even = lax.ppermute(even, axis, pairs_of(count, 0))  3.79 us
  transfers between devices with their start and end apart: 13, of which 3 were waited for; matrix products, arithmetic and copies ran while one was open for 0% of the time, Pallas kernels for 11%

profile of v10, /device:TPU:1, one launch (start us, length us, event | category | flops | bytes accessed | tf_op | source)
XLA Modules:
  0.0 78.3 jit_solution(12628004676068704442)
XLA Ops:
  0.7 1.1 %dynamic-slice_bitcast_fusion = (bf16[1,4,1,64,256]{4,3,2,1,0:T(8,128)(2,1)S(1)}, bf16[1,4,1,64,256]{4,3,2,1,0:T(8,128)(2,1)S(1)}, bf16[1,4,1,64,256]{4,3,2,1,0:T(8,128)(2,1)S(1)}, bf16[1,4,1,64,256]{4,3,2,1,0:T(8,128)(2,1)S(1)}) fusion(bf16[4,4,64,256]{3,2,1,0:T(8,128)(2,1)} %refs_13_.1, s32[]{:T(128)S(6)} %select_n.33, s32[]{:T(128)S(6)} %select_n.32, ...), kind=kLoop, calls=%fused_computation.4 | loop fusion | bytes 1048584 | tf_op jit(solution)/shard_map/stack | solution.py:430
  1.9 0.8 %collective-permute-start = (bf16[2,4,1,64,256]{4,3,2,1,0:T(8,128)(2,1)S(1)}, bf16[2,4,1,64,256]{4,3,2,1,0:T(8,128)(2,1)S(1)}, u32[]{:S(2)}, u32[]{:S(2)}) collective-permute-start(bf16[2,4,1,64,256]{4,3,2,1,0:T(8,128)(2,1)S(1)} %pad_maximum_fusion), channel_id=1, source_target_pairs={{1,2},{2,1},{3,4},{4,3},{5,6},{6,5},{7,8},{8,7},{9,10},{10,9},{11,... | collective-permute-start | bytes 786440 | tf_op jit(solution)/shard_map/ppermute | solution.py:416
  2.7 4.6 %collective-permute-start.1 = (bf16[2,4,1,64,256]{4,3,2,1,0:T(8,128)(2,1)S(1)}, bf16[2,4,1,64,256]{4,3,2,1,0:T(8,128)(2,1)S(1)}, u32[]{:S(2)}, u32[]{:S(2)}) collective-permute-start(bf16[2,4,1,64,256]{4,3,2,1,0:T(8,128)(2,1)S(1)} %pad_maximum_fusion.1), channel_id=1, source_target_pairs={{0,1},{1,0},{2,3},{3,2},{4,5},{5,4},{6,7},{7,6},{8,9},{9,8},{10,11... | collective-permute-start | bytes 786440 | tf_op jit(solution)/shard_map/ppermute | solution.py:415
  7.3 1.3 %collective-permute-start.5 = (bf16[2,4,64,256]{3,2,1,0:T(8,128)(2,1)S(1)}, bf16[2,4,64,256]{3,2,1,0:T(8,128)(2,1)S(1)}, u32[]{:S(2)}, u32[]{:S(2)}) collective-permute-start(bf16[2,4,64,256]{3,2,1,0:T(8,128)(2,1)S(1)} %get-tuple-element.81), channel_id=1, source_target_pairs={{0,32},{32,0},{64,96},{96,64},{1,33},{33,1},{65,97},{97,65},{2,34}... | collective-permute-start | bytes 786440 | tf_op jit(solution)/shard_map/ppermute | solution.py:415
  8.6 3.6 %collective-permute-start.4 = (bf16[2,4,64,256]{3,2,1,0:T(8,128)(2,1)S(1)}, bf16[2,4,64,256]{3,2,1,0:T(8,128)(2,1)S(1)}, u32[]{:S(2)}, u32[]{:S(2)}) collective-permute-start(bf16[2,4,64,256]{3,2,1,0:T(8,128)(2,1)S(1)} %get-tuple-element.82), channel_id=1, source_target_pairs={{32,64},{64,32},{33,65},{65,33},{34,66},{66,34},{35,67},{67,35},{3... | collective-permute-start | bytes 786440 | tf_op jit(solution)/shard_map/ppermute | solution.py:416
  12.3 0.6 copy-done.6
  12.9 0.9 %shard_map.92 = (bf16[192,576]{1,0:T(8,128)(2,1)S(1)}, bf16[192,576]{1,0:T(8,128)(2,1)S(1)}, bf16[192,576]{1,0:T(8,128)(2,1)S(1)}, bf16[192,576]{1,0:T(8,128)(2,1)S(1)}, f32[64,1]{1,0:T(8,128)S(1)}) custom-call(bf16[27,64,64]{2,1,0:T(8,128)(2,1)S(1)} %bitcast.14, bf16[27,64,64]{2,1,0:T(8,128)(2,1)S(1)} %bitcast.15, f32[1,64]{1,0:T(1,128)S(1)} %bitcast.16), custom_call_target="tpu_custom_call" | custom-call | bytes 1327616 | tf_op jit(solution)/shard_map/pallas_call | solution.py:312
  13.8 0.9 %shard_map.93 = (f32[2,2,64,256]{3,2,1,0:T(8,128)S(1)}, f32[2,2,64,256]{3,2,1,0:T(8,128)S(1)}) custom-call(bf16[4,4,64,256]{3,2,1,0:T(8,128)(2,1)S(1)} %copy-done.1, bf16[4,4,64,256]{3,2,1,0:T(8,128)(2,1)S(1)} %copy-done, bf16[192,576]{1,0:T(8,128)(2,1)S(1)} %get-tuple-element.43.wp.refs_8_.refs_13_, ...), custom_call_target="tpu_custom_call" | custom-call | flops 452984832 | bytes 2015488 | tf_op jit(solution)/shard_map/pallas_call | solution.py:312
  14.7 3.3 %collective-permute-start.2 = (bf16[2,2,64,256]{3,2,1,0:T(8,128)(2,1)S(1)}, bf16[2,2,64,256]{3,2,1,0:T(8,128)(2,1)S(1)}, u32[]{:S(2)}, u32[]{:S(2)}) collective-permute-start(bf16[2,2,64,256]{3,2,1,0:T(8,128)(2,1)S(1)} %get-tuple-element.49), channel_id=1, source_target_pairs={{32,64},{64,32},{33,65},{65,33},{34,66},{66,34},{35,67},{67,35},{3... | collective-permute-start | bytes 393224 | tf_op jit(solution)/shard_map/ppermute | solution.py:416
  18.1 3.8 %collective-permute-done.4.refs_4_ = bf16[2,4,64,256]{3,2,1,0:T(8,128)(2,1)S(1)} collective-permute-done((bf16[2,4,64,256]{3,2,1,0:T(8,128)(2,1)S(1)}, bf16[2,4,64,256]{3,2,1,0:T(8,128)(2,1)S(1)}, u32[]{:S(2)}, u32[]{:S(2)}) %collective-permute-start.4) | collective-permute-done | bytes 262176 | tf_op jit(solution)/shard_map/ppermute | solution.py:416
  21.9 2.9 %shard_map.95 = (bf16[4,2,64,256]{3,2,1,0:T(8,128)(2,1)S(1)}, bf16[4,2,64,256]{3,2,1,0:T(8,128)(2,1)S(1)}, bf16[2,4,64,256]{3,2,1,0:T(8,128)(2,1)S(1)}, bf16[2,4...) custom-call(bf16[4,4,64,256]{3,2,1,0:T(8,128)(2,1)S(1)} %copy-done.1, ...), custom_call_target="tpu_custom_call" | custom-call | flops 1811939328 | bytes 5587200 | tf_op jit(solution)/shard_map/pallas_call | solution.py:312
  24.9 2.4 %shard_map.96 = (bf16[2,4,64,256]{3,2,1,0:T(8,128)(2,1)S(1)}, bf16[2,4,64,256]{3,2,1,0:T(8,128)(2,1)S(1)}, bf16[128,16,128]{2,1,0:T(8,128)(2,1)S(1)}) custom-call(bf16[2,2,64,256]{3,2,1,0:T(8,128)(2,1)S(1)} %collective-permute-done.2.refs_0_, bf16[2,2,64,256]{3,2,1,0:T(8,128)(2,1)S(1)} %collective-permute-done.3.refs_1_, ...), custom_call_target="tpu_custom_call" | custom-call | flops 1358954496 | bytes 5325056 | tf_op jit(solution)/shard_map/pallas_call | solution.py:312
  27.3 21.5 %all_to_all.10.parts = bf16[128,16,128]{2,1,0:T(8,128)(2,1)S(1)} all-to-all(bf16[128,16,128]{2,1,0:T(8,128)(2,1)S(1)} %get-tuple-element.61), channel_id=1, replica_groups=mesh['frames'=4,'rows'=32] {'frames','rows'}, dimensions={0} | all-to-all | bytes 1048576 | tf_op jit(solution)/shard_map/all_to_all | solution.py:442
  48.8 0.9 %shard_map.97 = bf16[128,16,128]{2,1,0:T(8,128)(2,1)} custom-call(bf16[128,16,128]{2,1,0:T(8,128)(2,1)S(1)} %all_to_all.10.parts), custom_call_target="tpu_custom_call" | custom-call | bytes 1048576 | tf_op jit(solution)/shard_map/pallas_call | solution.py:312
  49.7 4.1 %all-to-all-start.1 = ((bf16[128,16,128]{2,1,0:T(8,128)(2,1)}), bf16[128,16,128]{2,1,0:T(8,128)(2,1)S(1)}, u32[]{:S(2)}, u32[]{:S(2)}) async-start(bf16[128,16,128]{2,1,0:T(8,128)(2,1)} %shard_map.97), calls=%async_computation.1 | async-start | bytes 1048576 | tf_op jit(solution)/shard_map/all_to_all | solution.py:444
  53.9 0.7 collective-permute-start.6
  54.6 3.8 %collective-permute-start.7 = (bf16[2,4,64,256]{3,2,1,0:T(8,128)(2,1)S(1)}, bf16[2,4,64,256]{3,2,1,0:T(8,128)(2,1)S(1)}, u32[]{:S(2)}, u32[]{:S(2)}) collective-permute-start(bf16[2,4,64,256]{3,2,1,0:T(8,128)(2,1)S(1)} %get-tuple-element.60.refs_3_.refs_5_), channel_id=1, source_target_pairs={{0,1},{1,0},{2,3},{3,2},{4,5},{5,4},{6,7},{7,6},{8,9},{9,8},{10,11... | collective-permute-start | bytes 786440 | tf_op jit(solution)/shard_map/ppermute | solution.py:415
  58.5 4.1 %collective-permute-start.10 = (bf16[2,4,64,256]{3,2,1,0:T(8,128)(2,1)S(1)}, bf16[2,4,64,256]{3,2,1,0:T(8,128)(2,1)S(1)}, u32[]{:S(2)}, u32[]{:S(2)}) collective-permute-start(bf16[2,4,64,256]{3,2,1,0:T(8,128)(2,1)S(1)} %get-tuple-element.68), channel_id=1, source_target_pairs={{32,64},{64,32},{33,65},{65,33},{34,66},{66,34},{35,67},{67,35},{3... | collective-permute-start | bytes 786440 | tf_op jit(solution)/shard_map/ppermute | solution.py:416
  62.7 3.8 %collective-permute-done.7.refs_1_.refs_5_.refs_7_ = bf16[2,4,64,256]{3,2,1,0:T(8,128)(2,1)S(1)} collective-permute-done((bf16[2,4,64,256]{3,2,1,0:T(8,128)(2,1)S(1)}, bf16[2,4,64,256]{3,2,1,0:T(8,128)(2,1)S(1)}, u32[]{:S(2)}, u32[]{:S(2)}) %collective-permute-start.7) | collective-permute-done | bytes 262176 | tf_op jit(solution)/shard_map/ppermute | solution.py:415
  66.5 4.1 %collective-permute-start.8 = (bf16[2,2,64,256]{3,2,1,0:T(8,128)(2,1)S(1)}, bf16[2,2,64,256]{3,2,1,0:T(8,128)(2,1)S(1)}, u32[]{:S(2)}, u32[]{:S(2)}) collective-permute-start(bf16[2,2,64,256]{3,2,1,0:T(8,128)(2,1)S(1)} %get-tuple-element.64), channel_id=1, source_target_pairs={{32,64},{64,32},{33,65},{65,33},{34,66},{66,34},{35,67},{67,35},{3... | collective-permute-start | bytes 393224 | tf_op jit(solution)/shard_map/ppermute | solution.py:416
  70.9 2.1 %collective-permute-done.10.refs_6_ = bf16[2,4,64,256]{3,2,1,0:T(8,128)(2,1)S(1)} collective-permute-done((bf16[2,4,64,256]{3,2,1,0:T(8,128)(2,1)S(1)}, bf16[2,4,64,256]{3,2,1,0:T(8,128)(2,1)S(1)}, u32[]{:S(2)}, u32[]{:S(2)}) %collective-permute-start.10) | collective-permute-done | bytes 262176 | tf_op jit(solution)/shard_map/ppermute | solution.py:416
  73.0 2.1 %shard_map.100 = (bf16[4,4,64,256]{3,2,1,0:T(8,128)(2,1)S(1)}, bf16[4,4,64,256]{3,2,1,0:T(8,128)(2,1)S(1)}, bf16[2,4,64,256]{3,2,1,0:T(8,128)(2,1)S(1)}, bf16[2,4,64,256]{3,2,1,0:T(8,128)(2,1)S(1)}) custom-call(bf16[4,2,64,256]{3,2,1,0:T(8,128)(2,1)S(1)} %get-tuple-element.66.refs_0_.refs_2_, bf16[4,2,64,256]{3,2,1,0:T(8,128)(2,1)S(1)} %get-tuple-element.67.refs_1_.refs_3_, ...), custom_call_target="tpu_custom_call" | custom-call | flops 1358954496 | bytes 5160960 | tf_op jit(solution)/shard_map/pallas_call | solution.py:312
  75.1 1.9 %shard_map.101 = (bf16[4,4,64,256]{3,2,1,0:T(8,128)(2,1)}, bf16[4,4,64,256]{3,2,1,0:T(8,128)(2,1)}) custom-call(bf16[2,2,64,256]{3,2,1,0:T(8,128)(2,1)S(1)} %collective-permute-done.8.refs_0_, bf16[2,2,64,256]{3,2,1,0:T(8,128)(2,1)S(1)} %collective-permute-done.9.refs_1_, bf16[4,2,64,256]{3,2,1,0:T(8,128)(2,1)S(1)} %get-tuple-element.66.refs_0_.refs_2_, ...), custom_call_target="tpu_custom_call" | custom-call | flops 452984832 | bytes 5947392 | tf_op jit(solution)/shard_map/pallas_call | solution.py:312
  77.0 1.3 %shard_map.102 = (f32[27,64,64]{2,1,0:T(8,128)}, f32[27,64,64]{2,1,0:T(8,128)}, f32[1,64]{1,0:T(1,128)}) custom-call(bf16[128,16,128]{2,1,0:T(8,128)(2,1)S(1)} %all-to-all-done.1.parts), custom_call_target="tpu_custom_call" | custom-call | bytes 1409280 | tf_op jit(solution)/shard_map/pallas_call | solution.py:312
  (32 shorter events, 0.7 us)
Async XLA Ops:
  1.8 5.5 %copy-start = (bf16[4,4,64,256]{3,2,1,0:T(8,128)(2,1)S(1)}, bf16[4,4,64,256]{3,2,1,0:T(8,128)(2,1)}, u32[]{:S(2)}) copy-start(bf16[4,4,64,256]{3,2,1,0:T(8,128)(2,1)} %refs_13_.1) | copy-start | bytes 1572868
  1.8 5.5 %copy-start.1 = (bf16[4,4,64,256]{3,2,1,0:T(8,128)(2,1)S(1)}, bf16[4,4,64,256]{3,2,1,0:T(8,128)(2,1)}, u32[]{:S(2)}) copy-start(bf16[4,4,64,256]{3,2,1,0:T(8,128)(2,1)} %refs_12_.1) | copy-start | bytes 1572868
  1.9 12.8 %collective-permute-start = (bf16[2,4,1,64,256]{4,3,2,1,0:T(8,128)(2,1)S(1)}, bf16[2,4,1,64,256]{4,3,2,1,0:T(8,128)(2,1)S(1)}, u32[]{:S(2)}, u32[]{:S(2)}) collective-permute-start(bf16[2,4,1,64,256]{4,3,2,1,0:T(8,128)(2,1)S(1)} %pad_maximum_fusion), channel_id=1, source_target_pairs={{1,2},{2,1},{3,4},{4,3},{5,6},{6,5},{7,8},{8,7},{9,10},{10,9},{11,... | collective-permute-start | bytes 786440 | tf_op jit(solution)/shard_map/ppermute | solution.py:416
  2.7 12.0 %collective-permute-start.1 = (bf16[2,4,1,64,256]{4,3,2,1,0:T(8,128)(2,1)S(1)}, bf16[2,4,1,64,256]{4,3,2,1,0:T(8,128)(2,1)S(1)}, u32[]{:S(2)}, u32[]{:S(2)}) collective-permute-start(bf16[2,4,1,64,256]{4,3,2,1,0:T(8,128)(2,1)S(1)} %pad_maximum_fusion.1), channel_id=1, source_target_pairs={{0,1},{1,0},{2,3},{3,2},{4,5},{5,4},{6,7},{7,6},{8,9},{9,8},{10,11... | collective-permute-start | bytes 786440 | tf_op jit(solution)/shard_map/ppermute | solution.py:415
  7.3 5.0 %copy-start.2 = (bf16[3,3,3,64,64]{4,3,2,1,0:T(8,128)(2,1)S(1)}, bf16[3,3,3,64,64]{4,3,2,1,0:T(8,128)(2,1)}, u32[]{:S(2)}) copy-start(bf16[3,3,3,64,64]{4,3,2,1,0:T(8,128)(2,1)} %param.6) | copy-start | bytes 663556
  7.3 5.0 %copy-start.3 = (bf16[3,3,3,64,64]{4,3,2,1,0:T(8,128)(2,1)S(1)}, bf16[3,3,3,64,64]{4,3,2,1,0:T(8,128)(2,1)}, u32[]{:S(2)}) copy-start(bf16[3,3,3,64,64]{4,3,2,1,0:T(8,128)(2,1)} %param.8) | copy-start | bytes 663556
  7.3 10.8 %collective-permute-start.5 = (bf16[2,4,64,256]{3,2,1,0:T(8,128)(2,1)S(1)}, bf16[2,4,64,256]{3,2,1,0:T(8,128)(2,1)S(1)}, u32[]{:S(2)}, u32[]{:S(2)}) collective-permute-start(bf16[2,4,64,256]{3,2,1,0:T(8,128)(2,1)S(1)} %get-tuple-element.81), channel_id=1, source_target_pairs={{0,32},{32,0},{64,96},{96,64},{1,33},{33,1},{65,97},{97,65},{2,34}... | collective-permute-start | bytes 786440 | tf_op jit(solution)/shard_map/ppermute | solution.py:415
  8.6 13.3 %collective-permute-start.4 = (bf16[2,4,64,256]{3,2,1,0:T(8,128)(2,1)S(1)}, bf16[2,4,64,256]{3,2,1,0:T(8,128)(2,1)S(1)}, u32[]{:S(2)}, u32[]{:S(2)}) collective-permute-start(bf16[2,4,64,256]{3,2,1,0:T(8,128)(2,1)S(1)} %get-tuple-element.82), channel_id=1, source_target_pairs={{32,64},{64,32},{33,65},{65,33},{34,66},{66,34},{35,67},{67,35},{3... | collective-permute-start | bytes 786440 | tf_op jit(solution)/shard_map/ppermute | solution.py:416
  12.2 0.7 copy-start.6
  13.7 0.9 %copy-start.4 = (bf16[192,576]{1,0:T(8,128)(2,1)}, bf16[192,576]{1,0:T(8,128)(2,1)S(1)}, u32[]{:S(2)}) copy-start(bf16[192,576]{1,0:T(8,128)(2,1)S(1)} %get-tuple-element.70.refs_8_.refs_10_) | copy-start | bytes 663556
  14.7 10.2 %collective-permute-start.2 = (bf16[2,2,64,256]{3,2,1,0:T(8,128)(2,1)S(1)}, bf16[2,2,64,256]{3,2,1,0:T(8,128)(2,1)S(1)}, u32[]{:S(2)}, u32[]{:S(2)}) collective-permute-start(bf16[2,2,64,256]{3,2,1,0:T(8,128)(2,1)S(1)} %get-tuple-element.49), channel_id=1, source_target_pairs={{32,64},{64,32},{33,65},{65,33},{34,66},{66,34},{35,67},{67,35},{3... | collective-permute-start | bytes 393224 | tf_op jit(solution)/shard_map/ppermute | solution.py:416
  18.0 6.9 %collective-permute-start.3 = (bf16[2,2,64,256]{3,2,1,0:T(8,128)(2,1)S(1)}, bf16[2,2,64,256]{3,2,1,0:T(8,128)(2,1)S(1)}, u32[]{:S(2)}, u32[]{:S(2)}) collective-permute-start(bf16[2,2,64,256]{3,2,1,0:T(8,128)(2,1)S(1)} %get-tuple-element.50), channel_id=1, source_target_pairs={{0,32},{32,0},{64,96},{96,64},{1,33},{33,1},{65,97},{97,65},{2,34}... | collective-permute-start | bytes 393224 | tf_op jit(solution)/shard_map/ppermute | solution.py:415
  49.7 27.3 %all-to-all-start.1 = ((bf16[128,16,128]{2,1,0:T(8,128)(2,1)}), bf16[128,16,128]{2,1,0:T(8,128)(2,1)S(1)}, u32[]{:S(2)}, u32[]{:S(2)}) async-start(bf16[128,16,128]{2,1,0:T(8,128)(2,1)} %shard_map.97), calls=%async_computation.1 | async-start | bytes 1048576 | tf_op jit(solution)/shard_map/all_to_all | solution.py:444
  53.9 8.8 %collective-permute-start.6 = (bf16[2,4,64,256]{3,2,1,0:T(8,128)(2,1)S(1)}, bf16[2,4,64,256]{3,2,1,0:T(8,128)(2,1)S(1)}, u32[]{:S(2)}, u32[]{:S(2)}) collective-permute-start(bf16[2,4,64,256]{3,2,1,0:T(8,128)(2,1)S(1)} %get-tuple-element.59.refs_2_.refs_4_), channel_id=1, source_target_pairs={{1,2},{2,1},{3,4},{4,3},{5,6},{6,5},{7,8},{8,7},{9,10},{10,9},{11,... | collective-permute-start | bytes 786440 | tf_op jit(solution)/shard_map/ppermute | solution.py:416
  54.6 11.9 %collective-permute-start.7 = (bf16[2,4,64,256]{3,2,1,0:T(8,128)(2,1)S(1)}, bf16[2,4,64,256]{3,2,1,0:T(8,128)(2,1)S(1)}, u32[]{:S(2)}, u32[]{:S(2)}) collective-permute-start(bf16[2,4,64,256]{3,2,1,0:T(8,128)(2,1)S(1)} %get-tuple-element.60.refs_3_.refs_5_), channel_id=1, source_target_pairs={{0,1},{1,0},{2,3},{3,2},{4,5},{5,4},{6,7},{7,6},{8,9},{9,8},{10,11... | collective-permute-start | bytes 786440 | tf_op jit(solution)/shard_map/ppermute | solution.py:415
  58.5 14.5 %collective-permute-start.10 = (bf16[2,4,64,256]{3,2,1,0:T(8,128)(2,1)S(1)}, bf16[2,4,64,256]{3,2,1,0:T(8,128)(2,1)S(1)}, u32[]{:S(2)}, u32[]{:S(2)}) collective-permute-start(bf16[2,4,64,256]{3,2,1,0:T(8,128)(2,1)S(1)} %get-tuple-element.68), channel_id=1, source_target_pairs={{32,64},{64,32},{33,65},{65,33},{34,66},{66,34},{35,67},{67,35},{3... | collective-permute-start | bytes 786440 | tf_op jit(solution)/shard_map/ppermute | solution.py:416
  62.6 10.4 %copy-start.5 = (bf16[192,576]{1,0:T(8,128)(2,1)S(1)}, bf16[192,576]{1,0:T(8,128)(2,1)}, u32[]{:S(2)}) copy-start(bf16[192,576]{1,0:T(8,128)(2,1)} %copy-done.4) | copy-start | bytes 663556
  62.6 10.4 %collective-permute-start.11 = (bf16[2,4,64,256]{3,2,1,0:T(8,128)(2,1)S(1)}, bf16[2,4,64,256]{3,2,1,0:T(8,128)(2,1)S(1)}, u32[]{:S(2)}, u32[]{:S(2)}) collective-permute-start(bf16[2,4,64,256]{3,2,1,0:T(8,128)(2,1)S(1)} %get-tuple-element.69), channel_id=1, source_target_pairs={{0,32},{32,0},{64,96},{96,64},{1,33},{33,1},{65,97},{97,65},{2,34}... | collective-permute-start | bytes 786440 | tf_op jit(solution)/shard_map/ppermute | solution.py:415
  66.5 8.6 %collective-permute-start.8 = (bf16[2,2,64,256]{3,2,1,0:T(8,128)(2,1)S(1)}, bf16[2,2,64,256]{3,2,1,0:T(8,128)(2,1)S(1)}, u32[]{:S(2)}, u32[]{:S(2)}) collective-permute-start(bf16[2,2,64,256]{3,2,1,0:T(8,128)(2,1)S(1)} %get-tuple-element.64), channel_id=1, source_target_pairs={{32,64},{64,32},{33,65},{65,33},{34,66},{66,34},{35,67},{67,35},{3... | collective-permute-start | bytes 393224 | tf_op jit(solution)/shard_map/ppermute | solution.py:416
  70.6 4.5 %collective-permute-start.9 = (bf16[2,2,64,256]{3,2,1,0:T(8,128)(2,1)S(1)}, bf16[2,2,64,256]{3,2,1,0:T(8,128)(2,1)S(1)}, u32[]{:S(2)}, u32[]{:S(2)}) collective-permute-start(bf16[2,2,64,256]{3,2,1,0:T(8,128)(2,1)S(1)} %get-tuple-element.65), channel_id=1, source_target_pairs={{0,32},{32,0},{64,96},{96,64},{1,33},{33,1},{65,97},{97,65},{2,34}... | collective-permute-start | bytes 393224 | tf_op jit(solution)/shard_map/ppermute | solution.py:415
